TPU v7x, 32 devices: a whole 2x2x4 slice. The times are simulated.
32 devices in a mesh: pairs: 8 (over z, y), win: 4 (over x, core).
Axes of the slice: x: 2, y: 2, z: 4, core: 2. Of those that a mesh axis runs over, the one named last changes fastest.
Arguments:
- traces: bfloat16 [128, 128, 4096], P('win', 'pairs'), may hold values from -16 to 16, as said below
- taps: float32 [129], replicated, may hold values from -0.5 to 0.5
- neighbours: int32 [128, 64], P('pairs'), may hold values from 0 to 127, as said below
- valid: int32 [128, 64], P('pairs'), may hold values 0 or 1
Outputs:
- stacks: float32 [128, 64, 1024], P('pairs', 'win')
Inputs may be any that keep to these rules, and one draw needn't show every extreme that they name: `neighbours`: every listed neighbour of a station of tile t (stations t * 16 to (t + 1) * 16 - 1) lies in tile t - 1, t or t + 1. `traces`: Station-wise amplitudes differ between stations.
All inputs are finite; a program needn't handle non-finite values. No bound on the sum of `valid` on one device may be relied on, other than what follows from the above.
Results may differ from a plain program's by a relative error of at most 0.0014.
Values may be sent and summed in bfloat16 or wider, within the bound.
No kernel may reach another device: no remote copies, remote signals or barrier semaphores. Data moves between devices by JAX's collectives and lax.ppermute only.
A program may use at most 128 MiB of HBM per device.

v0:
```python
import math

import jax
import jax.numpy as jnp
from jax import lax
from jax.sharding import PartitionSpec as P

SAMPLES = 4096
BINS = 512
BAND = 64
LOW_BIN = 64
LAGS = 1024
TAPS = 129


epsilon = 1e-06


def with_halo(x, sides, width):
    for axis, dim in sides:
        count, length = (lax.axis_size(axis), x.shape[dim])
        up = [(i, (i + 1) % count) for i in range(count - 1)]
        down = [(j, i) for i, j in up]
        last = lax.slice_in_dim(x, length - width, length, axis=dim)
        leading = lax.slice_in_dim(x, 0, width, axis=dim)
        before = lax.ppermute(last, axis, up)
        after = lax.ppermute(leading, axis, down)
        x = jnp.concatenate([before, x, after], axis=dim)
    return x


def phase_angles(times, frequency, samples):
    phases = times[:, None] * frequency[None, :] % samples
    return phases.astype(jnp.float32) * (2.0 * math.pi / samples)


def whiten(raw_rows, resp_re, resp_im):
    bins = raw_rows.shape[1] // 2
    real_part = raw_rows[:, :bins].reshape(-1, bins // BAND, BAND)
    imag_part = raw_rows[:, bins:].reshape(-1, bins // BAND, BAND)
    scaling = lax.rsqrt(
        jnp.mean(real_part * real_part + imag_part * imag_part, -1, keepdims=True) + epsilon
    )
    real_white = (real_part * scaling).reshape(-1, bins)
    imag_white = (imag_part * scaling).reshape(-1, bins)
    out_real = real_white * resp_re - imag_white * resp_im
    out_imag = real_white * resp_im + imag_white * resp_re
    return jnp.concatenate([out_real, out_imag], 1).astype(jnp.bfloat16)


def band_spectra(windows_raw, resp_re, resp_im):
    count_windows, count_nodes, samples = windows_raw.shape
    flat_rows = windows_raw.reshape(count_windows * count_nodes, samples)
    frequency = LOW_BIN + jnp.arange(BINS, dtype=jnp.int32)
    blocksize = min(1024, samples)
    totals = jnp.zeros((flat_rows.shape[0], 2 * BINS), jnp.float32)
    for offset in range(0, samples, blocksize):
        angles = phase_angles(offset + jnp.arange(blocksize, dtype=jnp.int32), frequency, samples)
        tables = jnp.concatenate([jnp.cos(angles), -jnp.sin(angles)], 1).astype(jnp.bfloat16)
        totals = totals + jnp.dot(
            flat_rows[:, offset : offset + blocksize], tables, preferred_element_type=jnp.float32
        )
    return whiten(totals, resp_re, resp_im).reshape(count_windows, count_nodes, 2 * BINS)


def all_cross(own_spectra, pooled):
    a_real = own_spectra[:, :, :BINS]
    a_imag = own_spectra[:, :, BINS:]
    b_real = pooled[:, :, :BINS]
    b_imag = pooled[:, :, BINS:]
    real_part = jnp.einsum("wnf,wmf->nmf", a_real, b_real, preferred_element_type=jnp.float32)
    real_part = real_part + jnp.einsum(
        "wnf,wmf->nmf", a_imag, b_imag, preferred_element_type=jnp.float32
    )
    imag_part = jnp.einsum("wnf,wmf->nmf", a_imag, b_real, preferred_element_type=jnp.float32)
    imag_part = imag_part - jnp.einsum(
        "wnf,wmf->nmf", a_real, b_imag, preferred_element_type=jnp.float32
    )
    return jnp.concatenate([real_part, imag_part], 2)


def inverse_lags(stack):
    bins = stack.shape[-1] // 2
    frequency = LOW_BIN + jnp.arange(bins, dtype=jnp.int32)
    lag_index = (jnp.arange(LAGS, dtype=jnp.int32) - LAGS // 2) % SAMPLES
    angles = phase_angles(frequency, lag_index, SAMPLES)
    flat_rows = stack.reshape(-1, 2 * bins)
    result = jnp.dot(flat_rows[:, :bins], jnp.cos(angles), precision=lax.Precision.HIGHEST)
    result = result - jnp.dot(flat_rows[:, bins:], jnp.sin(angles), precision=lax.Precision.HIGHEST)
    return result.reshape(stack.shape[:-1] + (LAGS,))


def per_device(traces, taps, neighbours, valid):
    windows_here = traces.shape[0]
    nodes_here = traces.shape[1]
    frequency = LOW_BIN + jnp.arange(BINS, dtype=jnp.int32)
    tap_angles = phase_angles(jnp.arange(TAPS, dtype=jnp.int32), frequency, SAMPLES)
    resp_re = jnp.dot(taps, jnp.cos(tap_angles), precision=lax.Precision.HIGHEST)
    resp_im = -jnp.dot(taps, jnp.sin(tap_angles), precision=lax.Precision.HIGHEST)
    pooled_raw = with_halo(traces, (("pairs", 1),), nodes_here)
    pooled = band_spectra(pooled_raw, resp_re, resp_im)
    own_spectra = pooled[:, nodes_here : 2 * nodes_here]
    first_node = (lax.axis_index("pairs") - 1) * nodes_here
    local_ids = neighbours - first_node
    crossed = all_cross(own_spectra, pooled)
    columns = jnp.arange(pooled.shape[1], dtype=jnp.int32)
    selector = (local_ids[:, :, None] == columns[None, None, :]).astype(jnp.float32)
    selector = selector * valid.astype(jnp.float32)[:, :, None]
    stack = jnp.einsum("njm,nmf->njf", selector, crossed, precision=lax.Precision.HIGHEST)
    factor = 1.0 / math.sqrt(BINS * windows_here * lax.axis_size("win"))
    correlated = inverse_lags(stack)
    summed = lax.psum_scatter(correlated, "win", scatter_dimension=1, tiled=True)
    return summed * factor


def solution(mesh):
    placed = (P("win", "pairs", None), P(), P("pairs", None), P("pairs", None))
    return jax.shard_map(
        per_device, mesh=mesh, in_specs=placed, out_specs=P("pairs", "win", None), check_vma=False
    )
```

profile of v0, /device:TPU:16, one launch (start us, length us, event | category | flops | bytes accessed | tf_op | source)
XLA Modules:
  0.0 378.2 jit_solution(854572686311619878)
XLA Ops:
  6.5 0.0 copy-start
  6.5 0.0 reduce-scatter.2.cloned.1.call-start
  6.5 3.6 collective-permute-start
  10.1 3.3 collective-permute-start.1
  13.4 1.3 fusion.52
  14.8 0.7 convert_element_type.40
  15.5 1.3 fusion.54
  16.8 0.0 copy-start.8
  16.8 35.5 %cosine_convert_fusion = (bf16[1024,512]{1,0:T(8,128)(2,1)}, bf16[1024,512]{1,0:T(8,128)(2,1)}, bf16[1024,512]{1,0:T(8,128)(2,1)S(1)}, bf16[1024,512]{1,0:T(8,12...) fusion(s32[512]{0:T(512)S(1)} %iota_add_fusion.3, ...), kind=kLoop, calls=%fused_computation.76 | loop fusion | flops 35651584 | bytes 8402944 | tf_op jit(solution)/shard_map/convert.4
  52.3 137.8 %collective-permute-done = bf16[32,16,4096]{2,1,0:T(8,128)(2,1)} collective-permute-done((bf16[32,16,4096]{2,1,0:T(8,128)(2,1)}, bf16[32,16,4096]{2,1,0:T(8,128)(2,1)}, u32[]{:S(2)}, u32[]{:S(2)}) %collective-permute-start) | collective-permute-done | bytes 4194336 | tf_op jit(solution)/shard_map/ppermute | solution.py:26
  190.1 1.9 collective-permute-done.1
  192.0 5.5 %pad_maximum_fusion = bf16[32,48,4096]{2,1,0:T(8,128)(2,1)S(1)} fusion(bf16[32,16,4096]{2,1,0:T(8,128)(2,1)} %collective-permute-done.1, bf16[32,16,4096]{2,1,0:T(8,128)(2,1)S(1)} %copy-done.8, bf16[32,16,4096]{2,1,0:T(8,128)(2,1)} %collective-permute-done), kind=kLoop, calls=%fused_computation | loop fusion | flops 37748736 | bytes 25165824 | tf_op jit(solution)/shard_map/concatenate | solution.py:28
  197.4 5.3 %fusion.3 = f32[1536,1024]{1,0:T(8,128)} fusion(bf16[1536,4096]{1,0:T(8,128)(2,1)S(1)} %bitcast.28, bf16[1024,512]{1,0:T(8,128)(2,1)S(1)} %get-tuple-element.14, bf16[1024,512]{1,0:T(8,128)(2,1)S(1)} %get-tuple-element.15), kind=kOutput, calls=%fused_computation.17 | convolution fusion | flops 3225419776 | bytes 11534336 | tf_op jit(solution)/shard_map/dot_general | solution.py:60
  202.7 5.3 %fusion.5 = f32[1536,1024]{1,0:T(8,128)} fusion(bf16[1536,4096]{1,0:T(8,128)(2,1)S(1)} %bitcast.29, bf16[1024,512]{1,0:T(8,128)(2,1)S(1)} %get-tuple-element.13, bf16[1024,512]{1,0:T(8,128)(2,1)S(1)} %get-tuple-element.18), kind=kOutput, calls=%fused_computation.19 | convolution fusion | flops 3225419776 | bytes 11534336 | tf_op jit(solution)/shard_map/dot_general | solution.py:60
  208.0 5.3 %fusion.1 = f32[1536,1024]{1,0:T(8,128)} fusion(bf16[1536,4096]{1,0:T(8,128)(2,1)S(1)} %bitcast.30, bf16[1024,512]{1,0:T(8,128)(2,1)S(1)} %get-tuple-element.16, bf16[1024,512]{1,0:T(8,128)(2,1)S(1)} %get-tuple-element.17), kind=kOutput, calls=%fused_computation.15 | convolution fusion | flops 3225419776 | bytes 11534336 | tf_op jit(solution)/shard_map/dot_general | solution.py:60
  213.2 8.9 %add_add_fusion = f32[1536,1024]{1,0:T(8,128)S(1)} fusion(f32[1536,1024]{1,0:T(8,128)} %fusion.1, f32[1536,1024]{1,0:T(8,128)} %fusion.5, f32[1536,1024]{1,0:T(8,128)} %fusion.3, bf16[1536,4096]{1,0:T(8,128)(2,1)S(1)} %bitcast.31, bf16[1024,512]{1,0:T(8,128)(2,1)} %get-tuple-element.8, bf16[1024,512]{1,0:T(8,128)(2,1)} %get-tuple-element.7), kind=kOutput, calls=%fused_computation.1 | convolution fusion | flops 3230138368 | bytes 30408704 | tf_op jit(solution)/shard_map/dot_general | solution.py:60
  222.2 2.6 copy-done.4
  224.8 2.5 multiply_add_fusion
  227.3 2.4 copy.5
  229.7 0.3 bitcast_reduce_fusion
  230.1 0.4 mul.239
  230.4 2.8 copy.6
  233.3 5.1 %subtract_convert_fusion = (bf16[1536,512]{1,0:T(8,128)(2,1)S(1)}, bf16[1536,512]{1,0:T(8,128)(2,1)S(1)}) fusion(f32[512]{0:T(512)S(1)} %neg.19, f32[512]{0:T(512)S(1)} %bitcast.40, f32[1536,512]{1,0:T(8,128)} %copy.6, f32[1536,1024]{1,0:T(8,128)} %copy-done.4), kind=kLoop, calls=%fused_computation.29 | loop fusion | flops 7864320 | bytes 12587008 | tf_op jit(solution)/shard_map/convert.3
  238.4 6.6 %copy.11 = bf16[32,48,512]{1,0,2:T(8,128)(2,1)} copy(bf16[32,48,512]{2,1,0:T(8,128)(2,1)S(1)} %bitcast.35) | data formatting | bytes 3145728 | tf_op jit(solution)/shard_map/concatenate | solution.py:48
  244.9 0.8 slice.54
  245.8 6.6 %copy.8 = bf16[32,48,512]{1,0,2:T(8,128)(2,1)} copy(bf16[32,48,512]{2,1,0:T(8,128)(2,1)S(1)} %bitcast.33) | data formatting | bytes 3145728 | tf_op jit(solution)/shard_map/concatenate | solution.py:48
  252.4 2.2 copy.12
  254.6 3.0 copy.9
  257.6 5.6 %fusion.91 = f32[512,48,16]{1,2,0:T(8,128)} fusion(bf16[32,16,512]{0,1,2:T(8,128)(2,1)S(1)} %copy.12, bf16[32,48,512]{1,0,2:T(8,128)(2,1)} %copy.11), kind=kOutput, calls=%fused_computation.143 | convolution fusion | flops 25165824 | bytes 3670016 | tf_op jit(solution)/shard_map/wnf,wmf->nmf/dot_general | solution.py:72
  263.2 0.0 copy-done.5
  263.2 3.2 fusion.93
  266.3 3.2 fusion.90
  269.5 3.2 fusion.92
  272.7 2.8 copy.13
  275.6 2.8 copy.10
  278.4 3.7 copy.15
  282.1 3.8 %copy.14 = f32[512,48,16]{0,1,2:T(8,128)} copy(f32[512,48,16]{1,2,0:T(8,128)} %fusion.92) | data formatting | bytes 3145728 | tf_op jit(solution)/shard_map/wnf,wmf->nmf/dot_general | solution.py:75
  286.0 0.3 add_bitcast_fusion
  286.4 1.0 copy-done.6
  287.4 0.5 copy-done.7
  287.9 0.3 subtract_bitcast_fusion
  288.2 3.8 %fusion.7 = f32[16,64,1024]{2,1,0:T(8,128)S(1)} fusion(f32[16,48,512]{2,1,0:T(8,128)S(1)} %subtract_bitcast_fusion, f32[16,48,512]{2,1,0:T(8,128)S(1)} %add_bitcast_fusion, f32[16,64]{1,0:T(8,128)S(1)} %convert_element_type.40, s32[16,64]{1,0:T(8,128)S(1)} %broadcast_subtract_fusion), kind=kOutput, calls=%fused_computation.21 | convolution fusion | flops 604864512 | bytes 7348224 | tf_op jit(solution)/shard_map/njm,nmf->njf/dot_general | solution.py:109
  292.0 15.0 %fusion.27 = f32[1024,1024]{1,0:T(8,128)S(1)} fusion(f32[1024,1024]{1,0:T(8,128)S(1)} %bitcast.37, s32[1024]{0:T(1024)S(1)} %add_select_fusion.6, s32[512]{0:T(512)S(1)} %iota_add_fusion.3), kind=kOutput, calls=%fused_computation.59 | convolution fusion | flops 6449790976 | bytes 6297600 | tf_op jit(solution)/shard_map/dot_general | solution.py:88
  307.1 16.9 %convolution_subtract_fusion = f32[1024,1024]{1,0:T(8,128)} fusion(f32[1024,1024]{1,0:T(8,128)S(1)} %fusion.27, f32[1024,1024]{1,0:T(8,128)S(1)} %bitcast.38, s32[1024]{0:T(1024)S(1)} %add_select_fusion.6, s32[512]{0:T(512)S(1)} %iota_add_fusion.3), kind=kOutput, calls=%fused_computation.42 | convolution fusion | flops 6450839552 | bytes 10491904 | tf_op jit(solution)/shard_map/dot_general | solution.py:89
  324.0 0.0 reduce-scatter.2.cloned.1.call-update
  324.0 0.0 copy-start.1
  324.0 44.8 %reduce-scatter.2.cloned.1.call-done = f32[16,16,1024]{2,1,0:T(8,128)} async-done(((f32[16,64,1024]{2,1,0:T(8,128)}), f32[16,16,1024]{2,1,0:T(8,128)}) %reduce-scatter.2.cloned.1.call-update) | async-done | bytes 1048592 | tf_op jit(solution)/shard_map/reduce_scatter | solution.py:112
  368.8 2.3 broadcast_multiply_fusion
  (23 shorter events, 0.1 us)
Async XLA Ops:
  6.5 6.9 %copy-start = (f32[129]{0:T(256)S(1)}, f32[129]{0:T(256)}, u32[]{:S(2)}) copy-start(f32[129]{0:T(256)} %param.5) | copy-start | bytes 1552
  6.5 10.2 %copy-start.10 = (s32[16,64]{1,0:T(8,128)S(1)}, s32[16,64]{1,0:T(8,128)}, u32[]{:S(2)}) copy-start(s32[16,64]{1,0:T(8,128)} %param.6) | copy-start | bytes 12292
  6.5 362.3 %reduce-scatter.2.cloned.1.call-start = ((), (), s32[]{:S(2)}) async-start(), calls=%async_computation.1 | async-start | bytes 5242880 | tf_op jit(solution)/shard_map/reduce_scatter | solution.py:112
  6.5 183.6 %collective-permute-start = (bf16[32,16,4096]{2,1,0:T(8,128)(2,1)}, bf16[32,16,4096]{2,1,0:T(8,128)(2,1)}, u32[]{:S(2)}, u32[]{:S(2)}) collective-permute-start(bf16[32,16,4096]{2,1,0:T(8,128)(2,1)} %param.4), channel_id=1, source_target_pairs={{0,4},{4,8},{8,12},{12,16},{16,20},{20,24},{24,28},{1,5},{5,9},{9,... | collective-permute-start | bytes 12582920 | tf_op jit(solution)/shard_map/ppermute | solution.py:26
  10.1 181.9 %collective-permute-start.1 = (bf16[32,16,4096]{2,1,0:T(8,128)(2,1)}, bf16[32,16,4096]{2,1,0:T(8,128)(2,1)}, u32[]{:S(2)}, u32[]{:S(2)}) collective-permute-start(bf16[32,16,4096]{2,1,0:T(8,128)(2,1)} %param.4), channel_id=1, source_target_pairs={{4,0},{8,4},{12,8},{16,12},{20,16},{24,20},{28,24},{5,1},{9,5},{13... | collective-permute-start | bytes 12582920 | tf_op jit(solution)/shard_map/ppermute | solution.py:27
  16.8 175.2 %copy-start.8 = (bf16[32,16,4096]{2,1,0:T(8,128)(2,1)S(1)}, bf16[32,16,4096]{2,1,0:T(8,128)(2,1)}, u32[]{:S(2)}) copy-start(bf16[32,16,4096]{2,1,0:T(8,128)(2,1)} %param.4) | copy-start | bytes 12582916
  222.2 2.6 copy-start.4
  245.8 6.6 %copy-start.9 = (bf16[32,16,512]{2,1,0:T(8,128)(2,1)S(1)}, bf16[32,16,512]{2,1,0:T(8,128)(2,1)}, u32[]{:S(2)}) copy-start(bf16[32,16,512]{2,1,0:T(8,128)(2,1)} %slice.54) | copy-start | bytes 1572868
  257.6 5.6 %copy-start.2 = (bf16[32,48,512]{1,0,2:T(8,128)(2,1)S(1)}, bf16[32,48,512]{1,0,2:T(8,128)(2,1)}, u32[]{:S(2)}) copy-start(bf16[32,48,512]{1,0,2:T(8,128)(2,1)} %copy.11) | copy-start | bytes 4718596
  257.6 5.6 %copy-start.5 = (bf16[32,16,512]{0,1,2:T(8,128)(2,1)S(1)}, bf16[32,16,512]{0,1,2:T(8,128)(2,1)}, u32[]{:S(2)}) copy-start(bf16[32,16,512]{0,1,2:T(8,128)(2,1)} %copy.9) | copy-start | bytes 1572868
  263.2 3.2 copy-start.3
  286.0 1.4 copy-start.6
  286.0 1.9 copy-start.7
  324.0 47.1 %copy-start.1 = (f32[129]{0:T(256)S(1)}, f32[129]{0:T(256)}, u32[]{:S(2)}) copy-start(f32[129]{0:T(256)} %param.5) | copy-start | bytes 1552
Sparse Core Ops, SparseCore 0:
  324.1 44.6 reduce-scatter.1
where the time goes:
time: 383 us; the launch traced here: 378 us
  waiting for transfers between devices  184 us (48%)
  matrix products  78.2 us (20%)
  other arithmetic  52.6 us (14%)
  local copies, waits for them, and re-layouts  42.2 us (11%)
  between operations  13.9 us (4%)
  starting transfers between devices  6.87 us (2%)
    ppermute x1, waiting for transfers between devices, with_halo(): before = lax.ppermute(last, axis, up)  138 us
    reduce_scatter x1, waiting for transfers between devices, per_device(): lax.psum_scatter(correlated, 'win', scatter_dimension=1, tiled=True)  44.8 us
    another operation x2, other arithmetic  40.6 us
    dot_general x4, matrix products, band_spectra(): jnp.dot(flat_rows[:, offset:offset + blocksize], tables, preferred_elemen...  24.7 us
    dot_general x1, matrix products, inverse_lags(): jnp.dot(flat_rows[:, bins:], jnp.sin(angles), precision=lax.Precision.HIG...  16.9 us
    dot_general x1, matrix products, inverse_lags(): jnp.dot(flat_rows[:, :bins], jnp.cos(angles), precision=lax.Precision.HIG...  15 us
    concatenate x2, local copies, waits for them, and re-layouts, whiten(): return jnp.concatenate([out_real, out_imag], 1).astype(jnp.bfloat16)  13.1 us
  transfers between devices with their start and end apart: 3, of which 3 were waited for; matrix products, arithmetic and copies ran while one was open for 10% of the time, Pallas kernels for 0%

commit v1 on v0

v1 whole, which is shorter than its diff:
```python
import functools
import math

import jax
import jax.numpy as jnp
import numpy as np
from jax import lax
from jax.experimental import pallas as pl
from jax.experimental.pallas import tpu as pltpu
from jax.sharding import PartitionSpec as P

SAMPLES = 4096
BINS = 512
BAND = 64
LOW_BIN = 64
LAGS = 1024
TAPS = 129
LANES = 2 * BAND
EPSILON = 1e-06
STEP = 64
CHUNK = 512
VMEM_LIMIT = 60 * 1024 * 1024


def unit_circle(products):
    angles = (products % SAMPLES).astype(np.float64) * (2.0 * math.pi / SAMPLES)
    return np.cos(angles).astype(np.float32), (-np.sin(angles)).astype(np.float32)


def banded(first, second):
    rows = first.shape[0]
    parts = [a.reshape(rows, BINS // BAND, 1, BAND) for a in (first, second)]
    return np.concatenate(parts, 2).reshape(rows, 2 * BINS)


def forward_tables():
    bins = LOW_BIN + np.arange(BINS, dtype=np.int64)
    cos, msin = unit_circle(np.arange(TAPS, dtype=np.int64)[:, None] * bins[None, :])
    fine = banded(cos, msin)
    starts = np.arange(0, SAMPLES, STEP, dtype=np.int64)
    cos, msin = unit_circle(starts[:, None] * bins[None, :])
    return fine, banded(cos, cos), banded(-msin, msin)


def lag_tables(parts):
    lags = np.arange(LAGS, dtype=np.int64) - LAGS // 2
    cos, msin = unit_circle(np.arange(BAND, dtype=np.int64)[:, None] * lags[None, :])
    first = LOW_BIN + BAND * np.arange(parts, dtype=np.int64)
    cos0, msin0 = unit_circle(first[:, None] * lags[None, :])
    return cos, msin, cos0, msin0


def spectra_kernel(x_ref, taps_ref, fine_ref, turn_c_ref, turn_s_ref, out_ref, total, swapped, table):
    step = pl.program_id(0)

    @pl.when(step == 0)
    def _():
        for band in range(BINS // BAND):
            cols = pl.ds(band * LANES, LANES)
            swapped[:, cols] = pltpu.roll(fine_ref[0:STEP, cols], BAND, 1)

    for block in range(CHUNK // STEP):
        row = pl.ds(step * (CHUNK // STEP) + block, 1)
        turned = fine_ref[0:STEP, :] * turn_c_ref[row, :] + swapped[...] * turn_s_ref[row, :]
        table[block * STEP : (block + 1) * STEP, :] = turned.astype(jnp.bfloat16)
    product = jnp.dot(x_ref[...], table[...], preferred_element_type=jnp.float32)

    @pl.when(step == 0)
    def _():
        total[...] = product

    @pl.when(step > 0)
    def _():
        total[...] += product

    @pl.when(step == pl.num_programs(0) - 1)
    def _():
        response = jnp.dot(
            taps_ref[:, 0:128],
            fine_ref[0:128, :],
            precision=lax.Precision.HIGHEST,
            preferred_element_type=jnp.float32,
        )
        response = response + taps_ref[:, 128:129] * fine_ref[128:129, :]
        low = lax.broadcasted_iota(jnp.int32, (1, LANES), 1) < BAND
        for band in range(BINS // BAND):
            here = response[:, band * LANES : (band + 1) * LANES]
            other = pltpu.roll(jnp.broadcast_to(here, (8, LANES)), BAND, 1)[0:1, :]
            same = jnp.where(low, here, other)
            cross = jnp.where(low, -other, here)
            raw = total[:, band * LANES : (band + 1) * LANES]
            power = jnp.sum(raw * raw, 1, keepdims=True) * (1.0 / BAND)
            white = raw * lax.rsqrt(power + EPSILON)
            turned = white * same + pltpu.roll(white, BAND, 1) * cross
            out_ref[band] = turned.astype(jnp.bfloat16)


def own_spectra(rows, taps):
    fine, turn_c, turn_s = (jnp.asarray(t) for t in forward_tables())
    count = rows.shape[0]
    bands = BINS // BAND
    fixed = lambda shape: pl.BlockSpec(shape, lambda i: (0,) * len(shape))
    return pl.pallas_call(
        spectra_kernel,
        grid=(SAMPLES // CHUNK,),
        in_specs=[
            pl.BlockSpec((count, CHUNK), lambda i: (0, i)),
            fixed(taps.shape),
            fixed(fine.shape),
            fixed(turn_c.shape),
            fixed(turn_s.shape),
        ],
        out_specs=fixed((bands, count, LANES)),
        out_shape=jax.ShapeDtypeStruct((bands, count, LANES), jnp.bfloat16),
        scratch_shapes=[
            pltpu.VMEM((count, 2 * BINS), jnp.float32),
            pltpu.VMEM((STEP, 2 * BINS), jnp.float32),
            pltpu.VMEM((CHUNK, 2 * BINS), jnp.bfloat16),
        ],
        compiler_params=pltpu.CompilerParams(vmem_limit_bytes=VMEM_LIMIT),
        name="own_spectra",
    )(rows, taps, fine, turn_c, turn_s)


def lag_table_kernel(cos_ref, msin_ref, cos0_ref, msin0_ref, high_ref, low_ref, *, factor):
    part = pl.program_id(0)
    c0 = cos0_ref[pl.ds(part, 1), :] * factor
    s0 = msin0_ref[pl.ds(part, 1), :] * factor
    cos, msin = cos_ref[...], msin_ref[...]
    for half, values in ((0, cos * c0 - msin * s0), (1, cos * s0 + msin * c0)):
        high = values.astype(jnp.bfloat16)
        rows = pl.ds(half * BAND, BAND)
        high_ref[0, rows, :] = high
        low_ref[0, rows, :] = (values - high.astype(jnp.float32)).astype(jnp.bfloat16)


def make_lag_tables(parts, factor):
    tables = [jnp.asarray(t) for t in lag_tables(parts)]
    shape = jax.ShapeDtypeStruct((parts, LANES, LAGS), jnp.bfloat16)
    block = pl.BlockSpec((1, LANES, LAGS), lambda i: (i, 0, 0))
    return pl.pallas_call(
        functools.partial(lag_table_kernel, factor=factor),
        grid=(parts,),
        in_specs=[pl.BlockSpec(t.shape, lambda i: (0, 0)) for t in tables],
        out_specs=[block, block],
        out_shape=[shape, shape],
        name="lag_tables",
    )(*tables)


def widen(src_ref, dst_ref, dst_tile, nodes, swap_ref):
    groups, rows = src_ref.shape[0], src_ref.shape[1]
    for group in range(groups):
        values = src_ref[group].astype(jnp.float32)
        dst_ref[dst_tile, pl.ds(group * rows, rows), :] = values
        if swap_ref is not None:
            swap_ref[dst_tile, pl.ds(group * rows, rows), :] = pltpu.roll(values, BAND, 1)


def correlate(a_ref, a_tile, b_ref, s_ref, b_tile, nodes, windows, store):
    group = 4
    eights = nodes // 8

    def nodes_block(index, _):
        first = index * group

        def window(w, totals):
            row = w * nodes
            b = [b_ref[b_tile, pl.ds(pl.multiple_of(row + 8 * v, 8), 8), :] for v in range(eights)]
            s = [s_ref[b_tile, pl.ds(pl.multiple_of(row + 8 * v, 8), 8), :] for v in range(eights)]
            out = []
            for i in range(group):
                a = a_ref[a_tile, pl.ds(row + first + i, 8, stride=0), :]
                for v in range(eights):
                    direct, crossed = totals[i * eights + v]
                    out.append((direct + a * b[v], crossed + a * s[v]))
            return tuple(out)

        zero = jnp.zeros((8, LANES), jnp.float32)
        totals = lax.fori_loop(0, windows, window, ((zero, zero),) * (group * eights), unroll=4)
        low = lax.broadcasted_iota(jnp.int32, (8, LANES), 1) < BAND
        for i in range(group):
            for v in range(eights):
                direct, crossed = totals[i * eights + v]
                real = direct + pltpu.roll(direct, BAND, 1)
                imag = crossed - pltpu.roll(crossed, BAND, 1)
                store(first + i, v, jnp.where(low, real, imag))
        return 0

    lax.fori_loop(0, nodes // group, nodes_block, 0)


def own_cross_kernel(x_ref, out_ref, wide, swap, *, nodes, windows):
    groups = x_ref.shape[0] // 2
    for tile in range(2):
        widen(x_ref.at[pl.ds(tile * groups, groups)], wide, tile, nodes, swap)
    for a_tile, b_tile in ((0, 0), (0, 1), (1, 1)):
        def store(node, v, values, a_tile=a_tile, b_tile=b_tile):
            row = ((a_tile * nodes + node) * 2 + b_tile) * nodes + 8 * v
            out_ref[pl.ds(pl.multiple_of(row, 8), 8), :] = values

        correlate(wide, a_tile, wide, swap, b_tile, nodes, windows, store)
    sign = jnp.where(lax.broadcasted_iota(jnp.int32, (1, LANES), 1) < BAND, 1.0, -1.0)
    for node in range(nodes):
        mirrored = out_ref[pl.ds(nodes + node, nodes, stride=2 * nodes), :]
        out_ref[pl.ds((nodes + node) * 2 * nodes, nodes), :] = mirrored * sign


def own_cross(received, nodes, windows):
    rows = windows * nodes
    return pl.pallas_call(
        functools.partial(own_cross_kernel, nodes=nodes, windows=windows),
        out_shape=jax.ShapeDtypeStruct((4 * nodes * nodes, LANES), jnp.float32),
        in_specs=[pl.BlockSpec(memory_space=pltpu.VMEM)],
        out_specs=pl.BlockSpec(memory_space=pltpu.VMEM),
        scratch_shapes=[pltpu.VMEM((2, rows, LANES), jnp.float32)] * 2,
        compiler_params=pltpu.CompilerParams(vmem_limit_bytes=VMEM_LIMIT),
        cost_estimate=pl.CostEstimate(
            flops=2 * 8 * nodes * nodes * windows * BAND, bytes_accessed=8 * rows * LANES, transcendentals=0
        ),
        name="own_cross",
    )(received)


def edge_select_kernel(odd_ref, x_ref, even_ref, odd_halo_ref, own_ref, select_ref, out_ref, wide, halo, swap, edge, *, nodes, windows):
    groups = x_ref.shape[0] // 2
    for tile in range(2):
        widen(x_ref.at[pl.ds(tile * groups, groups)], wide, tile, nodes, None)
    widen(even_ref, halo, 0, nodes, swap)
    widen(odd_halo_ref, halo, 1, nodes, swap)
    odd = odd_ref[0]
    for which in range(2):
        tile = (1 - odd) if which == 0 else odd

        def store(node, v, values, tile=tile):
            row = (tile * nodes + node) * nodes + 8 * v
            edge[pl.ds(pl.multiple_of(row, 8), 8), :] = values

        correlate(wide, tile, halo, swap, which, nodes, windows, store)
    slots = out_ref.shape[2]
    destinations = out_ref.shape[0] // 2

    def one(index, _):
        own = own_ref[pl.ds(pl.multiple_of(index * 2 * nodes, 8), 2 * nodes), :]
        far = edge[pl.ds(pl.multiple_of(index * nodes, 8), nodes), :]
        values = jnp.concatenate([own, far], 0)
        high = values.astype(jnp.bfloat16)
        low = (values - high.astype(jnp.float32)).astype(jnp.bfloat16)
        picked = jnp.dot(
            select_ref[index], jnp.concatenate([high, low], 0), preferred_element_type=jnp.float32
        )
        tile, node = index // nodes, index % nodes
        for d in range(destinations):
            out_ref[tile * destinations + d, node] = picked[d * slots : (d + 1) * slots, :]
        return 0

    lax.fori_loop(0, 2 * nodes, one, 0)


def edge_select(odd, received, halo_a, halo_b, own, select, nodes, windows, parts):
    rows = windows * nodes
    slots = select.shape[1] // (parts // 2)
    vmem = pl.BlockSpec(memory_space=pltpu.VMEM)
    return pl.pallas_call(
        functools.partial(edge_select_kernel, nodes=nodes, windows=windows),
        out_shape=jax.ShapeDtypeStruct((parts, nodes, slots, LANES), jnp.float32),
        in_specs=[pl.BlockSpec(memory_space=pltpu.SMEM)] + [vmem] * 5,
        out_specs=vmem,
        scratch_shapes=[
            pltpu.VMEM((2, rows, LANES), jnp.float32),
            pltpu.VMEM((2, rows, LANES), jnp.float32),
            pltpu.VMEM((2, rows, LANES), jnp.float32),
            pltpu.VMEM((2 * nodes * nodes, LANES), jnp.float32),
        ],
        compiler_params=pltpu.CompilerParams(vmem_limit_bytes=VMEM_LIMIT),
        name="edge_select",
    )(odd, received, halo_a, halo_b, own, select)


def inverse_kernel(x_ref, high_ref, low_ref, out_ref):
    parts, nodes, slots = x_ref.shape[0], x_ref.shape[1], x_ref.shape[2]
    total = None
    for part in range(parts):
        values = x_ref[part].reshape(nodes * slots, LANES)
        high = values.astype(jnp.bfloat16)
        low = (values - high.astype(jnp.float32)).astype(jnp.bfloat16)
        dot = functools.partial(jnp.dot, preferred_element_type=jnp.float32)
        term = dot(high, high_ref[part]) + (dot(low, high_ref[part]) + dot(high, low_ref[part]))
        total = term if total is None else total + term
    out_ref[...] = total.reshape(out_ref.shape)


def inverse(stack, high, low):
    parts, nodes, slots, _ = stack.shape
    block = 256
    table = pl.BlockSpec((parts, LANES, block), lambda i: (0, 0, i))
    return pl.pallas_call(
        inverse_kernel,
        grid=(LAGS // block,),
        in_specs=[pl.BlockSpec(stack.shape, lambda i: (0, 0, 0, 0)), table, table],
        out_specs=pl.BlockSpec((nodes, slots, block), lambda i: (0, 0, i)),
        out_shape=jax.ShapeDtypeStruct((nodes, slots, LAGS), jnp.float32),
        compiler_params=pltpu.CompilerParams(vmem_limit_bytes=VMEM_LIMIT),
        name="inverse",
    )(stack, high, low)


def per_device(traces, taps, neighbours, valid, *, pairs, wins):
    windows, nodes, samples = traces.shape
    parts = 2 * wins
    place = lax.axis_index("pairs")
    parity = place % 2
    both = ("pairs", "win")
    groups = [[p * wins + w for p in (k, k + 1) for w in range(wins)] for k in range(0, pairs, 2)]
    exchange = functools.partial(
        lax.all_to_all, axis_name=both, split_axis=0, concat_axis=0, tiled=True, axis_index_groups=groups
    )

    local = neighbours - (place - 1) * nodes
    local = jnp.where(parity == 0, (local + 2 * nodes) % (3 * nodes), local)
    code = jnp.where(valid != 0, local, -1)
    other = lax.ppermute(code, "pairs", [(i, i ^ 1) for i in range(pairs)])
    codes = jnp.where(parity == 0, jnp.concatenate([code, other], 0), jnp.concatenate([other, code], 0))
    columns = jnp.arange(6 * nodes, dtype=jnp.int32) % (3 * nodes)
    select = (codes[:, :, None] == columns[None, None, :]).astype(jnp.bfloat16)

    factor = 1.0 / math.sqrt(BINS * windows * wins)
    high, low = make_lag_tables(parts, factor)

    spectra = own_spectra(traces.reshape(windows * nodes, samples), taps.reshape(1, TAPS))
    received = exchange(spectra)

    odd = (place // 2) % 2
    swap_a = [(i, i ^ 2) for i in range(pairs) if (i ^ 2) < pairs]
    swap_b = [(i, j) for i in range(pairs) for j in [((i - 2) ^ 2) + 2] if 2 <= i and j < pairs]
    send_a = lax.dynamic_slice_in_dim(received, (1 - odd) * wins, wins, 0)
    send_b = lax.dynamic_slice_in_dim(received, odd * wins, wins, 0)
    halo_a = lax.ppermute(send_a, "pairs", swap_a)
    halo_b = lax.ppermute(send_b, "pairs", swap_b)

    own = own_cross(received, nodes, windows * wins)
    stack = edge_select(odd.reshape(1), received, halo_a, halo_b, own, select, nodes, windows * wins, parts)
    return inverse(exchange(stack), high, low)


def solution(mesh):
    placed = (P("win", "pairs", None), P(), P("pairs", None), P("pairs", None))
    body = functools.partial(per_device, pairs=mesh.shape["pairs"], wins=mesh.shape["win"])
    return jax.shard_map(
        body, mesh=mesh, in_specs=placed, out_specs=P("pairs", "win", None), check_vma=False
    )
```

time: 383 us -> 97.3 us (0.25)
  the two profiles are of different devices: /device:TPU:16 before, /device:TPU:0 now
where the time goes in v1:
time: 97.3 us; the launch traced here: 96.7 us
  Pallas kernels  49.9 us (51%)
  waiting for transfers between devices  28.9 us (30%)
  starting transfers between devices  14.6 us (15%)
  local copies, waits for them, and re-layouts  2.01 us (2%)
  other arithmetic  1.17 us (1%)
    all_to_all x1, waiting for transfers between devices, per_device(): received = exchange(spectra)  15.4 us
    pallas_call x1, Pallas kernels, edge_select(): pl.pallas_call(functools.partial(edge_select_kernel, nodes=nodes, windows...  14.1 us
    pallas_call x1, Pallas kernels, own_cross(): pl.pallas_call(functools.partial(own_cross_kernel, nodes=nodes, windows=w...  12.4 us
    pallas_call x1, Pallas kernels, own_spectra(): pl.pallas_call(spectra_kernel, grid=(SAMPLES // CHUNK,), in_specs=[pl.Blo...  12 us
    all_to_all x1, waiting for transfers between devices, per_device(): return inverse(exchange(stack), high, low)  10.4 us
    pallas_call x1, Pallas kernels, inverse(): pl.pallas_call(inverse_kernel, grid=(LAGS // block,), in_specs=[pl.BlockS...  6.57 us
    all_to_all x1, starting transfers between devices, per_device(): received = exchange(spectra)  5.3 us
    pallas_call x1, Pallas kernels, make_lag_tables(): pl.pallas_call(functools.partial(lag_table_kernel, factor=factor), grid=(...  4.89 us
  transfers between devices with their start and end apart: 5, of which 3 were waited for; matrix products, arithmetic and copies ran while one was open for 1% of the time, Pallas kernels for 18%

profile of v1, /device:TPU:0, one launch (start us, length us, event | category | flops | bytes accessed | tf_op | source)
XLA Modules:
  0.0 96.7 jit_solution(16192844151886235702)
XLA Ops:
  0.0 12.0 %own_spectra.1 = bf16[8,512,128]{2,1,0:T(8,128)(2,1)} custom-call(bf16[512,4096]{1,0:T(8,128)(2,1)} %bitcast.3, f32[1,129]{1,0:T(1,128)} %bitcast.4, f32[129,1024]{1,0:T(8,128)} %constant.82.clone.fine_ref, f32[64,1024]{1,0:T(8,128)} %constant.83.clone.turn_c_ref, f32[64,1024]{1,0:T(8,128)} %constant.84.clone.turn_s_ref), custom_call_target="tpu_custom_call" | custom-call | tf_op jit(solution)/shard_map/own_spectra/pallas_call | solution.py:103
  12.0 0.0 copy-start.4
  12.0 0.0 copy-start.5
  12.0 5.3 %all-to-all-start = ((bf16[8,512,128]{2,1,0:T(8,128)(2,1)}), bf16[8,512,128]{2,1,0:T(8,128)(2,1)S(1)}, u32[]{:S(2)}, u32[]{:S(2)}) async-start(bf16[8,512,128]{2,1,0:T(8,128)(2,1)} %own_spectra.1), calls=%async_computation | async-start | bytes 2097152 | tf_op jit(solution)/shard_map/all_to_all | solution.py:331
  17.3 15.4 %all-to-all-done.x_ref = bf16[8,512,128]{2,1,0:T(8,128)(2,1)S(1)} async-done(((bf16[8,512,128]{2,1,0:T(8,128)(2,1)}), bf16[8,512,128]{2,1,0:T(8,128)(2,1)S(1)}, u32[]{:S(2)}, u32[]{:S(2)}) %all-to-all-start) | async-done | bytes 1048608 | tf_op jit(solution)/shard_map/all_to_all | solution.py:331
  32.7 0.0 copy-start
  32.7 0.1 constant_dynamic-slice_fusion
  32.8 0.7 collective-permute-start.1
  33.5 4.4 %collective-permute-start = (bf16[4,512,128]{2,1,0:T(8,128)(2,1)S(1)}, bf16[4,512,128]{2,1,0:T(8,128)(2,1)S(1)}, u32[]{:S(2)}, u32[]{:S(2)}) collective-permute-start(bf16[4,512,128]{2,1,0:T(8,128)(2,1)S(1)} %get-tuple-element.10), channel_id=1, source_target_pairs={{0,8},{4,12},{8,0},{12,4},{16,24},{20,28},{24,16},{28,20},{1,9},{5... | collective-permute-start | bytes 1572872 | tf_op jit(solution)/shard_map/ppermute | solution.py:338
  37.9 0.0 copy-done.4
  37.9 0.0 copy-done.5
  37.9 0.6 collective-permute-start.2
  38.6 3.1 %collective-permute-done.2 = s32[16,64]{1,0:T(8,128)S(1)} collective-permute-done((s32[16,64]{1,0:T(8,128)S(1)}, s32[16,64]{1,0:T(8,128)S(1)}, u32[]{:S(2)}, u32[]{:S(2)}) %collective-permute-start.2) | collective-permute-done | bytes 4128 | tf_op jit(solution)/shard_map/ppermute | solution.py:322
  41.7 1.1 %compare_convert_fusion.select_ref = bf16[32,64,96]{2,1,0:T(8,128)(2,1)} fusion(s32[96]{0:T(128)S(1)} %and_select_fusion, s32[32,64]{1,0:T(8,128)S(1)} %add_select_fusion), kind=kLoop, calls=%fused_computation | loop fusion | flops 393216 | bytes 401792 | tf_op jit(solution)/shard_map/convert_element_type | solution.py:325
  42.8 0.0 copy-done
  42.8 12.4 %own_cross.1.own_ref = f32[1024,128]{1,0:T(8,128)} custom-call(bf16[8,512,128]{2,1,0:T(8,128)(2,1)} %copy-done), custom_call_target="tpu_custom_call" | custom-call | flops 33554432 | bytes 2097152 | tf_op jit(solution)/shard_map/own_cross/pallas_call | solution.py:211
  55.2 0.0 collective-permute-done.1.odd_halo_ref
  55.2 0.0 copy-start.2
  55.2 0.0 collective-permute-done.even_ref
  55.2 0.0 copy-start.3
  55.2 0.8 copy-done.2
  56.0 0.2 copy-done.3
  56.1 14.1 %edge_select.1 = f32[8,16,16,128]{3,2,1,0:T(8,128)} custom-call(s32[1]{0:T(128)} %bitcast.odd_ref, bf16[8,512,128]{2,1,0:T(8,128)(2,1)} %copy-done, bf16[4,512,128]{2,1,0:T(8,128)(2,1)} %copy-done.3, bf16[4,512,128]{2,1,0:T(8,128)(2,1)} %copy-done.2, f32[1024,128]{1,0:T(8,128)} %own_cross.1.own_ref, bf16[32,64,96]{2,1,0:T(8,128)(2,1)} %compare_convert_fusion.select_ref), custom_call_target="tpu_custom_call" | custom-call | tf_op jit(solution)/shard_map/edge_select/pallas_call | solution.py:264
  70.3 3.6 %all-to-all-start.1 = ((f32[8,16,16,128]{3,2,1,0:T(8,128)}), f32[8,16,16,128]{3,2,1,0:T(8,128)S(1)}, u32[]{:S(2)}, u32[]{:S(2)}) async-start(f32[8,16,16,128]{3,2,1,0:T(8,128)} %edge_select.1), calls=%async_computation.1 | async-start | bytes 2097152 | tf_op jit(solution)/shard_map/all_to_all | solution.py:343
  73.8 4.9 %lag_tables.1 = (bf16[8,128,1024]{2,1,0:T(8,128)(2,1)}, bf16[8,128,1024]{2,1,0:T(8,128)(2,1)}) custom-call(f32[64,1024]{1,0:T(8,128)} %constant.78.clone.cos_ref, f32[64,1024]{1,0:T(8,128)} %constant.79.clone.msin_ref, f32[8,1024]{1,0:T(8,128)} %constant.80.clone.cos0_ref, f32[8,1024]{1,0:T(8,128)} %constant.81.clone.msin0_ref), custom_call_target="tpu_custom_call" | custom-call | tf_op jit(solution)/shard_map/lag_tables/pallas_call | solution.py:141
  78.7 10.4 %all-to-all-done.1.x_ref = f32[8,16,16,128]{3,2,1,0:T(8,128)S(1)} async-done(((f32[8,16,16,128]{3,2,1,0:T(8,128)}), f32[8,16,16,128]{3,2,1,0:T(8,128)S(1)}, u32[]{:S(2)}, u32[]{:S(2)}) %all-to-all-start.1) | async-done | bytes 1048608 | tf_op jit(solution)/shard_map/all_to_all | solution.py:343
  89.2 0.0 copy-start.1
  89.2 1.0 %copy-done.1 = f32[8,16,16,128]{3,2,1,0:T(8,128)} copy-done((f32[8,16,16,128]{3,2,1,0:T(8,128)}, f32[8,16,16,128]{3,2,1,0:T(8,128)S(1)}, u32[]{:S(2)}) %copy-start.1) | copy-done | bytes 1048600
  90.1 6.6 %inverse.1 = f32[16,16,1024]{2,1,0:T(8,128)} custom-call(f32[8,16,16,128]{3,2,1,0:T(8,128)} %copy-done.1, bf16[8,128,1024]{2,1,0:T(8,128)(2,1)} %get-tuple-element.7.high_ref, bf16[8,128,1024]{2,1,0:T(8,128)(2,1)} %get-tuple-element.8.low_ref), custom_call_target="tpu_custom_call" | custom-call | tf_op jit(solution)/shard_map/inverse/pallas_call | solution.py:297
  (3 shorter events, 0.0 us)
Async XLA Ops:
  12.0 25.9 %copy-start.4 = (s32[16,64]{1,0:T(8,128)S(1)}, s32[16,64]{1,0:T(8,128)}, u32[]{:S(2)}) copy-start(s32[16,64]{1,0:T(8,128)} %param.13) | copy-start | bytes 12292
  12.0 25.9 %copy-start.5 = (s32[16,64]{1,0:T(8,128)S(1)}, s32[16,64]{1,0:T(8,128)}, u32[]{:S(2)}) copy-start(s32[16,64]{1,0:T(8,128)} %param.14) | copy-start | bytes 12292
  12.0 20.7 %all-to-all-start = ((bf16[8,512,128]{2,1,0:T(8,128)(2,1)}), bf16[8,512,128]{2,1,0:T(8,128)(2,1)S(1)}, u32[]{:S(2)}, u32[]{:S(2)}) async-start(bf16[8,512,128]{2,1,0:T(8,128)(2,1)} %own_spectra.1), calls=%async_computation | async-start | bytes 2097152 | tf_op jit(solution)/shard_map/all_to_all | solution.py:331
  32.7 10.1 %copy-start = (bf16[8,512,128]{2,1,0:T(8,128)(2,1)}, bf16[8,512,128]{2,1,0:T(8,128)(2,1)S(1)}, u32[]{:S(2)}) copy-start(bf16[8,512,128]{2,1,0:T(8,128)(2,1)S(1)} %all-to-all-done.x_ref) | copy-start | bytes 3145732
  32.8 22.4 %collective-permute-start.1 = (bf16[4,512,128]{2,1,0:T(8,128)(2,1)S(1)}, bf16[4,512,128]{2,1,0:T(8,128)(2,1)S(1)}, u32[]{:S(2)}, u32[]{:S(2)}) collective-permute-start(bf16[4,512,128]{2,1,0:T(8,128)(2,1)S(1)} %get-tuple-element.9), channel_id=1, source_target_pairs={{8,16},{12,20},{16,8},{20,12},{9,17},{13,21},{17,9},{21,13},{10,18... | collective-permute-start | bytes 1572872 | tf_op jit(solution)/shard_map/ppermute | solution.py:339
  33.5 21.7 %collective-permute-start = (bf16[4,512,128]{2,1,0:T(8,128)(2,1)S(1)}, bf16[4,512,128]{2,1,0:T(8,128)(2,1)S(1)}, u32[]{:S(2)}, u32[]{:S(2)}) collective-permute-start(bf16[4,512,128]{2,1,0:T(8,128)(2,1)S(1)} %get-tuple-element.10), channel_id=1, source_target_pairs={{0,8},{4,12},{8,0},{12,4},{16,24},{20,28},{24,16},{28,20},{1,9},{5... | collective-permute-start | bytes 1572872 | tf_op jit(solution)/shard_map/ppermute | solution.py:338
  37.9 3.7 %collective-permute-start.2 = (s32[16,64]{1,0:T(8,128)S(1)}, s32[16,64]{1,0:T(8,128)S(1)}, u32[]{:S(2)}, u32[]{:S(2)}) collective-permute-start(s32[16,64]{1,0:T(8,128)S(1)} %fusion.1), channel_id=1, source_target_pairs={{0,4},{4,0},{8,12},{12,8},{16,20},{20,16},{24,28},{28,24},{1,5},{5... | collective-permute-start | bytes 12296 | tf_op jit(solution)/shard_map/ppermute | solution.py:322
  55.2 0.8 copy-start.2
  55.2 1.0 %copy-start.3 = (bf16[4,512,128]{2,1,0:T(8,128)(2,1)}, bf16[4,512,128]{2,1,0:T(8,128)(2,1)S(1)}, u32[]{:S(2)}) copy-start(bf16[4,512,128]{2,1,0:T(8,128)(2,1)S(1)} %collective-permute-done.even_ref) | copy-start | bytes 1572868
  70.3 18.9 %all-to-all-start.1 = ((f32[8,16,16,128]{3,2,1,0:T(8,128)}), f32[8,16,16,128]{3,2,1,0:T(8,128)S(1)}, u32[]{:S(2)}, u32[]{:S(2)}) async-start(f32[8,16,16,128]{3,2,1,0:T(8,128)} %edge_select.1), calls=%async_computation.1 | async-start | bytes 2097152 | tf_op jit(solution)/shard_map/all_to_all | solution.py:343
  89.2 1.0 %copy-start.1 = (f32[8,16,16,128]{3,2,1,0:T(8,128)}, f32[8,16,16,128]{3,2,1,0:T(8,128)S(1)}, u32[]{:S(2)}) copy-start(f32[8,16,16,128]{3,2,1,0:T(8,128)S(1)} %all-to-all-done.1.x_ref) | copy-start | bytes 3145732

commit v2 on v1

v2 whole, which is shorter than its diff:
```python
import functools
import math

import jax
import jax.numpy as jnp
import numpy as np
from jax import lax
from jax.experimental import pallas as pl
from jax.experimental.pallas import tpu as pltpu
from jax.sharding import PartitionSpec as P

SAMPLES = 4096
BINS = 512
BAND = 64
LOW_BIN = 64
LAGS = 1024
TAPS = 129
LANES = 2 * BAND
EPSILON = 1e-06
STEP = 64
CHUNK = 512
MIB = 1024 * 1024


def unit_circle(products):
    angles = (products % SAMPLES).astype(np.float64) * (2.0 * math.pi / SAMPLES)
    return np.cos(angles).astype(np.float32), (-np.sin(angles)).astype(np.float32)


def banded(first, second):
    rows = first.shape[0]
    parts = [a.reshape(rows, BINS // BAND, 1, BAND) for a in (first, second)]
    return np.concatenate(parts, 2).reshape(rows, 2 * BINS)


def forward_tables():
    bins = LOW_BIN + np.arange(BINS, dtype=np.int64)
    cos, msin = unit_circle(np.arange(TAPS, dtype=np.int64)[:, None] * bins[None, :])
    fine = banded(cos, msin)
    starts = np.arange(0, SAMPLES, STEP, dtype=np.int64)
    cos, msin = unit_circle(starts[:, None] * bins[None, :])
    return fine, banded(cos, cos), banded(-msin, msin)


def lag_tables(parts):
    lags = np.arange(LAGS, dtype=np.int64) - LAGS // 2
    cos, msin = unit_circle(np.arange(BAND, dtype=np.int64)[:, None] * lags[None, :])
    first = LOW_BIN + BAND * np.arange(parts, dtype=np.int64)
    cos0, msin0 = unit_circle(first[:, None] * lags[None, :])
    return cos, msin, cos0, msin0


def spectra_kernel(x_ref, taps_ref, fine_ref, turn_c_ref, turn_s_ref, out_ref, total, swapped, table):
    step = pl.program_id(0)
    nodes = out_ref.shape[1]

    @pl.when(step == 0)
    def _():
        for band in range(BINS // BAND):
            cols = pl.ds(band * LANES, LANES)
            swapped[:, cols] = pltpu.roll(fine_ref[0:STEP, cols], BAND, 1)

    for block in range(CHUNK // STEP):
        row = pl.ds(step * (CHUNK // STEP) + block, 1)
        turned = fine_ref[0:STEP, :] * turn_c_ref[row, :] + swapped[...] * turn_s_ref[row, :]
        table[block * STEP : (block + 1) * STEP, :] = turned.astype(jnp.bfloat16)
    product = jnp.dot(x_ref[...], table[...], preferred_element_type=jnp.float32)

    for band in range(BINS // BAND):
        here = product[:, band * LANES : (band + 1) * LANES]

        @pl.when(step == 0)
        def _(band=band, here=here):
            total[band] = here

        @pl.when(step > 0)
        def _(band=band, here=here):
            total[band] += here

    @pl.when(step == pl.num_programs(0) - 1)
    def _():
        response = jnp.dot(
            taps_ref[:, 0:128],
            fine_ref[0:128, :],
            precision=lax.Precision.HIGHEST,
            preferred_element_type=jnp.float32,
        )
        response = response + taps_ref[:, 128:129] * fine_ref[128:129, :]
        low = lax.broadcasted_iota(jnp.int32, (1, LANES), 1) < BAND
        for band in range(BINS // BAND):
            here = response[:, band * LANES : (band + 1) * LANES]
            other = pltpu.roll(jnp.broadcast_to(here, (8, LANES)), BAND, 1)[0:1, :]
            same = jnp.where(low, here, other)
            cross = jnp.where(low, -other, here)
            for node in range(nodes):
                rows = pl.ds(node, out_ref.shape[2], stride=nodes)
                raw = total[band, rows, :]
                power = jnp.sum(raw * raw, 1, keepdims=True) * (1.0 / BAND)
                white = raw * lax.rsqrt(power + EPSILON)
                turned = white * same + pltpu.roll(white, BAND, 1) * cross
                out_ref[band, node] = turned.astype(jnp.bfloat16)


def own_spectra(rows, taps, nodes):
    fine, turn_c, turn_s = (jnp.asarray(t) for t in forward_tables())
    count = rows.shape[0]
    bands = BINS // BAND
    fixed = lambda shape: pl.BlockSpec(shape, lambda i: (0,) * len(shape))
    return pl.pallas_call(
        spectra_kernel,
        grid=(SAMPLES // CHUNK,),
        in_specs=[
            pl.BlockSpec((count, CHUNK), lambda i: (0, i)),
            fixed(taps.shape),
            fixed(fine.shape),
            fixed(turn_c.shape),
            fixed(turn_s.shape),
        ],
        out_specs=fixed((bands, nodes, count // nodes, LANES)),
        out_shape=jax.ShapeDtypeStruct((bands, nodes, count // nodes, LANES), jnp.bfloat16),
        scratch_shapes=[
            pltpu.VMEM((bands, count, LANES), jnp.float32),
            pltpu.VMEM((STEP, 2 * BINS), jnp.float32),
            pltpu.VMEM((CHUNK, 2 * BINS), jnp.bfloat16),
        ],
        compiler_params=pltpu.CompilerParams(vmem_limit_bytes=60 * MIB),
        name="own_spectra",
    )(rows, taps, fine, turn_c, turn_s)


def lag_table_kernel(cos_ref, msin_ref, cos0_ref, msin0_ref, high_ref, low_ref, *, factor):
    part = pl.program_id(0)
    c0 = cos0_ref[pl.ds(part, 1), :] * factor
    s0 = msin0_ref[pl.ds(part, 1), :] * factor
    cos, msin = cos_ref[...], msin_ref[...]
    for half, values in ((0, cos * c0 - msin * s0), (1, cos * s0 + msin * c0)):
        high = values.astype(jnp.bfloat16)
        rows = pl.ds(half * BAND, BAND)
        high_ref[0, rows, :] = high
        low_ref[0, rows, :] = (values - high.astype(jnp.float32)).astype(jnp.bfloat16)


def make_lag_tables(parts, factor):
    tables = [jnp.asarray(t) for t in lag_tables(parts)]
    shape = jax.ShapeDtypeStruct((parts, LANES, LAGS), jnp.bfloat16)
    block = pl.BlockSpec((1, LANES, LAGS), lambda i: (i, 0, 0))
    return pl.pallas_call(
        functools.partial(lag_table_kernel, factor=factor),
        grid=(parts,),
        in_specs=[pl.BlockSpec(t.shape, lambda i: (0, 0)) for t in tables],
        out_specs=[block, block],
        out_shape=[shape, shape],
        compiler_params=pltpu.CompilerParams(vmem_limit_bytes=6 * MIB),
        name="lag_tables",
    )(*tables)


def by_bin_kernel(odd_ref, x_ref, first_ref, second_ref, turned, *, groups, nodes):
    windows = x_ref.shape[2]
    row = lax.broadcasted_iota(jnp.int32, (LANES, LANES), 0)
    unit = (row == lax.broadcasted_iota(jnp.int32, (LANES, LANES), 1)).astype(jnp.bfloat16)

    def turn(index, _):
        tile, node = index // nodes, index % nodes
        parts = [x_ref[tile * groups + g, node] for g in range(groups)]
        values = lax.dot_general(
            unit, jnp.concatenate(parts, 0), (((1,), (1,)), ((), ())), preferred_element_type=jnp.float32
        )
        turned[pl.ds(pl.multiple_of(index * LANES, LANES), LANES), :] = values
        return 0

    lax.fori_loop(0, 2 * nodes, turn, 0, unroll=4)
    odd = odd_ref[0]
    for out_ref, tile in ((first_ref, 1 - odd), (second_ref, odd)):
        start = tile * (nodes * LANES)

        def one(f, _, out_ref=out_ref, start=start):
            real = turned[pl.ds(start + f, nodes, stride=LANES), :]
            imag = turned[pl.ds(start + BAND + f, nodes, stride=LANES), :]
            out_ref[f] = jnp.concatenate([real, imag], 1).astype(jnp.bfloat16)
            return 0

        lax.fori_loop(0, BAND, one, 0, unroll=4)


def by_bin(odd, received, nodes):
    parts, _, windows, _ = received.shape
    groups = parts // 2
    shape = jax.ShapeDtypeStruct((BAND, nodes, 2 * groups * windows), jnp.bfloat16)
    vmem = pl.BlockSpec(memory_space=pltpu.VMEM)
    return pl.pallas_call(
        functools.partial(by_bin_kernel, groups=groups, nodes=nodes),
        out_shape=[shape, shape],
        in_specs=[pl.BlockSpec(memory_space=pltpu.SMEM), vmem],
        out_specs=[vmem, vmem],
        scratch_shapes=[pltpu.VMEM((2 * nodes * LANES, groups * windows), jnp.float32)],
        compiler_params=pltpu.CompilerParams(vmem_limit_bytes=8 * MIB),
        name="by_bin",
    )(odd, received)


def cross_select_kernel(odd_ref, a_ref, b_ref, ha_ref, hb_ref, select_ref, out_ref, cross):
    nodes, width = a_ref.shape[1], a_ref.shape[2]
    stations, count = 2 * nodes, 4 * nodes
    contract = (((1,), (1,)), ((), ()))

    def one_bin(f, _):
        own = jnp.concatenate([a_ref[f], b_ref[f]], 0)
        partners = jnp.concatenate([own, ha_ref[f], hb_ref[f]], 0)
        turned = jnp.concatenate([own[:, width // 2 :], -own[:, : width // 2]], 1)
        both = jnp.concatenate([own, turned], 0)
        partners = jnp.concatenate([partners, partners], 0)
        cross[pl.ds(pl.multiple_of(f * count, count), count), :] = lax.dot_general(
            both, partners, contract, preferred_element_type=jnp.float32
        )
        return 0

    lax.fori_loop(0, BAND, one_bin, 0, unroll=4)
    slots = out_ref.shape[2]
    destinations = out_ref.shape[0] // 2
    odd = odd_ref[0]
    left = lax.broadcasted_iota(jnp.int32, (2 * BAND, 2 * count), 1) < count

    def one_node(index, _):
        real = cross[pl.ds(index, BAND, stride=count), :]
        imag = cross[pl.ds(stations + index, BAND, stride=count), :]
        values = jnp.concatenate([real, imag], 0)
        high = values.astype(jnp.bfloat16).astype(jnp.float32)
        split = jnp.where(left, high, values - high).astype(jnp.bfloat16)
        picked = lax.dot_general(select_ref[index], split, contract, preferred_element_type=jnp.float32)
        which, node = index // nodes, index % nodes
        tile = jnp.where(which == 0, 1 - odd, odd)
        for d in range(destinations):
            out_ref[tile * destinations + d, node] = picked[d * slots : (d + 1) * slots, :]
        return 0

    lax.fori_loop(0, stations, one_node, 0, unroll=2)


def cross_select(odd, a, b, halo_a, halo_b, select, parts):
    nodes = a.shape[1]
    slots = select.shape[1] // (parts // 2)
    vmem = pl.BlockSpec(memory_space=pltpu.VMEM)
    return pl.pallas_call(
        cross_select_kernel,
        out_shape=jax.ShapeDtypeStruct((parts, nodes, slots, LANES), jnp.float32),
        in_specs=[pl.BlockSpec(memory_space=pltpu.SMEM)] + [vmem] * 5,
        out_specs=vmem,
        scratch_shapes=[pltpu.VMEM((BAND * 4 * nodes, 8 * nodes), jnp.float32)],
        compiler_params=pltpu.CompilerParams(vmem_limit_bytes=12 * MIB),
        name="cross_select",
    )(odd, a, b, halo_a, halo_b, select)


def inverse_kernel(x_ref, high_ref, low_ref, out_ref):
    parts, nodes, slots = x_ref.shape[0], x_ref.shape[1], x_ref.shape[2]
    total = None
    for part in range(parts):
        values = x_ref[part].reshape(nodes * slots, LANES)
        high = values.astype(jnp.bfloat16)
        low = (values - high.astype(jnp.float32)).astype(jnp.bfloat16)
        dot = functools.partial(jnp.dot, preferred_element_type=jnp.float32)
        term = dot(high, high_ref[part]) + (dot(low, high_ref[part]) + dot(high, low_ref[part]))
        total = term if total is None else total + term
    out_ref[...] = total.reshape(out_ref.shape)


def inverse(stack, high, low):
    parts, nodes, slots, _ = stack.shape
    block = 256
    table = pl.BlockSpec((parts, LANES, block), lambda i: (0, 0, i))
    return pl.pallas_call(
        inverse_kernel,
        grid=(LAGS // block,),
        in_specs=[pl.BlockSpec(stack.shape, lambda i: (0, 0, 0, 0)), table, table],
        out_specs=pl.BlockSpec((nodes, slots, block), lambda i: (0, 0, i)),
        out_shape=jax.ShapeDtypeStruct((nodes, slots, LAGS), jnp.float32),
        compiler_params=pltpu.CompilerParams(vmem_limit_bytes=10 * MIB),
        name="inverse",
    )(stack, high, low)


def per_device(traces, taps, neighbours, valid, *, pairs, wins):
    windows, nodes, samples = traces.shape
    parts = 2 * wins
    place = lax.axis_index("pairs")
    parity = place % 2
    both = ("pairs", "win")
    groups = [[p * wins + w for p in (k, k + 1) for w in range(wins)] for k in range(0, pairs, 2)]
    exchange = functools.partial(
        lax.all_to_all, axis_name=both, split_axis=0, concat_axis=0, tiled=True, axis_index_groups=groups
    )

    odd = (place // 2) % 2
    first = 1 - odd
    is_first = parity == first
    tile, member = neighbours // nodes, neighbours % nodes
    inside = tile // 2 == place // 2
    block = jnp.where(inside, jnp.where(tile % 2 == first, 0, 1), jnp.where(is_first, 2, 3))
    code = jnp.where(valid != 0, block * nodes + member, -1)
    other = lax.ppermute(code, "pairs", [(i, i ^ 1) for i in range(pairs)])
    codes = jnp.where(is_first, jnp.concatenate([code, other], 0), jnp.concatenate([other, code], 0))
    columns = jnp.arange(8 * nodes, dtype=jnp.int32) % (4 * nodes)
    select = (codes[:, :, None] == columns[None, None, :]).astype(jnp.bfloat16)

    factor = 1.0 / math.sqrt(BINS * windows * wins)
    high, low = make_lag_tables(parts, factor)

    spectra = own_spectra(traces.reshape(windows * nodes, samples), taps.reshape(1, TAPS), nodes)
    odd = odd.reshape(1)
    a, b = by_bin(odd, exchange(spectra), nodes)
    swap_a = [(i, i ^ 2) for i in range(pairs) if (i ^ 2) < pairs]
    swap_b = [(i, j) for i in range(2, pairs) for j in [((i - 2) ^ 2) + 2] if j < pairs]
    halo_a = lax.ppermute(a, "pairs", swap_a)
    halo_b = lax.ppermute(b, "pairs", swap_b)
    stack = cross_select(odd, a, b, halo_a, halo_b, select, parts)
    return inverse(exchange(stack), high, low)


def solution(mesh):
    placed = (P("win", "pairs", None), P(), P("pairs", None), P("pairs", None))
    body = functools.partial(per_device, pairs=mesh.shape["pairs"], wins=mesh.shape["win"])
    return jax.shard_map(
        body, mesh=mesh, in_specs=placed, out_specs=P("pairs", "win", None), check_vma=False
    )
```

time: 97.3 us -> 95.4 us (0.980)
  the two profiles are of different devices: /device:TPU:0 before, /device:TPU:16 now
where the time goes in v2:
time: 95.4 us; the launch traced here: 94.9 us
  Pallas kernels  40.7 us (43%)
  waiting for transfers between devices  36.9 us (39%)
  starting transfers between devices  12.8 us (13%)
  local copies, waits for them, and re-layouts  3.89 us (4%)
    pallas_call x1, Pallas kernels, own_spectra(): pl.pallas_call(spectra_kernel, grid=(SAMPLES // CHUNK,), in_specs=[pl.Blo...  23.8 us
    all_to_all x1, waiting for transfers between devices, per_device(): a, b = by_bin(odd, exchange(spectra), nodes)  15.4 us
    all_to_all x1, waiting for transfers between devices, per_device(): return inverse(exchange(stack), high, low)  12 us
    pallas_call x1, Pallas kernels, cross_select(): pl.pallas_call(cross_select_kernel, out_shape=jax.ShapeDtypeStruct((parts...  7.55 us
    pallas_call x1, Pallas kernels, inverse(): pl.pallas_call(inverse_kernel, grid=(LAGS // block,), in_specs=[pl.BlockS...  5.15 us
    all_to_all x1, starting transfers between devices, per_device(): return inverse(exchange(stack), high, low)  4.8 us
    unnamed x16, local copies, waits for them, and re-layouts  3.89 us
    all_to_all x1, starting transfers between devices, per_device(): a, b = by_bin(odd, exchange(spectra), nodes)  3.85 us
  transfers between devices with their start and end apart: 5, of which 5 were waited for; matrix products, arithmetic and copies ran while one was open for 0% of the time, Pallas kernels for 1%

profile of v2, /device:TPU:16, one launch (start us, length us, event | category | flops | bytes accessed | tf_op | source)
XLA Modules:
  0.0 94.9 jit_solution(15857971538787295066)
XLA Ops:
  0.0 23.8 %own_spectra.1 = bf16[8,16,32,128]{3,2,1,0:T(8,128)(2,1)} custom-call(bf16[512,4096]{1,0:T(8,128)(2,1)} %bitcast.3, f32[1,129]{1,0:T(1,128)} %bitcast.4, f32[129,1024]{1,0:T(8,128)} %constant.113.clone.fine_ref, f32[64,1024]{1,0:T(8,128)} %constant.114.clone.turn_c_ref, f32[64,1024]{1,0:T(8,128)} %constant.115.clone.turn_s_ref), custom_call_target="tpu_custom_call" | custom-call | tf_op jit(solution)/shard_map/own_spectra/pallas_call | solution.py:109
  23.8 0.0 copy-start.6
  23.8 0.0 copy-start.7
  23.8 3.9 %all-to-all-start = ((bf16[8,16,32,128]{3,2,1,0:T(8,128)(2,1)}), bf16[8,16,32,128]{3,2,1,0:T(8,128)(2,1)S(1)}, u32[]{:S(2)}, u32[]{:S(2)}) async-start(bf16[8,16,32,128]{3,2,1,0:T(8,128)(2,1)} %own_spectra.1), calls=%async_computation | async-start | bytes 2097152 | tf_op jit(solution)/shard_map/all_to_all | solution.py:311
  27.7 15.4 %all-to-all-done.x_ref = bf16[8,16,32,128]{3,2,1,0:T(8,128)(2,1)S(1)} async-done(((bf16[8,16,32,128]{3,2,1,0:T(8,128)(2,1)}), bf16[8,16,32,128]{3,2,1,0:T(8,128)(2,1)S(1)}, u32[]{:S(2)}, u32[]{:S(2)}) %all-to-all-start) | async-done | bytes 1048608 | tf_op jit(solution)/shard_map/all_to_all | solution.py:311
  43.1 3.1 %by_bin.1 = (bf16[64,16,256]{2,1,0:T(8,128)(2,1)S(1)}, bf16[64,16,256]{2,1,0:T(8,128)(2,1)S(1)}) custom-call(s32[1]{0:T(128)} %bitcast.odd_ref, bf16[8,16,32,128]{3,2,1,0:T(8,128)(2,1)S(1)} %all-to-all-done.x_ref), custom_call_target="tpu_custom_call" | custom-call | tf_op jit(solution)/shard_map/by_bin/pallas_call | solution.py:191
  46.3 1.6 %collective-permute-start = (bf16[64,16,256]{2,1,0:T(8,128)(2,1)S(1)}, bf16[64,16,256]{2,1,0:T(8,128)(2,1)S(1)}, u32[]{:S(2)}, u32[]{:S(2)}) collective-permute-start(bf16[64,16,256]{2,1,0:T(8,128)(2,1)S(1)} %get-tuple-element.9.a_ref), channel_id=1, source_target_pairs={{0,8},{4,12},{8,0},{12,4},{16,24},{20,28},{24,16},{28,20},{1,9},{5... | collective-permute-start | bytes 1572872 | tf_op jit(solution)/shard_map/ppermute | solution.py:314
  47.9 1.9 %collective-permute-start.1 = (bf16[64,16,256]{2,1,0:T(8,128)(2,1)S(1)}, bf16[64,16,256]{2,1,0:T(8,128)(2,1)S(1)}, u32[]{:S(2)}, u32[]{:S(2)}) collective-permute-start(bf16[64,16,256]{2,1,0:T(8,128)(2,1)S(1)} %get-tuple-element.10.b_ref), channel_id=1, source_target_pairs={{8,16},{12,20},{16,8},{20,12},{9,17},{13,21},{17,9},{21,13},{10,18... | collective-permute-start | bytes 1572872 | tf_op jit(solution)/shard_map/ppermute | solution.py:315
  49.8 0.0 copy-done.6
  49.8 0.0 copy-done.7
  49.9 0.6 collective-permute-start.2
  50.5 3.1 %collective-permute-done.2 = s32[16,64]{1,0:T(8,128)S(1)} collective-permute-done((s32[16,64]{1,0:T(8,128)S(1)}, s32[16,64]{1,0:T(8,128)S(1)}, u32[]{:S(2)}, u32[]{:S(2)}) %collective-permute-start.2) | collective-permute-done | bytes 4128 | tf_op jit(solution)/shard_map/ppermute | solution.py:301
  53.6 0.3 compare_convert_fusion.select_ref
  53.9 0.0 copy-start.2
  54.0 0.0 copy-start.4
  54.0 0.0 copy-start.5
  54.0 3.2 %collective-permute-done.ha_ref = bf16[64,16,256]{2,1,0:T(8,128)(2,1)S(1)} collective-permute-done((bf16[64,16,256]{2,1,0:T(8,128)(2,1)S(1)}, bf16[64,16,256]{2,1,0:T(8,128)(2,1)S(1)}, u32[]{:S(2)}, u32[]{:S(2)}) %collective-permute-start) | collective-permute-done | bytes 524320 | tf_op jit(solution)/shard_map/ppermute | solution.py:314
  57.2 3.2 %collective-permute-done.1.hb_ref = bf16[64,16,256]{2,1,0:T(8,128)(2,1)S(1)} collective-permute-done((bf16[64,16,256]{2,1,0:T(8,128)(2,1)S(1)}, bf16[64,16,256]{2,1,0:T(8,128)(2,1)S(1)}, u32[]{:S(2)}, u32[]{:S(2)}) %collective-permute-start.1) | collective-permute-done | bytes 524320 | tf_op jit(solution)/shard_map/ppermute | solution.py:315
  60.4 7.5 %cross_select.1 = f32[8,16,16,128]{3,2,1,0:T(8,128)} custom-call(s32[1]{0:T(128)} %bitcast.odd_ref, bf16[64,16,256]{2,1,0:T(8,128)(2,1)S(1)} %get-tuple-element.9.a_ref, bf16[64,16,256]{2,1,0:T(8,128)(2,1)S(1)} %get-tuple-element.10.b_ref, bf16[64,16,256]{2,1,0:T(8,128)(2,1)S(1)} %collective-permute-done.ha_ref, ...), custom_call_target="tpu_custom_call" | custom-call | tf_op jit(solution)/shard_map/cross_select/pallas_call | solution.py:244
  67.9 4.8 %all-to-all-start.1 = ((f32[8,16,16,128]{3,2,1,0:T(8,128)}), f32[8,16,16,128]{3,2,1,0:T(8,128)S(1)}, u32[]{:S(2)}, u32[]{:S(2)}) async-start(f32[8,16,16,128]{3,2,1,0:T(8,128)} %cross_select.1), calls=%async_computation.1 | async-start | bytes 2097152 | tf_op jit(solution)/shard_map/all_to_all | solution.py:317
  72.7 0.0 copy-done.2
  72.7 0.0 copy-done.4
  72.7 0.0 copy-done.5
  72.8 0.0 copy-start.3
  72.8 0.9 copy-done.3
  73.7 1.1 %lag_tables.1 = (bf16[8,128,1024]{2,1,0:T(8,128)(2,1)S(1)}, bf16[8,128,1024]{2,1,0:T(8,128)(2,1)S(1)}) custom-call(f32[64,1024]{1,0:T(8,128)S(1)} %copy-done.3, f32[64,1024]{1,0:T(8,128)S(1)} %copy-done.2, f32[8,1024]{1,0:T(8,128)S(1)} %copy-done.5, f32[8,1024]{1,0:T(8,128)S(1)} %copy-done.4), custom_call_target="tpu_custom_call" | custom-call | tf_op jit(solution)/shard_map/lag_tables/pallas_call | solution.py:147
  74.8 0.0 copy-start
  74.8 1.3 %copy-done = bf16[8,128,1024]{2,1,0:T(8,128)(2,1)} copy-done((bf16[8,128,1024]{2,1,0:T(8,128)(2,1)}, bf16[8,128,1024]{2,1,0:T(8,128)(2,1)S(1)}, u32[]{:S(2)}) %copy-start) | copy-done | bytes 2097176
  76.1 12.0 %all-to-all-done.1.x_ref = f32[8,16,16,128]{3,2,1,0:T(8,128)S(1)} async-done(((f32[8,16,16,128]{3,2,1,0:T(8,128)}), f32[8,16,16,128]{3,2,1,0:T(8,128)S(1)}, u32[]{:S(2)}, u32[]{:S(2)}) %all-to-all-start.1) | async-done | bytes 1048608 | tf_op jit(solution)/shard_map/all_to_all | solution.py:317
  88.1 0.0 copy-start.1
  88.1 1.6 %copy-done.1 = bf16[8,128,1024]{2,1,0:T(8,128)(2,1)S(1)} copy-done((bf16[8,128,1024]{2,1,0:T(8,128)(2,1)S(1)}, bf16[8,128,1024]{2,1,0:T(8,128)(2,1)}, u32[]{:S(2)}) %copy-start.1) | copy-done | bytes 2097176
  89.7 5.2 %inverse.1 = f32[16,16,1024]{2,1,0:T(8,128)} custom-call(f32[8,16,16,128]{3,2,1,0:T(8,128)S(1)} %all-to-all-done.1.x_ref, bf16[8,128,1024]{2,1,0:T(8,128)(2,1)S(1)} %get-tuple-element.11.high_ref, bf16[8,128,1024]{2,1,0:T(8,128)(2,1)S(1)} %copy-done.1), custom_call_target="tpu_custom_call" | custom-call | tf_op jit(solution)/shard_map/inverse/pallas_call | solution.py:272
  (3 shorter events, 0.0 us)
Async XLA Ops:
  23.8 26.0 %copy-start.6 = (s32[16,64]{1,0:T(8,128)S(1)}, s32[16,64]{1,0:T(8,128)}, u32[]{:S(2)}) copy-start(s32[16,64]{1,0:T(8,128)} %param.13) | copy-start | bytes 12292
  23.8 26.0 %copy-start.7 = (s32[16,64]{1,0:T(8,128)S(1)}, s32[16,64]{1,0:T(8,128)}, u32[]{:S(2)}) copy-start(s32[16,64]{1,0:T(8,128)} %param.14) | copy-start | bytes 12292
  23.8 19.3 %all-to-all-start = ((bf16[8,16,32,128]{3,2,1,0:T(8,128)(2,1)}), bf16[8,16,32,128]{3,2,1,0:T(8,128)(2,1)S(1)}, u32[]{:S(2)}, u32[]{:S(2)}) async-start(bf16[8,16,32,128]{3,2,1,0:T(8,128)(2,1)} %own_spectra.1), calls=%async_computation | async-start | bytes 2097152 | tf_op jit(solution)/shard_map/all_to_all | solution.py:311
  46.3 10.9 %collective-permute-start = (bf16[64,16,256]{2,1,0:T(8,128)(2,1)S(1)}, bf16[64,16,256]{2,1,0:T(8,128)(2,1)S(1)}, u32[]{:S(2)}, u32[]{:S(2)}) collective-permute-start(bf16[64,16,256]{2,1,0:T(8,128)(2,1)S(1)} %get-tuple-element.9.a_ref), channel_id=1, source_target_pairs={{0,8},{4,12},{8,0},{12,4},{16,24},{20,28},{24,16},{28,20},{1,9},{5... | collective-permute-start | bytes 1572872 | tf_op jit(solution)/shard_map/ppermute | solution.py:314
  47.9 12.5 %collective-permute-start.1 = (bf16[64,16,256]{2,1,0:T(8,128)(2,1)S(1)}, bf16[64,16,256]{2,1,0:T(8,128)(2,1)S(1)}, u32[]{:S(2)}, u32[]{:S(2)}) collective-permute-start(bf16[64,16,256]{2,1,0:T(8,128)(2,1)S(1)} %get-tuple-element.10.b_ref), channel_id=1, source_target_pairs={{8,16},{12,20},{16,8},{20,12},{9,17},{13,21},{17,9},{21,13},{10,18... | collective-permute-start | bytes 1572872 | tf_op jit(solution)/shard_map/ppermute | solution.py:315
  49.9 3.7 %collective-permute-start.2 = (s32[16,64]{1,0:T(8,128)S(1)}, s32[16,64]{1,0:T(8,128)S(1)}, u32[]{:S(2)}, u32[]{:S(2)}) collective-permute-start(s32[16,64]{1,0:T(8,128)S(1)} %fusion.3), channel_id=1, source_target_pairs={{0,4},{4,0},{8,12},{12,8},{16,20},{20,16},{24,28},{28,24},{1,5},{5... | collective-permute-start | bytes 12296 | tf_op jit(solution)/shard_map/ppermute | solution.py:301
  53.9 18.8 %copy-start.2 = (f32[64,1024]{1,0:T(8,128)S(1)}, f32[64,1024]{1,0:T(8,128)}, u32[]{:S(2)}) copy-start(f32[64,1024]{1,0:T(8,128)} %constant.110.clone.msin_ref) | copy-start | bytes 786436
  54.0 18.8 %copy-start.4 = (f32[8,1024]{1,0:T(8,128)S(1)}, f32[8,1024]{1,0:T(8,128)}, u32[]{:S(2)}) copy-start(f32[8,1024]{1,0:T(8,128)} %constant.112.clone.msin0_ref) | copy-start | bytes 98308
  54.0 18.8 %copy-start.5 = (f32[8,1024]{1,0:T(8,128)S(1)}, f32[8,1024]{1,0:T(8,128)}, u32[]{:S(2)}) copy-start(f32[8,1024]{1,0:T(8,128)} %constant.111.clone.cos0_ref) | copy-start | bytes 98308
  67.9 20.2 %all-to-all-start.1 = ((f32[8,16,16,128]{3,2,1,0:T(8,128)}), f32[8,16,16,128]{3,2,1,0:T(8,128)S(1)}, u32[]{:S(2)}, u32[]{:S(2)}) async-start(f32[8,16,16,128]{3,2,1,0:T(8,128)} %cross_select.1), calls=%async_computation.1 | async-start | bytes 2097152 | tf_op jit(solution)/shard_map/all_to_all | solution.py:317
  72.8 1.0 %copy-start.3 = (f32[64,1024]{1,0:T(8,128)S(1)}, f32[64,1024]{1,0:T(8,128)}, u32[]{:S(2)}) copy-start(f32[64,1024]{1,0:T(8,128)} %constant.109.clone.cos_ref) | copy-start | bytes 786436
  74.8 1.3 %copy-start = (bf16[8,128,1024]{2,1,0:T(8,128)(2,1)}, bf16[8,128,1024]{2,1,0:T(8,128)(2,1)S(1)}, u32[]{:S(2)}) copy-start(bf16[8,128,1024]{2,1,0:T(8,128)(2,1)S(1)} %get-tuple-element.12.low_ref) | copy-start | bytes 6291460
  88.1 1.6 %copy-start.1 = (bf16[8,128,1024]{2,1,0:T(8,128)(2,1)S(1)}, bf16[8,128,1024]{2,1,0:T(8,128)(2,1)}, u32[]{:S(2)}) copy-start(bf16[8,128,1024]{2,1,0:T(8,128)(2,1)} %copy-done) | copy-start | bytes 6291460

commit v3 on v2

v3 whole, which is shorter than its diff:
```python
import functools
import math

import jax
import jax.numpy as jnp
import numpy as np
from jax import lax
from jax.experimental import pallas as pl
from jax.experimental.pallas import tpu as pltpu
from jax.sharding import PartitionSpec as P

SAMPLES = 4096
BINS = 512
BAND = 64
LOW_BIN = 64
LAGS = 1024
TAPS = 129
LANES = 2 * BAND
EPSILON = 1e-06
STEP = 64
CHUNK = 512
MIB = 1024 * 1024
CONTRACT_LAST = (((1,), (1,)), ((), ()))


def unit_circle(products):
    angles = (products % SAMPLES).astype(np.float64) * (2.0 * math.pi / SAMPLES)
    return np.cos(angles).astype(np.float32), (-np.sin(angles)).astype(np.float32)


def banded(first, second):
    rows = first.shape[0]
    parts = [a.reshape(rows, BINS // BAND, 1, BAND) for a in (first, second)]
    return np.concatenate(parts, 2).reshape(rows, 2 * BINS)


def forward_tables():
    bins = LOW_BIN + np.arange(BINS, dtype=np.int64)
    cos, msin = unit_circle(np.arange(TAPS, dtype=np.int64)[:, None] * bins[None, :])
    fine = banded(cos, msin)
    starts = np.arange(0, SAMPLES, STEP, dtype=np.int64)
    cos, msin = unit_circle(starts[:, None] * bins[None, :])
    return fine, banded(cos, cos), banded(-msin, msin)


def lag_tables(parts):
    lags = np.arange(LAGS, dtype=np.int64) - LAGS // 2
    cos, msin = unit_circle(np.arange(BAND, dtype=np.int64)[:, None] * lags[None, :])
    first = LOW_BIN + BAND * np.arange(parts, dtype=np.int64)
    cos0, msin0 = unit_circle(first[:, None] * lags[None, :])
    return cos, msin, cos0, msin0


def spectra_kernel(me_ref, x_hbm, taps_ref, fine_hbm, turn_c_hbm, turn_s_hbm, *refs, steps):
    outs, refs = refs[: 2 * len(steps)], refs[2 * len(steps) :]
    x_ref, fine_ref, turn_c_ref, turn_s_ref, table, total, stage, sems = refs
    count = x_ref.shape[0]
    nodes, windows = outs[0].shape[0], outs[0].shape[1]
    width, halves = 2 * LANES, 2
    rows = count // halves
    me = me_ref[0]
    copies = [
        pltpu.make_async_copy(source, target, sems.at[i])
        for i, (source, target) in enumerate(
            ((fine_hbm, fine_ref), (turn_c_hbm, turn_c_ref), (turn_s_hbm, turn_s_ref))
        )
    ]
    chunks = [
        pltpu.make_async_copy(x_hbm.at[pl.ds(i * rows, rows), :], x_ref.at[pl.ds(i * rows, rows), :], sems.at[3 + i])
        for i in range(halves)
    ]
    for copy in copies + chunks:
        copy.start()

    def start_of(step):
        return pl.multiple_of(((me // 2) ^ step) * width, width)

    def generate(i):
        columns = pl.ds(start_of(steps[i]), width)
        base = fine_ref[0:STEP, columns]
        swapped = jnp.concatenate(
            [pltpu.roll(base[:, c : c + LANES], BAND, 1) for c in range(0, width, LANES)], 1
        )
        for j in range(SAMPLES // STEP):
            row = pl.ds(j, 1)
            turned = base * turn_c_ref[row, columns] + swapped * turn_s_ref[row, columns]
            table[i % 2, j * STEP : (j + 1) * STEP, :] = turned.astype(jnp.bfloat16)

    low = lax.broadcasted_iota(jnp.int32, (1, LANES), 1) < BAND

    def whiten(i):
        columns = pl.ds(start_of(steps[i]), width)
        response = jnp.dot(
            taps_ref[:, 0:128],
            fine_ref[0:128, columns],
            precision=lax.Precision.HIGHEST,
            preferred_element_type=jnp.float32,
        )
        response = response + taps_ref[:, 128:129] * fine_ref[128:129, columns]
        for c in range(2):
            here = response[:, c * LANES : (c + 1) * LANES]
            other = pltpu.roll(jnp.broadcast_to(here, (8, LANES)), BAND, 1)[0:1, :]
            same = jnp.where(low, here, other)
            cross = jnp.where(low, -other, here)
            raw = total[i % 2, c]
            power = jnp.sum(raw * raw, 1, keepdims=True) * (1.0 / BAND)
            white = raw * lax.rsqrt(power + EPSILON)
            stage[c ^ (me % 2)] = white * same + pltpu.roll(white, BAND, 1) * cross
        for c in range(2):
            for node in range(nodes):
                outs[2 * i + c][node] = stage[c, pl.ds(node, windows, stride=nodes), :].astype(jnp.bfloat16)

    for copy in copies:
        copy.wait()
    for i in range(len(steps)):
        if i == 0:
            generate(0)
        for part in range(halves if i == 0 else 1):
            if i == 0:
                chunks[part].wait()
                here = pl.ds(part * rows, rows)
            else:
                here = pl.ds(0, count)
            product = jnp.dot(x_ref[here, :], table[i % 2], preferred_element_type=jnp.float32)
            for c in range(2):
                total[i % 2, c, here, :] = product[:, c * LANES : (c + 1) * LANES]
        if i + 1 < len(steps):
            generate(i + 1)
        if i > 0:
            whiten(i - 1)
    whiten(len(steps) - 1)


def own_spectra(me, rows, taps, nodes, steps):
    tables = [jnp.asarray(t) for t in forward_tables()]
    count = rows.shape[0]
    hbm = pl.BlockSpec(memory_space=pltpu.HBM)
    vmem = pl.BlockSpec(memory_space=pltpu.VMEM)
    shape = jax.ShapeDtypeStruct((nodes, count // nodes, LANES), jnp.bfloat16)
    return pl.pallas_call(
        functools.partial(spectra_kernel, steps=steps),
        in_specs=[pl.BlockSpec(memory_space=pltpu.SMEM), hbm, vmem, hbm, hbm, hbm],
        out_specs=[vmem] * (2 * len(steps)),
        out_shape=[shape] * (2 * len(steps)),
        scratch_shapes=[
            pltpu.VMEM(rows.shape, jnp.bfloat16),
            *[pltpu.VMEM(t.shape, jnp.float32) for t in tables],
            pltpu.VMEM((2, SAMPLES, 2 * LANES), jnp.bfloat16),
            pltpu.VMEM((2, 2, count, LANES), jnp.float32),
            pltpu.VMEM((2, count, LANES), jnp.float32),
            pltpu.SemaphoreType.DMA((5,)),
        ],
        compiler_params=pltpu.CompilerParams(vmem_limit_bytes=60 * MIB),
        cost_estimate=pl.CostEstimate(
            flops=4 * len(steps) * count * SAMPLES * LANES, bytes_accessed=2 * count * SAMPLES, transcendentals=0
        ),
        name="own_spectra",
    )(me, rows, taps, *tables)


def lag_table_kernel(cos_ref, msin_ref, cos0_ref, msin0_ref, high_ref, low_ref, *, factor):
    part = pl.program_id(0)
    c0 = cos0_ref[pl.ds(part, 1), :] * factor
    s0 = msin0_ref[pl.ds(part, 1), :] * factor
    cos, msin = cos_ref[...], msin_ref[...]
    for half, values in ((0, cos * c0 - msin * s0), (1, cos * s0 + msin * c0)):
        high = values.astype(jnp.bfloat16)
        rows = pl.ds(half * BAND, BAND)
        high_ref[0, rows, :] = high
        low_ref[0, rows, :] = (values - high.astype(jnp.float32)).astype(jnp.bfloat16)


def make_lag_tables(parts, factor):
    tables = [jnp.asarray(t) for t in lag_tables(parts)]
    shape = jax.ShapeDtypeStruct((parts, LANES, LAGS), jnp.bfloat16)
    block = pl.BlockSpec((1, LANES, LAGS), lambda i: (i, 0, 0))
    return pl.pallas_call(
        functools.partial(lag_table_kernel, factor=factor),
        grid=(parts,),
        in_specs=[pl.BlockSpec(t.shape, lambda i: (0, 0)) for t in tables],
        out_specs=[block, block],
        out_shape=[shape, shape],
        compiler_params=pltpu.CompilerParams(vmem_limit_bytes=6 * MIB),
        name="lag_tables",
    )(*tables)


def by_bin_kernel(place_ref, *refs):
    blocks, (first_ref, second_ref, turned) = refs[:-3], refs[-3:]
    groups = len(blocks) // 2
    nodes = blocks[0].shape[0]
    row = lax.broadcasted_iota(jnp.int32, (LANES, LANES), 0)
    unit = (row == lax.broadcasted_iota(jnp.int32, (LANES, LANES), 1)).astype(jnp.bfloat16)
    for tile in range(2):
        here = blocks[tile * groups : (tile + 1) * groups]

        def turn(node, _, here=here, tile=tile):
            values = jnp.concatenate([block[node] for block in here], 0)
            values = lax.dot_general(unit, values, CONTRACT_LAST, preferred_element_type=jnp.float32)
            turned[pl.ds(pl.multiple_of((tile * nodes + node) * LANES, LANES), LANES), :] = values
            return 0

        lax.fori_loop(0, nodes, turn, 0, unroll=4)
    own_at = place_ref[1]
    for out_ref, tile in ((first_ref, own_at), (second_ref, 1 - own_at)):
        start = tile * (nodes * LANES)

        def one(f, _, out_ref=out_ref, start=start):
            real = turned[pl.ds(start + f, nodes, stride=LANES), :]
            imag = turned[pl.ds(start + BAND + f, nodes, stride=LANES), :]
            out_ref[f] = jnp.concatenate([real, imag], 1).astype(jnp.bfloat16)
            return 0

        lax.fori_loop(0, BAND, one, 0, unroll=4)


def by_bin(place, blocks):
    nodes, windows, _ = blocks[0].shape
    windows = windows * len(blocks) // 2
    shape = jax.ShapeDtypeStruct((BAND, nodes, 2 * windows), jnp.bfloat16)
    vmem = pl.BlockSpec(memory_space=pltpu.VMEM)
    return pl.pallas_call(
        by_bin_kernel,
        out_shape=[shape, shape],
        in_specs=[pl.BlockSpec(memory_space=pltpu.SMEM)] + [vmem] * len(blocks),
        out_specs=[vmem, vmem],
        scratch_shapes=[pltpu.VMEM((2 * nodes * LANES, windows), jnp.float32)],
        compiler_params=pltpu.CompilerParams(vmem_limit_bytes=8 * MIB),
        name="by_bin",
    )(place, *blocks)


def pick_slots(cross_ref, select_ref, outs, where, nodes):
    stations, count = 2 * nodes, 4 * nodes
    slots = outs[0].shape[1]
    left = lax.broadcasted_iota(jnp.int32, (2 * BAND, 2 * count), 1) < count

    def one_node(node, _):
        index = where * nodes + node
        real = cross_ref[pl.ds(index, BAND, stride=count), :]
        imag = cross_ref[pl.ds(stations + index, BAND, stride=count), :]
        values = jnp.concatenate([real, imag], 0)
        high = values.astype(jnp.bfloat16).astype(jnp.float32)
        split = jnp.where(left, high, values - high).astype(jnp.bfloat16)
        picked = lax.dot_general(select_ref[index], split, CONTRACT_LAST, preferred_element_type=jnp.float32)
        for d, out_ref in enumerate(outs):
            out_ref[node] = picked[d * slots : (d + 1) * slots, :]
        return 0

    lax.fori_loop(0, nodes, one_node, 0, unroll=4)


def cross_kernel(place_ref, a_ref, b_ref, ha_ref, hb_ref, select_ref, cross, *outs):
    nodes, width = a_ref.shape[1], a_ref.shape[2]
    count = 4 * nodes

    def one_bin(f, _):
        own = jnp.concatenate([a_ref[f], b_ref[f]], 0)
        partners = jnp.concatenate([own, ha_ref[f], hb_ref[f]], 0)
        turned = jnp.concatenate([own[:, width // 2 :], -own[:, : width // 2]], 1)
        both = jnp.concatenate([own, turned], 0)
        partners = jnp.concatenate([partners, partners], 0)
        cross[pl.ds(pl.multiple_of(f * count, count), count), :] = lax.dot_general(
            both, partners, CONTRACT_LAST, preferred_element_type=jnp.float32
        )
        return 0

    lax.fori_loop(0, BAND, one_bin, 0, unroll=8)
    pick_slots(cross, select_ref, outs, 1 - place_ref[1], nodes)


def own_slots_kernel(place_ref, cross_ref, select_ref, *outs):
    pick_slots(cross_ref, select_ref, outs, place_ref[1], outs[0].shape[0])


def cross_products(place, a, b, halo_a, halo_b, select, wins):
    nodes = a.shape[1]
    block = jax.ShapeDtypeStruct((nodes, select.shape[1] // wins, LANES), jnp.float32)
    vmem = pl.BlockSpec(memory_space=pltpu.VMEM)
    cross, *others = pl.pallas_call(
        cross_kernel,
        out_shape=[jax.ShapeDtypeStruct((BAND * 4 * nodes, 8 * nodes), jnp.float32)] + [block] * wins,
        in_specs=[pl.BlockSpec(memory_space=pltpu.SMEM)] + [vmem] * 5,
        out_specs=[vmem] * (1 + wins),
        compiler_params=pltpu.CompilerParams(vmem_limit_bytes=12 * MIB),
        name="cross_products",
    )(place, a, b, halo_a, halo_b, select)
    own = pl.pallas_call(
        own_slots_kernel,
        out_shape=[block] * wins,
        in_specs=[pl.BlockSpec(memory_space=pltpu.SMEM)] + [vmem] * 2,
        out_specs=[vmem] * wins,
        compiler_params=pltpu.CompilerParams(vmem_limit_bytes=8 * MIB),
        cost_estimate=pl.CostEstimate(flops=1 << 32, bytes_accessed=1 << 24, transcendentals=0),
        name="own_slots",
    )(place, cross, select)
    return own, others


def inverse_kernel(me_ref, high_ref, low_ref, *refs):
    blocks, out_ref = refs[:-1], refs[-1]
    nodes, slots, _ = blocks[0].shape
    me = me_ref[0]
    dot = functools.partial(jnp.dot, preferred_element_type=jnp.float32)
    total = None
    for d, block in enumerate(blocks):
        part = me ^ d
        values = block[...].reshape(nodes * slots, LANES)
        high = values.astype(jnp.bfloat16)
        low = (values - high.astype(jnp.float32)).astype(jnp.bfloat16)
        term = dot(high, high_ref[part]) + (dot(low, high_ref[part]) + dot(high, low_ref[part]))
        total = term if total is None else total + term
    out_ref[...] = total.reshape(out_ref.shape)


def inverse(me, blocks, high, low):
    nodes, slots, _ = blocks[0].shape
    width = 256
    table = pl.BlockSpec((high.shape[0], LANES, width), lambda i: (0, 0, i))
    return pl.pallas_call(
        inverse_kernel,
        grid=(LAGS // width,),
        in_specs=[pl.BlockSpec(memory_space=pltpu.SMEM), table, table]
        + [pl.BlockSpec(blocks[0].shape, lambda i: (0, 0, 0))] * len(blocks),
        out_specs=pl.BlockSpec((nodes, slots, width), lambda i: (0, 0, i)),
        out_shape=jax.ShapeDtypeStruct((nodes, slots, LAGS), jnp.float32),
        compiler_params=pltpu.CompilerParams(vmem_limit_bytes=10 * MIB),
        name="inverse",
    )(me, high, low, *blocks)


def per_device(traces, taps, neighbours, valid, *, pairs, wins):
    windows, nodes, samples = traces.shape
    parts = 2 * wins
    place = lax.axis_index("pairs")
    win = lax.axis_index("win")
    parity = place % 2
    me = parity * wins + win

    def exchange(blocks):
        moved = list(blocks)
        for d in range(parts - 1, 0, -1):
            hop = [(i, (((i // wins) ^ (d // wins)) * wins) + ((i % wins) ^ (d % wins))) for i in range(pairs * wins)]
            moved[d] = lax.ppermute(blocks[d], ("pairs", "win"), hop)
        return moved

    odd = (place // 2) % 2
    first = 1 - odd
    is_first = parity == first
    tile, member = neighbours // nodes, neighbours % nodes
    inside = tile // 2 == place // 2
    block = jnp.where(inside, jnp.where(tile % 2 == first, 0, 1), jnp.where(is_first, 2, 3))
    code = jnp.where(valid != 0, block * nodes + member, -1)
    other = lax.ppermute(code, "pairs", [(i, i ^ 1) for i in range(pairs)])
    codes = jnp.where(is_first, jnp.concatenate([code, other], 0), jnp.concatenate([other, code], 0))
    codes = codes.reshape(2 * nodes, wins, -1)
    for bit in (1 << k for k in range((wins - 1).bit_length())):
        split = codes.reshape(2 * nodes, wins // (2 * bit), 2, -1)
        codes = jnp.where(win & bit != 0, split[:, :, ::-1], split)
    codes = codes.reshape(2 * nodes, -1)
    columns = jnp.arange(8 * nodes, dtype=jnp.int32) % (4 * nodes)
    select = (codes[:, :, None] == columns[None, None, :]).astype(jnp.bfloat16)

    factor = 1.0 / math.sqrt(BINS * windows * wins)
    high, low = make_lag_tables(parts, factor)

    where = jnp.stack([me, jnp.where(is_first, 0, 1)]).astype(jnp.int32)
    rows, taps = traces.reshape(windows * nodes, samples), taps.reshape(1, TAPS)
    spectra = [None] * parts
    for steps in ((3, 1), (2, 0)):
        found = own_spectra(where, rows, taps, nodes, steps)
        for i, step in enumerate(steps):
            spectra[2 * step], spectra[2 * step + 1] = found[2 * i], found[2 * i + 1]
    a, b = by_bin(where, exchange(spectra))
    swap_a = [(i, i ^ 2) for i in range(pairs) if (i ^ 2) < pairs]
    swap_b = [(i, j) for i in range(2, pairs) for j in [((i - 2) ^ 2) + 2] if j < pairs]
    halo_a = lax.ppermute(a, "pairs", swap_a)
    halo_b = lax.ppermute(b, "pairs", swap_b)
    own, others = cross_products(where, a, b, halo_a, halo_b, select, wins)
    return inverse(where, exchange([*own, *others]), high, low)


def solution(mesh):
    placed = (P("win", "pairs", None), P(), P("pairs", None), P("pairs", None))
    body = functools.partial(per_device, pairs=mesh.shape["pairs"], wins=mesh.shape["win"])
    return jax.shard_map(
        body, mesh=mesh, in_specs=placed, out_specs=P("pairs", "win", None), check_vma=False
    )
```

time: 95.4 us -> 81.4 us (0.85)
  Pallas kernels: 40.7 us -> 31.7 us
  waiting for transfers between devices: 36.9 us -> 28.6 us
  starting transfers between devices: 12.8 us -> 17 us
  local copies, waits for them, and re-layouts: 3.89 us -> 1.17 us
  other arithmetic: 0.38 us -> 1.84 us
    all_to_all x2 -> x0, waiting for transfers between devices: 27.4 us -> none  [the longest x1 15.4 us: per_device(): a, b = by_bin(odd, exchange(spectra), nodes)]
    ppermute x0 -> x14, waiting for transfers between devices: none -> 15.4 us  [exchange(): moved[d] = lax.ppermute(blocks[d], ('pairs', 'win'), hop)]
    ppermute x0 -> x14, starting transfers between devices: none -> 11.7 us  [exchange(): moved[d] = lax.ppermute(blocks[d], ('pairs', 'win'), hop)]
    pallas_call x4 -> x6, Pallas kernels: 39.7 us -> 30.6 us  [the longest x2 15.7 us: own_spectra(): pl.pallas_call(functools.partial(spectra_kernel, steps=steps), in_specs=[...]
    all_to_all x2 -> x0, starting transfers between devices: 8.65 us -> none  [the longest x1 4.8 us: per_device(): return inverse(exchange(stack), high, low)]
    ppermute x1, waiting for transfers between devices: 3.22 us -> 9.99 us  [per_device(): halo_a = lax.ppermute(a, 'pairs', swap_a)]
    ppermute x1, waiting for transfers between devices: 3.1 us -> 0.01 us  [per_device(): other = lax.ppermute(code, 'pairs', [(i, i ^ 1) for i in range(pairs)])]
    unnamed x16 -> x12, local copies, waits for them, and re-layouts: 3.89 us -> 0.94 us
  transfers between devices with their start and end apart: 5 -> 17, of which waited for: 5 -> 7; matrix products, arithmetic and copies ran while one was open for 0% -> 2% of each run, Pallas kernels for 1% -> 21%
where the time goes in v3:
time: 81.4 us; the launch traced here: 80.5 us
  Pallas kernels  31.7 us (39%)
  waiting for transfers between devices  28.6 us (35%)
  starting transfers between devices  17 us (21%)
  other arithmetic  1.84 us (2%)
  local copies, waits for them, and re-layouts  1.17 us (1%)
    pallas_call x2, Pallas kernels, own_spectra(): pl.pallas_call(functools.partial(spectra_kernel, steps=steps), in_specs=[...  15.7 us
    ppermute x14, waiting for transfers between devices, exchange(): moved[d] = lax.ppermute(blocks[d], ('pairs', 'win'), hop)  15.4 us
    ppermute x14, starting transfers between devices, exchange(): moved[d] = lax.ppermute(blocks[d], ('pairs', 'win'), hop)  11.7 us
    ppermute x1, waiting for transfers between devices, per_device(): halo_a = lax.ppermute(a, 'pairs', swap_a)  9.99 us
    pallas_call x1, Pallas kernels, inverse(): pl.pallas_call(inverse_kernel, grid=(LAGS // width,), in_specs=[pl.BlockS...  5.67 us
    pallas_call x1, Pallas kernels, cross_products(): pl.pallas_call(cross_kernel, out_shape=[jax.ShapeDtypeStruct((BAND * 4 *...  3.97 us
    pallas_call x1, Pallas kernels, by_bin(): pl.pallas_call(by_bin_kernel, out_shape=[shape, shape], in_specs=[pl.Bloc...  3.61 us
    ppermute x1, waiting for transfers between devices, per_device(): halo_b = lax.ppermute(b, 'pairs', swap_b)  3.18 us
  transfers between devices with their start and end apart: 17, of which 7 were waited for; matrix products, arithmetic and copies ran while one was open for 2% of the time, Pallas kernels for 21%

profile of v3, /device:TPU:16, one launch (start us, length us, event | category | flops | bytes accessed | tf_op | source)
XLA Modules:
  0.0 80.5 jit_solution(6234133476625148552)
XLA Ops:
  0.0 0.7 fusion.3
  0.7 1.6 %collective-permute-start.9 = (s32[16,64]{1,0:T(8,128)S(1)}, s32[16,64]{1,0:T(8,128)S(1)}, u32[]{:S(2)}, u32[]{:S(2)}) collective-permute-start(s32[16,64]{1,0:T(8,128)S(1)} %fusion.3), channel_id=1, source_target_pairs={{0,4},{4,0},{8,12},{12,8},{16,20},{20,16},{24,28},{28,24},{1,5},{5... | collective-permute-start | bytes 12296 | tf_op jit(solution)/shard_map/ppermute | solution.py:354
  2.3 0.7 pad_add_fusion.me_ref.place_ref
  3.0 7.9 %own_spectra.3 = (bf16[16,32,128]{2,1,0:T(8,128)(2,1)}, bf16[16,32,128]{2,1,0:T(8,128)(2,1)}, bf16[16,32,128]{2,1,0:T(8,128)(2,1)}, bf16[16,32,128]{2,1,0:T(8,128)(2,1)}) custom-call(s32[2]{0:T(128)} %pad_add_fusion.me_ref.place_ref, bf16[512,4096]{1,0:T(8,128)(2,1)} %bitcast.12, f32[1,129]{1,0:T(1,128)} %bitcast.14, f32[129,1024]{1,0:T(8,128)} %constant.117.clone.fine_hbm, ...), custom_call_target="tpu_custom_call" | custom-call | flops 2147483648 | bytes 4194304 | tf_op jit(solution)/shard_map/own_spectra/pallas_call | solution.py:140
  10.9 1.5 %collective-permute-start.1 = (bf16[16,32,128]{2,1,0:T(8,128)(2,1)}, bf16[16,32,128]{2,1,0:T(8,128)(2,1)S(1)}, u32[]{:S(2)}, u32[]{:S(2)}) collective-permute-start(bf16[16,32,128]{2,1,0:T(8,128)(2,1)} %get-tuple-element.30), channel_id=1, source_target_pairs={{0,2},{1,3},{2,0},{3,1},{4,6},{5,7},{6,4},{7,5},{8,10},{9,11},{10,... | collective-permute-start | bytes 393224 | tf_op jit(solution)/shard_map/ppermute | solution.py:344
  12.4 0.0 collective-permute-start.2
  12.4 0.8 %collective-permute-start.5 = (bf16[16,32,128]{2,1,0:T(8,128)(2,1)}, bf16[16,32,128]{2,1,0:T(8,128)(2,1)S(1)}, u32[]{:S(2)}, u32[]{:S(2)}) collective-permute-start(bf16[16,32,128]{2,1,0:T(8,128)(2,1)} %get-tuple-element.34), channel_id=1, source_target_pairs={{0,6},{1,7},{2,4},{3,5},{4,2},{5,3},{6,0},{7,1},{8,14},{9,15},{10,... | collective-permute-start | bytes 393224 | tf_op jit(solution)/shard_map/ppermute | solution.py:344
  13.2 2.1 %collective-permute-start.6 = (bf16[16,32,128]{2,1,0:T(8,128)(2,1)}, bf16[16,32,128]{2,1,0:T(8,128)(2,1)S(1)}, u32[]{:S(2)}, u32[]{:S(2)}) collective-permute-start(bf16[16,32,128]{2,1,0:T(8,128)(2,1)} %get-tuple-element.35), channel_id=1, source_target_pairs={{0,7},{1,6},{2,5},{3,4},{4,3},{5,2},{6,1},{7,0},{8,15},{9,14},{10,... | collective-permute-start | bytes 393224 | tf_op jit(solution)/shard_map/ppermute | solution.py:344
  15.4 7.8 %own_spectra.2 = (bf16[16,32,128]{2,1,0:T(8,128)(2,1)}, bf16[16,32,128]{2,1,0:T(8,128)(2,1)}, bf16[16,32,128]{2,1,0:T(8,128)(2,1)}, bf16[16,32,128]{2,1,0:T(8,128)(2,1)}) custom-call(s32[2]{0:T(128)} %pad_add_fusion.me_ref.place_ref, bf16[512,4096]{1,0:T(8,128)(2,1)} %bitcast.13, f32[1,129]{1,0:T(1,128)} %bitcast.15, f32[129,1024]{1,0:T(8,128)} %constant.117.clone.fine_hbm, ...), custom_call_target="tpu_custom_call" | custom-call | flops 2147483648 | bytes 4194304 | tf_op jit(solution)/shard_map/own_spectra/pallas_call | solution.py:140
  23.2 0.0 collective-permute-done.9
  23.2 0.1 collective-permute-start
  23.4 0.0 collective-permute-done.1.refs_2_
  23.4 0.5 collective-permute-start.3
  23.9 1.3 %collective-permute-start.4 = (bf16[16,32,128]{2,1,0:T(8,128)(2,1)}, bf16[16,32,128]{2,1,0:T(8,128)(2,1)S(1)}, u32[]{:S(2)}, u32[]{:S(2)}) collective-permute-start(bf16[16,32,128]{2,1,0:T(8,128)(2,1)} %get-tuple-element.33), channel_id=1, source_target_pairs={{0,5},{1,4},{2,7},{3,6},{4,1},{5,0},{6,3},{7,2},{8,13},{9,12},{10,... | collective-permute-start | bytes 393224 | tf_op jit(solution)/shard_map/ppermute | solution.py:344
  25.2 0.1 copy.15
  25.3 0.1 copy.16
  25.3 0.1 add_select_fusion
  25.4 0.0 collective-permute-done.refs_1_
  25.5 4.4 %collective-permute-done.3.refs_4_ = bf16[16,32,128]{2,1,0:T(8,128)(2,1)S(1)} collective-permute-done((bf16[16,32,128]{2,1,0:T(8,128)(2,1)}, bf16[16,32,128]{2,1,0:T(8,128)(2,1)S(1)}, u32[]{:S(2)}, u32[]{:S(2)}) %collective-permute-start.3) | collective-permute-done | bytes 131104 | tf_op jit(solution)/shard_map/ppermute | solution.py:344
  29.9 1.9 %collective-permute-done.4.refs_5_ = bf16[16,32,128]{2,1,0:T(8,128)(2,1)S(1)} collective-permute-done((bf16[16,32,128]{2,1,0:T(8,128)(2,1)}, bf16[16,32,128]{2,1,0:T(8,128)(2,1)S(1)}, u32[]{:S(2)}, u32[]{:S(2)}) %collective-permute-start.4) | collective-permute-done | bytes 131104 | tf_op jit(solution)/shard_map/ppermute | solution.py:344
  31.8 0.9 %copy-done.2 = bf16[16,32,128]{2,1,0:T(8,128)(2,1)S(1)} copy-done((bf16[16,32,128]{2,1,0:T(8,128)(2,1)S(1)}, bf16[16,32,128]{2,1,0:T(8,128)(2,1)}, u32[]{:S(2)}) %copy-start.2) | copy-done | bytes 131096
  32.7 3.6 %by_bin.1 = (bf16[64,16,256]{2,1,0:T(8,128)(2,1)S(1)}, bf16[64,16,256]{2,1,0:T(8,128)(2,1)S(1)}) custom-call(s32[2]{0:T(128)S(1)} %copy-done.5, bf16[16,32,128]{2,1,0:T(8,128)(2,1)S(1)} %copy-done.2, bf16[16,32,128]{2,1,0:T(8,128)(2,1)S(1)} %collective-permute-done.refs_1_, bf16[16,32,128]{2,1,0:T(8,128)(2,1)S(1)} %collective-permute-done.1.refs_2_, ...), custom_call_target="tpu_custom_call" | custom-call | tf_op jit(solution)/shard_map/by_bin/pallas_call | solution.py:222
  36.3 1.6 %collective-permute-start.7 = (bf16[64,16,256]{2,1,0:T(8,128)(2,1)S(1)}, bf16[64,16,256]{2,1,0:T(8,128)(2,1)S(1)}, u32[]{:S(2)}, u32[]{:S(2)}) collective-permute-start(bf16[64,16,256]{2,1,0:T(8,128)(2,1)S(1)} %get-tuple-element.36.a_ref), channel_id=1, source_target_pairs={{0,8},{4,12},{8,0},{12,4},{16,24},{20,28},{24,16},{28,20},{1,9},{5... | collective-permute-start | bytes 1572872 | tf_op jit(solution)/shard_map/ppermute | solution.py:377
  37.9 2.1 %collective-permute-start.8 = (bf16[64,16,256]{2,1,0:T(8,128)(2,1)S(1)}, bf16[64,16,256]{2,1,0:T(8,128)(2,1)S(1)}, u32[]{:S(2)}, u32[]{:S(2)}) collective-permute-start(bf16[64,16,256]{2,1,0:T(8,128)(2,1)S(1)} %get-tuple-element.37.b_ref), channel_id=1, source_target_pairs={{8,16},{12,20},{16,8},{20,12},{9,17},{13,21},{17,9},{21,13},{10,18... | collective-permute-start | bytes 1572872 | tf_op jit(solution)/shard_map/ppermute | solution.py:378
  40.1 0.1 copy.17
  40.1 0.3 compare_convert_fusion.select_ref
  40.5 10.0 %collective-permute-done.7.ha_ref = bf16[64,16,256]{2,1,0:T(8,128)(2,1)S(1)} collective-permute-done((bf16[64,16,256]{2,1,0:T(8,128)(2,1)S(1)}, bf16[64,16,256]{2,1,0:T(8,128)(2,1)S(1)}, u32[]{:S(2)}, u32[]{:S(2)}) %collective-permute-start.7) | collective-permute-done | bytes 524320 | tf_op jit(solution)/shard_map/ppermute | solution.py:377
  50.5 3.2 %collective-permute-done.8.hb_ref = bf16[64,16,256]{2,1,0:T(8,128)(2,1)S(1)} collective-permute-done((bf16[64,16,256]{2,1,0:T(8,128)(2,1)S(1)}, bf16[64,16,256]{2,1,0:T(8,128)(2,1)S(1)}, u32[]{:S(2)}, u32[]{:S(2)}) %collective-permute-start.8) | collective-permute-done | bytes 524320 | tf_op jit(solution)/shard_map/ppermute | solution.py:378
  53.7 4.0 %cross_products.1 = (f32[4096,128]{1,0:T(8,128)S(1)}, f32[16,16,128]{2,1,0:T(8,128)S(1)}, f32[16,16,128]{2,1,0:T(8,128)S(1)}, f32[16,16,128]{2,1,0:T(8,128)S(1)}, f32[16,16,128]{2,1,0:T(8,128)S(1)}) custom-call(s32[2]{0:T(128)S(1)} %copy-done.5, bf16[64,16,256]{2,1,0:T(8,128)(2,1)S(1)} %get-tuple-element.36.a_ref, ...), custom_call_target="tpu_custom_call" | custom-call | tf_op jit(solution)/shard_map/cross_products/pallas_call | solution.py:280
  57.6 0.0 copy-start
  57.6 0.0 copy-start.1
  57.6 0.0 copy-start.3
  57.7 0.0 copy-start.4
  57.7 1.6 %own_slots.1 = (f32[16,16,128]{2,1,0:T(8,128)S(1)}, f32[16,16,128]{2,1,0:T(8,128)S(1)}, f32[16,16,128]{2,1,0:T(8,128)S(1)}, f32[16,16,128]{2,1,0:T(8,128)S(1)}) custom-call(s32[2]{0:T(128)S(1)} %copy-done.5, f32[4096,128]{1,0:T(8,128)S(1)} %get-tuple-element.38.cross_ref, bf16[32,64,128]{2,1,0:T(8,128)(2,1)S(1)} %compare_convert_fusion.select_ref), custom_call_target="tpu_custom_call" | custom-call | flops 4294967296 | bytes 16777216 | tf_op jit(solution)/shard_map/own_slots/pallas_call | solution.py:288
  59.3 0.1 collective-permute-start.10
  59.4 1.5 %collective-permute-start.11 = (f32[16,16,128]{2,1,0:T(8,128)S(1)}, f32[16,16,128]{2,1,0:T(8,128)S(1)}, u32[]{:S(2)}, u32[]{:S(2)}) collective-permute-start(f32[16,16,128]{2,1,0:T(8,128)S(1)} %get-tuple-element.41), channel_id=1, source_target_pairs={{0,2},{1,3},{2,0},{3,1},{4,6},{5,7},{6,4},{7,5},{8,10},{9,11},{10,... | collective-permute-start | bytes 393224 | tf_op jit(solution)/shard_map/ppermute | solution.py:344
  60.9 0.3 collective-permute-start.12
  61.2 0.5 collective-permute-start.13
  61.7 1.2 %collective-permute-start.14 = (f32[16,16,128]{2,1,0:T(8,128)S(1)}, f32[16,16,128]{2,1,0:T(8,128)S(1)}, u32[]{:S(2)}, u32[]{:S(2)}) collective-permute-start(f32[16,16,128]{2,1,0:T(8,128)S(1)} %get-tuple-element.44), channel_id=1, source_target_pairs={{0,5},{1,4},{2,7},{3,6},{4,1},{5,0},{6,3},{7,2},{8,13},{9,12},{10,... | collective-permute-start | bytes 393224 | tf_op jit(solution)/shard_map/ppermute | solution.py:344
  62.9 1.4 %collective-permute-start.15 = (f32[16,16,128]{2,1,0:T(8,128)S(1)}, f32[16,16,128]{2,1,0:T(8,128)S(1)}, u32[]{:S(2)}, u32[]{:S(2)}) collective-permute-start(f32[16,16,128]{2,1,0:T(8,128)S(1)} %get-tuple-element.45), channel_id=1, source_target_pairs={{0,6},{1,7},{2,4},{3,5},{4,2},{5,3},{6,0},{7,1},{8,14},{9,15},{10,... | collective-permute-start | bytes 393224 | tf_op jit(solution)/shard_map/ppermute | solution.py:344
  64.4 1.4 %collective-permute-done.11.refs_2_ = f32[16,16,128]{2,1,0:T(8,128)S(1)} collective-permute-done((f32[16,16,128]{2,1,0:T(8,128)S(1)}, f32[16,16,128]{2,1,0:T(8,128)S(1)}, u32[]{:S(2)}, u32[]{:S(2)}) %collective-permute-start.11) | collective-permute-done | bytes 131104 | tf_op jit(solution)/shard_map/ppermute | solution.py:344
  65.7 0.2 collective-permute-start.16
  66.0 1.1 %lag_tables.1 = (bf16[8,128,1024]{2,1,0:T(8,128)(2,1)S(1)}, bf16[8,128,1024]{2,1,0:T(8,128)(2,1)S(1)}) custom-call(f32[64,1024]{1,0:T(8,128)S(1)} %copy-done.1, f32[64,1024]{1,0:T(8,128)S(1)} %copy-done, f32[8,1024]{1,0:T(8,128)S(1)} %copy-done.4, f32[8,1024]{1,0:T(8,128)S(1)} %copy-done.3), custom_call_target="tpu_custom_call" | custom-call | tf_op jit(solution)/shard_map/lag_tables/pallas_call | solution.py:177
  67.1 0.5 collective-permute-done.12.refs_3_
  67.6 7.2 %collective-permute-done.14.refs_5_ = f32[16,16,128]{2,1,0:T(8,128)S(1)} collective-permute-done((f32[16,16,128]{2,1,0:T(8,128)S(1)}, f32[16,16,128]{2,1,0:T(8,128)S(1)}, u32[]{:S(2)}, u32[]{:S(2)}) %collective-permute-start.14) | collective-permute-done | bytes 131104 | tf_op jit(solution)/shard_map/ppermute | solution.py:344
  74.8 0.0 collective-permute-done.15.refs_6_
  74.8 0.0 collective-permute-done.16.refs_7_
  74.8 5.7 %inverse.1 = f32[16,16,1024]{2,1,0:T(8,128)} custom-call(s32[2]{0:T(128)S(1)} %copy-done.5, bf16[8,128,1024]{2,1,0:T(8,128)(2,1)S(1)} %get-tuple-element.26.high_ref, bf16[8,128,1024]{2,1,0:T(8,128)(2,1)S(1)} %get-tuple-element.27.low_ref, f32[16,16,128]{2,1,0:T(8,128)S(1)} %get-tuple-element.39.refs_0_, f32[16,16,128]{2,1,0:T(8,128)S(1)} %collective-permute-done.10.refs_1_, ...), custom_call_target="tpu_custom_call" | custom-call | tf_op jit(solution)/shard_map/inverse/pallas_call | solution.py:320
  (15 shorter events, 0.1 us)
Async XLA Ops:
  0.7 22.5 %collective-permute-start.9 = (s32[16,64]{1,0:T(8,128)S(1)}, s32[16,64]{1,0:T(8,128)S(1)}, u32[]{:S(2)}, u32[]{:S(2)}) collective-permute-start(s32[16,64]{1,0:T(8,128)S(1)} %fusion.3), channel_id=1, source_target_pairs={{0,4},{4,0},{8,12},{12,8},{16,20},{20,16},{24,28},{28,24},{1,5},{5... | collective-permute-start | bytes 12296 | tf_op jit(solution)/shard_map/ppermute | solution.py:354
  10.9 12.5 %collective-permute-start.1 = (bf16[16,32,128]{2,1,0:T(8,128)(2,1)}, bf16[16,32,128]{2,1,0:T(8,128)(2,1)S(1)}, u32[]{:S(2)}, u32[]{:S(2)}) collective-permute-start(bf16[16,32,128]{2,1,0:T(8,128)(2,1)} %get-tuple-element.30), channel_id=1, source_target_pairs={{0,2},{1,3},{2,0},{3,1},{4,6},{5,7},{6,4},{7,5},{8,10},{9,11},{10,... | collective-permute-start | bytes 393224 | tf_op jit(solution)/shard_map/ppermute | solution.py:344
  12.4 11.5 %collective-permute-start.2 = (bf16[16,32,128]{2,1,0:T(8,128)(2,1)}, bf16[16,32,128]{2,1,0:T(8,128)(2,1)S(1)}, u32[]{:S(2)}, u32[]{:S(2)}) collective-permute-start(bf16[16,32,128]{2,1,0:T(8,128)(2,1)} %get-tuple-element.31), channel_id=1, source_target_pairs={{0,3},{1,2},{2,1},{3,0},{4,7},{5,6},{6,5},{7,4},{8,11},{9,10},{10,... | collective-permute-start | bytes 393224 | tf_op jit(solution)/shard_map/ppermute | solution.py:344
  12.4 13.0 %collective-permute-start.5 = (bf16[16,32,128]{2,1,0:T(8,128)(2,1)}, bf16[16,32,128]{2,1,0:T(8,128)(2,1)S(1)}, u32[]{:S(2)}, u32[]{:S(2)}) collective-permute-start(bf16[16,32,128]{2,1,0:T(8,128)(2,1)} %get-tuple-element.34), channel_id=1, source_target_pairs={{0,6},{1,7},{2,4},{3,5},{4,2},{5,3},{6,0},{7,1},{8,14},{9,15},{10,... | collective-permute-start | bytes 393224 | tf_op jit(solution)/shard_map/ppermute | solution.py:344
  13.2 18.5 %copy-start.5 = (s32[2]{0:T(128)S(1)}, s32[2]{0:T(128)}, u32[]{:S(2)}) copy-start(s32[2]{0:T(128)} %pad_add_fusion.me_ref.place_ref) | copy-start | bytes 28
  13.2 12.2 %collective-permute-start.6 = (bf16[16,32,128]{2,1,0:T(8,128)(2,1)}, bf16[16,32,128]{2,1,0:T(8,128)(2,1)S(1)}, u32[]{:S(2)}, u32[]{:S(2)}) collective-permute-start(bf16[16,32,128]{2,1,0:T(8,128)(2,1)} %get-tuple-element.35), channel_id=1, source_target_pairs={{0,7},{1,6},{2,5},{3,4},{4,3},{5,2},{6,1},{7,0},{8,15},{9,14},{10,... | collective-permute-start | bytes 393224 | tf_op jit(solution)/shard_map/ppermute | solution.py:344
  23.2 2.2 %collective-permute-start = (bf16[16,32,128]{2,1,0:T(8,128)(2,1)}, bf16[16,32,128]{2,1,0:T(8,128)(2,1)S(1)}, u32[]{:S(2)}, u32[]{:S(2)}) collective-permute-start(bf16[16,32,128]{2,1,0:T(8,128)(2,1)} %get-tuple-element.29), channel_id=1, source_target_pairs={{0,1},{1,0},{2,3},{3,2},{4,5},{5,4},{6,7},{7,6},{8,9},{9,8},{10,11... | collective-permute-start | bytes 393224 | tf_op jit(solution)/shard_map/ppermute | solution.py:344
  23.4 6.5 %collective-permute-start.3 = (bf16[16,32,128]{2,1,0:T(8,128)(2,1)}, bf16[16,32,128]{2,1,0:T(8,128)(2,1)S(1)}, u32[]{:S(2)}, u32[]{:S(2)}) collective-permute-start(bf16[16,32,128]{2,1,0:T(8,128)(2,1)} %get-tuple-element.32), channel_id=1, source_target_pairs={{0,4},{1,5},{2,6},{3,7},{4,0},{5,1},{6,2},{7,3},{8,12},{9,13},{10,... | collective-permute-start | bytes 393224 | tf_op jit(solution)/shard_map/ppermute | solution.py:344
  23.9 7.9 %collective-permute-start.4 = (bf16[16,32,128]{2,1,0:T(8,128)(2,1)}, bf16[16,32,128]{2,1,0:T(8,128)(2,1)S(1)}, u32[]{:S(2)}, u32[]{:S(2)}) collective-permute-start(bf16[16,32,128]{2,1,0:T(8,128)(2,1)} %get-tuple-element.33), channel_id=1, source_target_pairs={{0,5},{1,4},{2,7},{3,6},{4,1},{5,0},{6,3},{7,2},{8,13},{9,12},{10,... | collective-permute-start | bytes 393224 | tf_op jit(solution)/shard_map/ppermute | solution.py:344
  31.8 0.9 %copy-start.2 = (bf16[16,32,128]{2,1,0:T(8,128)(2,1)S(1)}, bf16[16,32,128]{2,1,0:T(8,128)(2,1)}, u32[]{:S(2)}) copy-start(bf16[16,32,128]{2,1,0:T(8,128)(2,1)} %get-tuple-element.28.refs_0_) | copy-start | bytes 393220
  36.3 14.2 %collective-permute-start.7 = (bf16[64,16,256]{2,1,0:T(8,128)(2,1)S(1)}, bf16[64,16,256]{2,1,0:T(8,128)(2,1)S(1)}, u32[]{:S(2)}, u32[]{:S(2)}) collective-permute-start(bf16[64,16,256]{2,1,0:T(8,128)(2,1)S(1)} %get-tuple-element.36.a_ref), channel_id=1, source_target_pairs={{0,8},{4,12},{8,0},{12,4},{16,24},{20,28},{24,16},{28,20},{1,9},{5... | collective-permute-start | bytes 1572872 | tf_op jit(solution)/shard_map/ppermute | solution.py:377
  37.9 15.7 %collective-permute-start.8 = (bf16[64,16,256]{2,1,0:T(8,128)(2,1)S(1)}, bf16[64,16,256]{2,1,0:T(8,128)(2,1)S(1)}, u32[]{:S(2)}, u32[]{:S(2)}) collective-permute-start(bf16[64,16,256]{2,1,0:T(8,128)(2,1)S(1)} %get-tuple-element.37.b_ref), channel_id=1, source_target_pairs={{8,16},{12,20},{16,8},{20,12},{9,17},{13,21},{17,9},{21,13},{10,18... | collective-permute-start | bytes 1572872 | tf_op jit(solution)/shard_map/ppermute | solution.py:378
  57.6 8.4 %copy-start = (f32[64,1024]{1,0:T(8,128)S(1)}, f32[64,1024]{1,0:T(8,128)}, u32[]{:S(2)}) copy-start(f32[64,1024]{1,0:T(8,128)} %constant.114.clone.msin_ref) | copy-start | bytes 786436
  57.6 8.3 %copy-start.1 = (f32[64,1024]{1,0:T(8,128)S(1)}, f32[64,1024]{1,0:T(8,128)}, u32[]{:S(2)}) copy-start(f32[64,1024]{1,0:T(8,128)} %constant.113.clone.cos_ref) | copy-start | bytes 786436
  57.6 8.3 %copy-start.3 = (f32[8,1024]{1,0:T(8,128)S(1)}, f32[8,1024]{1,0:T(8,128)}, u32[]{:S(2)}) copy-start(f32[8,1024]{1,0:T(8,128)} %constant.116.clone.msin0_ref) | copy-start | bytes 98308
  57.7 8.3 %copy-start.4 = (f32[8,1024]{1,0:T(8,128)S(1)}, f32[8,1024]{1,0:T(8,128)}, u32[]{:S(2)}) copy-start(f32[8,1024]{1,0:T(8,128)} %constant.115.clone.cos0_ref) | copy-start | bytes 98308
  59.3 3.6 %collective-permute-start.10 = (f32[16,16,128]{2,1,0:T(8,128)S(1)}, f32[16,16,128]{2,1,0:T(8,128)S(1)}, u32[]{:S(2)}, u32[]{:S(2)}) collective-permute-start(f32[16,16,128]{2,1,0:T(8,128)S(1)} %get-tuple-element.40), channel_id=1, source_target_pairs={{0,1},{1,0},{2,3},{3,2},{4,5},{5,4},{6,7},{7,6},{8,9},{9,8},{10,11... | collective-permute-start | bytes 393224 | tf_op jit(solution)/shard_map/ppermute | solution.py:344
  59.4 6.4 %collective-permute-start.11 = (f32[16,16,128]{2,1,0:T(8,128)S(1)}, f32[16,16,128]{2,1,0:T(8,128)S(1)}, u32[]{:S(2)}, u32[]{:S(2)}) collective-permute-start(f32[16,16,128]{2,1,0:T(8,128)S(1)} %get-tuple-element.41), channel_id=1, source_target_pairs={{0,2},{1,3},{2,0},{3,1},{4,6},{5,7},{6,4},{7,5},{8,10},{9,11},{10,... | collective-permute-start | bytes 393224 | tf_op jit(solution)/shard_map/ppermute | solution.py:344
  60.9 6.7 %collective-permute-start.12 = (f32[16,16,128]{2,1,0:T(8,128)S(1)}, f32[16,16,128]{2,1,0:T(8,128)S(1)}, u32[]{:S(2)}, u32[]{:S(2)}) collective-permute-start(f32[16,16,128]{2,1,0:T(8,128)S(1)} %get-tuple-element.42), channel_id=1, source_target_pairs={{0,3},{1,2},{2,1},{3,0},{4,7},{5,6},{6,5},{7,4},{8,11},{9,10},{10,... | collective-permute-start | bytes 393224 | tf_op jit(solution)/shard_map/ppermute | solution.py:344
  61.2 6.4 %collective-permute-start.13 = (f32[16,16,128]{2,1,0:T(8,128)S(1)}, f32[16,16,128]{2,1,0:T(8,128)S(1)}, u32[]{:S(2)}, u32[]{:S(2)}) collective-permute-start(f32[16,16,128]{2,1,0:T(8,128)S(1)} %get-tuple-element.43), channel_id=1, source_target_pairs={{0,4},{1,5},{2,6},{3,7},{4,0},{5,1},{6,2},{7,3},{8,12},{9,13},{10,... | collective-permute-start | bytes 393224 | tf_op jit(solution)/shard_map/ppermute | solution.py:344
  61.7 13.1 %collective-permute-start.14 = (f32[16,16,128]{2,1,0:T(8,128)S(1)}, f32[16,16,128]{2,1,0:T(8,128)S(1)}, u32[]{:S(2)}, u32[]{:S(2)}) collective-permute-start(f32[16,16,128]{2,1,0:T(8,128)S(1)} %get-tuple-element.44), channel_id=1, source_target_pairs={{0,5},{1,4},{2,7},{3,6},{4,1},{5,0},{6,3},{7,2},{8,13},{9,12},{10,... | collective-permute-start | bytes 393224 | tf_op jit(solution)/shard_map/ppermute | solution.py:344
  62.9 11.9 %collective-permute-start.15 = (f32[16,16,128]{2,1,0:T(8,128)S(1)}, f32[16,16,128]{2,1,0:T(8,128)S(1)}, u32[]{:S(2)}, u32[]{:S(2)}) collective-permute-start(f32[16,16,128]{2,1,0:T(8,128)S(1)} %get-tuple-element.45), channel_id=1, source_target_pairs={{0,6},{1,7},{2,4},{3,5},{4,2},{5,3},{6,0},{7,1},{8,14},{9,15},{10,... | collective-permute-start | bytes 393224 | tf_op jit(solution)/shard_map/ppermute | solution.py:344
  65.7 9.1 %collective-permute-start.16 = (f32[16,16,128]{2,1,0:T(8,128)S(1)}, f32[16,16,128]{2,1,0:T(8,128)S(1)}, u32[]{:S(2)}, u32[]{:S(2)}) collective-permute-start(f32[16,16,128]{2,1,0:T(8,128)S(1)} %get-tuple-element.46), channel_id=1, source_target_pairs={{0,7},{1,6},{2,5},{3,4},{4,3},{5,2},{6,1},{7,0},{8,15},{9,14},{10,... | collective-permute-start | bytes 393224 | tf_op jit(solution)/shard_map/ppermute | solution.py:344

commit v4 on v3

v4 whole, which is shorter than its diff:
```python
import functools
import math

import jax
import jax.numpy as jnp
import numpy as np
from jax import lax
from jax.experimental import pallas as pl
from jax.experimental.pallas import tpu as pltpu
from jax.sharding import PartitionSpec as P

SAMPLES = 4096
BINS = 512
BAND = 64
LOW_BIN = 64
LAGS = 1024
TAPS = 129
LANES = 2 * BAND
EPSILON = 1e-06
STEP = 64
CHUNK = 512
MIB = 1024 * 1024
CONTRACT_LAST = (((1,), (1,)), ((), ()))


def unit_circle(products):
    angles = (products % SAMPLES).astype(np.float64) * (2.0 * math.pi / SAMPLES)
    return np.cos(angles).astype(np.float32), (-np.sin(angles)).astype(np.float32)


def banded(first, second):
    rows = first.shape[0]
    parts = [a.reshape(rows, BINS // BAND, 1, BAND) for a in (first, second)]
    return np.concatenate(parts, 2).reshape(rows, 2 * BINS)


def forward_tables():
    bins = LOW_BIN + np.arange(BINS, dtype=np.int64)
    cos, msin = unit_circle(np.arange(TAPS, dtype=np.int64)[:, None] * bins[None, :])
    fine = banded(cos, msin)
    starts = np.arange(0, SAMPLES, STEP, dtype=np.int64)
    cos, msin = unit_circle(starts[:, None] * bins[None, :])
    return fine, banded(cos, cos), banded(-msin, msin)


def lag_tables(parts):
    lags = np.arange(LAGS, dtype=np.int64) - LAGS // 2
    cos, msin = unit_circle(np.arange(BAND, dtype=np.int64)[:, None] * lags[None, :])
    first = LOW_BIN + BAND * np.arange(parts, dtype=np.int64)
    cos0, msin0 = unit_circle(first[:, None] * lags[None, :])
    return cos, msin, cos0, msin0


def position(wins):
    place = lax.axis_index("pairs")
    me = (place % 2) * wins + lax.axis_index("win")
    return me, place % 2 != (place // 2) % 2


def spectra_kernel(x_hbm, taps_ref, fine_hbm, turn_c_hbm, turn_s_hbm, *refs, steps, wins):
    outs, refs = refs[: 2 * len(steps)], refs[2 * len(steps) :]
    x_ref, fine_ref, turn_c_ref, turn_s_ref, *refs, sems = refs
    tables, totals, stages = refs[0:2], refs[2:4], refs[4:6]
    count = x_ref.shape[0]
    nodes, windows = outs[0].shape[0], outs[0].shape[1]
    width = 2 * LANES
    pieces = SAMPLES // CHUNK
    me, _ = position(wins)
    copies = [
        pltpu.make_async_copy(source, target, sems.at[pieces + i])
        for i, (source, target) in enumerate(
            ((fine_hbm, fine_ref), (turn_c_hbm, turn_c_ref), (turn_s_hbm, turn_s_ref))
        )
    ]
    chunks = [
        pltpu.make_async_copy(
            x_hbm.at[:, pl.ds(i * CHUNK, CHUNK)], x_ref.at[:, pl.ds(i * CHUNK, CHUNK)], sems.at[i]
        )
        for i in range(pieces)
    ]
    for copy in copies + chunks:
        copy.start()

    def columns_of(i):
        return pl.ds(pl.multiple_of(((me // 2) ^ steps[i]) * width, width), width)

    def generate(i, piece):
        columns = columns_of(i)
        base = fine_ref[0:STEP, columns]
        swapped = jnp.concatenate(
            [pltpu.roll(base[:, c : c + LANES], BAND, 1) for c in range(0, width, LANES)], 1
        )
        for j in range(piece * (CHUNK // STEP), (piece + 1) * (CHUNK // STEP)):
            row = pl.ds(j, 1)
            turned = base * turn_c_ref[row, columns] + swapped * turn_s_ref[row, columns]
            tables[i % 2][j * STEP : (j + 1) * STEP, :] = turned.astype(jnp.bfloat16)

    low = lax.broadcasted_iota(jnp.int32, (1, LANES), 1) < BAND
    responses = {}

    def respond(i):
        columns = columns_of(i)
        response = jnp.dot(
            taps_ref[:, 0:128],
            fine_ref[0:128, columns],
            precision=lax.Precision.HIGHEST,
            preferred_element_type=jnp.float32,
        )
        response = response + taps_ref[:, 128:129] * fine_ref[128:129, columns]
        responses[i] = []
        for c in range(2):
            here = response[:, c * LANES : (c + 1) * LANES]
            other = pltpu.roll(jnp.broadcast_to(here, (8, LANES)), BAND, 1)[0:1, :]
            responses[i].append((jnp.where(low, here, other), jnp.where(low, -other, here)))

    def whiten(i, piece):
        rows = pl.ds(piece * (count // pieces), count // pieces)
        for c in range(2):
            same, cross = responses[i][c]
            raw = totals[i % 2][c, rows, :]
            power = jnp.sum(raw * raw, 1, keepdims=True) * (1.0 / BAND)
            white = raw * lax.rsqrt(power + EPSILON)
            stages[i % 2][c ^ (me % 2), rows, :] = white * same + pltpu.roll(white, BAND, 1) * cross

    def give(i, piece):
        for c in range(2):
            for node in range(piece * nodes // pieces, (piece + 1) * nodes // pieces):
                values = stages[i % 2][c, pl.ds(node, windows, stride=nodes), :]
                outs[2 * i + c][node] = values.astype(jnp.bfloat16)

    for copy in copies:
        copy.wait()
    for piece in range(pieces):
        generate(0, piece)
    last = len(steps) - 1
    for i in range(len(steps)):
        respond(i)
        for piece in range(pieces):
            part = pl.ds(piece * CHUNK, CHUNK)
            if i == 0:
                chunks[piece].wait()
            product = jnp.dot(x_ref[:, part], tables[i % 2][part, :], preferred_element_type=jnp.float32)
            for c in range(2):
                here = product[:, c * LANES : (c + 1) * LANES]
                totals[i % 2][c] = here if piece == 0 else totals[i % 2][c] + here
            if i < last:
                generate(i + 1, piece)
            if i > 0:
                whiten(i - 1, piece)
            if i > 1:
                give(i - 2, piece)
    for piece in range(pieces):
        whiten(last, piece)
        if last > 0:
            give(last - 1, piece)
    for piece in range(pieces):
        give(last, piece)


def own_spectra(rows, taps, nodes, steps):
    tables = [jnp.asarray(t) for t in forward_tables()]
    count = rows.shape[0]
    hbm = pl.BlockSpec(memory_space=pltpu.HBM)
    vmem = pl.BlockSpec(memory_space=pltpu.VMEM)
    shape = jax.ShapeDtypeStruct((nodes, count // nodes, LANES), jnp.bfloat16)
    return pl.pallas_call(
        functools.partial(spectra_kernel, steps=steps, wins=len(steps)),
        in_specs=[hbm, vmem, hbm, hbm, hbm],
        out_specs=[vmem] * (2 * len(steps)),
        out_shape=[shape] * (2 * len(steps)),
        scratch_shapes=[
            pltpu.VMEM(rows.shape, jnp.bfloat16),
            *[pltpu.VMEM(t.shape, jnp.float32) for t in tables],
            *[pltpu.VMEM((SAMPLES, 2 * LANES), jnp.bfloat16)] * 2,
            *[pltpu.VMEM((2, count, LANES), jnp.float32)] * 4,
            pltpu.SemaphoreType.DMA((SAMPLES // CHUNK + 3,)),
        ],
        compiler_params=pltpu.CompilerParams(vmem_limit_bytes=60 * MIB),
        cost_estimate=pl.CostEstimate(
            flops=4 * len(steps) * count * SAMPLES * LANES, bytes_accessed=2 * count * SAMPLES, transcendentals=0
        ),
        name="own_spectra",
    )(rows, taps, *tables)


def lag_table_kernel(cos_ref, msin_ref, cos0_ref, msin0_ref, high_ref, low_ref, *, factor):
    part = pl.program_id(0)
    c0 = cos0_ref[pl.ds(part, 1), :] * factor
    s0 = msin0_ref[pl.ds(part, 1), :] * factor
    cos, msin = cos_ref[...], msin_ref[...]
    for half, values in ((0, cos * c0 - msin * s0), (1, cos * s0 + msin * c0)):
        high = values.astype(jnp.bfloat16)
        rows = pl.ds(half * BAND, BAND)
        high_ref[0, rows, :] = high
        low_ref[0, rows, :] = (values - high.astype(jnp.float32)).astype(jnp.bfloat16)


def make_lag_tables(parts, factor):
    tables = [jnp.asarray(t) for t in lag_tables(parts)]
    shape = jax.ShapeDtypeStruct((parts, LANES, LAGS), jnp.bfloat16)
    block = pl.BlockSpec((1, LANES, LAGS), lambda i: (i, 0, 0))
    return pl.pallas_call(
        functools.partial(lag_table_kernel, factor=factor),
        grid=(parts,),
        in_specs=[pl.BlockSpec(t.shape, lambda i: (0, 0)) for t in tables],
        out_specs=[block, block],
        out_shape=[shape, shape],
        compiler_params=pltpu.CompilerParams(vmem_limit_bytes=6 * MIB),
        name="lag_tables",
    )(*tables)


def by_bin_kernel(*refs):
    blocks, (first_ref, second_ref, turned) = refs[:-3], refs[-3:]
    groups = len(blocks) // 2
    nodes = blocks[0].shape[0]
    _, is_first = position(groups)
    own_at = jnp.where(is_first, 0, 1)
    row = lax.broadcasted_iota(jnp.int32, (LANES, LANES), 0)
    unit = (row == lax.broadcasted_iota(jnp.int32, (LANES, LANES), 1)).astype(jnp.bfloat16)
    for tile in range(2):
        here = blocks[tile * groups : (tile + 1) * groups]

        def turn(node, _, here=here, tile=tile):
            values = jnp.concatenate([block[node] for block in here], 0)
            values = lax.dot_general(unit, values, CONTRACT_LAST, preferred_element_type=jnp.float32)
            turned[pl.ds(pl.multiple_of((tile * nodes + node) * LANES, LANES), LANES), :] = values
            return 0

        lax.fori_loop(0, nodes, turn, 0, unroll=8)
    for out_ref, tile in ((first_ref, own_at), (second_ref, 1 - own_at)):
        start = tile * (nodes * LANES)

        def one(f, _, out_ref=out_ref, start=start):
            real = turned[pl.ds(start + f, nodes, stride=LANES), :]
            imag = turned[pl.ds(start + BAND + f, nodes, stride=LANES), :]
            out_ref[f] = jnp.concatenate([real, imag], 1).astype(jnp.bfloat16)
            return 0

        lax.fori_loop(0, BAND, one, 0, unroll=8)


def by_bin(blocks):
    nodes, windows, _ = blocks[0].shape
    windows = windows * len(blocks) // 2
    shape = jax.ShapeDtypeStruct((BAND, nodes, 2 * windows), jnp.bfloat16)
    vmem = pl.BlockSpec(memory_space=pltpu.VMEM)
    return pl.pallas_call(
        by_bin_kernel,
        out_shape=[shape, shape],
        in_specs=[vmem] * len(blocks),
        out_specs=[vmem, vmem],
        scratch_shapes=[pltpu.VMEM((2 * nodes * LANES, windows), jnp.float32)],
        compiler_params=pltpu.CompilerParams(vmem_limit_bytes=8 * MIB),
        name="by_bin",
    )(*blocks)


def pick_slots(cross_ref, select_ref, outs, where, nodes):
    stations, count = 2 * nodes, 4 * nodes
    slots = outs[0].shape[1]
    left = lax.broadcasted_iota(jnp.int32, (2 * BAND, 2 * count), 1) < count

    def one_node(node, _):
        index = where * nodes + node
        real = cross_ref[pl.ds(index, BAND, stride=count), :]
        imag = cross_ref[pl.ds(stations + index, BAND, stride=count), :]
        values = jnp.concatenate([real, imag], 0)
        high = values.astype(jnp.bfloat16).astype(jnp.float32)
        split = jnp.where(left, high, values - high).astype(jnp.bfloat16)
        picked = lax.dot_general(select_ref[index], split, CONTRACT_LAST, preferred_element_type=jnp.float32)
        for d, out_ref in enumerate(outs):
            out_ref[node] = picked[d * slots : (d + 1) * slots, :]
        return 0

    lax.fori_loop(0, nodes, one_node, 0, unroll=4)


def cross_kernel(a_ref, b_ref, ha_ref, hb_ref, select_ref, cross, *outs):
    nodes, width = a_ref.shape[1], a_ref.shape[2]
    count = 4 * nodes

    def one_bin(f, _):
        own = jnp.concatenate([a_ref[f], b_ref[f]], 0)
        partners = jnp.concatenate([own, ha_ref[f], hb_ref[f]], 0)
        turned = jnp.concatenate([own[:, width // 2 :], -own[:, : width // 2]], 1)
        both = jnp.concatenate([own, turned], 0)
        partners = jnp.concatenate([partners, partners], 0)
        cross[pl.ds(pl.multiple_of(f * count, count), count), :] = lax.dot_general(
            both, partners, CONTRACT_LAST, preferred_element_type=jnp.float32
        )
        return 0

    lax.fori_loop(0, BAND, one_bin, 0, unroll=8)
    _, is_first = position(len(outs))
    pick_slots(cross, select_ref, outs, jnp.where(is_first, 1, 0), nodes)


def own_slots_kernel(cross_ref, select_ref, *outs):
    _, is_first = position(len(outs))
    pick_slots(cross_ref, select_ref, outs, jnp.where(is_first, 0, 1), outs[0].shape[0])


def cross_products(a, b, halo_a, halo_b, select, wins):
    nodes = a.shape[1]
    block = jax.ShapeDtypeStruct((nodes, select.shape[1] // wins, LANES), jnp.float32)
    vmem = pl.BlockSpec(memory_space=pltpu.VMEM)
    cross, *others = pl.pallas_call(
        cross_kernel,
        out_shape=[jax.ShapeDtypeStruct((BAND * 4 * nodes, 8 * nodes), jnp.float32)] + [block] * wins,
        in_specs=[vmem] * 5,
        out_specs=[vmem] * (1 + wins),
        compiler_params=pltpu.CompilerParams(vmem_limit_bytes=12 * MIB),
        name="cross_products",
    )(a, b, halo_a, halo_b, select)
    own = pl.pallas_call(
        own_slots_kernel,
        out_shape=[block] * wins,
        in_specs=[vmem] * 2,
        out_specs=[vmem] * wins,
        compiler_params=pltpu.CompilerParams(vmem_limit_bytes=8 * MIB),
        cost_estimate=pl.CostEstimate(flops=1 << 32, bytes_accessed=1 << 24, transcendentals=0),
        name="own_slots",
    )(cross, select)
    return own, others


def inverse_kernel(high_ref, low_ref, *refs):
    blocks, (out_ref, both) = refs[:-2], refs[-2:]
    nodes, slots, _ = blocks[0].shape
    rows = nodes * slots

    @pl.when(pl.program_id(0) == 0)
    def _():
        me, _ = position(len(blocks) // 2)
        for d, block in enumerate(blocks):
            columns = pl.ds(pl.multiple_of((me ^ d) * LANES, LANES), LANES)
            values = block[...].reshape(rows, LANES)
            high = values.astype(jnp.bfloat16)
            both[0:rows, columns] = high
            both[rows : 2 * rows, columns] = (values - high.astype(jnp.float32)).astype(jnp.bfloat16)

    first = jnp.dot(both[...], high_ref[...], preferred_element_type=jnp.float32)
    second = jnp.dot(both[0:rows, :], low_ref[...], preferred_element_type=jnp.float32)
    out_ref[...] = (first[0:rows, :] + (first[rows : 2 * rows, :] + second)).reshape(out_ref.shape)


def inverse(blocks, high, low):
    nodes, slots, _ = blocks[0].shape
    depth = high.shape[0] * LANES
    width = 256
    table = pl.BlockSpec((depth, width), lambda i: (0, i))
    return pl.pallas_call(
        inverse_kernel,
        grid=(LAGS // width,),
        in_specs=[table, table] + [pl.BlockSpec(blocks[0].shape, lambda i: (0, 0, 0))] * len(blocks),
        out_specs=pl.BlockSpec((nodes, slots, width), lambda i: (0, 0, i)),
        out_shape=jax.ShapeDtypeStruct((nodes, slots, LAGS), jnp.float32),
        scratch_shapes=[pltpu.VMEM((2 * nodes * slots, depth), jnp.bfloat16)],
        compiler_params=pltpu.CompilerParams(vmem_limit_bytes=12 * MIB),
        name="inverse",
    )(high.reshape(depth, LAGS), low.reshape(depth, LAGS), *blocks)


def per_device(traces, taps, neighbours, valid, *, pairs, wins):
    windows, nodes, samples = traces.shape
    parts = 2 * wins
    place = lax.axis_index("pairs")
    win = lax.axis_index("win")

    def exchange(blocks):
        moved = list(blocks)
        for d in range(parts - 1, 0, -1):
            hop = [(i, (((i // wins) ^ (d // wins)) * wins) + ((i % wins) ^ (d % wins))) for i in range(pairs * wins)]
            moved[d] = lax.ppermute(blocks[d], ("pairs", "win"), hop)
        return moved

    rows, taps = traces.reshape(windows * nodes, samples), taps.reshape(1, TAPS)
    steps = tuple(range(wins))[::-1]
    found = own_spectra(rows, taps, nodes, steps)
    found, neighbours, valid = lax.optimization_barrier((found, neighbours, valid))
    spectra = [found[2 * steps.index(d // 2) + d % 2] for d in range(parts)]

    _, is_first = position(wins)
    tile, member = neighbours // nodes, neighbours % nodes
    inside = tile // 2 == place // 2
    leading = 1 - (place // 2) % 2
    block = jnp.where(inside, jnp.where(tile % 2 == leading, 0, 1), jnp.where(is_first, 2, 3))
    code = jnp.where(valid != 0, block * nodes + member, -1)
    other = lax.ppermute(code, "pairs", [(i, i ^ 1) for i in range(pairs)])
    codes = jnp.where(is_first, jnp.concatenate([code, other], 0), jnp.concatenate([other, code], 0))
    for bit in (1 << k for k in range((wins - 1).bit_length())):
        split = codes.reshape(2 * nodes, wins // (2 * bit), 2, -1)
        codes = jnp.where(win & bit != 0, split[:, :, ::-1], split)
    codes = codes.reshape(2 * nodes, -1)
    columns = jnp.arange(8 * nodes, dtype=jnp.int32) % (4 * nodes)
    select = (codes[:, :, None] == columns[None, None, :]).astype(jnp.bfloat16)

    factor = 1.0 / math.sqrt(BINS * windows * wins)
    high, low = make_lag_tables(parts, factor)

    a, b = by_bin(exchange(spectra))
    swap_a = [(i, i ^ 2) for i in range(pairs) if (i ^ 2) < pairs]
    swap_b = [(i, j) for i in range(2, pairs) for j in [((i - 2) ^ 2) + 2] if j < pairs]
    halo_a = lax.ppermute(a, "pairs", swap_a)
    halo_b = lax.ppermute(b, "pairs", swap_b)
    own, others = cross_products(a, b, halo_a, halo_b, select, wins)
    return inverse(exchange([*own, *others]), high, low)


def solution(mesh):
    placed = (P("win", "pairs", None), P(), P("pairs", None), P("pairs", None))
    body = functools.partial(per_device, pairs=mesh.shape["pairs"], wins=mesh.shape["win"])
    return jax.shard_map(
        body, mesh=mesh, in_specs=placed, out_specs=P("pairs", "win", None), check_vma=False
    )
```

time: 81.4 us -> 74.4 us (0.914)
  Pallas kernels: 31.7 us -> 23.2 us
  waiting for transfers between devices: 28.6 us -> 31.7 us
  other arithmetic: 1.84 us -> 0.47 us
    pallas_call x5 -> x4, Pallas kernels: 26.6 us -> 18.7 us  [the longest x1 11.2 us: own_spectra(): pl.pallas_call(functools.partial(spectra_kernel, steps=steps, wins=len(st...]
    ppermute x1, waiting for transfers between devices: 0.01 us -> 1.62 us  [per_device(): other = lax.ppermute(code, 'pairs', [(i, i ^ 1) for i in range(pairs)])]
    ppermute x14, waiting for transfers between devices: 15.4 us -> 16.9 us  [exchange(): moved[d] = lax.ppermute(blocks[d], ('pairs', 'win'), hop)]
  transfers between devices with their start and end apart: 17 -> 17, of which waited for: 7 -> 8; matrix products, arithmetic and copies ran while one was open for 2% -> 1% of each run, Pallas kernels for 21% -> 1%
where the time goes in v4:
time: 74.4 us; the launch traced here: 73.5 us
  waiting for transfers between devices  31.7 us (43%)
  Pallas kernels  23.2 us (31%)
  starting transfers between devices  16.8 us (23%)
  local copies, waits for them, and re-layouts  1.17 us (2%)
    ppermute x14, waiting for transfers between devices, exchange(): moved[d] = lax.ppermute(blocks[d], ('pairs', 'win'), hop)  16.9 us
    ppermute x14, starting transfers between devices, exchange(): moved[d] = lax.ppermute(blocks[d], ('pairs', 'win'), hop)  11.6 us
    pallas_call x1, Pallas kernels, own_spectra(): pl.pallas_call(functools.partial(spectra_kernel, steps=steps, wins=len(st...  11.2 us
    ppermute x1, waiting for transfers between devices, per_device(): halo_a = lax.ppermute(a, 'pairs', swap_a)  10 us
    pallas_call x1, Pallas kernels, inverse(): pl.pallas_call(inverse_kernel, grid=(LAGS // width,), in_specs=[table, ta...  3.95 us
    pallas_call x1, Pallas kernels, cross_products(): pl.pallas_call(cross_kernel, out_shape=[jax.ShapeDtypeStruct((BAND * 4 *...  3.43 us
    ppermute x1, waiting for transfers between devices, per_device(): halo_b = lax.ppermute(b, 'pairs', swap_b)  3.18 us
    pallas_call x1, Pallas kernels, by_bin(): pl.pallas_call(by_bin_kernel, out_shape=[shape, shape], in_specs=[vmem] *...  2.46 us
  transfers between devices with their start and end apart: 17, of which 8 were waited for; matrix products, arithmetic and copies ran while one was open for 1% of the time, Pallas kernels for 1%

profile of v4, /device:TPU:16, one launch (start us, length us, event | category | flops | bytes accessed | tf_op | source)
XLA Modules:
  0.0 73.5 jit_solution(17121197242141933014)
XLA Ops:
  0.0 11.2 %own_spectra.1 = (bf16[16,32,128]{2,1,0:T(8,128)(2,1)}, bf16[16,32,128]{2,1,0:T(8,128)(2,1)}, bf16[16,32,128]{2,1,0:T(8,128)(2,1)}, bf16[16,32,128]{2,1,0:T(8,12...) custom-call(bf16[512,4096]{1,0:T(8,128)(2,1)} %bitcast.14, ...), custom_call_target="tpu_custom_call" | custom-call | flops 4294967296 | bytes 4194304 | tf_op jit(solution)/shard_map/own_spectra/pallas_call | solution.py:166
  11.2 0.1 collective-permute-start
  11.3 1.6 %collective-permute-start.1 = (bf16[16,32,128]{2,1,0:T(8,128)(2,1)}, bf16[16,32,128]{2,1,0:T(8,128)(2,1)S(1)}, u32[]{:S(2)}, u32[]{:S(2)}) collective-permute-start(bf16[16,32,128]{2,1,0:T(8,128)(2,1)} %get-tuple-element.48), channel_id=1, source_target_pairs={{0,2},{1,3},{2,0},{3,1},{4,6},{5,7},{6,4},{7,5},{8,10},{9,11},{10,... | collective-permute-start | bytes 393224 | tf_op jit(solution)/shard_map/ppermute | solution.py:375
  13.0 1.6 %collective-permute-start.9 = (s32[16,64]{1,0:T(8,128)S(1)}, s32[16,64]{1,0:T(8,128)S(1)}, u32[]{:S(2)}, u32[]{:S(2)}) collective-permute-start(s32[16,64]{1,0:T(8,128)S(1)} %fusion.3), channel_id=1, source_target_pairs={{0,4},{4,0},{8,12},{12,8},{16,20},{20,16},{24,28},{28,24},{1,5},{5... | collective-permute-start | bytes 12296 | tf_op jit(solution)/shard_map/ppermute | solution.py:390
  14.5 0.0 collective-permute-start.2
  14.5 0.5 collective-permute-start.3
  15.1 1.6 %collective-permute-done.9 = s32[16,64]{1,0:T(8,128)S(1)} collective-permute-done((s32[16,64]{1,0:T(8,128)S(1)}, s32[16,64]{1,0:T(8,128)S(1)}, u32[]{:S(2)}, u32[]{:S(2)}) %collective-permute-start.9) | collective-permute-done | bytes 4128 | tf_op jit(solution)/shard_map/ppermute | solution.py:390
  16.7 0.4 collective-permute-start.4
  17.1 0.0 collective-permute-done.refs_1_
  17.1 1.0 %collective-permute-start.5 = (bf16[16,32,128]{2,1,0:T(8,128)(2,1)}, bf16[16,32,128]{2,1,0:T(8,128)(2,1)S(1)}, u32[]{:S(2)}, u32[]{:S(2)}) collective-permute-start(bf16[16,32,128]{2,1,0:T(8,128)(2,1)} %get-tuple-element.52), channel_id=1, source_target_pairs={{0,6},{1,7},{2,4},{3,5},{4,2},{5,3},{6,0},{7,1},{8,14},{9,15},{10,... | collective-permute-start | bytes 393224 | tf_op jit(solution)/shard_map/ppermute | solution.py:375
  18.1 0.0 collective-permute-done.1.refs_2_
  18.1 2.5 %collective-permute-start.6 = (bf16[16,32,128]{2,1,0:T(8,128)(2,1)}, bf16[16,32,128]{2,1,0:T(8,128)(2,1)S(1)}, u32[]{:S(2)}, u32[]{:S(2)}) collective-permute-start(bf16[16,32,128]{2,1,0:T(8,128)(2,1)} %get-tuple-element.53), channel_id=1, source_target_pairs={{0,7},{1,6},{2,5},{3,4},{4,3},{5,2},{6,1},{7,0},{8,15},{9,14},{10,... | collective-permute-start | bytes 393224 | tf_op jit(solution)/shard_map/ppermute | solution.py:375
  20.6 0.1 copy.12
  20.7 0.1 copy.13
  20.7 0.1 add_select_fusion
  20.8 0.0 collective-permute-done.2.refs_3_
  20.8 0.2 collective-permute-done.3.refs_4_
  21.0 7.8 %collective-permute-done.4.refs_5_ = bf16[16,32,128]{2,1,0:T(8,128)(2,1)S(1)} collective-permute-done((bf16[16,32,128]{2,1,0:T(8,128)(2,1)}, bf16[16,32,128]{2,1,0:T(8,128)(2,1)S(1)}, u32[]{:S(2)}, u32[]{:S(2)}) %collective-permute-start.4) | collective-permute-done | bytes 131104 | tf_op jit(solution)/shard_map/ppermute | solution.py:375
  28.9 0.0 collective-permute-done.5.refs_6_
  28.9 0.0 collective-permute-done.6.refs_7_
  28.9 0.9 %copy-done.2 = bf16[16,32,128]{2,1,0:T(8,128)(2,1)S(1)} copy-done((bf16[16,32,128]{2,1,0:T(8,128)(2,1)S(1)}, bf16[16,32,128]{2,1,0:T(8,128)(2,1)}, u32[]{:S(2)}) %copy-start.2) | copy-done | bytes 131096
  29.8 2.5 %by_bin.1 = (bf16[64,16,256]{2,1,0:T(8,128)(2,1)S(1)}, bf16[64,16,256]{2,1,0:T(8,128)(2,1)S(1)}) custom-call(bf16[16,32,128]{2,1,0:T(8,128)(2,1)S(1)} %copy-done.2, bf16[16,32,128]{2,1,0:T(8,128)(2,1)S(1)} %collective-permute-done.refs_1_, bf16[16,32,128]{2,1,0:T(8,128)(2,1)S(1)} %collective-permute-done.1.refs_2_, ...), custom_call_target="tpu_custom_call" | custom-call | tf_op jit(solution)/shard_map/by_bin/pallas_call | solution.py:248
  32.2 1.6 %collective-permute-start.7 = (bf16[64,16,256]{2,1,0:T(8,128)(2,1)S(1)}, bf16[64,16,256]{2,1,0:T(8,128)(2,1)S(1)}, u32[]{:S(2)}, u32[]{:S(2)}) collective-permute-start(bf16[64,16,256]{2,1,0:T(8,128)(2,1)S(1)} %get-tuple-element.54.a_ref), channel_id=1, source_target_pairs={{0,8},{4,12},{8,0},{12,4},{16,24},{20,28},{24,16},{28,20},{1,9},{5... | collective-permute-start | bytes 1572872 | tf_op jit(solution)/shard_map/ppermute | solution.py:405
  33.9 1.9 %collective-permute-start.8 = (bf16[64,16,256]{2,1,0:T(8,128)(2,1)S(1)}, bf16[64,16,256]{2,1,0:T(8,128)(2,1)S(1)}, u32[]{:S(2)}, u32[]{:S(2)}) collective-permute-start(bf16[64,16,256]{2,1,0:T(8,128)(2,1)S(1)} %get-tuple-element.55.b_ref), channel_id=1, source_target_pairs={{8,16},{12,20},{16,8},{20,12},{9,17},{13,21},{17,9},{21,13},{10,18... | collective-permute-start | bytes 1572872 | tf_op jit(solution)/shard_map/ppermute | solution.py:406
  35.8 0.1 copy.14
  35.9 0.3 compare_convert_fusion.select_ref
  36.2 10.0 %collective-permute-done.7.ha_ref = bf16[64,16,256]{2,1,0:T(8,128)(2,1)S(1)} collective-permute-done((bf16[64,16,256]{2,1,0:T(8,128)(2,1)S(1)}, bf16[64,16,256]{2,1,0:T(8,128)(2,1)S(1)}, u32[]{:S(2)}, u32[]{:S(2)}) %collective-permute-start.7) | collective-permute-done | bytes 524320 | tf_op jit(solution)/shard_map/ppermute | solution.py:405
  46.2 3.2 %collective-permute-done.8.hb_ref = bf16[64,16,256]{2,1,0:T(8,128)(2,1)S(1)} collective-permute-done((bf16[64,16,256]{2,1,0:T(8,128)(2,1)S(1)}, bf16[64,16,256]{2,1,0:T(8,128)(2,1)S(1)}, u32[]{:S(2)}, u32[]{:S(2)}) %collective-permute-start.8) | collective-permute-done | bytes 524320 | tf_op jit(solution)/shard_map/ppermute | solution.py:406
  49.4 3.4 %cross_products.1 = (f32[4096,128]{1,0:T(8,128)S(1)}, f32[16,16,128]{2,1,0:T(8,128)S(1)}, f32[16,16,128]{2,1,0:T(8,128)S(1)}, f32[16,16,128]{2,1,0:T(8,128)S(1)}, f32[16,16,128]{2,1,0:T(8,128)S(1)}) custom-call(bf16[64,16,256]{2,1,0:T(8,128)(2,1)S(1)} %get-tuple-element.54.a_ref, bf16[64,16,256]{2,1,0:T(8,128)(2,1)S(1)} %get-tuple-element.55.b_ref, ...), custom_call_target="tpu_custom_call" | custom-call | tf_op jit(solution)/shard_map/cross_products/pallas_call | solution.py:308
  52.9 0.0 copy-start
  52.9 0.0 copy-start.1
  52.9 0.0 copy-start.3
  52.9 0.0 copy-start.4
  52.9 1.1 %own_slots.1 = (f32[16,16,128]{2,1,0:T(8,128)S(1)}, f32[16,16,128]{2,1,0:T(8,128)S(1)}, f32[16,16,128]{2,1,0:T(8,128)S(1)}, f32[16,16,128]{2,1,0:T(8,128)S(1)}) custom-call(f32[4096,128]{1,0:T(8,128)S(1)} %get-tuple-element.58.cross_ref, bf16[32,64,128]{2,1,0:T(8,128)(2,1)S(1)} %compare_convert_fusion.select_ref), custom_call_target="tpu_custom_call" | custom-call | flops 4294967296 | bytes 16777216 | tf_op jit(solution)/shard_map/own_slots/pallas_call | solution.py:316
  54.0 0.1 collective-permute-start.10
  54.1 1.7 %collective-permute-start.11 = (f32[16,16,128]{2,1,0:T(8,128)S(1)}, f32[16,16,128]{2,1,0:T(8,128)S(1)}, u32[]{:S(2)}, u32[]{:S(2)}) collective-permute-start(f32[16,16,128]{2,1,0:T(8,128)S(1)} %get-tuple-element.61), channel_id=1, source_target_pairs={{0,2},{1,3},{2,0},{3,1},{4,6},{5,7},{6,4},{7,5},{8,10},{9,11},{10,... | collective-permute-start | bytes 393224 | tf_op jit(solution)/shard_map/ppermute | solution.py:375
  55.8 0.2 collective-permute-start.12
  55.9 0.6 collective-permute-start.13
  56.5 1.1 %collective-permute-start.14 = (f32[16,16,128]{2,1,0:T(8,128)S(1)}, f32[16,16,128]{2,1,0:T(8,128)S(1)}, u32[]{:S(2)}, u32[]{:S(2)}) collective-permute-start(f32[16,16,128]{2,1,0:T(8,128)S(1)} %get-tuple-element.64), channel_id=1, source_target_pairs={{0,5},{1,4},{2,7},{3,6},{4,1},{5,0},{6,3},{7,2},{8,13},{9,12},{10,... | collective-permute-start | bytes 393224 | tf_op jit(solution)/shard_map/ppermute | solution.py:375
  57.6 1.6 %collective-permute-start.15 = (f32[16,16,128]{2,1,0:T(8,128)S(1)}, f32[16,16,128]{2,1,0:T(8,128)S(1)}, u32[]{:S(2)}, u32[]{:S(2)}) collective-permute-start(f32[16,16,128]{2,1,0:T(8,128)S(1)} %get-tuple-element.65), channel_id=1, source_target_pairs={{0,6},{1,7},{2,4},{3,5},{4,2},{5,3},{6,0},{7,1},{8,14},{9,15},{10,... | collective-permute-start | bytes 393224 | tf_op jit(solution)/shard_map/ppermute | solution.py:375
  59.2 1.2 %collective-permute-done.11.refs_2_ = f32[16,16,128]{2,1,0:T(8,128)S(1)} collective-permute-done((f32[16,16,128]{2,1,0:T(8,128)S(1)}, f32[16,16,128]{2,1,0:T(8,128)S(1)}, u32[]{:S(2)}, u32[]{:S(2)}) %collective-permute-start.11) | collective-permute-done | bytes 131104 | tf_op jit(solution)/shard_map/ppermute | solution.py:375
  60.4 0.4 collective-permute-start.16
  60.8 1.1 %lag_tables.1 = (bf16[8,128,1024]{2,1,0:T(8,128)(2,1)S(1)}, bf16[8,128,1024]{2,1,0:T(8,128)(2,1)S(1)}) custom-call(f32[64,1024]{1,0:T(8,128)S(1)} %copy-done.1, f32[64,1024]{1,0:T(8,128)S(1)} %copy-done, f32[8,1024]{1,0:T(8,128)S(1)} %copy-done.4, f32[8,1024]{1,0:T(8,128)S(1)} %copy-done.3), custom_call_target="tpu_custom_call" | custom-call | tf_op jit(solution)/shard_map/lag_tables/pallas_call | solution.py:202
  61.9 0.5 collective-permute-done.12.refs_3_
  62.4 0.0 collective-permute-done.13.refs_4_
  62.4 7.1 %collective-permute-done.14.refs_5_ = f32[16,16,128]{2,1,0:T(8,128)S(1)} collective-permute-done((f32[16,16,128]{2,1,0:T(8,128)S(1)}, f32[16,16,128]{2,1,0:T(8,128)S(1)}, u32[]{:S(2)}, u32[]{:S(2)}) %collective-permute-start.14) | collective-permute-done | bytes 131104 | tf_op jit(solution)/shard_map/ppermute | solution.py:375
  69.6 0.0 collective-permute-done.15.refs_6_
  69.6 4.0 %inverse.1 = f32[16,16,1024]{2,1,0:T(8,128)} custom-call(bf16[1024,1024]{1,0:T(8,128)(2,1)S(1)} %bitcast.8, bf16[1024,1024]{1,0:T(8,128)(2,1)S(1)} %bitcast.9, f32[16,16,128]{2,1,0:T(8,128)S(1)} %get-tuple-element.59.refs_0_, f32[16,16,128]{2,1,0:T(8,128)S(1)} %collective-permute-done.10.refs_1_, f32[16,16,128]{2,1,0:T(8,128)S(1)} %collective-permute-done.11.refs_2_, ...), custom_call_target="tpu_custom_call" | custom-call | tf_op jit(solution)/shard_map/inverse/pallas_call | solution.py:353
  (15 shorter events, 0.1 us)
Async XLA Ops:
  0.0 12.9 %copy-start.5 = (s32[16,64]{1,0:T(8,128)S(1)}, s32[16,64]{1,0:T(8,128)}, u32[]{:S(2)}) copy-start(s32[16,64]{1,0:T(8,128)} %param.13) | copy-start | bytes 12292
  0.0 12.9 %copy-start.6 = (s32[16,64]{1,0:T(8,128)S(1)}, s32[16,64]{1,0:T(8,128)}, u32[]{:S(2)}) copy-start(s32[16,64]{1,0:T(8,128)} %param.14) | copy-start | bytes 12292
  11.2 5.9 %collective-permute-start = (bf16[16,32,128]{2,1,0:T(8,128)(2,1)}, bf16[16,32,128]{2,1,0:T(8,128)(2,1)S(1)}, u32[]{:S(2)}, u32[]{:S(2)}) collective-permute-start(bf16[16,32,128]{2,1,0:T(8,128)(2,1)} %get-tuple-element.47), channel_id=1, source_target_pairs={{0,1},{1,0},{2,3},{3,2},{4,5},{5,4},{6,7},{7,6},{8,9},{9,8},{10,11... | collective-permute-start | bytes 393224 | tf_op jit(solution)/shard_map/ppermute | solution.py:375
  11.3 6.8 %collective-permute-start.1 = (bf16[16,32,128]{2,1,0:T(8,128)(2,1)}, bf16[16,32,128]{2,1,0:T(8,128)(2,1)S(1)}, u32[]{:S(2)}, u32[]{:S(2)}) collective-permute-start(bf16[16,32,128]{2,1,0:T(8,128)(2,1)} %get-tuple-element.48), channel_id=1, source_target_pairs={{0,2},{1,3},{2,0},{3,1},{4,6},{5,7},{6,4},{7,5},{8,10},{9,11},{10,... | collective-permute-start | bytes 393224 | tf_op jit(solution)/shard_map/ppermute | solution.py:375
  13.0 3.7 %collective-permute-start.9 = (s32[16,64]{1,0:T(8,128)S(1)}, s32[16,64]{1,0:T(8,128)S(1)}, u32[]{:S(2)}, u32[]{:S(2)}) collective-permute-start(s32[16,64]{1,0:T(8,128)S(1)} %fusion.3), channel_id=1, source_target_pairs={{0,4},{4,0},{8,12},{12,8},{16,20},{20,16},{24,28},{28,24},{1,5},{5... | collective-permute-start | bytes 12296 | tf_op jit(solution)/shard_map/ppermute | solution.py:390
  14.5 6.3 %collective-permute-start.2 = (bf16[16,32,128]{2,1,0:T(8,128)(2,1)}, bf16[16,32,128]{2,1,0:T(8,128)(2,1)S(1)}, u32[]{:S(2)}, u32[]{:S(2)}) collective-permute-start(bf16[16,32,128]{2,1,0:T(8,128)(2,1)} %get-tuple-element.49), channel_id=1, source_target_pairs={{0,3},{1,2},{2,1},{3,0},{4,7},{5,6},{6,5},{7,4},{8,11},{9,10},{10,... | collective-permute-start | bytes 393224 | tf_op jit(solution)/shard_map/ppermute | solution.py:375
  14.5 6.5 %collective-permute-start.3 = (bf16[16,32,128]{2,1,0:T(8,128)(2,1)}, bf16[16,32,128]{2,1,0:T(8,128)(2,1)S(1)}, u32[]{:S(2)}, u32[]{:S(2)}) collective-permute-start(bf16[16,32,128]{2,1,0:T(8,128)(2,1)} %get-tuple-element.50), channel_id=1, source_target_pairs={{0,4},{1,5},{2,6},{3,7},{4,0},{5,1},{6,2},{7,3},{8,12},{9,13},{10,... | collective-permute-start | bytes 393224 | tf_op jit(solution)/shard_map/ppermute | solution.py:375
  16.7 12.2 %collective-permute-start.4 = (bf16[16,32,128]{2,1,0:T(8,128)(2,1)}, bf16[16,32,128]{2,1,0:T(8,128)(2,1)S(1)}, u32[]{:S(2)}, u32[]{:S(2)}) collective-permute-start(bf16[16,32,128]{2,1,0:T(8,128)(2,1)} %get-tuple-element.51), channel_id=1, source_target_pairs={{0,5},{1,4},{2,7},{3,6},{4,1},{5,0},{6,3},{7,2},{8,13},{9,12},{10,... | collective-permute-start | bytes 393224 | tf_op jit(solution)/shard_map/ppermute | solution.py:375
  17.1 11.7 %collective-permute-start.5 = (bf16[16,32,128]{2,1,0:T(8,128)(2,1)}, bf16[16,32,128]{2,1,0:T(8,128)(2,1)S(1)}, u32[]{:S(2)}, u32[]{:S(2)}) collective-permute-start(bf16[16,32,128]{2,1,0:T(8,128)(2,1)} %get-tuple-element.52), channel_id=1, source_target_pairs={{0,6},{1,7},{2,4},{3,5},{4,2},{5,3},{6,0},{7,1},{8,14},{9,15},{10,... | collective-permute-start | bytes 393224 | tf_op jit(solution)/shard_map/ppermute | solution.py:375
  18.1 10.8 %collective-permute-start.6 = (bf16[16,32,128]{2,1,0:T(8,128)(2,1)}, bf16[16,32,128]{2,1,0:T(8,128)(2,1)S(1)}, u32[]{:S(2)}, u32[]{:S(2)}) collective-permute-start(bf16[16,32,128]{2,1,0:T(8,128)(2,1)} %get-tuple-element.53), channel_id=1, source_target_pairs={{0,7},{1,6},{2,5},{3,4},{4,3},{5,2},{6,1},{7,0},{8,15},{9,14},{10,... | collective-permute-start | bytes 393224 | tf_op jit(solution)/shard_map/ppermute | solution.py:375
  28.9 0.9 %copy-start.2 = (bf16[16,32,128]{2,1,0:T(8,128)(2,1)S(1)}, bf16[16,32,128]{2,1,0:T(8,128)(2,1)}, u32[]{:S(2)}) copy-start(bf16[16,32,128]{2,1,0:T(8,128)(2,1)} %get-tuple-element.46.refs_0_) | copy-start | bytes 393220
  32.2 14.0 %collective-permute-start.7 = (bf16[64,16,256]{2,1,0:T(8,128)(2,1)S(1)}, bf16[64,16,256]{2,1,0:T(8,128)(2,1)S(1)}, u32[]{:S(2)}, u32[]{:S(2)}) collective-permute-start(bf16[64,16,256]{2,1,0:T(8,128)(2,1)S(1)} %get-tuple-element.54.a_ref), channel_id=1, source_target_pairs={{0,8},{4,12},{8,0},{12,4},{16,24},{20,28},{24,16},{28,20},{1,9},{5... | collective-permute-start | bytes 1572872 | tf_op jit(solution)/shard_map/ppermute | solution.py:405
  33.9 15.6 %collective-permute-start.8 = (bf16[64,16,256]{2,1,0:T(8,128)(2,1)S(1)}, bf16[64,16,256]{2,1,0:T(8,128)(2,1)S(1)}, u32[]{:S(2)}, u32[]{:S(2)}) collective-permute-start(bf16[64,16,256]{2,1,0:T(8,128)(2,1)S(1)} %get-tuple-element.55.b_ref), channel_id=1, source_target_pairs={{8,16},{12,20},{16,8},{20,12},{9,17},{13,21},{17,9},{21,13},{10,18... | collective-permute-start | bytes 1572872 | tf_op jit(solution)/shard_map/ppermute | solution.py:406
  52.9 8.0 %copy-start = (f32[64,1024]{1,0:T(8,128)S(1)}, f32[64,1024]{1,0:T(8,128)}, u32[]{:S(2)}) copy-start(f32[64,1024]{1,0:T(8,128)} %constant.120.clone.msin_ref) | copy-start | bytes 786436
  52.9 8.0 %copy-start.1 = (f32[64,1024]{1,0:T(8,128)S(1)}, f32[64,1024]{1,0:T(8,128)}, u32[]{:S(2)}) copy-start(f32[64,1024]{1,0:T(8,128)} %constant.119.clone.cos_ref) | copy-start | bytes 786436
  52.9 7.9 %copy-start.3 = (f32[8,1024]{1,0:T(8,128)S(1)}, f32[8,1024]{1,0:T(8,128)}, u32[]{:S(2)}) copy-start(f32[8,1024]{1,0:T(8,128)} %constant.122.clone.msin0_ref) | copy-start | bytes 98308
  52.9 7.9 %copy-start.4 = (f32[8,1024]{1,0:T(8,128)S(1)}, f32[8,1024]{1,0:T(8,128)}, u32[]{:S(2)}) copy-start(f32[8,1024]{1,0:T(8,128)} %constant.121.clone.cos0_ref) | copy-start | bytes 98308
  54.0 3.6 %collective-permute-start.10 = (f32[16,16,128]{2,1,0:T(8,128)S(1)}, f32[16,16,128]{2,1,0:T(8,128)S(1)}, u32[]{:S(2)}, u32[]{:S(2)}) collective-permute-start(f32[16,16,128]{2,1,0:T(8,128)S(1)} %get-tuple-element.60), channel_id=1, source_target_pairs={{0,1},{1,0},{2,3},{3,2},{4,5},{5,4},{6,7},{7,6},{8,9},{9,8},{10,11... | collective-permute-start | bytes 393224 | tf_op jit(solution)/shard_map/ppermute | solution.py:375
  54.1 6.4 %collective-permute-start.11 = (f32[16,16,128]{2,1,0:T(8,128)S(1)}, f32[16,16,128]{2,1,0:T(8,128)S(1)}, u32[]{:S(2)}, u32[]{:S(2)}) collective-permute-start(f32[16,16,128]{2,1,0:T(8,128)S(1)} %get-tuple-element.61), channel_id=1, source_target_pairs={{0,2},{1,3},{2,0},{3,1},{4,6},{5,7},{6,4},{7,5},{8,10},{9,11},{10,... | collective-permute-start | bytes 393224 | tf_op jit(solution)/shard_map/ppermute | solution.py:375
  55.8 6.6 %collective-permute-start.12 = (f32[16,16,128]{2,1,0:T(8,128)S(1)}, f32[16,16,128]{2,1,0:T(8,128)S(1)}, u32[]{:S(2)}, u32[]{:S(2)}) collective-permute-start(f32[16,16,128]{2,1,0:T(8,128)S(1)} %get-tuple-element.62), channel_id=1, source_target_pairs={{0,3},{1,2},{2,1},{3,0},{4,7},{5,6},{6,5},{7,4},{8,11},{9,10},{10,... | collective-permute-start | bytes 393224 | tf_op jit(solution)/shard_map/ppermute | solution.py:375
  55.9 6.5 %collective-permute-start.13 = (f32[16,16,128]{2,1,0:T(8,128)S(1)}, f32[16,16,128]{2,1,0:T(8,128)S(1)}, u32[]{:S(2)}, u32[]{:S(2)}) collective-permute-start(f32[16,16,128]{2,1,0:T(8,128)S(1)} %get-tuple-element.63), channel_id=1, source_target_pairs={{0,4},{1,5},{2,6},{3,7},{4,0},{5,1},{6,2},{7,3},{8,12},{9,13},{10,... | collective-permute-start | bytes 393224 | tf_op jit(solution)/shard_map/ppermute | solution.py:375
  56.5 13.0 %collective-permute-start.14 = (f32[16,16,128]{2,1,0:T(8,128)S(1)}, f32[16,16,128]{2,1,0:T(8,128)S(1)}, u32[]{:S(2)}, u32[]{:S(2)}) collective-permute-start(f32[16,16,128]{2,1,0:T(8,128)S(1)} %get-tuple-element.64), channel_id=1, source_target_pairs={{0,5},{1,4},{2,7},{3,6},{4,1},{5,0},{6,3},{7,2},{8,13},{9,12},{10,... | collective-permute-start | bytes 393224 | tf_op jit(solution)/shard_map/ppermute | solution.py:375
  57.6 11.9 %collective-permute-start.15 = (f32[16,16,128]{2,1,0:T(8,128)S(1)}, f32[16,16,128]{2,1,0:T(8,128)S(1)}, u32[]{:S(2)}, u32[]{:S(2)}) collective-permute-start(f32[16,16,128]{2,1,0:T(8,128)S(1)} %get-tuple-element.65), channel_id=1, source_target_pairs={{0,6},{1,7},{2,4},{3,5},{4,2},{5,3},{6,0},{7,1},{8,14},{9,15},{10,... | collective-permute-start | bytes 393224 | tf_op jit(solution)/shard_map/ppermute | solution.py:375
  60.4 9.1 %collective-permute-start.16 = (f32[16,16,128]{2,1,0:T(8,128)S(1)}, f32[16,16,128]{2,1,0:T(8,128)S(1)}, u32[]{:S(2)}, u32[]{:S(2)}) collective-permute-start(f32[16,16,128]{2,1,0:T(8,128)S(1)} %get-tuple-element.66), channel_id=1, source_target_pairs={{0,7},{1,6},{2,5},{3,4},{4,3},{5,2},{6,1},{7,0},{8,15},{9,14},{10,... | collective-permute-start | bytes 393224 | tf_op jit(solution)/shard_map/ppermute | solution.py:375

commit v5 on v4

--- a/solution.py
+++ b/solution.py
@@ -19,6 +19,7 @@
 EPSILON = 1e-06
 STEP = 64
 CHUNK = 512
+HALVES = 2
 MIB = 1024 * 1024
 CONTRACT_LAST = (((1,), (1,)), ((), ()))
 
@@ -58,11 +59,11 @@
 
 
 def spectra_kernel(x_hbm, taps_ref, fine_hbm, turn_c_hbm, turn_s_hbm, *refs, steps, wins):
-    outs, refs = refs[: 2 * len(steps)], refs[2 * len(steps) :]
+    outs, refs = refs[: HALVES * len(steps)], refs[HALVES * len(steps) :]
     x_ref, fine_ref, turn_c_ref, turn_s_ref, *refs, sems = refs
     tables, totals, stages = refs[0:2], refs[2:4], refs[4:6]
     count = x_ref.shape[0]
-    nodes, windows = outs[0].shape[0], outs[0].shape[1]
+    nodes, windows = outs[0].shape[1], outs[0].shape[2]
     width = 2 * LANES
     pieces = SAMPLES // CHUNK
     me, _ = position(wins)
@@ -84,13 +85,13 @@
     def columns_of(i):
         return pl.ds(pl.multiple_of(((me // 2) ^ steps[i]) * width, width), width)
 
-    def generate(i, piece):
+    def generate(i):
         columns = columns_of(i)
         base = fine_ref[0:STEP, columns]
         swapped = jnp.concatenate(
             [pltpu.roll(base[:, c : c + LANES], BAND, 1) for c in range(0, width, LANES)], 1
         )
-        for j in range(piece * (CHUNK // STEP), (piece + 1) * (CHUNK // STEP)):
+        for j in range(SAMPLES // STEP):
             row = pl.ds(j, 1)
             turned = base * turn_c_ref[row, columns] + swapped * turn_s_ref[row, columns]
             tables[i % 2][j * STEP : (j + 1) * STEP, :] = turned.astype(jnp.bfloat16)
@@ -113,48 +114,50 @@
             other = pltpu.roll(jnp.broadcast_to(here, (8, LANES)), BAND, 1)[0:1, :]
             responses[i].append((jnp.where(low, here, other), jnp.where(low, -other, here)))
 
-    def whiten(i, piece):
-        rows = pl.ds(piece * (count // pieces), count // pieces)
-        for c in range(2):
-            same, cross = responses[i][c]
-            raw = totals[i % 2][c, rows, :]
-            power = jnp.sum(raw * raw, 1, keepdims=True) * (1.0 / BAND)
-            white = raw * lax.rsqrt(power + EPSILON)
-            stages[i % 2][c ^ (me % 2), rows, :] = white * same + pltpu.roll(white, BAND, 1) * cross
-
-    def give(i, piece):
-        for c in range(2):
-            for node in range(piece * nodes // pieces, (piece + 1) * nodes // pieces):
-                values = stages[i % 2][c, pl.ds(node, windows, stride=nodes), :]
-                outs[2 * i + c][node] = values.astype(jnp.bfloat16)
+    row = lax.broadcasted_iota(jnp.int32, (width, width), 0)
+    same_band = (row // LANES) == (lax.broadcasted_iota(jnp.int32, (width, width), 1) // LANES)
+    summing = same_band.astype(jnp.bfloat16)
+
+    def whiten(i):
+        raw = jnp.concatenate([totals[i % 2][c] for c in range(2)], 1)
+        square = raw * raw
+        high = square.astype(jnp.bfloat16)
+        rest = (square - high.astype(jnp.float32)).astype(jnp.bfloat16)
+        sums = jnp.dot(jnp.concatenate([high, rest], 0), summing, preferred_element_type=jnp.float32)
+        white = raw * lax.rsqrt((sums[0:count, :] + sums[count:, :]) * (1.0 / BAND) + EPSILON)
+        for c, (same, cross) in enumerate(responses[i]):
+            part = white[:, c * LANES : (c + 1) * LANES]
+            stages[i % 2][c ^ (me % 2)] = part * same + pltpu.roll(part, BAND, 1) * cross
+
+    def give(i):
+        for half in range(HALVES):
+            first = half * windows * nodes
+            for c in range(2):
+                for node in range(nodes):
+                    values = stages[i % 2][c, pl.ds(first + node, windows, stride=nodes), :]
+                    outs[half * len(steps) + i][c, node] = values.astype(jnp.bfloat16)
 
     for copy in copies:
         copy.wait()
-    for piece in range(pieces):
-        generate(0, piece)
+    generate(0)
     last = len(steps) - 1
+    for copy in chunks:
+        copy.wait()
     for i in range(len(steps)):
         respond(i)
-        for piece in range(pieces):
-            part = pl.ds(piece * CHUNK, CHUNK)
-            if i == 0:
-                chunks[piece].wait()
-            product = jnp.dot(x_ref[:, part], tables[i % 2][part, :], preferred_element_type=jnp.float32)
-            for c in range(2):
-                here = product[:, c * LANES : (c + 1) * LANES]
-                totals[i % 2][c] = here if piece == 0 else totals[i % 2][c] + here
-            if i < last:
-                generate(i + 1, piece)
-            if i > 0:
-                whiten(i - 1, piece)
-            if i > 1:
-                give(i - 2, piece)
-    for piece in range(pieces):
-        whiten(last, piece)
-        if last > 0:
-            give(last - 1, piece)
-    for piece in range(pieces):
-        give(last, piece)
+        product = jnp.dot(x_ref[...], tables[i % 2][...], preferred_element_type=jnp.float32)
+        for c in range(2):
+            totals[i % 2][c] = product[:, c * LANES : (c + 1) * LANES]
+        if i < last:
+            generate(i + 1)
+        if i > 0:
+            whiten(i - 1)
+        if i > 1:
+            give(i - 2)
+    if last > 0:
+        give(last - 1)
+    whiten(last)
+    give(last)
 
 
 def own_spectra(rows, taps, nodes, steps):
@@ -162,12 +165,12 @@
     count = rows.shape[0]
     hbm = pl.BlockSpec(memory_space=pltpu.HBM)
     vmem = pl.BlockSpec(memory_space=pltpu.VMEM)
-    shape = jax.ShapeDtypeStruct((nodes, count // nodes, LANES), jnp.bfloat16)
+    shape = jax.ShapeDtypeStruct((2, nodes, count // nodes // HALVES, LANES), jnp.bfloat16)
     return pl.pallas_call(
         functools.partial(spectra_kernel, steps=steps, wins=len(steps)),
         in_specs=[hbm, vmem, hbm, hbm, hbm],
-        out_specs=[vmem] * (2 * len(steps)),
-        out_shape=[shape] * (2 * len(steps)),
+        out_specs=[vmem] * (HALVES * len(steps)),
+        out_shape=[shape] * (HALVES * len(steps)),
         scratch_shapes=[
             pltpu.VMEM(rows.shape, jnp.bfloat16),
             *[pltpu.VMEM(t.shape, jnp.float32) for t in tables],
@@ -210,55 +213,69 @@
     )(*tables)
 
 
-def by_bin_kernel(*refs):
-    blocks, (first_ref, second_ref, turned) = refs[:-3], refs[-3:]
-    groups = len(blocks) // 2
-    nodes = blocks[0].shape[0]
-    _, is_first = position(groups)
+def by_bin_kernel(*refs, steps):
+    blocks, refs = refs[: 2 * steps], refs[2 * steps :]
+    first_ref, second_ref, turned_ref, turned, near, sem = refs
+    nodes, windows = near.shape[0], near.shape[1]
+    _, is_first = position(steps)
     own_at = jnp.where(is_first, 0, 1)
+    copy = pltpu.make_async_copy(blocks[0].at[0], near, sem)
+    copy.start()
     row = lax.broadcasted_iota(jnp.int32, (LANES, LANES), 0)
     unit = (row == lax.broadcasted_iota(jnp.int32, (LANES, LANES), 1)).astype(jnp.bfloat16)
-    for tile in range(2):
-        here = blocks[tile * groups : (tile + 1) * groups]
+    for tile in (1, 0):
+        here = []
+        for step in range(tile * steps // 2, (tile + 1) * steps // 2):
+            here.append(near if step == 0 else blocks[2 * step].at[0])
+            here.append(blocks[2 * step + 1].at[1])
+        if tile == 0:
+            copy.wait()
 
         def turn(node, _, here=here, tile=tile):
-            values = jnp.concatenate([block[node] for block in here], 0)
+            values = jnp.concatenate([block[node] for block in here] * 2, 0)
             values = lax.dot_general(unit, values, CONTRACT_LAST, preferred_element_type=jnp.float32)
             turned[pl.ds(pl.multiple_of((tile * nodes + node) * LANES, LANES), LANES), :] = values
             return 0
 
         lax.fori_loop(0, nodes, turn, 0, unroll=8)
-    for out_ref, tile in ((first_ref, own_at), (second_ref, 1 - own_at)):
+    left = lax.broadcasted_iota(jnp.int32, (nodes, LANES), 1) < LANES // 2
+    for which, (out_ref, tile) in enumerate(((first_ref, own_at), (second_ref, 1 - own_at))):
         start = tile * (nodes * LANES)
 
-        def one(f, _, out_ref=out_ref, start=start):
+        def one(f, _, out_ref=out_ref, start=start, which=which):
             real = turned[pl.ds(start + f, nodes, stride=LANES), :]
             imag = turned[pl.ds(start + BAND + f, nodes, stride=LANES), :]
-            out_ref[f] = jnp.concatenate([real, imag], 1).astype(jnp.bfloat16)
+            out_ref[f] = jnp.where(left, real, imag).astype(jnp.bfloat16)
+            turned_ref[f, which * nodes : (which + 1) * nodes, :] = jnp.where(left, imag, -real).astype(jnp.bfloat16)
             return 0
 
         lax.fori_loop(0, BAND, one, 0, unroll=8)
 
 
 def by_bin(blocks):
-    nodes, windows, _ = blocks[0].shape
-    windows = windows * len(blocks) // 2
-    shape = jax.ShapeDtypeStruct((BAND, nodes, 2 * windows), jnp.bfloat16)
+    _, nodes, windows, _ = blocks[0].shape
+    steps = len(blocks) // 2
+    shape = jax.ShapeDtypeStruct((BAND, nodes, LANES), jnp.bfloat16)
     vmem = pl.BlockSpec(memory_space=pltpu.VMEM)
     return pl.pallas_call(
-        by_bin_kernel,
-        out_shape=[shape, shape],
-        in_specs=[vmem] * len(blocks),
-        out_specs=[vmem, vmem],
-        scratch_shapes=[pltpu.VMEM((2 * nodes * LANES, windows), jnp.float32)],
+        functools.partial(by_bin_kernel, steps=steps),
+        out_shape=[shape, shape, jax.ShapeDtypeStruct((BAND, 2 * nodes, LANES), jnp.bfloat16)],
+        in_specs=[pl.BlockSpec(memory_space=pl.ANY)] + [vmem] * (len(blocks) - 1),
+        out_specs=[vmem] * 3,
+        scratch_shapes=[
+            pltpu.VMEM((2 * nodes * LANES, LANES), jnp.float32),
+            pltpu.VMEM((nodes, windows, LANES), jnp.bfloat16),
+            pltpu.SemaphoreType.DMA,
+        ],
         compiler_params=pltpu.CompilerParams(vmem_limit_bytes=8 * MIB),
+        cost_estimate=pl.CostEstimate(flops=1 << 31, bytes_accessed=1 << 22, transcendentals=0),
         name="by_bin",
     )(*blocks)
 
 
 def pick_slots(cross_ref, select_ref, outs, where, nodes):
     stations, count = 2 * nodes, 4 * nodes
-    slots = outs[0].shape[1]
+    slots = outs[0].shape[2]
     left = lax.broadcasted_iota(jnp.int32, (2 * BAND, 2 * count), 1) < count
 
     def one_node(node, _):
@@ -269,65 +286,67 @@
         high = values.astype(jnp.bfloat16).astype(jnp.float32)
         split = jnp.where(left, high, values - high).astype(jnp.bfloat16)
         picked = lax.dot_general(select_ref[index], split, CONTRACT_LAST, preferred_element_type=jnp.float32)
-        for d, out_ref in enumerate(outs):
-            out_ref[node] = picked[d * slots : (d + 1) * slots, :]
+        for d in range(2 * len(outs)):
+            outs[d // 2][d % 2, node] = picked[d * slots : (d + 1) * slots, :]
         return 0
 
     lax.fori_loop(0, nodes, one_node, 0, unroll=4)
 
 
-def cross_kernel(a_ref, b_ref, ha_ref, hb_ref, select_ref, cross, *outs):
-    nodes, width = a_ref.shape[1], a_ref.shape[2]
+def cross_kernel(*refs):
+    halves = [refs[5 * h : 5 * h + 5] for h in range(HALVES)]
+    select_ref, cross, *outs = refs[5 * HALVES :]
+    nodes = halves[0][0].shape[1]
     count = 4 * nodes
 
     def one_bin(f, _):
-        own = jnp.concatenate([a_ref[f], b_ref[f]], 0)
-        partners = jnp.concatenate([own, ha_ref[f], hb_ref[f]], 0)
-        turned = jnp.concatenate([own[:, width // 2 :], -own[:, : width // 2]], 1)
-        both = jnp.concatenate([own, turned], 0)
-        partners = jnp.concatenate([partners, partners], 0)
+        wide = lambda k: jnp.concatenate([half[k][f] for half in halves], 1)
+        own = jnp.concatenate([wide(0), wide(1)], 0)
+        both = jnp.concatenate([own, wide(2)], 0)
+        partners = jnp.concatenate([own, wide(3), wide(4)] * 2, 0)
         cross[pl.ds(pl.multiple_of(f * count, count), count), :] = lax.dot_general(
             both, partners, CONTRACT_LAST, preferred_element_type=jnp.float32
         )
         return 0
 
     lax.fori_loop(0, BAND, one_bin, 0, unroll=8)
-    _, is_first = position(len(outs))
+    _, is_first = position(2 * len(outs))
     pick_slots(cross, select_ref, outs, jnp.where(is_first, 1, 0), nodes)
 
 
 def own_slots_kernel(cross_ref, select_ref, *outs):
-    _, is_first = position(len(outs))
-    pick_slots(cross_ref, select_ref, outs, jnp.where(is_first, 0, 1), outs[0].shape[0])
-
-
-def cross_products(a, b, halo_a, halo_b, select, wins):
-    nodes = a.shape[1]
-    block = jax.ShapeDtypeStruct((nodes, select.shape[1] // wins, LANES), jnp.float32)
+    _, is_first = position(2 * len(outs))
+    pick_slots(cross_ref, select_ref, outs, jnp.where(is_first, 0, 1), outs[0].shape[1])
+
+
+def cross_products(halves, select, wins):
+    nodes = halves[0][0].shape[1]
+    block = jax.ShapeDtypeStruct((2, nodes, select.shape[1] // wins, LANES), jnp.float32)
     vmem = pl.BlockSpec(memory_space=pltpu.VMEM)
+    operands = [x for half in halves for x in half]
     cross, *others = pl.pallas_call(
         cross_kernel,
-        out_shape=[jax.ShapeDtypeStruct((BAND * 4 * nodes, 8 * nodes), jnp.float32)] + [block] * wins,
-        in_specs=[vmem] * 5,
-        out_specs=[vmem] * (1 + wins),
+        out_shape=[jax.ShapeDtypeStruct((BAND * 4 * nodes, 8 * nodes), jnp.float32)] + [block] * (wins // 2),
+        in_specs=[vmem] * (len(operands) + 1),
+        out_specs=[vmem] * (1 + wins // 2),
         compiler_params=pltpu.CompilerParams(vmem_limit_bytes=12 * MIB),
         name="cross_products",
-    )(a, b, halo_a, halo_b, select)
+    )(*operands, select)
     own = pl.pallas_call(
         own_slots_kernel,
-        out_shape=[block] * wins,
+        out_shape=[block] * (wins // 2),
         in_specs=[vmem] * 2,
-        out_specs=[vmem] * wins,
+        out_specs=[vmem] * (wins // 2),
         compiler_params=pltpu.CompilerParams(vmem_limit_bytes=8 * MIB),
         cost_estimate=pl.CostEstimate(flops=1 << 32, bytes_accessed=1 << 24, transcendentals=0),
         name="own_slots",
     )(cross, select)
-    return own, others
+    return [*own, *others]
 
 
 def inverse_kernel(high_ref, low_ref, *refs):
     blocks, (out_ref, both) = refs[:-2], refs[-2:]
-    nodes, slots, _ = blocks[0].shape
+    _, nodes, slots, _ = blocks[0].shape
     rows = nodes * slots
 
     @pl.when(pl.program_id(0) == 0)
@@ -335,7 +354,7 @@
         me, _ = position(len(blocks) // 2)
         for d, block in enumerate(blocks):
             columns = pl.ds(pl.multiple_of((me ^ d) * LANES, LANES), LANES)
-            values = block[...].reshape(rows, LANES)
+            values = block[0].reshape(rows, LANES)
             high = values.astype(jnp.bfloat16)
             both[0:rows, columns] = high
             both[rows : 2 * rows, columns] = (values - high.astype(jnp.float32)).astype(jnp.bfloat16)
@@ -346,14 +365,15 @@
 
 
 def inverse(blocks, high, low):
-    nodes, slots, _ = blocks[0].shape
+    _, nodes, slots, _ = blocks[0].shape
     depth = high.shape[0] * LANES
     width = 256
     table = pl.BlockSpec((depth, width), lambda i: (0, i))
     return pl.pallas_call(
         inverse_kernel,
         grid=(LAGS // width,),
-        in_specs=[table, table] + [pl.BlockSpec(blocks[0].shape, lambda i: (0, 0, 0))] * len(blocks),
+        in_specs=[table, table]
+        + [pl.BlockSpec((1, nodes, slots, LANES), lambda i, j=d % 2: (j, 0, 0, 0)) for d in range(len(blocks))],
         out_specs=pl.BlockSpec((nodes, slots, width), lambda i: (0, 0, i)),
         out_shape=jax.ShapeDtypeStruct((nodes, slots, LAGS), jnp.float32),
         scratch_shapes=[pltpu.VMEM((2 * nodes * slots, depth), jnp.bfloat16)],
@@ -368,18 +388,22 @@
     place = lax.axis_index("pairs")
     win = lax.axis_index("win")
 
-    def exchange(blocks):
-        moved = list(blocks)
-        for d in range(parts - 1, 0, -1):
-            hop = [(i, (((i // wins) ^ (d // wins)) * wins) + ((i % wins) ^ (d % wins))) for i in range(pairs * wins)]
-            moved[d] = lax.ppermute(blocks[d], ("pairs", "win"), hop)
-        return moved
+    def hop(array, d):
+        pairing = [
+            (i, ((i // wins) ^ (d // wins)) * wins + ((i % wins) ^ (d % wins))) for i in range(pairs * wins)
+        ]
+        return lax.ppermute(array, ("pairs", "win"), pairing)
+
+    def between_chips(blocks):
+        return [hop(block, 2 * s) if s else block for s, block in enumerate(blocks)]
+
+    def within_chip(moved):
+        return [x for block in moved for x in (block, hop(block, 1))]
 
     rows, taps = traces.reshape(windows * nodes, samples), taps.reshape(1, TAPS)
     steps = tuple(range(wins))[::-1]
     found = own_spectra(rows, taps, nodes, steps)
     found, neighbours, valid = lax.optimization_barrier((found, neighbours, valid))
-    spectra = [found[2 * steps.index(d // 2) + d % 2] for d in range(parts)]
 
     _, is_first = position(wins)
     tile, member = neighbours // nodes, neighbours % nodes
@@ -399,13 +423,23 @@
     factor = 1.0 / math.sqrt(BINS * windows * wins)
     high, low = make_lag_tables(parts, factor)
 
-    a, b = by_bin(exchange(spectra))
     swap_a = [(i, i ^ 2) for i in range(pairs) if (i ^ 2) < pairs]
     swap_b = [(i, j) for i in range(2, pairs) for j in [((i - 2) ^ 2) + 2] if j < pairs]
-    halo_a = lax.ppermute(a, "pairs", swap_a)
-    halo_b = lax.ppermute(b, "pairs", swap_b)
-    own, others = cross_products(a, b, halo_a, halo_b, select, wins)
-    return inverse(exchange([*own, *others]), high, low)
+    halves, moved = [], []
+
+    def finish(moved):
+        a, b, turned = by_bin(within_chip(moved))
+        halves.append((a, b, turned, lax.ppermute(a, "pairs", swap_a), lax.ppermute(b, "pairs", swap_b)))
+
+    for half in range(HALVES):
+        blocks = [found[half * wins + steps.index(s)] for s in range(wins)]
+        if half:
+            blocks, moved[1] = lax.optimization_barrier((blocks, moved[1]))
+            finish(moved)
+        moved = between_chips(blocks)
+    finish(moved)
+    stack = cross_products(halves, select, wins)
+    return inverse(within_chip(between_chips(stack)), high, low)
 
 
 def solution(mesh):

time: 74.4 us -> 73.7 us (level)
  waiting for transfers between devices: 31.7 us -> 23.5 us
  starting transfers between devices: 16.8 us -> 22.7 us
  Pallas kernels: 23.2 us -> 25.1 us
    ppermute x16 -> x25, waiting for transfers between devices: 30.1 us -> 23.5 us  [the longest x21 16.7 us: hop(): return lax.ppermute(array, ('pairs', 'win'), pairing)]
    ppermute x16 -> x25, starting transfers between devices: 15.2 us -> 21.1 us  [the longest x21 13.6 us: hop(): return lax.ppermute(array, ('pairs', 'win'), pairing)]
    pallas_call x2 -> x3, Pallas kernels: 3.56 us -> 6.25 us  [the longest x2 5.14 us: by_bin(): pl.pallas_call(functools.partial(by_bin_kernel, steps=steps), out_shape=[...]
    ppermute x1, waiting for transfers between devices: 1.62 us -> 0.01 us  [per_device(): other = lax.ppermute(code, 'pairs', [(i, i ^ 1) for i in range(pairs)])]
    pallas_call x1, Pallas kernels: 11.2 us -> 10.4 us  [own_spectra(): pl.pallas_call(functools.partial(spectra_kernel, steps=steps, wins=len(st...]
  transfers between devices with their start and end apart: 17 -> 26, of which waited for: 8 -> 11; matrix products, arithmetic and copies ran while one was open for 1% -> 1% of each run, Pallas kernels for 1% -> 9%
where the time goes in v5:
time: 73.7 us; the launch traced here: 73.2 us
  Pallas kernels  25.1 us (34%)
  waiting for transfers between devices  23.5 us (32%)
  starting transfers between devices  22.7 us (31%)
  local copies, waits for them, and re-layouts  1.18 us (2%)
    ppermute x21, waiting for transfers between devices, hop(): return lax.ppermute(array, ('pairs', 'win'), pairing)  16.7 us
    ppermute x21, starting transfers between devices, hop(): return lax.ppermute(array, ('pairs', 'win'), pairing)  13.6 us
    pallas_call x1, Pallas kernels, own_spectra(): pl.pallas_call(functools.partial(spectra_kernel, steps=steps, wins=len(st...  10.4 us
    ppermute x2, starting transfers between devices, finish(): lax.ppermute(b, 'pairs', swap_b)  5.85 us
    pallas_call x2, Pallas kernels, by_bin(): pl.pallas_call(functools.partial(by_bin_kernel, steps=steps), out_shape=[...  5.14 us
    ppermute x2, waiting for transfers between devices, finish(): lax.ppermute(b, 'pairs', swap_b)  4.87 us
    pallas_call x1, Pallas kernels, inverse(): pl.pallas_call(inverse_kernel, grid=(LAGS // width,), in_specs=[table, ta...  3.94 us
    pallas_call x1, Pallas kernels, cross_products(): pl.pallas_call(cross_kernel, out_shape=[jax.ShapeDtypeStruct((BAND * 4 *...  3.43 us
  transfers between devices with their start and end apart: 26, of which 11 were waited for; matrix products, arithmetic and copies ran while one was open for 1% of the time, Pallas kernels for 9%

profile of v5, /device:TPU:16, one launch (start us, length us, event | category | flops | bytes accessed | tf_op | source)
XLA Modules:
  0.0 73.2 jit_solution(3728364527975964291)
XLA Ops:
  0.0 10.4 %own_spectra.1 = (bf16[2,16,16,128]{3,2,1,0:T(8,128)(2,1)}, bf16[2,16,16,128]{3,2,1,0:T(8,128)(2,1)}, bf16[2,16,16,128]{3,2,1,0:T(8,128)(2,1)}, bf16[2,16,16,128...) custom-call(bf16[512,4096]{1,0:T(8,128)(2,1)} %bitcast.14, ...), custom_call_target="tpu_custom_call" | custom-call | flops 4294967296 | bytes 4194304 | tf_op jit(solution)/shard_map/own_spectra/pallas_call | solution.py:169
  10.4 1.6 %collective-permute-start.1 = (bf16[2,16,16,128]{3,2,1,0:T(8,128)(2,1)}, bf16[2,16,16,128]{3,2,1,0:T(8,128)(2,1)S(1)}, u32[]{:S(2)}, u32[]{:S(2)}) collective-permute-start(bf16[2,16,16,128]{3,2,1,0:T(8,128)(2,1)} %get-tuple-element.56), channel_id=1, source_target_pairs={{0,2},{1,3},{2,0},{3,1},{4,6},{5,7},{6,4},{7,5},{8,10},{9,11},{10,... | collective-permute-start | bytes 393224 | tf_op jit(solution)/shard_map/ppermute | solution.py:395
  12.0 1.6 %collective-permute-start.18 = (s32[16,64]{1,0:T(8,128)S(1)}, s32[16,64]{1,0:T(8,128)S(1)}, u32[]{:S(2)}, u32[]{:S(2)}) collective-permute-start(s32[16,64]{1,0:T(8,128)S(1)} %fusion.3), channel_id=1, source_target_pairs={{0,4},{4,0},{8,12},{12,8},{16,20},{20,16},{24,28},{28,24},{1,5},{5... | collective-permute-start | bytes 12296 | tf_op jit(solution)/shard_map/ppermute | solution.py:414
  13.6 0.5 collective-permute-start.3
  14.1 1.5 %collective-permute-start.5 = (bf16[2,16,16,128]{3,2,1,0:T(8,128)(2,1)}, bf16[2,16,16,128]{3,2,1,0:T(8,128)(2,1)S(1)}, u32[]{:S(2)}, u32[]{:S(2)}) collective-permute-start(bf16[2,16,16,128]{3,2,1,0:T(8,128)(2,1)} %get-tuple-element.59), channel_id=1, source_target_pairs={{0,6},{1,7},{2,4},{3,5},{4,2},{5,3},{6,0},{7,1},{8,14},{9,15},{10,... | collective-permute-start | bytes 393224 | tf_op jit(solution)/shard_map/ppermute | solution.py:395
  15.6 0.0 collective-permute-start
  15.6 0.3 collective-permute-done.1.refs_2_
  15.9 1.5 %collective-permute-start.10 = (bf16[2,16,16,128]{3,2,1,0:T(8,128)(2,1)}, bf16[2,16,16,128]{3,2,1,0:T(8,128)(2,1)S(1)}, u32[]{:S(2)}, u32[]{:S(2)}) collective-permute-start(bf16[2,16,16,128]{3,2,1,0:T(8,128)(2,1)} %get-tuple-element.64), channel_id=1, source_target_pairs={{0,2},{1,3},{2,0},{3,1},{4,6},{5,7},{6,4},{7,5},{8,10},{9,11},{10,... | collective-permute-start | bytes 393224 | tf_op jit(solution)/shard_map/ppermute | solution.py:395
  17.4 0.1 copy.12
  17.5 0.0 collective-permute-done.18
  17.5 0.1 copy.13
  17.6 0.1 add_select_fusion
  17.7 2.7 %collective-permute-start.12 = (bf16[2,16,16,128]{3,2,1,0:T(8,128)(2,1)}, bf16[2,16,16,128]{3,2,1,0:T(8,128)(2,1)S(1)}, u32[]{:S(2)}, u32[]{:S(2)}) collective-permute-start(bf16[2,16,16,128]{3,2,1,0:T(8,128)(2,1)} %get-tuple-element.65), channel_id=1, source_target_pairs={{0,4},{1,5},{2,6},{3,7},{4,0},{5,1},{6,2},{7,3},{8,12},{9,13},{10,... | collective-permute-start | bytes 393224 | tf_op jit(solution)/shard_map/ppermute | solution.py:395
  20.3 1.3 %collective-permute-done.3.refs_4_ = bf16[2,16,16,128]{3,2,1,0:T(8,128)(2,1)S(1)} collective-permute-done((bf16[2,16,16,128]{3,2,1,0:T(8,128)(2,1)}, bf16[2,16,16,128]{3,2,1,0:T(8,128)(2,1)S(1)}, u32[]{:S(2)}, u32[]{:S(2)}) %collective-permute-start.3) | collective-permute-done | bytes 131104 | tf_op jit(solution)/shard_map/ppermute | solution.py:395
  21.6 0.7 collective-permute-start.14
  22.3 0.5 collective-permute-start.4
  22.8 1.5 %collective-permute-done.10.refs_2_ = bf16[2,16,16,128]{3,2,1,0:T(8,128)(2,1)S(1)} collective-permute-done((bf16[2,16,16,128]{3,2,1,0:T(8,128)(2,1)}, bf16[2,16,16,128]{3,2,1,0:T(8,128)(2,1)S(1)}, u32[]{:S(2)}, u32[]{:S(2)}) %collective-permute-start.10) | collective-permute-done | bytes 131104 | tf_op jit(solution)/shard_map/ppermute | solution.py:395
  24.4 1.2 %collective-permute-done.12.refs_4_ = bf16[2,16,16,128]{3,2,1,0:T(8,128)(2,1)S(1)} collective-permute-done((bf16[2,16,16,128]{3,2,1,0:T(8,128)(2,1)}, bf16[2,16,16,128]{3,2,1,0:T(8,128)(2,1)S(1)}, u32[]{:S(2)}, u32[]{:S(2)}) %collective-permute-start.12) | collective-permute-done | bytes 131104 | tf_op jit(solution)/shard_map/ppermute | solution.py:395
  25.5 2.2 %collective-permute-done.14.refs_6_ = bf16[2,16,16,128]{3,2,1,0:T(8,128)(2,1)S(1)} collective-permute-done((bf16[2,16,16,128]{3,2,1,0:T(8,128)(2,1)}, bf16[2,16,16,128]{3,2,1,0:T(8,128)(2,1)S(1)}, u32[]{:S(2)}, u32[]{:S(2)}) %collective-permute-start.14) | collective-permute-done | bytes 131104 | tf_op jit(solution)/shard_map/ppermute | solution.py:395
  27.7 0.5 collective-permute-start.13
  28.2 0.1 collective-permute-start.15
  28.3 0.9 %copy-done.5 = bf16[2,16,16,128]{3,2,1,0:T(8,128)(2,1)S(1)} copy-done((bf16[2,16,16,128]{3,2,1,0:T(8,128)(2,1)S(1)}, bf16[2,16,16,128]{3,2,1,0:T(8,128)(2,1)}, u32[]{:S(2)}) %copy-start.5) | copy-done | bytes 131096
  29.2 2.5 %by_bin.2 = (bf16[64,16,128]{2,1,0:T(8,128)(2,1)S(1)}, bf16[64,16,128]{2,1,0:T(8,128)(2,1)S(1)}, bf16[64,32,128]{2,1,0:T(8,128)(2,1)S(1)}) custom-call(bf16[2,16,16,128]{3,2,1,0:T(8,128)(2,1)S(1)} %copy-done.5, bf16[2,16,16,128]{3,2,1,0:T(8,128)(2,1)S(1)} %collective-permute-done.refs_1_, bf16[2,16,16,128]{3,2,1,0:T(8,128)(2,1)S(1)} %collective-permute-done.1.refs_2_, ...), custom_call_target="tpu_custom_call" | custom-call | flops 2147483648 | bytes 4194304 | tf_op jit(solution)/shard_map/by_bin/pallas_call | solution.py:260
  31.7 1.6 %collective-permute-start.7 = (bf16[64,16,128]{2,1,0:T(8,128)(2,1)S(1)}, bf16[64,16,128]{2,1,0:T(8,128)(2,1)S(1)}, u32[]{:S(2)}, u32[]{:S(2)}) collective-permute-start(bf16[64,16,128]{2,1,0:T(8,128)(2,1)S(1)} %get-tuple-element.60.refs_0_), channel_id=1, source_target_pairs={{0,8},{4,12},{8,0},{12,4},{16,24},{20,28},{24,16},{28,20},{1,9},{5... | collective-permute-start | bytes 786440 | tf_op jit(solution)/shard_map/ppermute | solution.py:432
  33.4 1.9 %collective-permute-start.8 = (bf16[64,16,128]{2,1,0:T(8,128)(2,1)S(1)}, bf16[64,16,128]{2,1,0:T(8,128)(2,1)S(1)}, u32[]{:S(2)}, u32[]{:S(2)}) collective-permute-start(bf16[64,16,128]{2,1,0:T(8,128)(2,1)S(1)} %get-tuple-element.61.refs_1_), channel_id=1, source_target_pairs={{8,16},{12,20},{16,8},{20,12},{9,17},{13,21},{17,9},{21,13},{10,18... | collective-permute-start | bytes 786440 | tf_op jit(solution)/shard_map/ppermute | solution.py:432
  35.3 2.6 %by_bin.3 = (bf16[64,16,128]{2,1,0:T(8,128)(2,1)S(1)}, bf16[64,16,128]{2,1,0:T(8,128)(2,1)S(1)}, bf16[64,32,128]{2,1,0:T(8,128)(2,1)S(1)}) custom-call(bf16[2,16,16,128]{3,2,1,0:T(8,128)(2,1)S(1)} %copy-done.4, bf16[2,16,16,128]{3,2,1,0:T(8,128)(2,1)S(1)} %collective-permute-done.9.refs_1_, bf16[2,16,16,128]{3,2,1,0:T(8,128)(2,1)S(1)} %collective-permute-done.10.refs_2_, ...), custom_call_target="tpu_custom_call" | custom-call | flops 2147483648 | bytes 4194304 | tf_op jit(solution)/shard_map/by_bin/pallas_call | solution.py:260
  38.0 0.1 collective-permute-start.16
  38.0 3.9 %collective-permute-start.17 = (bf16[64,16,128]{2,1,0:T(8,128)(2,1)S(1)}, bf16[64,16,128]{2,1,0:T(8,128)(2,1)S(1)}, u32[]{:S(2)}, u32[]{:S(2)}) collective-permute-start(bf16[64,16,128]{2,1,0:T(8,128)(2,1)S(1)} %get-tuple-element.68.refs_6_), channel_id=1, source_target_pairs={{8,16},{12,20},{16,8},{20,12},{9,17},{13,21},{17,9},{21,13},{10,18... | collective-permute-start | bytes 786440 | tf_op jit(solution)/shard_map/ppermute | solution.py:432
  42.0 0.1 copy.14
  42.1 0.3 compare_convert_fusion.refs_10_.select_ref
  42.4 2.0 %collective-permute-done.8.refs_4_ = bf16[64,16,128]{2,1,0:T(8,128)(2,1)S(1)} collective-permute-done((bf16[64,16,128]{2,1,0:T(8,128)(2,1)S(1)}, bf16[64,16,128]{2,1,0:T(8,128)(2,1)S(1)}, u32[]{:S(2)}, u32[]{:S(2)}) %collective-permute-start.8) | collective-permute-done | bytes 262176 | tf_op jit(solution)/shard_map/ppermute | solution.py:432
  44.4 2.0 %collective-permute-done.16.refs_8_ = bf16[64,16,128]{2,1,0:T(8,128)(2,1)S(1)} collective-permute-done((bf16[64,16,128]{2,1,0:T(8,128)(2,1)S(1)}, bf16[64,16,128]{2,1,0:T(8,128)(2,1)S(1)}, u32[]{:S(2)}, u32[]{:S(2)}) %collective-permute-start.16) | collective-permute-done | bytes 262176 | tf_op jit(solution)/shard_map/ppermute | solution.py:432
  46.4 2.9 %collective-permute-done.17.refs_9_ = bf16[64,16,128]{2,1,0:T(8,128)(2,1)S(1)} collective-permute-done((bf16[64,16,128]{2,1,0:T(8,128)(2,1)S(1)}, bf16[64,16,128]{2,1,0:T(8,128)(2,1)S(1)}, u32[]{:S(2)}, u32[]{:S(2)}) %collective-permute-start.17) | collective-permute-done | bytes 262176 | tf_op jit(solution)/shard_map/ppermute | solution.py:432
  49.3 3.4 %cross_products.1 = (f32[4096,128]{1,0:T(8,128)S(1)}, f32[2,16,16,128]{3,2,1,0:T(8,128)S(1)}, f32[2,16,16,128]{3,2,1,0:T(8,128)S(1)}) custom-call(bf16[64,16,128]{2,1,0:T(8,128)(2,1)S(1)} %get-tuple-element.60.refs_0_, bf16[64,16,128]{2,1,0:T(8,128)(2,1)S(1)} %get-tuple-element.61.refs_1_, bf16[64,32,128]{2,1,0:T(8,128)(2,1)S(1)} %get-tuple-element.62.refs_2_, ...), custom_call_target="tpu_custom_call" | custom-call | tf_op jit(solution)/shard_map/cross_products/pallas_call | solution.py:327
  52.7 0.0 copy-start
  52.7 0.0 copy-start.1
  52.7 0.0 copy-start.2
  52.7 0.0 copy-start.3
  52.8 1.1 %own_slots.1 = (f32[2,16,16,128]{3,2,1,0:T(8,128)S(1)}, f32[2,16,16,128]{3,2,1,0:T(8,128)S(1)}) custom-call(f32[4096,128]{1,0:T(8,128)S(1)} %get-tuple-element.72.cross_ref, bf16[32,64,128]{2,1,0:T(8,128)(2,1)S(1)} %compare_convert_fusion.refs_10_.select_ref), custom_call_target="tpu_custom_call" | custom-call | flops 4294967296 | bytes 16777216 | tf_op jit(solution)/shard_map/own_slots/pallas_call | solution.py:335
  53.9 0.6 collective-permute-start.20
  54.5 0.7 collective-permute-start.22
  55.2 2.2 %collective-permute-start.24 = (f32[2,16,16,128]{3,2,1,0:T(8,128)S(1)}, f32[2,16,16,128]{3,2,1,0:T(8,128)S(1)}, u32[]{:S(2)}, u32[]{:S(2)}) collective-permute-start(f32[2,16,16,128]{3,2,1,0:T(8,128)S(1)} %get-tuple-element.76), channel_id=1, source_target_pairs={{0,6},{1,7},{2,4},{3,5},{4,2},{5,3},{6,0},{7,1},{8,14},{9,15},{10,... | collective-permute-start | bytes 786440 | tf_op jit(solution)/shard_map/ppermute | solution.py:395
  57.4 5.8 %collective-permute-done.20.refs_2_ = f32[2,16,16,128]{3,2,1,0:T(8,128)S(1)} collective-permute-done((f32[2,16,16,128]{3,2,1,0:T(8,128)S(1)}, f32[2,16,16,128]{3,2,1,0:T(8,128)S(1)}, u32[]{:S(2)}, u32[]{:S(2)}) %collective-permute-start.20) | collective-permute-done | bytes 262176 | tf_op jit(solution)/shard_map/ppermute | solution.py:395
  63.2 4.2 %collective-permute-done.22.refs_4_ = f32[2,16,16,128]{3,2,1,0:T(8,128)S(1)} collective-permute-done((f32[2,16,16,128]{3,2,1,0:T(8,128)S(1)}, f32[2,16,16,128]{3,2,1,0:T(8,128)S(1)}, u32[]{:S(2)}, u32[]{:S(2)}) %collective-permute-start.22) | collective-permute-done | bytes 262176 | tf_op jit(solution)/shard_map/ppermute | solution.py:395
  67.3 0.5 collective-permute-start.25
  67.9 1.1 %lag_tables.1 = (bf16[8,128,1024]{2,1,0:T(8,128)(2,1)S(1)}, bf16[8,128,1024]{2,1,0:T(8,128)(2,1)S(1)}) custom-call(f32[64,1024]{1,0:T(8,128)S(1)} %copy-done.1, f32[64,1024]{1,0:T(8,128)S(1)} %copy-done, f32[8,1024]{1,0:T(8,128)S(1)} %copy-done.3, f32[8,1024]{1,0:T(8,128)S(1)} %copy-done.2), custom_call_target="tpu_custom_call" | custom-call | tf_op jit(solution)/shard_map/lag_tables/pallas_call | solution.py:205
  69.0 0.2 collective-permute-done.25.refs_7_
  69.3 3.9 %inverse.1 = f32[16,16,1024]{2,1,0:T(8,128)} custom-call(bf16[1024,1024]{1,0:T(8,128)(2,1)S(1)} %bitcast.8, bf16[1024,1024]{1,0:T(8,128)(2,1)S(1)} %bitcast.9, f32[2,16,16,128]{3,2,1,0:T(8,128)S(1)} %get-tuple-element.73.refs_0_, f32[2,16,16,128]{3,2,1,0:T(8,128)S(1)} %collective-permute-done.19.refs_1_, ...), custom_call_target="tpu_custom_call" | custom-call | tf_op jit(solution)/shard_map/inverse/pallas_call | solution.py:372
  (36 shorter events, 0.1 us)
Async XLA Ops:
  0.0 11.9 %copy-start.6 = (s32[16,64]{1,0:T(8,128)S(1)}, s32[16,64]{1,0:T(8,128)}, u32[]{:S(2)}) copy-start(s32[16,64]{1,0:T(8,128)} %param.13) | copy-start | bytes 12292
  0.0 11.9 %copy-start.7 = (s32[16,64]{1,0:T(8,128)S(1)}, s32[16,64]{1,0:T(8,128)}, u32[]{:S(2)}) copy-start(s32[16,64]{1,0:T(8,128)} %param.14) | copy-start | bytes 12292
  10.4 5.5 %collective-permute-start.1 = (bf16[2,16,16,128]{3,2,1,0:T(8,128)(2,1)}, bf16[2,16,16,128]{3,2,1,0:T(8,128)(2,1)S(1)}, u32[]{:S(2)}, u32[]{:S(2)}) collective-permute-start(bf16[2,16,16,128]{3,2,1,0:T(8,128)(2,1)} %get-tuple-element.56), channel_id=1, source_target_pairs={{0,2},{1,3},{2,0},{3,1},{4,6},{5,7},{6,4},{7,5},{8,10},{9,11},{10,... | collective-permute-start | bytes 393224 | tf_op jit(solution)/shard_map/ppermute | solution.py:395
  12.0 5.5 %collective-permute-start.18 = (s32[16,64]{1,0:T(8,128)S(1)}, s32[16,64]{1,0:T(8,128)S(1)}, u32[]{:S(2)}, u32[]{:S(2)}) collective-permute-start(s32[16,64]{1,0:T(8,128)S(1)} %fusion.3), channel_id=1, source_target_pairs={{0,4},{4,0},{8,12},{12,8},{16,20},{20,16},{24,28},{28,24},{1,5},{5... | collective-permute-start | bytes 12296 | tf_op jit(solution)/shard_map/ppermute | solution.py:414
  13.6 8.0 %collective-permute-start.3 = (bf16[2,16,16,128]{3,2,1,0:T(8,128)(2,1)}, bf16[2,16,16,128]{3,2,1,0:T(8,128)(2,1)S(1)}, u32[]{:S(2)}, u32[]{:S(2)}) collective-permute-start(bf16[2,16,16,128]{3,2,1,0:T(8,128)(2,1)} %get-tuple-element.58), channel_id=1, source_target_pairs={{0,4},{1,5},{2,6},{3,7},{4,0},{5,1},{6,2},{7,3},{8,12},{9,13},{10,... | collective-permute-start | bytes 393224 | tf_op jit(solution)/shard_map/ppermute | solution.py:395
  14.1 8.2 %collective-permute-start.5 = (bf16[2,16,16,128]{3,2,1,0:T(8,128)(2,1)}, bf16[2,16,16,128]{3,2,1,0:T(8,128)(2,1)S(1)}, u32[]{:S(2)}, u32[]{:S(2)}) collective-permute-start(bf16[2,16,16,128]{3,2,1,0:T(8,128)(2,1)} %get-tuple-element.59), channel_id=1, source_target_pairs={{0,6},{1,7},{2,4},{3,5},{4,2},{5,3},{6,0},{7,1},{8,14},{9,15},{10,... | collective-permute-start | bytes 393224 | tf_op jit(solution)/shard_map/ppermute | solution.py:395
  15.6 6.7 %collective-permute-start = (bf16[2,16,16,128]{3,2,1,0:T(8,128)(2,1)}, bf16[2,16,16,128]{3,2,1,0:T(8,128)(2,1)S(1)}, u32[]{:S(2)}, u32[]{:S(2)}) collective-permute-start(bf16[2,16,16,128]{3,2,1,0:T(8,128)(2,1)} %get-tuple-element.51.refs_0_), channel_id=1, source_target_pairs={{0,1},{1,0},{2,3},{3,2},{4,5},{5,4},{6,7},{7,6},{8,9},{9,8},{10,11... | collective-permute-start | bytes 393224 | tf_op jit(solution)/shard_map/ppermute | solution.py:395
  15.9 8.4 %collective-permute-start.10 = (bf16[2,16,16,128]{3,2,1,0:T(8,128)(2,1)}, bf16[2,16,16,128]{3,2,1,0:T(8,128)(2,1)S(1)}, u32[]{:S(2)}, u32[]{:S(2)}) collective-permute-start(bf16[2,16,16,128]{3,2,1,0:T(8,128)(2,1)} %get-tuple-element.64), channel_id=1, source_target_pairs={{0,2},{1,3},{2,0},{3,1},{4,6},{5,7},{6,4},{7,5},{8,10},{9,11},{10,... | collective-permute-start | bytes 393224 | tf_op jit(solution)/shard_map/ppermute | solution.py:395
  17.7 7.9 %collective-permute-start.12 = (bf16[2,16,16,128]{3,2,1,0:T(8,128)(2,1)}, bf16[2,16,16,128]{3,2,1,0:T(8,128)(2,1)S(1)}, u32[]{:S(2)}, u32[]{:S(2)}) collective-permute-start(bf16[2,16,16,128]{3,2,1,0:T(8,128)(2,1)} %get-tuple-element.65), channel_id=1, source_target_pairs={{0,4},{1,5},{2,6},{3,7},{4,0},{5,1},{6,2},{7,3},{8,12},{9,13},{10,... | collective-permute-start | bytes 393224 | tf_op jit(solution)/shard_map/ppermute | solution.py:395
  21.6 6.1 %collective-permute-start.14 = (bf16[2,16,16,128]{3,2,1,0:T(8,128)(2,1)}, bf16[2,16,16,128]{3,2,1,0:T(8,128)(2,1)S(1)}, u32[]{:S(2)}, u32[]{:S(2)}) collective-permute-start(bf16[2,16,16,128]{3,2,1,0:T(8,128)(2,1)} %get-tuple-element.66), channel_id=1, source_target_pairs={{0,6},{1,7},{2,4},{3,5},{4,2},{5,3},{6,0},{7,1},{8,14},{9,15},{10,... | collective-permute-start | bytes 393224 | tf_op jit(solution)/shard_map/ppermute | solution.py:395
  22.3 5.4 %collective-permute-start.2 = (bf16[2,16,16,128]{3,2,1,0:T(8,128)(2,1)S(1)}, bf16[2,16,16,128]{3,2,1,0:T(8,128)(2,1)S(1)}, u32[]{:S(2)}, u32[]{:S(2)}) collective-permute-start(bf16[2,16,16,128]{3,2,1,0:T(8,128)(2,1)S(1)} %collective-permute-done.1.refs_2_), channel_id=1, source_target_pairs={{0,1},{1,0},{2,3},{3,2},{4,5},{5,4},{6,7},{7,6},{8,9},{9,8},{10,11... | collective-permute-start | bytes 393224 | tf_op jit(solution)/shard_map/ppermute | solution.py:395
  22.3 5.9 %collective-permute-start.4 = (bf16[2,16,16,128]{3,2,1,0:T(8,128)(2,1)S(1)}, bf16[2,16,16,128]{3,2,1,0:T(8,128)(2,1)S(1)}, u32[]{:S(2)}, u32[]{:S(2)}) collective-permute-start(bf16[2,16,16,128]{3,2,1,0:T(8,128)(2,1)S(1)} %collective-permute-done.3.refs_4_), channel_id=1, source_target_pairs={{0,1},{1,0},{2,3},{3,2},{4,5},{5,4},{6,7},{7,6},{8,9},{9,8},{10,11... | collective-permute-start | bytes 393224 | tf_op jit(solution)/shard_map/ppermute | solution.py:395
  24.3 3.9 %collective-permute-start.6 = (bf16[2,16,16,128]{3,2,1,0:T(8,128)(2,1)S(1)}, bf16[2,16,16,128]{3,2,1,0:T(8,128)(2,1)S(1)}, u32[]{:S(2)}, u32[]{:S(2)}) collective-permute-start(bf16[2,16,16,128]{3,2,1,0:T(8,128)(2,1)S(1)} %collective-permute-done.5.refs_6_), channel_id=1, source_target_pairs={{0,1},{1,0},{2,3},{3,2},{4,5},{5,4},{6,7},{7,6},{8,9},{9,8},{10,11... | collective-permute-start | bytes 393224 | tf_op jit(solution)/shard_map/ppermute | solution.py:395
  24.3 11.0 %copy-start.4 = (bf16[2,16,16,128]{3,2,1,0:T(8,128)(2,1)S(1)}, bf16[2,16,16,128]{3,2,1,0:T(8,128)(2,1)}, u32[]{:S(2)}) copy-start(bf16[2,16,16,128]{3,2,1,0:T(8,128)(2,1)} %get-tuple-element.63.refs_0_) | copy-start | bytes 393220
  25.5 7.9 %collective-permute-start.9 = (bf16[2,16,16,128]{3,2,1,0:T(8,128)(2,1)}, bf16[2,16,16,128]{3,2,1,0:T(8,128)(2,1)S(1)}, u32[]{:S(2)}, u32[]{:S(2)}) collective-permute-start(bf16[2,16,16,128]{3,2,1,0:T(8,128)(2,1)} %get-tuple-element.63.refs_0_), channel_id=1, source_target_pairs={{0,1},{1,0},{2,3},{3,2},{4,5},{5,4},{6,7},{7,6},{8,9},{9,8},{10,11... | collective-permute-start | bytes 393224 | tf_op jit(solution)/shard_map/ppermute | solution.py:395
  27.7 7.6 %collective-permute-start.11 = (bf16[2,16,16,128]{3,2,1,0:T(8,128)(2,1)S(1)}, bf16[2,16,16,128]{3,2,1,0:T(8,128)(2,1)S(1)}, u32[]{:S(2)}, u32[]{:S(2)}) collective-permute-start(bf16[2,16,16,128]{3,2,1,0:T(8,128)(2,1)S(1)} %collective-permute-done.10.refs_2_), channel_id=1, source_target_pairs={{0,1},{1,0},{2,3},{3,2},{4,5},{5,4},{6,7},{7,6},{8,9},{9,8},{10,11... | collective-permute-start | bytes 393224 | tf_op jit(solution)/shard_map/ppermute | solution.py:395
  27.7 7.6 %collective-permute-start.13 = (bf16[2,16,16,128]{3,2,1,0:T(8,128)(2,1)S(1)}, bf16[2,16,16,128]{3,2,1,0:T(8,128)(2,1)S(1)}, u32[]{:S(2)}, u32[]{:S(2)}) collective-permute-start(bf16[2,16,16,128]{3,2,1,0:T(8,128)(2,1)S(1)} %collective-permute-done.12.refs_4_), channel_id=1, source_target_pairs={{0,1},{1,0},{2,3},{3,2},{4,5},{5,4},{6,7},{7,6},{8,9},{9,8},{10,11... | collective-permute-start | bytes 393224 | tf_op jit(solution)/shard_map/ppermute | solution.py:395
  28.2 7.1 %collective-permute-start.15 = (bf16[2,16,16,128]{3,2,1,0:T(8,128)(2,1)S(1)}, bf16[2,16,16,128]{3,2,1,0:T(8,128)(2,1)S(1)}, u32[]{:S(2)}, u32[]{:S(2)}) collective-permute-start(bf16[2,16,16,128]{3,2,1,0:T(8,128)(2,1)S(1)} %collective-permute-done.14.refs_6_), channel_id=1, source_target_pairs={{0,1},{1,0},{2,3},{3,2},{4,5},{5,4},{6,7},{7,6},{8,9},{9,8},{10,11... | collective-permute-start | bytes 393224 | tf_op jit(solution)/shard_map/ppermute | solution.py:395
  28.3 0.9 %copy-start.5 = (bf16[2,16,16,128]{3,2,1,0:T(8,128)(2,1)S(1)}, bf16[2,16,16,128]{3,2,1,0:T(8,128)(2,1)}, u32[]{:S(2)}) copy-start(bf16[2,16,16,128]{3,2,1,0:T(8,128)(2,1)} %get-tuple-element.51.refs_0_) | copy-start | bytes 393220
  31.7 10.7 %collective-permute-start.7 = (bf16[64,16,128]{2,1,0:T(8,128)(2,1)S(1)}, bf16[64,16,128]{2,1,0:T(8,128)(2,1)S(1)}, u32[]{:S(2)}, u32[]{:S(2)}) collective-permute-start(bf16[64,16,128]{2,1,0:T(8,128)(2,1)S(1)} %get-tuple-element.60.refs_0_), channel_id=1, source_target_pairs={{0,8},{4,12},{8,0},{12,4},{16,24},{20,28},{24,16},{28,20},{1,9},{5... | collective-permute-start | bytes 786440 | tf_op jit(solution)/shard_map/ppermute | solution.py:432
  33.4 11.0 %collective-permute-start.8 = (bf16[64,16,128]{2,1,0:T(8,128)(2,1)S(1)}, bf16[64,16,128]{2,1,0:T(8,128)(2,1)S(1)}, u32[]{:S(2)}, u32[]{:S(2)}) collective-permute-start(bf16[64,16,128]{2,1,0:T(8,128)(2,1)S(1)} %get-tuple-element.61.refs_1_), channel_id=1, source_target_pairs={{8,16},{12,20},{16,8},{20,12},{9,17},{13,21},{17,9},{21,13},{10,18... | collective-permute-start | bytes 786440 | tf_op jit(solution)/shard_map/ppermute | solution.py:432
  38.0 8.4 %collective-permute-start.16 = (bf16[64,16,128]{2,1,0:T(8,128)(2,1)S(1)}, bf16[64,16,128]{2,1,0:T(8,128)(2,1)S(1)}, u32[]{:S(2)}, u32[]{:S(2)}) collective-permute-start(bf16[64,16,128]{2,1,0:T(8,128)(2,1)S(1)} %get-tuple-element.67.refs_5_), channel_id=1, source_target_pairs={{0,8},{4,12},{8,0},{12,4},{16,24},{20,28},{24,16},{28,20},{1,9},{5... | collective-permute-start | bytes 786440 | tf_op jit(solution)/shard_map/ppermute | solution.py:432
  38.0 11.2 %collective-permute-start.17 = (bf16[64,16,128]{2,1,0:T(8,128)(2,1)S(1)}, bf16[64,16,128]{2,1,0:T(8,128)(2,1)S(1)}, u32[]{:S(2)}, u32[]{:S(2)}) collective-permute-start(bf16[64,16,128]{2,1,0:T(8,128)(2,1)S(1)} %get-tuple-element.68.refs_6_), channel_id=1, source_target_pairs={{8,16},{12,20},{16,8},{20,12},{9,17},{13,21},{17,9},{21,13},{10,18... | collective-permute-start | bytes 786440 | tf_op jit(solution)/shard_map/ppermute | solution.py:432
  52.7 15.2 %copy-start = (f32[64,1024]{1,0:T(8,128)S(1)}, f32[64,1024]{1,0:T(8,128)}, u32[]{:S(2)}) copy-start(f32[64,1024]{1,0:T(8,128)} %constant.120.clone.msin_ref) | copy-start | bytes 786436
  52.7 15.1 %copy-start.1 = (f32[64,1024]{1,0:T(8,128)S(1)}, f32[64,1024]{1,0:T(8,128)}, u32[]{:S(2)}) copy-start(f32[64,1024]{1,0:T(8,128)} %constant.119.clone.cos_ref) | copy-start | bytes 786436
  52.7 15.1 %copy-start.2 = (f32[8,1024]{1,0:T(8,128)S(1)}, f32[8,1024]{1,0:T(8,128)}, u32[]{:S(2)}) copy-start(f32[8,1024]{1,0:T(8,128)} %constant.122.clone.msin0_ref) | copy-start | bytes 98308
  52.7 15.1 %copy-start.3 = (f32[8,1024]{1,0:T(8,128)S(1)}, f32[8,1024]{1,0:T(8,128)}, u32[]{:S(2)}) copy-start(f32[8,1024]{1,0:T(8,128)} %constant.121.clone.cos0_ref) | copy-start | bytes 98308
  53.9 9.3 %collective-permute-start.20 = (f32[2,16,16,128]{3,2,1,0:T(8,128)S(1)}, f32[2,16,16,128]{3,2,1,0:T(8,128)S(1)}, u32[]{:S(2)}, u32[]{:S(2)}) collective-permute-start(f32[2,16,16,128]{3,2,1,0:T(8,128)S(1)} %get-tuple-element.74), channel_id=1, source_target_pairs={{0,2},{1,3},{2,0},{3,1},{4,6},{5,7},{6,4},{7,5},{8,10},{9,11},{10,... | collective-permute-start | bytes 786440 | tf_op jit(solution)/shard_map/ppermute | solution.py:395
  54.5 12.9 %collective-permute-start.22 = (f32[2,16,16,128]{3,2,1,0:T(8,128)S(1)}, f32[2,16,16,128]{3,2,1,0:T(8,128)S(1)}, u32[]{:S(2)}, u32[]{:S(2)}) collective-permute-start(f32[2,16,16,128]{3,2,1,0:T(8,128)S(1)} %get-tuple-element.75), channel_id=1, source_target_pairs={{0,4},{1,5},{2,6},{3,7},{4,0},{5,1},{6,2},{7,3},{8,12},{9,13},{10,... | collective-permute-start | bytes 786440 | tf_op jit(solution)/shard_map/ppermute | solution.py:395
  55.2 12.2 %collective-permute-start.24 = (f32[2,16,16,128]{3,2,1,0:T(8,128)S(1)}, f32[2,16,16,128]{3,2,1,0:T(8,128)S(1)}, u32[]{:S(2)}, u32[]{:S(2)}) collective-permute-start(f32[2,16,16,128]{3,2,1,0:T(8,128)S(1)} %get-tuple-element.76), channel_id=1, source_target_pairs={{0,6},{1,7},{2,4},{3,5},{4,2},{5,3},{6,0},{7,1},{8,14},{9,15},{10,... | collective-permute-start | bytes 786440 | tf_op jit(solution)/shard_map/ppermute | solution.py:395
  57.4 11.6 %collective-permute-start.19 = (f32[2,16,16,128]{3,2,1,0:T(8,128)S(1)}, f32[2,16,16,128]{3,2,1,0:T(8,128)S(1)}, u32[]{:S(2)}, u32[]{:S(2)}) collective-permute-start(f32[2,16,16,128]{3,2,1,0:T(8,128)S(1)} %get-tuple-element.73.refs_0_), channel_id=1, source_target_pairs={{0,1},{1,0},{2,3},{3,2},{4,5},{5,4},{6,7},{7,6},{8,9},{9,8},{10,11... | collective-permute-start | bytes 786440 | tf_op jit(solution)/shard_map/ppermute | solution.py:395
  63.2 5.8 %collective-permute-start.21 = (f32[2,16,16,128]{3,2,1,0:T(8,128)S(1)}, f32[2,16,16,128]{3,2,1,0:T(8,128)S(1)}, u32[]{:S(2)}, u32[]{:S(2)}) collective-permute-start(f32[2,16,16,128]{3,2,1,0:T(8,128)S(1)} %collective-permute-done.20.refs_2_), channel_id=1, source_target_pairs={{0,1},{1,0},{2,3},{3,2},{4,5},{5,4},{6,7},{7,6},{8,9},{9,8},{10,11... | collective-permute-start | bytes 786440 | tf_op jit(solution)/shard_map/ppermute | solution.py:395
  67.3 1.7 %collective-permute-start.23 = (f32[2,16,16,128]{3,2,1,0:T(8,128)S(1)}, f32[2,16,16,128]{3,2,1,0:T(8,128)S(1)}, u32[]{:S(2)}, u32[]{:S(2)}) collective-permute-start(f32[2,16,16,128]{3,2,1,0:T(8,128)S(1)} %collective-permute-done.22.refs_4_), channel_id=1, source_target_pairs={{0,1},{1,0},{2,3},{3,2},{4,5},{5,4},{6,7},{7,6},{8,9},{9,8},{10,11... | collective-permute-start | bytes 786440 | tf_op jit(solution)/shard_map/ppermute | solution.py:395
  67.3 1.9 %collective-permute-start.25 = (f32[2,16,16,128]{3,2,1,0:T(8,128)S(1)}, f32[2,16,16,128]{3,2,1,0:T(8,128)S(1)}, u32[]{:S(2)}, u32[]{:S(2)}) collective-permute-start(f32[2,16,16,128]{3,2,1,0:T(8,128)S(1)} %collective-permute-done.24.refs_6_), channel_id=1, source_target_pairs={{0,1},{1,0},{2,3},{3,2},{4,5},{5,4},{6,7},{7,6},{8,9},{9,8},{10,11... | collective-permute-start | bytes 786440 | tf_op jit(solution)/shard_map/ppermute | solution.py:395

commit v6 on v5

--- a/solution.py
+++ b/solution.py
@@ -59,11 +59,11 @@
 
 
 def spectra_kernel(x_hbm, taps_ref, fine_hbm, turn_c_hbm, turn_s_hbm, *refs, steps, wins):
-    outs, refs = refs[: HALVES * len(steps)], refs[HALVES * len(steps) :]
+    outs, refs = refs[: len(steps)], refs[len(steps) :]
     x_ref, fine_ref, turn_c_ref, turn_s_ref, *refs, sems = refs
     tables, totals, stages = refs[0:2], refs[2:4], refs[4:6]
     count = x_ref.shape[0]
-    nodes, windows = outs[0].shape[1], outs[0].shape[2]
+    nodes, windows = outs[0].shape[0], outs[0].shape[1]
     width = 2 * LANES
     pieces = SAMPLES // CHUNK
     me, _ = position(wins)
@@ -83,34 +83,30 @@
         copy.start()
 
     def columns_of(i):
-        return pl.ds(pl.multiple_of(((me // 2) ^ steps[i]) * width, width), width)
+        return [pl.ds(pl.multiple_of((me ^ (2 * step)) * LANES, LANES), LANES) for step in steps[2 * i : 2 * i + 2]]
 
     def generate(i):
-        columns = columns_of(i)
-        base = fine_ref[0:STEP, columns]
-        swapped = jnp.concatenate(
-            [pltpu.roll(base[:, c : c + LANES], BAND, 1) for c in range(0, width, LANES)], 1
-        )
-        for j in range(SAMPLES // STEP):
-            row = pl.ds(j, 1)
-            turned = base * turn_c_ref[row, columns] + swapped * turn_s_ref[row, columns]
-            tables[i % 2][j * STEP : (j + 1) * STEP, :] = turned.astype(jnp.bfloat16)
+        for c, columns in enumerate(columns_of(i)):
+            base = fine_ref[0:STEP, columns]
+            swapped = pltpu.roll(base, BAND, 1)
+            for j in range(SAMPLES // STEP):
+                row = pl.ds(j, 1)
+                turned = base * turn_c_ref[row, columns] + swapped * turn_s_ref[row, columns]
+                tables[i % 2][j * STEP : (j + 1) * STEP, c * LANES : (c + 1) * LANES] = turned.astype(jnp.bfloat16)
 
     low = lax.broadcasted_iota(jnp.int32, (1, LANES), 1) < BAND
     responses = {}
 
     def respond(i):
-        columns = columns_of(i)
-        response = jnp.dot(
-            taps_ref[:, 0:128],
-            fine_ref[0:128, columns],
-            precision=lax.Precision.HIGHEST,
-            preferred_element_type=jnp.float32,
-        )
-        response = response + taps_ref[:, 128:129] * fine_ref[128:129, columns]
         responses[i] = []
-        for c in range(2):
-            here = response[:, c * LANES : (c + 1) * LANES]
+        for columns in columns_of(i):
+            here = jnp.dot(
+                taps_ref[:, 0:128],
+                fine_ref[0:128, columns],
+                precision=lax.Precision.HIGHEST,
+                preferred_element_type=jnp.float32,
+            )
+            here = here + taps_ref[:, 128:129] * fine_ref[128:129, columns]
             other = pltpu.roll(jnp.broadcast_to(here, (8, LANES)), BAND, 1)[0:1, :]
             responses[i].append((jnp.where(low, here, other), jnp.where(low, -other, here)))
 
@@ -127,23 +123,21 @@
         white = raw * lax.rsqrt((sums[0:count, :] + sums[count:, :]) * (1.0 / BAND) + EPSILON)
         for c, (same, cross) in enumerate(responses[i]):
             part = white[:, c * LANES : (c + 1) * LANES]
-            stages[i % 2][c ^ (me % 2)] = part * same + pltpu.roll(part, BAND, 1) * cross
+            stages[i % 2][c] = part * same + pltpu.roll(part, BAND, 1) * cross
 
     def give(i):
-        for half in range(HALVES):
-            first = half * windows * nodes
-            for c in range(2):
-                for node in range(nodes):
-                    values = stages[i % 2][c, pl.ds(first + node, windows, stride=nodes), :]
-                    outs[half * len(steps) + i][c, node] = values.astype(jnp.bfloat16)
+        for c in range(2):
+            for node in range(nodes):
+                values = stages[i % 2][c, pl.ds(node, windows, stride=nodes), :]
+                outs[2 * i + c][node] = values.astype(jnp.bfloat16)
 
     for copy in copies:
         copy.wait()
     generate(0)
-    last = len(steps) - 1
+    last = len(steps) // 2 - 1
     for copy in chunks:
         copy.wait()
-    for i in range(len(steps)):
+    for i in range(len(steps) // 2):
         respond(i)
         product = jnp.dot(x_ref[...], tables[i % 2][...], preferred_element_type=jnp.float32)
         for c in range(2):
@@ -165,12 +159,12 @@
     count = rows.shape[0]
     hbm = pl.BlockSpec(memory_space=pltpu.HBM)
     vmem = pl.BlockSpec(memory_space=pltpu.VMEM)
-    shape = jax.ShapeDtypeStruct((2, nodes, count // nodes // HALVES, LANES), jnp.bfloat16)
+    shape = jax.ShapeDtypeStruct((nodes, count // nodes, LANES), jnp.bfloat16)
     return pl.pallas_call(
         functools.partial(spectra_kernel, steps=steps, wins=len(steps)),
         in_specs=[hbm, vmem, hbm, hbm, hbm],
-        out_specs=[vmem] * (HALVES * len(steps)),
-        out_shape=[shape] * (HALVES * len(steps)),
+        out_specs=[vmem] * len(steps),
+        out_shape=[shape] * len(steps),
         scratch_shapes=[
             pltpu.VMEM(rows.shape, jnp.bfloat16),
             *[pltpu.VMEM(t.shape, jnp.float32) for t in tables],
@@ -180,7 +174,7 @@
         ],
         compiler_params=pltpu.CompilerParams(vmem_limit_bytes=60 * MIB),
         cost_estimate=pl.CostEstimate(
-            flops=4 * len(steps) * count * SAMPLES * LANES, bytes_accessed=2 * count * SAMPLES, transcendentals=0
+            flops=2 * len(steps) * count * SAMPLES * LANES, bytes_accessed=2 * count * SAMPLES, transcendentals=0
         ),
         name="own_spectra",
     )(rows, taps, *tables)
@@ -214,20 +208,17 @@
 
 
 def by_bin_kernel(*refs, steps):
-    blocks, refs = refs[: 2 * steps], refs[2 * steps :]
+    blocks, refs = refs[:steps], refs[steps:]
     first_ref, second_ref, turned_ref, turned, near, sem = refs
     nodes, windows = near.shape[0], near.shape[1]
     _, is_first = position(steps)
     own_at = jnp.where(is_first, 0, 1)
-    copy = pltpu.make_async_copy(blocks[0].at[0], near, sem)
+    copy = pltpu.make_async_copy(blocks[0], near, sem)
     copy.start()
     row = lax.broadcasted_iota(jnp.int32, (LANES, LANES), 0)
     unit = (row == lax.broadcasted_iota(jnp.int32, (LANES, LANES), 1)).astype(jnp.bfloat16)
     for tile in (1, 0):
-        here = []
-        for step in range(tile * steps // 2, (tile + 1) * steps // 2):
-            here.append(near if step == 0 else blocks[2 * step].at[0])
-            here.append(blocks[2 * step + 1].at[1])
+        here = [near if s == 0 else blocks[s] for s in range(tile * steps // 2, (tile + 1) * steps // 2)]
         if tile == 0:
             copy.wait()
 
@@ -253,8 +244,8 @@
 
 
 def by_bin(blocks):
-    _, nodes, windows, _ = blocks[0].shape
-    steps = len(blocks) // 2
+    nodes, windows, _ = blocks[0].shape
+    steps = len(blocks)
     shape = jax.ShapeDtypeStruct((BAND, nodes, LANES), jnp.bfloat16)
     vmem = pl.BlockSpec(memory_space=pltpu.VMEM)
     return pl.pallas_call(
@@ -402,6 +393,7 @@
 
     rows, taps = traces.reshape(windows * nodes, samples), taps.reshape(1, TAPS)
     steps = tuple(range(wins))[::-1]
+    partner_rows = hop(rows, 1)
     found = own_spectra(rows, taps, nodes, steps)
     found, neighbours, valid = lax.optimization_barrier((found, neighbours, valid))
 
@@ -425,19 +417,12 @@
 
     swap_a = [(i, i ^ 2) for i in range(pairs) if (i ^ 2) < pairs]
     swap_b = [(i, j) for i in range(2, pairs) for j in [((i - 2) ^ 2) + 2] if j < pairs]
-    halves, moved = [], []
-
-    def finish(moved):
-        a, b, turned = by_bin(within_chip(moved))
+    halves = []
+    for half in range(HALVES):
+        if half:
+            found = own_spectra(partner_rows, taps, nodes, steps)
+        a, b, turned = by_bin(between_chips([found[steps.index(s)] for s in range(wins)]))
         halves.append((a, b, turned, lax.ppermute(a, "pairs", swap_a), lax.ppermute(b, "pairs", swap_b)))
-
-    for half in range(HALVES):
-        blocks = [found[half * wins + steps.index(s)] for s in range(wins)]
-        if half:
-            blocks, moved[1] = lax.optimization_barrier((blocks, moved[1]))
-            finish(moved)
-        moved = between_chips(blocks)
-    finish(moved)
     stack = cross_products(halves, select, wins)
     return inverse(within_chip(between_chips(stack)), high, low)
 

time: 73.7 us -> 67.4 us (0.915)
  waiting for transfers between devices: 23.5 us -> 14.8 us
  Pallas kernels: 25.1 us -> 29.9 us
  starting transfers between devices: 22.7 us -> 20.4 us
  local copies, waits for them, and re-layouts: 1.18 us -> 0.27 us
    ppermute x21 -> x14, waiting for transfers between devices: 16.7 us -> 8.94 us  [hop(): return lax.ppermute(array, ('pairs', 'win'), pairing)]
    pallas_call x1 -> x2, Pallas kernels: 10.4 us -> 15 us  [own_spectra(): pl.pallas_call(functools.partial(spectra_kernel, steps=steps, wins=len(st...]
    ppermute x21 -> x14, starting transfers between devices: 13.6 us -> 11.1 us  [hop(): return lax.ppermute(array, ('pairs', 'win'), pairing)]
    ppermute x4, waiting for transfers between devices: 6.84 us -> 5.91 us  [the longest x2 4.71 us: per_device(): lax.ppermute(b, 'pairs', swap_b)]
    unnamed x16, local copies, waits for them, and re-layouts: 0.95 us -> 0.04 us
  transfers between devices with their start and end apart: 26 -> 19, of which waited for: 11 -> 5; matrix products, arithmetic and copies ran while one was open for 1% -> 1% of each run, Pallas kernels for 9% -> 32%
where the time goes in v6:
time: 67.4 us; the launch traced here: 66.2 us
  Pallas kernels  29.9 us (44%)
  starting transfers between devices  20.4 us (30%)
  waiting for transfers between devices  14.8 us (22%)
    pallas_call x2, Pallas kernels, own_spectra(): pl.pallas_call(functools.partial(spectra_kernel, steps=steps, wins=len(st...  15 us
    ppermute x14, starting transfers between devices, hop(): return lax.ppermute(array, ('pairs', 'win'), pairing)  11.1 us
    ppermute x14, waiting for transfers between devices, hop(): return lax.ppermute(array, ('pairs', 'win'), pairing)  8.94 us
    ppermute x2, starting transfers between devices, per_device(): lax.ppermute(b, 'pairs', swap_b)  6.01 us
    pallas_call x2, Pallas kernels, by_bin(): pl.pallas_call(functools.partial(by_bin_kernel, steps=steps), out_shape=[...  5.39 us
    ppermute x2, waiting for transfers between devices, per_device(): lax.ppermute(b, 'pairs', swap_b)  4.71 us
    pallas_call x1, Pallas kernels, inverse(): pl.pallas_call(inverse_kernel, grid=(LAGS // width,), in_specs=[table, ta...  3.94 us
    pallas_call x1, Pallas kernels, cross_products(): pl.pallas_call(cross_kernel, out_shape=[jax.ShapeDtypeStruct((BAND * 4 *...  3.45 us
  transfers between devices with their start and end apart: 19, of which 5 were waited for; matrix products, arithmetic and copies ran while one was open for 1% of the time, Pallas kernels for 32%

profile of v6, /device:TPU:16, one launch (start us, length us, event | category | flops | bytes accessed | tf_op | source)
XLA Modules:
  0.0 66.2 jit_solution(17583049588623475262)
XLA Ops:
  0.0 7.5 %own_spectra.2 = (bf16[16,32,128]{2,1,0:T(8,128)(2,1)}, bf16[16,32,128]{2,1,0:T(8,128)(2,1)}, bf16[16,32,128]{2,1,0:T(8,128)(2,1)}, bf16[16,32,128]{2,1,0:T(8,128)(2,1)}) custom-call(bf16[512,4096]{1,0:T(8,128)(2,1)} %bitcast.15, f32[1,129]{1,0:T(1,128)} %bitcast.16, f32[129,1024]{1,0:T(8,128)} %constant.116.clone.fine_hbm, ...), custom_call_target="tpu_custom_call" | custom-call | flops 2147483648 | bytes 4194304 | tf_op jit(solution)/shard_map/own_spectra/pallas_call | solution.py:163
  7.5 1.6 %collective-permute-start.11 = (s32[16,64]{1,0:T(8,128)S(1)}, s32[16,64]{1,0:T(8,128)S(1)}, u32[]{:S(2)}, u32[]{:S(2)}) collective-permute-start(s32[16,64]{1,0:T(8,128)S(1)} %fusion.3), channel_id=1, source_target_pairs={{0,4},{4,0},{8,12},{12,8},{16,20},{20,16},{24,28},{28,24},{1,5},{5... | collective-permute-start | bytes 12296 | tf_op jit(solution)/shard_map/ppermute | solution.py:406
  9.1 1.5 %collective-permute-start = (bf16[16,32,128]{2,1,0:T(8,128)(2,1)}, bf16[16,32,128]{2,1,0:T(8,128)(2,1)S(1)}, u32[]{:S(2)}, u32[]{:S(2)}) collective-permute-start(bf16[16,32,128]{2,1,0:T(8,128)(2,1)} %get-tuple-element.39), channel_id=1, source_target_pairs={{0,2},{1,3},{2,0},{3,1},{4,6},{5,7},{6,4},{7,5},{8,10},{9,11},{10,... | collective-permute-start | bytes 393224 | tf_op jit(solution)/shard_map/ppermute | solution.py:386
  10.6 0.5 collective-permute-start.1
  11.1 1.5 %collective-permute-start.2 = (bf16[16,32,128]{2,1,0:T(8,128)(2,1)}, bf16[16,32,128]{2,1,0:T(8,128)(2,1)S(1)}, u32[]{:S(2)}, u32[]{:S(2)}) collective-permute-start(bf16[16,32,128]{2,1,0:T(8,128)(2,1)} %get-tuple-element.41), channel_id=1, source_target_pairs={{0,6},{1,7},{2,4},{3,5},{4,2},{5,3},{6,0},{7,1},{8,14},{9,15},{10,... | collective-permute-start | bytes 393224 | tf_op jit(solution)/shard_map/ppermute | solution.py:386
  12.6 0.1 copy.15
  12.7 0.0 collective-permute-done.11
  12.7 0.1 copy.16
  12.8 0.1 add_select_fusion
  12.9 7.5 %own_spectra.3 = (bf16[16,32,128]{2,1,0:T(8,128)(2,1)}, bf16[16,32,128]{2,1,0:T(8,128)(2,1)}, bf16[16,32,128]{2,1,0:T(8,128)(2,1)}, bf16[16,32,128]{2,1,0:T(8,128)(2,1)}) custom-call(bf16[512,4096]{1,0:T(8,128)(2,1)} %collective-permute-done.5.x_hbm, f32[1,129]{1,0:T(1,128)} %bitcast.17, f32[129,1024]{1,0:T(8,128)} %constant.116.clone.fine_hbm, ...), custom_call_target="tpu_custom_call" | custom-call | flops 2147483648 | bytes 4194304 | tf_op jit(solution)/shard_map/own_spectra/pallas_call | solution.py:163
  20.4 1.5 %collective-permute-start.6 = (bf16[16,32,128]{2,1,0:T(8,128)(2,1)}, bf16[16,32,128]{2,1,0:T(8,128)(2,1)S(1)}, u32[]{:S(2)}, u32[]{:S(2)}) collective-permute-start(bf16[16,32,128]{2,1,0:T(8,128)(2,1)} %get-tuple-element.46), channel_id=1, source_target_pairs={{0,2},{1,3},{2,0},{3,1},{4,6},{5,7},{6,4},{7,5},{8,10},{9,11},{10,... | collective-permute-start | bytes 393224 | tf_op jit(solution)/shard_map/ppermute | solution.py:386
  22.0 0.5 collective-permute-start.7
  22.5 0.0 collective-permute-done.refs_1_
  22.5 1.5 %collective-permute-start.8 = (bf16[16,32,128]{2,1,0:T(8,128)(2,1)}, bf16[16,32,128]{2,1,0:T(8,128)(2,1)S(1)}, u32[]{:S(2)}, u32[]{:S(2)}) collective-permute-start(bf16[16,32,128]{2,1,0:T(8,128)(2,1)} %get-tuple-element.48), channel_id=1, source_target_pairs={{0,6},{1,7},{2,4},{3,5},{4,2},{5,3},{6,0},{7,1},{8,14},{9,15},{10,... | collective-permute-start | bytes 393224 | tf_op jit(solution)/shard_map/ppermute | solution.py:386
  24.0 0.0 collective-permute-done.1.refs_2_
  24.0 0.0 collective-permute-done.2.refs_3_
  24.0 2.7 %by_bin.2 = (bf16[64,16,128]{2,1,0:T(8,128)(2,1)S(1)}, bf16[64,16,128]{2,1,0:T(8,128)(2,1)S(1)}, bf16[64,32,128]{2,1,0:T(8,128)(2,1)S(1)}) custom-call(bf16[16,32,128]{2,1,0:T(8,128)(2,1)S(1)} %copy-done.4, bf16[16,32,128]{2,1,0:T(8,128)(2,1)S(1)} %collective-permute-done.refs_1_, bf16[16,32,128]{2,1,0:T(8,128)(2,1)S(1)} %collective-permute-done.1.refs_2_, ...), custom_call_target="tpu_custom_call" | custom-call | flops 2147483648 | bytes 4194304 | tf_op jit(solution)/shard_map/by_bin/pallas_call | solution.py:251
  26.7 1.6 %collective-permute-start.3 = (bf16[64,16,128]{2,1,0:T(8,128)(2,1)S(1)}, bf16[64,16,128]{2,1,0:T(8,128)(2,1)S(1)}, u32[]{:S(2)}, u32[]{:S(2)}) collective-permute-start(bf16[64,16,128]{2,1,0:T(8,128)(2,1)S(1)} %get-tuple-element.42.refs_0_), channel_id=1, source_target_pairs={{0,8},{4,12},{8,0},{12,4},{16,24},{20,28},{24,16},{28,20},{1,9},{5... | collective-permute-start | bytes 786440 | tf_op jit(solution)/shard_map/ppermute | solution.py:425
  28.3 1.9 %collective-permute-start.4 = (bf16[64,16,128]{2,1,0:T(8,128)(2,1)S(1)}, bf16[64,16,128]{2,1,0:T(8,128)(2,1)S(1)}, u32[]{:S(2)}, u32[]{:S(2)}) collective-permute-start(bf16[64,16,128]{2,1,0:T(8,128)(2,1)S(1)} %get-tuple-element.43.refs_1_), channel_id=1, source_target_pairs={{8,16},{12,20},{16,8},{20,12},{9,17},{13,21},{17,9},{21,13},{10,18... | collective-permute-start | bytes 786440 | tf_op jit(solution)/shard_map/ppermute | solution.py:425
  30.3 0.0 collective-permute-done.6.refs_1_
  30.3 0.0 collective-permute-done.7.refs_2_
  30.3 2.7 %by_bin.3 = (bf16[64,16,128]{2,1,0:T(8,128)(2,1)S(1)}, bf16[64,16,128]{2,1,0:T(8,128)(2,1)S(1)}, bf16[64,32,128]{2,1,0:T(8,128)(2,1)S(1)}) custom-call(bf16[16,32,128]{2,1,0:T(8,128)(2,1)S(1)} %copy-done.5, bf16[16,32,128]{2,1,0:T(8,128)(2,1)S(1)} %collective-permute-done.6.refs_1_, bf16[16,32,128]{2,1,0:T(8,128)(2,1)S(1)} %collective-permute-done.7.refs_2_, ...), custom_call_target="tpu_custom_call" | custom-call | flops 2147483648 | bytes 4194304 | tf_op jit(solution)/shard_map/by_bin/pallas_call | solution.py:251
  33.0 4.1 %collective-permute-start.10 = (bf16[64,16,128]{2,1,0:T(8,128)(2,1)S(1)}, bf16[64,16,128]{2,1,0:T(8,128)(2,1)S(1)}, u32[]{:S(2)}, u32[]{:S(2)}) collective-permute-start(bf16[64,16,128]{2,1,0:T(8,128)(2,1)S(1)} %get-tuple-element.50.refs_6_), channel_id=1, source_target_pairs={{8,16},{12,20},{16,8},{20,12},{9,17},{13,21},{17,9},{21,13},{10,18... | collective-permute-start | bytes 786440 | tf_op jit(solution)/shard_map/ppermute | solution.py:425
  37.1 0.1 collective-permute-start.9
  37.2 0.1 copy.17
  37.3 0.3 compare_convert_fusion.refs_10_.select_ref
  37.6 0.0 collective-permute-done.3.refs_3_
  37.6 4.7 %collective-permute-done.10.refs_9_ = bf16[64,16,128]{2,1,0:T(8,128)(2,1)S(1)} collective-permute-done((bf16[64,16,128]{2,1,0:T(8,128)(2,1)S(1)}, bf16[64,16,128]{2,1,0:T(8,128)(2,1)S(1)}, u32[]{:S(2)}, u32[]{:S(2)}) %collective-permute-start.10) | collective-permute-done | bytes 262176 | tf_op jit(solution)/shard_map/ppermute | solution.py:425
  42.3 1.2 %collective-permute-done.9.refs_8_ = bf16[64,16,128]{2,1,0:T(8,128)(2,1)S(1)} collective-permute-done((bf16[64,16,128]{2,1,0:T(8,128)(2,1)S(1)}, bf16[64,16,128]{2,1,0:T(8,128)(2,1)S(1)}, u32[]{:S(2)}, u32[]{:S(2)}) %collective-permute-start.9) | collective-permute-done | bytes 262176 | tf_op jit(solution)/shard_map/ppermute | solution.py:425
  43.5 3.5 %cross_products.1 = (f32[4096,128]{1,0:T(8,128)S(1)}, f32[2,16,16,128]{3,2,1,0:T(8,128)S(1)}, f32[2,16,16,128]{3,2,1,0:T(8,128)S(1)}) custom-call(bf16[64,16,128]{2,1,0:T(8,128)(2,1)S(1)} %get-tuple-element.42.refs_0_, bf16[64,16,128]{2,1,0:T(8,128)(2,1)S(1)} %get-tuple-element.43.refs_1_, bf16[64,32,128]{2,1,0:T(8,128)(2,1)S(1)} %get-tuple-element.44.refs_2_, ...), custom_call_target="tpu_custom_call" | custom-call | tf_op jit(solution)/shard_map/cross_products/pallas_call | solution.py:318
  47.0 0.0 copy-start
  47.0 0.0 copy-start.1
  47.0 0.0 copy-start.2
  47.0 0.0 copy-start.3
  47.0 1.1 %own_slots.1 = (f32[2,16,16,128]{3,2,1,0:T(8,128)S(1)}, f32[2,16,16,128]{3,2,1,0:T(8,128)S(1)}) custom-call(f32[4096,128]{1,0:T(8,128)S(1)} %get-tuple-element.54.cross_ref, bf16[32,64,128]{2,1,0:T(8,128)(2,1)S(1)} %compare_convert_fusion.refs_10_.select_ref), custom_call_target="tpu_custom_call" | custom-call | flops 4294967296 | bytes 16777216 | tf_op jit(solution)/shard_map/own_slots/pallas_call | solution.py:326
  48.2 1.5 %collective-permute-start.13 = (f32[2,16,16,128]{3,2,1,0:T(8,128)S(1)}, f32[2,16,16,128]{3,2,1,0:T(8,128)S(1)}, u32[]{:S(2)}, u32[]{:S(2)}) collective-permute-start(f32[2,16,16,128]{3,2,1,0:T(8,128)S(1)} %get-tuple-element.56), channel_id=1, source_target_pairs={{0,2},{1,3},{2,0},{3,1},{4,6},{5,7},{6,4},{7,5},{8,10},{9,11},{10,... | collective-permute-start | bytes 786440 | tf_op jit(solution)/shard_map/ppermute | solution.py:386
  49.7 0.5 collective-permute-start.15
  50.2 1.5 %collective-permute-start.17 = (f32[2,16,16,128]{3,2,1,0:T(8,128)S(1)}, f32[2,16,16,128]{3,2,1,0:T(8,128)S(1)}, u32[]{:S(2)}, u32[]{:S(2)}) collective-permute-start(f32[2,16,16,128]{3,2,1,0:T(8,128)S(1)} %get-tuple-element.58), channel_id=1, source_target_pairs={{0,6},{1,7},{2,4},{3,5},{4,2},{5,3},{6,0},{7,1},{8,14},{9,15},{10,... | collective-permute-start | bytes 786440 | tf_op jit(solution)/shard_map/ppermute | solution.py:386
  51.7 4.7 %collective-permute-done.13.refs_2_ = f32[2,16,16,128]{3,2,1,0:T(8,128)S(1)} collective-permute-done((f32[2,16,16,128]{3,2,1,0:T(8,128)S(1)}, f32[2,16,16,128]{3,2,1,0:T(8,128)S(1)}, u32[]{:S(2)}, u32[]{:S(2)}) %collective-permute-start.13) | collective-permute-done | bytes 262176 | tf_op jit(solution)/shard_map/ppermute | solution.py:386
  56.4 0.0 collective-permute-start.14
  56.4 4.0 %collective-permute-done.15.refs_4_ = f32[2,16,16,128]{3,2,1,0:T(8,128)S(1)} collective-permute-done((f32[2,16,16,128]{3,2,1,0:T(8,128)S(1)}, f32[2,16,16,128]{3,2,1,0:T(8,128)S(1)}, u32[]{:S(2)}, u32[]{:S(2)}) %collective-permute-start.15) | collective-permute-done | bytes 262176 | tf_op jit(solution)/shard_map/ppermute | solution.py:386
  60.4 0.0 collective-permute-start.16
  60.4 0.0 collective-permute-done.17.refs_6_
  60.4 0.5 collective-permute-start.18
  60.9 1.1 %lag_tables.1 = (bf16[8,128,1024]{2,1,0:T(8,128)(2,1)S(1)}, bf16[8,128,1024]{2,1,0:T(8,128)(2,1)S(1)}) custom-call(f32[64,1024]{1,0:T(8,128)S(1)} %copy-done, f32[64,1024]{1,0:T(8,128)S(1)} %copy-done.1, f32[8,1024]{1,0:T(8,128)S(1)} %copy-done.2, f32[8,1024]{1,0:T(8,128)S(1)} %copy-done.3), custom_call_target="tpu_custom_call" | custom-call | tf_op jit(solution)/shard_map/lag_tables/pallas_call | solution.py:199
  62.0 0.0 collective-permute-done.16.refs_5_
  62.0 0.2 collective-permute-done.18.refs_7_
  62.3 3.9 %inverse.1 = f32[16,16,1024]{2,1,0:T(8,128)} custom-call(bf16[1024,1024]{1,0:T(8,128)(2,1)S(1)} %bitcast.8, bf16[1024,1024]{1,0:T(8,128)(2,1)S(1)} %bitcast.9, f32[2,16,16,128]{3,2,1,0:T(8,128)S(1)} %get-tuple-element.55.refs_0_, f32[2,16,16,128]{3,2,1,0:T(8,128)S(1)} %collective-permute-done.12.refs_1_, ...), custom_call_target="tpu_custom_call" | custom-call | tf_op jit(solution)/shard_map/inverse/pallas_call | solution.py:363
  (23 shorter events, 0.1 us)
Async XLA Ops:
  0.0 12.9 %collective-permute-start.5 = (bf16[512,4096]{1,0:T(8,128)(2,1)}, bf16[512,4096]{1,0:T(8,128)(2,1)}, u32[]{:S(2)}, u32[]{:S(2)}) collective-permute-start(bf16[512,4096]{1,0:T(8,128)(2,1)} %bitcast.14), channel_id=1, source_target_pairs={{0,1},{1,0},{2,3},{3,2},{4,5},{5,4},{6,7},{7,6},{8,9},{9,8},{10,11... | collective-permute-start | bytes 12582920 | tf_op jit(solution)/shard_map/ppermute | solution.py:386
  0.0 7.5 %copy-start.6 = (s32[16,64]{1,0:T(8,128)S(1)}, s32[16,64]{1,0:T(8,128)}, u32[]{:S(2)}) copy-start(s32[16,64]{1,0:T(8,128)} %param.16) | copy-start | bytes 12292
  0.0 7.5 %copy-start.7 = (s32[16,64]{1,0:T(8,128)S(1)}, s32[16,64]{1,0:T(8,128)}, u32[]{:S(2)}) copy-start(s32[16,64]{1,0:T(8,128)} %param.17) | copy-start | bytes 12292
  7.5 5.2 %collective-permute-start.11 = (s32[16,64]{1,0:T(8,128)S(1)}, s32[16,64]{1,0:T(8,128)S(1)}, u32[]{:S(2)}, u32[]{:S(2)}) collective-permute-start(s32[16,64]{1,0:T(8,128)S(1)} %fusion.3), channel_id=1, source_target_pairs={{0,4},{4,0},{8,12},{12,8},{16,20},{20,16},{24,28},{28,24},{1,5},{5... | collective-permute-start | bytes 12296 | tf_op jit(solution)/shard_map/ppermute | solution.py:406
  9.1 13.4 %collective-permute-start = (bf16[16,32,128]{2,1,0:T(8,128)(2,1)}, bf16[16,32,128]{2,1,0:T(8,128)(2,1)S(1)}, u32[]{:S(2)}, u32[]{:S(2)}) collective-permute-start(bf16[16,32,128]{2,1,0:T(8,128)(2,1)} %get-tuple-element.39), channel_id=1, source_target_pairs={{0,2},{1,3},{2,0},{3,1},{4,6},{5,7},{6,4},{7,5},{8,10},{9,11},{10,... | collective-permute-start | bytes 393224 | tf_op jit(solution)/shard_map/ppermute | solution.py:386
  10.6 13.4 %collective-permute-start.1 = (bf16[16,32,128]{2,1,0:T(8,128)(2,1)}, bf16[16,32,128]{2,1,0:T(8,128)(2,1)S(1)}, u32[]{:S(2)}, u32[]{:S(2)}) collective-permute-start(bf16[16,32,128]{2,1,0:T(8,128)(2,1)} %get-tuple-element.40), channel_id=1, source_target_pairs={{0,4},{1,5},{2,6},{3,7},{4,0},{5,1},{6,2},{7,3},{8,12},{9,13},{10,... | collective-permute-start | bytes 393224 | tf_op jit(solution)/shard_map/ppermute | solution.py:386
  11.1 12.9 %collective-permute-start.2 = (bf16[16,32,128]{2,1,0:T(8,128)(2,1)}, bf16[16,32,128]{2,1,0:T(8,128)(2,1)S(1)}, u32[]{:S(2)}, u32[]{:S(2)}) collective-permute-start(bf16[16,32,128]{2,1,0:T(8,128)(2,1)} %get-tuple-element.41), channel_id=1, source_target_pairs={{0,6},{1,7},{2,4},{3,5},{4,2},{5,3},{6,0},{7,1},{8,14},{9,15},{10,... | collective-permute-start | bytes 393224 | tf_op jit(solution)/shard_map/ppermute | solution.py:386
  12.9 11.1 %copy-start.4 = (bf16[16,32,128]{2,1,0:T(8,128)(2,1)S(1)}, bf16[16,32,128]{2,1,0:T(8,128)(2,1)}, u32[]{:S(2)}) copy-start(bf16[16,32,128]{2,1,0:T(8,128)(2,1)} %get-tuple-element.38.refs_0_) | copy-start | bytes 393220
  20.4 9.8 %collective-permute-start.6 = (bf16[16,32,128]{2,1,0:T(8,128)(2,1)}, bf16[16,32,128]{2,1,0:T(8,128)(2,1)S(1)}, u32[]{:S(2)}, u32[]{:S(2)}) collective-permute-start(bf16[16,32,128]{2,1,0:T(8,128)(2,1)} %get-tuple-element.46), channel_id=1, source_target_pairs={{0,2},{1,3},{2,0},{3,1},{4,6},{5,7},{6,4},{7,5},{8,10},{9,11},{10,... | collective-permute-start | bytes 393224 | tf_op jit(solution)/shard_map/ppermute | solution.py:386
  22.0 8.3 %collective-permute-start.7 = (bf16[16,32,128]{2,1,0:T(8,128)(2,1)}, bf16[16,32,128]{2,1,0:T(8,128)(2,1)S(1)}, u32[]{:S(2)}, u32[]{:S(2)}) collective-permute-start(bf16[16,32,128]{2,1,0:T(8,128)(2,1)} %get-tuple-element.47), channel_id=1, source_target_pairs={{0,4},{1,5},{2,6},{3,7},{4,0},{5,1},{6,2},{7,3},{8,12},{9,13},{10,... | collective-permute-start | bytes 393224 | tf_op jit(solution)/shard_map/ppermute | solution.py:386
  22.5 7.8 %copy-start.5 = (bf16[16,32,128]{2,1,0:T(8,128)(2,1)S(1)}, bf16[16,32,128]{2,1,0:T(8,128)(2,1)}, u32[]{:S(2)}) copy-start(bf16[16,32,128]{2,1,0:T(8,128)(2,1)} %get-tuple-element.45.refs_0_) | copy-start | bytes 393220
  22.5 7.8 %collective-permute-start.8 = (bf16[16,32,128]{2,1,0:T(8,128)(2,1)}, bf16[16,32,128]{2,1,0:T(8,128)(2,1)S(1)}, u32[]{:S(2)}, u32[]{:S(2)}) collective-permute-start(bf16[16,32,128]{2,1,0:T(8,128)(2,1)} %get-tuple-element.48), channel_id=1, source_target_pairs={{0,6},{1,7},{2,4},{3,5},{4,2},{5,3},{6,0},{7,1},{8,14},{9,15},{10,... | collective-permute-start | bytes 393224 | tf_op jit(solution)/shard_map/ppermute | solution.py:386
  26.7 10.9 %collective-permute-start.3 = (bf16[64,16,128]{2,1,0:T(8,128)(2,1)S(1)}, bf16[64,16,128]{2,1,0:T(8,128)(2,1)S(1)}, u32[]{:S(2)}, u32[]{:S(2)}) collective-permute-start(bf16[64,16,128]{2,1,0:T(8,128)(2,1)S(1)} %get-tuple-element.42.refs_0_), channel_id=1, source_target_pairs={{0,8},{4,12},{8,0},{12,4},{16,24},{20,28},{24,16},{28,20},{1,9},{5... | collective-permute-start | bytes 786440 | tf_op jit(solution)/shard_map/ppermute | solution.py:425
  28.3 9.3 %collective-permute-start.4 = (bf16[64,16,128]{2,1,0:T(8,128)(2,1)S(1)}, bf16[64,16,128]{2,1,0:T(8,128)(2,1)S(1)}, u32[]{:S(2)}, u32[]{:S(2)}) collective-permute-start(bf16[64,16,128]{2,1,0:T(8,128)(2,1)S(1)} %get-tuple-element.43.refs_1_), channel_id=1, source_target_pairs={{8,16},{12,20},{16,8},{20,12},{9,17},{13,21},{17,9},{21,13},{10,18... | collective-permute-start | bytes 786440 | tf_op jit(solution)/shard_map/ppermute | solution.py:425
  33.0 9.3 %collective-permute-start.10 = (bf16[64,16,128]{2,1,0:T(8,128)(2,1)S(1)}, bf16[64,16,128]{2,1,0:T(8,128)(2,1)S(1)}, u32[]{:S(2)}, u32[]{:S(2)}) collective-permute-start(bf16[64,16,128]{2,1,0:T(8,128)(2,1)S(1)} %get-tuple-element.50.refs_6_), channel_id=1, source_target_pairs={{8,16},{12,20},{16,8},{20,12},{9,17},{13,21},{17,9},{21,13},{10,18... | collective-permute-start | bytes 786440 | tf_op jit(solution)/shard_map/ppermute | solution.py:425
  37.1 6.4 %collective-permute-start.9 = (bf16[64,16,128]{2,1,0:T(8,128)(2,1)S(1)}, bf16[64,16,128]{2,1,0:T(8,128)(2,1)S(1)}, u32[]{:S(2)}, u32[]{:S(2)}) collective-permute-start(bf16[64,16,128]{2,1,0:T(8,128)(2,1)S(1)} %get-tuple-element.49.refs_5_), channel_id=1, source_target_pairs={{0,8},{4,12},{8,0},{12,4},{16,24},{20,28},{24,16},{28,20},{1,9},{5... | collective-permute-start | bytes 786440 | tf_op jit(solution)/shard_map/ppermute | solution.py:425
  47.0 13.9 %copy-start = (f32[64,1024]{1,0:T(8,128)S(1)}, f32[64,1024]{1,0:T(8,128)}, u32[]{:S(2)}) copy-start(f32[64,1024]{1,0:T(8,128)} %constant.119.clone.cos_ref) | copy-start | bytes 786436
  47.0 13.9 %copy-start.1 = (f32[64,1024]{1,0:T(8,128)S(1)}, f32[64,1024]{1,0:T(8,128)}, u32[]{:S(2)}) copy-start(f32[64,1024]{1,0:T(8,128)} %constant.120.clone.msin_ref) | copy-start | bytes 786436
  47.0 13.9 %copy-start.2 = (f32[8,1024]{1,0:T(8,128)S(1)}, f32[8,1024]{1,0:T(8,128)}, u32[]{:S(2)}) copy-start(f32[8,1024]{1,0:T(8,128)} %constant.121.clone.cos0_ref) | copy-start | bytes 98308
  47.0 13.9 %copy-start.3 = (f32[8,1024]{1,0:T(8,128)S(1)}, f32[8,1024]{1,0:T(8,128)}, u32[]{:S(2)}) copy-start(f32[8,1024]{1,0:T(8,128)} %constant.122.clone.msin0_ref) | copy-start | bytes 98308
  48.2 8.2 %collective-permute-start.13 = (f32[2,16,16,128]{3,2,1,0:T(8,128)S(1)}, f32[2,16,16,128]{3,2,1,0:T(8,128)S(1)}, u32[]{:S(2)}, u32[]{:S(2)}) collective-permute-start(f32[2,16,16,128]{3,2,1,0:T(8,128)S(1)} %get-tuple-element.56), channel_id=1, source_target_pairs={{0,2},{1,3},{2,0},{3,1},{4,6},{5,7},{6,4},{7,5},{8,10},{9,11},{10,... | collective-permute-start | bytes 786440 | tf_op jit(solution)/shard_map/ppermute | solution.py:386
  49.7 10.7 %collective-permute-start.15 = (f32[2,16,16,128]{3,2,1,0:T(8,128)S(1)}, f32[2,16,16,128]{3,2,1,0:T(8,128)S(1)}, u32[]{:S(2)}, u32[]{:S(2)}) collective-permute-start(f32[2,16,16,128]{3,2,1,0:T(8,128)S(1)} %get-tuple-element.57), channel_id=1, source_target_pairs={{0,4},{1,5},{2,6},{3,7},{4,0},{5,1},{6,2},{7,3},{8,12},{9,13},{10,... | collective-permute-start | bytes 786440 | tf_op jit(solution)/shard_map/ppermute | solution.py:386
  50.2 10.2 %collective-permute-start.17 = (f32[2,16,16,128]{3,2,1,0:T(8,128)S(1)}, f32[2,16,16,128]{3,2,1,0:T(8,128)S(1)}, u32[]{:S(2)}, u32[]{:S(2)}) collective-permute-start(f32[2,16,16,128]{3,2,1,0:T(8,128)S(1)} %get-tuple-element.58), channel_id=1, source_target_pairs={{0,6},{1,7},{2,4},{3,5},{4,2},{5,3},{6,0},{7,1},{8,14},{9,15},{10,... | collective-permute-start | bytes 786440 | tf_op jit(solution)/shard_map/ppermute | solution.py:386
  51.7 10.3 %collective-permute-start.12 = (f32[2,16,16,128]{3,2,1,0:T(8,128)S(1)}, f32[2,16,16,128]{3,2,1,0:T(8,128)S(1)}, u32[]{:S(2)}, u32[]{:S(2)}) collective-permute-start(f32[2,16,16,128]{3,2,1,0:T(8,128)S(1)} %get-tuple-element.55.refs_0_), channel_id=1, source_target_pairs={{0,1},{1,0},{2,3},{3,2},{4,5},{5,4},{6,7},{7,6},{8,9},{9,8},{10,11... | collective-permute-start | bytes 786440 | tf_op jit(solution)/shard_map/ppermute | solution.py:386
  56.4 5.6 %collective-permute-start.14 = (f32[2,16,16,128]{3,2,1,0:T(8,128)S(1)}, f32[2,16,16,128]{3,2,1,0:T(8,128)S(1)}, u32[]{:S(2)}, u32[]{:S(2)}) collective-permute-start(f32[2,16,16,128]{3,2,1,0:T(8,128)S(1)} %collective-permute-done.13.refs_2_), channel_id=1, source_target_pairs={{0,1},{1,0},{2,3},{3,2},{4,5},{5,4},{6,7},{7,6},{8,9},{9,8},{10,11... | collective-permute-start | bytes 786440 | tf_op jit(solution)/shard_map/ppermute | solution.py:386
  60.4 1.7 %collective-permute-start.16 = (f32[2,16,16,128]{3,2,1,0:T(8,128)S(1)}, f32[2,16,16,128]{3,2,1,0:T(8,128)S(1)}, u32[]{:S(2)}, u32[]{:S(2)}) collective-permute-start(f32[2,16,16,128]{3,2,1,0:T(8,128)S(1)} %collective-permute-done.15.refs_4_), channel_id=1, source_target_pairs={{0,1},{1,0},{2,3},{3,2},{4,5},{5,4},{6,7},{7,6},{8,9},{9,8},{10,11... | collective-permute-start | bytes 786440 | tf_op jit(solution)/shard_map/ppermute | solution.py:386
  60.4 1.9 %collective-permute-start.18 = (f32[2,16,16,128]{3,2,1,0:T(8,128)S(1)}, f32[2,16,16,128]{3,2,1,0:T(8,128)S(1)}, u32[]{:S(2)}, u32[]{:S(2)}) collective-permute-start(f32[2,16,16,128]{3,2,1,0:T(8,128)S(1)} %collective-permute-done.17.refs_6_), channel_id=1, source_target_pairs={{0,1},{1,0},{2,3},{3,2},{4,5},{5,4},{6,7},{7,6},{8,9},{9,8},{10,11... | collective-permute-start | bytes 786440 | tf_op jit(solution)/shard_map/ppermute | solution.py:386

commit v7 on v6

--- a/solution.py
+++ b/solution.py
@@ -20,6 +20,7 @@
 STEP = 64
 CHUNK = 512
 HALVES = 2
+PITCH = LANES + 8
 MIB = 1024 * 1024
 CONTRACT_LAST = (((1,), (1,)), ((), ()))
 
@@ -65,6 +66,7 @@
     count = x_ref.shape[0]
     nodes, windows = outs[0].shape[0], outs[0].shape[1]
     width = 2 * LANES
+    pitch = stages[0].shape[1] // windows
     pieces = SAMPLES // CHUNK
     me, _ = position(wins)
     copies = [
@@ -123,12 +125,14 @@
         white = raw * lax.rsqrt((sums[0:count, :] + sums[count:, :]) * (1.0 / BAND) + EPSILON)
         for c, (same, cross) in enumerate(responses[i]):
             part = white[:, c * LANES : (c + 1) * LANES]
-            stages[i % 2][c] = part * same + pltpu.roll(part, BAND, 1) * cross
+            turned = part * same + pltpu.roll(part, BAND, 1) * cross
+            for window in range(windows):
+                stages[i % 2][c, window * pitch : window * pitch + nodes, :] = turned[window * nodes : (window + 1) * nodes]
 
     def give(i):
         for c in range(2):
             for node in range(nodes):
-                values = stages[i % 2][c, pl.ds(node, windows, stride=nodes), :]
+                values = stages[i % 2][c, pl.ds(node, windows, stride=pitch), :]
                 outs[2 * i + c][node] = values.astype(jnp.bfloat16)
 
     for copy in copies:
@@ -169,7 +173,8 @@
             pltpu.VMEM(rows.shape, jnp.bfloat16),
             *[pltpu.VMEM(t.shape, jnp.float32) for t in tables],
             *[pltpu.VMEM((SAMPLES, 2 * LANES), jnp.bfloat16)] * 2,
-            *[pltpu.VMEM((2, count, LANES), jnp.float32)] * 4,
+            *[pltpu.VMEM((2, count, LANES), jnp.float32)] * 2,
+            *[pltpu.VMEM((2, (nodes + 8) * (count // nodes), LANES), jnp.float32)] * 2,
             pltpu.SemaphoreType.DMA((SAMPLES // CHUNK + 3,)),
         ],
         compiler_params=pltpu.CompilerParams(vmem_limit_bytes=60 * MIB),
@@ -225,22 +230,22 @@
         def turn(node, _, here=here, tile=tile):
             values = jnp.concatenate([block[node] for block in here] * 2, 0)
             values = lax.dot_general(unit, values, CONTRACT_LAST, preferred_element_type=jnp.float32)
-            turned[pl.ds(pl.multiple_of((tile * nodes + node) * LANES, LANES), LANES), :] = values
+            turned[pl.ds(pl.multiple_of((tile * nodes + node) * PITCH, 8), LANES), :] = values
             return 0
 
-        lax.fori_loop(0, nodes, turn, 0, unroll=8)
+        lax.fori_loop(0, nodes, turn, 0, unroll=16)
     left = lax.broadcasted_iota(jnp.int32, (nodes, LANES), 1) < LANES // 2
     for which, (out_ref, tile) in enumerate(((first_ref, own_at), (second_ref, 1 - own_at))):
-        start = tile * (nodes * LANES)
+        start = tile * (nodes * PITCH)
 
         def one(f, _, out_ref=out_ref, start=start, which=which):
-            real = turned[pl.ds(start + f, nodes, stride=LANES), :]
-            imag = turned[pl.ds(start + BAND + f, nodes, stride=LANES), :]
+            real = turned[pl.ds(start + f, nodes, stride=PITCH), :]
+            imag = turned[pl.ds(start + BAND + f, nodes, stride=PITCH), :]
             out_ref[f] = jnp.where(left, real, imag).astype(jnp.bfloat16)
             turned_ref[f, which * nodes : (which + 1) * nodes, :] = jnp.where(left, imag, -real).astype(jnp.bfloat16)
             return 0
 
-        lax.fori_loop(0, BAND, one, 0, unroll=8)
+        lax.fori_loop(0, BAND, one, 0, unroll=16)
 
 
 def by_bin(blocks):
@@ -254,7 +259,7 @@
         in_specs=[pl.BlockSpec(memory_space=pl.ANY)] + [vmem] * (len(blocks) - 1),
         out_specs=[vmem] * 3,
         scratch_shapes=[
-            pltpu.VMEM((2 * nodes * LANES, LANES), jnp.float32),
+            pltpu.VMEM((2 * nodes * PITCH, LANES), jnp.float32),
             pltpu.VMEM((nodes, windows, LANES), jnp.bfloat16),
             pltpu.SemaphoreType.DMA,
         ],
@@ -264,50 +269,44 @@
     )(*blocks)
 
 
-def pick_slots(cross_ref, select_ref, outs, where, nodes):
-    stations, count = 2 * nodes, 4 * nodes
-    slots = outs[0].shape[2]
-    left = lax.broadcasted_iota(jnp.int32, (2 * BAND, 2 * count), 1) < count
-
-    def one_node(node, _):
-        index = where * nodes + node
-        real = cross_ref[pl.ds(index, BAND, stride=count), :]
-        imag = cross_ref[pl.ds(stations + index, BAND, stride=count), :]
-        values = jnp.concatenate([real, imag], 0)
-        high = values.astype(jnp.bfloat16).astype(jnp.float32)
-        split = jnp.where(left, high, values - high).astype(jnp.bfloat16)
-        picked = lax.dot_general(select_ref[index], split, CONTRACT_LAST, preferred_element_type=jnp.float32)
-        for d in range(2 * len(outs)):
-            outs[d // 2][d % 2, node] = picked[d * slots : (d + 1) * slots, :]
-        return 0
-
-    lax.fori_loop(0, nodes, one_node, 0, unroll=4)
-
-
 def cross_kernel(*refs):
     halves = [refs[5 * h : 5 * h + 5] for h in range(HALVES)]
-    select_ref, cross, *outs = refs[5 * HALVES :]
+    select_ref, *outs, cross = refs[5 * HALVES :]
     nodes = halves[0][0].shape[1]
-    count = 4 * nodes
+    slots = outs[0].shape[2]
+    stations, count = 2 * nodes, 4 * nodes
+    pitch = count + 8
 
     def one_bin(f, _):
         wide = lambda k: jnp.concatenate([half[k][f] for half in halves], 1)
         own = jnp.concatenate([wide(0), wide(1)], 0)
         both = jnp.concatenate([own, wide(2)], 0)
         partners = jnp.concatenate([own, wide(3), wide(4)] * 2, 0)
-        cross[pl.ds(pl.multiple_of(f * count, count), count), :] = lax.dot_general(
+        cross[pl.ds(pl.multiple_of(f * pitch, 8), count), :] = lax.dot_general(
             both, partners, CONTRACT_LAST, preferred_element_type=jnp.float32
         )
         return 0
 
     lax.fori_loop(0, BAND, one_bin, 0, unroll=8)
-    _, is_first = position(2 * len(outs))
-    pick_slots(cross, select_ref, outs, jnp.where(is_first, 1, 0), nodes)
-
-
-def own_slots_kernel(cross_ref, select_ref, *outs):
-    _, is_first = position(2 * len(outs))
-    pick_slots(cross_ref, select_ref, outs, jnp.where(is_first, 0, 1), outs[0].shape[1])
+    _, is_first = position(len(outs))
+    own_at = jnp.where(is_first, 0, 1)
+    left = lax.broadcasted_iota(jnp.int32, (2 * BAND, 2 * count), 1) < count
+    tiles = (outs[: len(outs) // 2], own_at), (outs[len(outs) // 2 :], 1 - own_at)
+    for shares, where in tiles:
+
+        def one_node(node, _, shares=shares, where=where):
+            index = where * nodes + node
+            real = cross[pl.ds(index, BAND, stride=pitch), :]
+            imag = cross[pl.ds(stations + index, BAND, stride=pitch), :]
+            values = jnp.concatenate([real, imag], 0)
+            high = values.astype(jnp.bfloat16).astype(jnp.float32)
+            split = jnp.where(left, high, values - high).astype(jnp.bfloat16)
+            picked = lax.dot_general(select_ref[index], split, CONTRACT_LAST, preferred_element_type=jnp.float32)
+            for d in range(2 * len(shares)):
+                shares[d // 2][d % 2, node] = picked[d * slots : (d + 1) * slots, :]
+            return 0
+
+        lax.fori_loop(0, nodes, one_node, 0, unroll=8)
 
 
 def cross_products(halves, select, wins):
@@ -315,62 +314,62 @@
     block = jax.ShapeDtypeStruct((2, nodes, select.shape[1] // wins, LANES), jnp.float32)
     vmem = pl.BlockSpec(memory_space=pltpu.VMEM)
     operands = [x for half in halves for x in half]
-    cross, *others = pl.pallas_call(
+    return pl.pallas_call(
         cross_kernel,
-        out_shape=[jax.ShapeDtypeStruct((BAND * 4 * nodes, 8 * nodes), jnp.float32)] + [block] * (wins // 2),
+        out_shape=[block] * wins,
         in_specs=[vmem] * (len(operands) + 1),
-        out_specs=[vmem] * (1 + wins // 2),
+        out_specs=[vmem] * wins,
+        scratch_shapes=[pltpu.VMEM((BAND * (4 * nodes + 8), 8 * nodes), jnp.float32)],
         compiler_params=pltpu.CompilerParams(vmem_limit_bytes=12 * MIB),
         name="cross_products",
     )(*operands, select)
-    own = pl.pallas_call(
-        own_slots_kernel,
-        out_shape=[block] * (wins // 2),
-        in_specs=[vmem] * 2,
-        out_specs=[vmem] * (wins // 2),
-        compiler_params=pltpu.CompilerParams(vmem_limit_bytes=8 * MIB),
-        cost_estimate=pl.CostEstimate(flops=1 << 32, bytes_accessed=1 << 24, transcendentals=0),
-        name="own_slots",
-    )(cross, select)
-    return [*own, *others]
-
-
-def inverse_kernel(high_ref, low_ref, *refs):
-    blocks, (out_ref, both) = refs[:-2], refs[-2:]
+
+
+def inverse_kernel(high_ref, low_ref, *refs, far, wins):
+    *refs, out_ref, both = refs
+    blocks, before = refs[:wins], refs[wins:]
     _, nodes, slots, _ = blocks[0].shape
-    rows = nodes * slots
+    rows, depth = nodes * slots, both.shape[1]
+    me, _ = position(wins)
 
     @pl.when(pl.program_id(0) == 0)
     def _():
-        me, _ = position(len(blocks) // 2)
         for d, block in enumerate(blocks):
-            columns = pl.ds(pl.multiple_of((me ^ d) * LANES, LANES), LANES)
+            columns = pl.ds(pl.multiple_of(((me ^ d) % wins) * LANES, LANES), LANES)
             values = block[0].reshape(rows, LANES)
             high = values.astype(jnp.bfloat16)
             both[0:rows, columns] = high
             both[rows : 2 * rows, columns] = (values - high.astype(jnp.float32)).astype(jnp.bfloat16)
 
-    first = jnp.dot(both[...], high_ref[...], preferred_element_type=jnp.float32)
-    second = jnp.dot(both[0:rows, :], low_ref[...], preferred_element_type=jnp.float32)
-    out_ref[...] = (first[0:rows, :] + (first[rows : 2 * rows, :] + second)).reshape(out_ref.shape)
-
-
-def inverse(blocks, high, low):
+    here = pl.ds(pl.multiple_of(((me // wins) ^ far) * depth, depth), depth)
+    first = jnp.dot(both[...], high_ref[here, :], preferred_element_type=jnp.float32)
+    second = jnp.dot(both[0:rows, :], low_ref[here, :], preferred_element_type=jnp.float32)
+    total = (first[0:rows, :] + (first[rows : 2 * rows, :] + second)).reshape(out_ref.shape)
+    for ref in before:
+        total = total + ref[...]
+    out_ref[...] = total
+
+
+def inverse(blocks, high, low, far, before):
     _, nodes, slots, _ = blocks[0].shape
+    wins = len(blocks)
     depth = high.shape[0] * LANES
     width = 256
     table = pl.BlockSpec((depth, width), lambda i: (0, i))
+    lags = pl.BlockSpec((nodes, slots, width), lambda i: (0, 0, i))
     return pl.pallas_call(
-        inverse_kernel,
+        functools.partial(inverse_kernel, far=far, wins=wins),
         grid=(LAGS // width,),
         in_specs=[table, table]
-        + [pl.BlockSpec((1, nodes, slots, LANES), lambda i, j=d % 2: (j, 0, 0, 0)) for d in range(len(blocks))],
-        out_specs=pl.BlockSpec((nodes, slots, width), lambda i: (0, 0, i)),
+        + [pl.BlockSpec((1, nodes, slots, LANES), lambda i, j=d % 2: (j, 0, 0, 0)) for d in range(wins)]
+        + [lags] * len(before),
+        out_specs=lags,
         out_shape=jax.ShapeDtypeStruct((nodes, slots, LAGS), jnp.float32),
-        scratch_shapes=[pltpu.VMEM((2 * nodes * slots, depth), jnp.bfloat16)],
+        scratch_shapes=[pltpu.VMEM((2 * nodes * slots, wins * LANES), jnp.bfloat16)],
         compiler_params=pltpu.CompilerParams(vmem_limit_bytes=12 * MIB),
+        cost_estimate=pl.CostEstimate(flops=1 << 31, bytes_accessed=1 << 22, transcendentals=0),
         name="inverse",
-    )(high.reshape(depth, LAGS), low.reshape(depth, LAGS), *blocks)
+    )(high.reshape(depth, LAGS), low.reshape(depth, LAGS), *blocks, *before)
 
 
 def per_device(traces, taps, neighbours, valid, *, pairs, wins):
@@ -421,10 +420,13 @@
     for half in range(HALVES):
         if half:
             found = own_spectra(partner_rows, taps, nodes, steps)
-        a, b, turned = by_bin(between_chips([found[steps.index(s)] for s in range(wins)]))
+        blocks = between_chips([found[steps.index(s)] for s in range(wins)])
+        a, b, turned = by_bin(blocks)
         halves.append((a, b, turned, lax.ppermute(a, "pairs", swap_a), lax.ppermute(b, "pairs", swap_b)))
     stack = cross_products(halves, select, wins)
-    return inverse(within_chip(between_chips(stack)), high, low)
+    blocks = within_chip(between_chips(stack))
+    total = inverse(blocks[:wins], high, low, 0, [])
+    return inverse(blocks[wins:], high, low, 1, [total])
 
 
 def solution(mesh):

time: 67.4 us -> 65.1 us (0.966); the launches traced: 66.2 us -> 64.8 us
  Pallas kernels: 29.9 us -> 27.9 us
  waiting for transfers between devices: 14.8 us -> 15.9 us
    pallas_call x2, Pallas kernels: 5.39 us -> 3.08 us  [by_bin(): pl.pallas_call(functools.partial(by_bin_kernel, steps=steps), out_shape=[...]
    ppermute x2, waiting for transfers between devices: 4.71 us -> 5.79 us  [per_device(): lax.ppermute(b, 'pairs', swap_b)]
    ppermute x2, waiting for transfers between devices: 1.2 us -> 0.13 us  [per_device(): lax.ppermute(a, 'pairs', swap_a)]
    ppermute x14, waiting for transfers between devices: 8.94 us -> 9.97 us  [hop(): return lax.ppermute(array, ('pairs', 'win'), pairing)]
  transfers between devices with their start and end apart: 19 -> 19, of which waited for: 5 -> 6; matrix products, arithmetic and copies ran while one was open for 1% -> 1% of each run, Pallas kernels for 32% -> 33%
where the time goes in v7:
time: 65.1 us; the launch traced here: 64.8 us
  Pallas kernels  27.9 us (43%)
  starting transfers between devices  20 us (31%)
  waiting for transfers between devices  15.9 us (24%)
    pallas_call x2, Pallas kernels, own_spectra(): pl.pallas_call(functools.partial(spectra_kernel, steps=steps, wins=len(st...  14.6 us
    ppermute x14, starting transfers between devices, hop(): return lax.ppermute(array, ('pairs', 'win'), pairing)  11.1 us
    ppermute x14, waiting for transfers between devices, hop(): return lax.ppermute(array, ('pairs', 'win'), pairing)  9.97 us
    ppermute x2, waiting for transfers between devices, per_device(): lax.ppermute(b, 'pairs', swap_b)  5.79 us
    ppermute x2, starting transfers between devices, per_device(): lax.ppermute(b, 'pairs', swap_b)  5.57 us
    pallas_call x2, Pallas kernels, inverse(): pl.pallas_call(functools.partial(inverse_kernel, far=far, wins=wins), gri...  5.57 us
    pallas_call x1, Pallas kernels, cross_products(): pl.pallas_call(cross_kernel, out_shape=[block] * wins, in_specs=[vmem] *...  3.53 us
    pallas_call x2, Pallas kernels, by_bin(): pl.pallas_call(functools.partial(by_bin_kernel, steps=steps), out_shape=[...  3.08 us
  transfers between devices with their start and end apart: 19, of which 6 were waited for; matrix products, arithmetic and copies ran while one was open for 1% of the time, Pallas kernels for 33%

profile of v7, /device:TPU:16, one launch (start us, length us, event | category | flops | bytes accessed | tf_op | source)
XLA Modules:
  0.0 64.8 jit_solution(7196651978582741520)
XLA Ops:
  0.0 0.0 collective-permute-start.5
  0.1 7.3 %own_spectra.2 = (bf16[16,32,128]{2,1,0:T(8,128)(2,1)}, bf16[16,32,128]{2,1,0:T(8,128)(2,1)}, bf16[16,32,128]{2,1,0:T(8,128)(2,1)}, bf16[16,32,128]{2,1,0:T(8,128)(2,1)}) custom-call(bf16[512,4096]{1,0:T(8,128)(2,1)} %bitcast.17, f32[1,129]{1,0:T(1,128)} %bitcast.18, f32[129,1024]{1,0:T(8,128)} %constant.116.clone.fine_hbm, ...), custom_call_target="tpu_custom_call" | custom-call | flops 2147483648 | bytes 4194304 | tf_op jit(solution)/shard_map/own_spectra/pallas_call | solution.py:167
  7.4 1.6 %collective-permute-start.11 = (s32[16,64]{1,0:T(8,128)S(1)}, s32[16,64]{1,0:T(8,128)S(1)}, u32[]{:S(2)}, u32[]{:S(2)}) collective-permute-start(s32[16,64]{1,0:T(8,128)S(1)} %fusion.3), channel_id=1, source_target_pairs={{0,4},{4,0},{8,12},{12,8},{16,20},{20,16},{24,28},{28,24},{1,5},{5... | collective-permute-start | bytes 12296 | tf_op jit(solution)/shard_map/ppermute | solution.py:405
  9.0 1.5 %collective-permute-start = (bf16[16,32,128]{2,1,0:T(8,128)(2,1)}, bf16[16,32,128]{2,1,0:T(8,128)(2,1)S(1)}, u32[]{:S(2)}, u32[]{:S(2)}) collective-permute-start(bf16[16,32,128]{2,1,0:T(8,128)(2,1)} %get-tuple-element.38), channel_id=1, source_target_pairs={{0,2},{1,3},{2,0},{3,1},{4,6},{5,7},{6,4},{7,5},{8,10},{9,11},{10,... | collective-permute-start | bytes 393224 | tf_op jit(solution)/shard_map/ppermute | solution.py:385
  10.5 0.5 collective-permute-start.1
  11.0 1.5 %collective-permute-start.2 = (bf16[16,32,128]{2,1,0:T(8,128)(2,1)}, bf16[16,32,128]{2,1,0:T(8,128)(2,1)S(1)}, u32[]{:S(2)}, u32[]{:S(2)}) collective-permute-start(bf16[16,32,128]{2,1,0:T(8,128)(2,1)} %get-tuple-element.40), channel_id=1, source_target_pairs={{0,6},{1,7},{2,4},{3,5},{4,2},{5,3},{6,0},{7,1},{8,14},{9,15},{10,... | collective-permute-start | bytes 393224 | tf_op jit(solution)/shard_map/ppermute | solution.py:385
  12.5 0.1 copy.15
  12.6 0.0 collective-permute-done.11
  12.6 0.1 copy.16
  12.7 0.1 add_select_fusion
  12.8 0.0 collective-permute-done.5.x_hbm
  12.8 7.3 %own_spectra.3 = (bf16[16,32,128]{2,1,0:T(8,128)(2,1)}, bf16[16,32,128]{2,1,0:T(8,128)(2,1)}, bf16[16,32,128]{2,1,0:T(8,128)(2,1)}, bf16[16,32,128]{2,1,0:T(8,128)(2,1)}) custom-call(bf16[512,4096]{1,0:T(8,128)(2,1)} %collective-permute-done.5.x_hbm, f32[1,129]{1,0:T(1,128)} %bitcast.19, f32[129,1024]{1,0:T(8,128)} %constant.116.clone.fine_hbm, ...), custom_call_target="tpu_custom_call" | custom-call | flops 2147483648 | bytes 4194304 | tf_op jit(solution)/shard_map/own_spectra/pallas_call | solution.py:167
  20.1 1.5 %collective-permute-start.6 = (bf16[16,32,128]{2,1,0:T(8,128)(2,1)}, bf16[16,32,128]{2,1,0:T(8,128)(2,1)S(1)}, u32[]{:S(2)}, u32[]{:S(2)}) collective-permute-start(bf16[16,32,128]{2,1,0:T(8,128)(2,1)} %get-tuple-element.45), channel_id=1, source_target_pairs={{0,2},{1,3},{2,0},{3,1},{4,6},{5,7},{6,4},{7,5},{8,10},{9,11},{10,... | collective-permute-start | bytes 393224 | tf_op jit(solution)/shard_map/ppermute | solution.py:385
  21.7 0.5 collective-permute-start.7
  22.2 0.0 collective-permute-done.refs_1_
  22.2 1.5 %collective-permute-start.8 = (bf16[16,32,128]{2,1,0:T(8,128)(2,1)}, bf16[16,32,128]{2,1,0:T(8,128)(2,1)S(1)}, u32[]{:S(2)}, u32[]{:S(2)}) collective-permute-start(bf16[16,32,128]{2,1,0:T(8,128)(2,1)} %get-tuple-element.47), channel_id=1, source_target_pairs={{0,6},{1,7},{2,4},{3,5},{4,2},{5,3},{6,0},{7,1},{8,14},{9,15},{10,... | collective-permute-start | bytes 393224 | tf_op jit(solution)/shard_map/ppermute | solution.py:385
  23.7 0.0 collective-permute-done.1.refs_2_
  23.7 0.0 collective-permute-done.2.refs_3_
  23.7 1.5 %by_bin.2 = (bf16[64,16,128]{2,1,0:T(8,128)(2,1)S(1)}, bf16[64,16,128]{2,1,0:T(8,128)(2,1)S(1)}, bf16[64,32,128]{2,1,0:T(8,128)(2,1)S(1)}) custom-call(bf16[16,32,128]{2,1,0:T(8,128)(2,1)S(1)} %copy-done.4, bf16[16,32,128]{2,1,0:T(8,128)(2,1)S(1)} %collective-permute-done.refs_1_, bf16[16,32,128]{2,1,0:T(8,128)(2,1)S(1)} %collective-permute-done.1.refs_2_, ...), custom_call_target="tpu_custom_call" | custom-call | flops 2147483648 | bytes 4194304 | tf_op jit(solution)/shard_map/by_bin/pallas_call | solution.py:256
  25.2 1.6 %collective-permute-start.3 = (bf16[64,16,128]{2,1,0:T(8,128)(2,1)S(1)}, bf16[64,16,128]{2,1,0:T(8,128)(2,1)S(1)}, u32[]{:S(2)}, u32[]{:S(2)}) collective-permute-start(bf16[64,16,128]{2,1,0:T(8,128)(2,1)S(1)} %get-tuple-element.41.refs_0_), channel_id=1, source_target_pairs={{0,8},{4,12},{8,0},{12,4},{16,24},{20,28},{24,16},{28,20},{1,9},{5... | collective-permute-start | bytes 786440 | tf_op jit(solution)/shard_map/ppermute | solution.py:425
  26.9 1.9 %collective-permute-start.4 = (bf16[64,16,128]{2,1,0:T(8,128)(2,1)S(1)}, bf16[64,16,128]{2,1,0:T(8,128)(2,1)S(1)}, u32[]{:S(2)}, u32[]{:S(2)}) collective-permute-start(bf16[64,16,128]{2,1,0:T(8,128)(2,1)S(1)} %get-tuple-element.42.refs_1_), channel_id=1, source_target_pairs={{8,16},{12,20},{16,8},{20,12},{9,17},{13,21},{17,9},{21,13},{10,18... | collective-permute-start | bytes 786440 | tf_op jit(solution)/shard_map/ppermute | solution.py:425
  28.8 0.0 collective-permute-done.6.refs_1_
  28.8 0.5 collective-permute-done.7.refs_2_
  29.3 0.0 collective-permute-done.8.refs_3_
  29.3 0.0 copy-start.2
  29.3 0.0 copy-start.3
  29.3 1.5 %by_bin.3 = (bf16[64,16,128]{2,1,0:T(8,128)(2,1)S(1)}, bf16[64,16,128]{2,1,0:T(8,128)(2,1)S(1)}, bf16[64,32,128]{2,1,0:T(8,128)(2,1)S(1)}) custom-call(bf16[16,32,128]{2,1,0:T(8,128)(2,1)S(1)} %copy-done.5, bf16[16,32,128]{2,1,0:T(8,128)(2,1)S(1)} %collective-permute-done.6.refs_1_, bf16[16,32,128]{2,1,0:T(8,128)(2,1)S(1)} %collective-permute-done.7.refs_2_, ...), custom_call_target="tpu_custom_call" | custom-call | flops 2147483648 | bytes 4194304 | tf_op jit(solution)/shard_map/by_bin/pallas_call | solution.py:256
  30.8 3.7 %collective-permute-start.10 = (bf16[64,16,128]{2,1,0:T(8,128)(2,1)S(1)}, bf16[64,16,128]{2,1,0:T(8,128)(2,1)S(1)}, u32[]{:S(2)}, u32[]{:S(2)}) collective-permute-start(bf16[64,16,128]{2,1,0:T(8,128)(2,1)S(1)} %get-tuple-element.49.refs_6_), channel_id=1, source_target_pairs={{8,16},{12,20},{16,8},{20,12},{9,17},{13,21},{17,9},{21,13},{10,18... | collective-permute-start | bytes 786440 | tf_op jit(solution)/shard_map/ppermute | solution.py:425
  34.5 0.1 collective-permute-start.9
  34.6 0.1 copy.17
  34.7 0.3 compare_convert_fusion.refs_10_
  35.0 2.3 %collective-permute-done.4.refs_4_ = bf16[64,16,128]{2,1,0:T(8,128)(2,1)S(1)} collective-permute-done((bf16[64,16,128]{2,1,0:T(8,128)(2,1)S(1)}, bf16[64,16,128]{2,1,0:T(8,128)(2,1)S(1)}, u32[]{:S(2)}, u32[]{:S(2)}) %collective-permute-start.4) | collective-permute-done | bytes 262176 | tf_op jit(solution)/shard_map/ppermute | solution.py:425
  37.3 3.5 %collective-permute-done.10.refs_9_ = bf16[64,16,128]{2,1,0:T(8,128)(2,1)S(1)} collective-permute-done((bf16[64,16,128]{2,1,0:T(8,128)(2,1)S(1)}, bf16[64,16,128]{2,1,0:T(8,128)(2,1)S(1)}, u32[]{:S(2)}, u32[]{:S(2)}) %collective-permute-start.10) | collective-permute-done | bytes 262176 | tf_op jit(solution)/shard_map/ppermute | solution.py:425
  40.8 0.1 collective-permute-done.9.refs_8_
  41.0 3.5 %cross_products.1 = (f32[2,16,16,128]{3,2,1,0:T(8,128)S(1)}, f32[2,16,16,128]{3,2,1,0:T(8,128)S(1)}, f32[2,16,16,128]{3,2,1,0:T(8,128)S(1)}, f32[2,16,16,128]{3,2,1,0:T(8,128)S(1)}) custom-call(bf16[64,16,128]{2,1,0:T(8,128)(2,1)S(1)} %get-tuple-element.41.refs_0_, bf16[64,16,128]{2,1,0:T(8,128)(2,1)S(1)} %get-tuple-element.42.refs_1_, ...), custom_call_target="tpu_custom_call" | custom-call | tf_op jit(solution)/shard_map/cross_products/pallas_call | solution.py:317
  44.5 1.5 %collective-permute-start.17 = (f32[2,16,16,128]{3,2,1,0:T(8,128)S(1)}, f32[2,16,16,128]{3,2,1,0:T(8,128)S(1)}, u32[]{:S(2)}, u32[]{:S(2)}) collective-permute-start(f32[2,16,16,128]{3,2,1,0:T(8,128)S(1)} %get-tuple-element.56), channel_id=1, source_target_pairs={{0,2},{1,3},{2,0},{3,1},{4,6},{5,7},{6,4},{7,5},{8,10},{9,11},{10,... | collective-permute-start | bytes 786440 | tf_op jit(solution)/shard_map/ppermute | solution.py:385
  46.0 0.5 collective-permute-start.12
  46.5 1.5 %collective-permute-start.14 = (f32[2,16,16,128]{3,2,1,0:T(8,128)S(1)}, f32[2,16,16,128]{3,2,1,0:T(8,128)S(1)}, u32[]{:S(2)}, u32[]{:S(2)}) collective-permute-start(f32[2,16,16,128]{3,2,1,0:T(8,128)S(1)} %get-tuple-element.54), channel_id=1, source_target_pairs={{0,6},{1,7},{2,4},{3,5},{4,2},{5,3},{6,0},{7,1},{8,14},{9,15},{10,... | collective-permute-start | bytes 786440 | tf_op jit(solution)/shard_map/ppermute | solution.py:385
  48.0 0.0 collective-permute-start.16
  48.0 5.4 %collective-permute-done.17.refs_2_ = f32[2,16,16,128]{3,2,1,0:T(8,128)S(1)} collective-permute-done((f32[2,16,16,128]{3,2,1,0:T(8,128)S(1)}, f32[2,16,16,128]{3,2,1,0:T(8,128)S(1)}, u32[]{:S(2)}, u32[]{:S(2)}) %collective-permute-start.17) | collective-permute-done | bytes 262176 | tf_op jit(solution)/shard_map/ppermute | solution.py:385
  53.5 4.1 %collective-permute-done.12.refs_0_ = f32[2,16,16,128]{3,2,1,0:T(8,128)S(1)} collective-permute-done((f32[2,16,16,128]{3,2,1,0:T(8,128)S(1)}, f32[2,16,16,128]{3,2,1,0:T(8,128)S(1)}, u32[]{:S(2)}, u32[]{:S(2)}) %collective-permute-start.12) | collective-permute-done | bytes 262176 | tf_op jit(solution)/shard_map/ppermute | solution.py:385
  57.5 0.5 collective-permute-start.15
  58.0 1.1 %lag_tables.1 = (bf16[8,128,1024]{2,1,0:T(8,128)(2,1)S(1)}, bf16[8,128,1024]{2,1,0:T(8,128)(2,1)S(1)}) custom-call(f32[64,1024]{1,0:T(8,128)S(1)} %copy-done, f32[64,1024]{1,0:T(8,128)S(1)} %copy-done.1, f32[8,1024]{1,0:T(8,128)S(1)} %copy-done.2, f32[8,1024]{1,0:T(8,128)S(1)} %copy-done.3), custom_call_target="tpu_custom_call" | custom-call | tf_op jit(solution)/shard_map/lag_tables/pallas_call | solution.py:204
  59.1 0.0 collective-permute-done.16.refs_1_
  59.1 0.0 collective-permute-done.18.refs_3_
  59.2 2.3 %inverse.2.refs_4_ = f32[16,16,1024]{2,1,0:T(8,128)S(1)} custom-call(bf16[1024,1024]{1,0:T(8,128)(2,1)S(1)} %bitcast.8, bf16[1024,1024]{1,0:T(8,128)(2,1)S(1)} %bitcast.10, f32[2,16,16,128]{3,2,1,0:T(8,128)S(1)} %get-tuple-element.55.refs_0_, f32[2,16,16,128]{3,2,1,0:T(8,128)S(1)} %collective-permute-done.16.refs_1_, ...), custom_call_target="tpu_custom_call" | custom-call | flops 2147483648 | bytes 4194304 | tf_op jit(solution)/shard_map/inverse/pallas_call | solution.py:360
  61.5 0.0 collective-permute-done.15.refs_3_
  61.5 3.2 %inverse.3 = f32[16,16,1024]{2,1,0:T(8,128)} custom-call(bf16[1024,1024]{1,0:T(8,128)(2,1)S(1)} %bitcast.9, bf16[1024,1024]{1,0:T(8,128)(2,1)S(1)} %bitcast.11, f32[2,16,16,128]{3,2,1,0:T(8,128)S(1)} %collective-permute-done.12.refs_0_, f32[2,16,16,128]{3,2,1,0:T(8,128)S(1)} %collective-permute-done.13.refs_1_, ...), custom_call_target="tpu_custom_call" | custom-call | flops 2147483648 | bytes 4194304 | tf_op jit(solution)/shard_map/inverse/pallas_call | solution.py:360
  (23 shorter events, 0.1 us)
Async XLA Ops:
  0.0 7.4 %copy-start.6 = (s32[16,64]{1,0:T(8,128)S(1)}, s32[16,64]{1,0:T(8,128)}, u32[]{:S(2)}) copy-start(s32[16,64]{1,0:T(8,128)} %param.16) | copy-start | bytes 12292
  0.0 7.4 %copy-start.7 = (s32[16,64]{1,0:T(8,128)S(1)}, s32[16,64]{1,0:T(8,128)}, u32[]{:S(2)}) copy-start(s32[16,64]{1,0:T(8,128)} %param.17) | copy-start | bytes 12292
  0.0 12.8 %collective-permute-start.5 = (bf16[512,4096]{1,0:T(8,128)(2,1)}, bf16[512,4096]{1,0:T(8,128)(2,1)}, u32[]{:S(2)}, u32[]{:S(2)}) collective-permute-start(bf16[512,4096]{1,0:T(8,128)(2,1)} %bitcast.16), channel_id=1, source_target_pairs={{0,1},{1,0},{2,3},{3,2},{4,5},{5,4},{6,7},{7,6},{8,9},{9,8},{10,11... | collective-permute-start | bytes 12582920 | tf_op jit(solution)/shard_map/ppermute | solution.py:385
  7.3 16.3 %copy-start.4 = (bf16[16,32,128]{2,1,0:T(8,128)(2,1)S(1)}, bf16[16,32,128]{2,1,0:T(8,128)(2,1)}, u32[]{:S(2)}) copy-start(bf16[16,32,128]{2,1,0:T(8,128)(2,1)} %get-tuple-element.37.refs_0_) | copy-start | bytes 393220
  7.4 5.2 %collective-permute-start.11 = (s32[16,64]{1,0:T(8,128)S(1)}, s32[16,64]{1,0:T(8,128)S(1)}, u32[]{:S(2)}, u32[]{:S(2)}) collective-permute-start(s32[16,64]{1,0:T(8,128)S(1)} %fusion.3), channel_id=1, source_target_pairs={{0,4},{4,0},{8,12},{12,8},{16,20},{20,16},{24,28},{28,24},{1,5},{5... | collective-permute-start | bytes 12296 | tf_op jit(solution)/shard_map/ppermute | solution.py:405
  9.0 13.2 %collective-permute-start = (bf16[16,32,128]{2,1,0:T(8,128)(2,1)}, bf16[16,32,128]{2,1,0:T(8,128)(2,1)S(1)}, u32[]{:S(2)}, u32[]{:S(2)}) collective-permute-start(bf16[16,32,128]{2,1,0:T(8,128)(2,1)} %get-tuple-element.38), channel_id=1, source_target_pairs={{0,2},{1,3},{2,0},{3,1},{4,6},{5,7},{6,4},{7,5},{8,10},{9,11},{10,... | collective-permute-start | bytes 393224 | tf_op jit(solution)/shard_map/ppermute | solution.py:385
  10.5 13.2 %collective-permute-start.1 = (bf16[16,32,128]{2,1,0:T(8,128)(2,1)}, bf16[16,32,128]{2,1,0:T(8,128)(2,1)S(1)}, u32[]{:S(2)}, u32[]{:S(2)}) collective-permute-start(bf16[16,32,128]{2,1,0:T(8,128)(2,1)} %get-tuple-element.39), channel_id=1, source_target_pairs={{0,4},{1,5},{2,6},{3,7},{4,0},{5,1},{6,2},{7,3},{8,12},{9,13},{10,... | collective-permute-start | bytes 393224 | tf_op jit(solution)/shard_map/ppermute | solution.py:385
  11.0 12.7 %collective-permute-start.2 = (bf16[16,32,128]{2,1,0:T(8,128)(2,1)}, bf16[16,32,128]{2,1,0:T(8,128)(2,1)S(1)}, u32[]{:S(2)}, u32[]{:S(2)}) collective-permute-start(bf16[16,32,128]{2,1,0:T(8,128)(2,1)} %get-tuple-element.40), channel_id=1, source_target_pairs={{0,6},{1,7},{2,4},{3,5},{4,2},{5,3},{6,0},{7,1},{8,14},{9,15},{10,... | collective-permute-start | bytes 393224 | tf_op jit(solution)/shard_map/ppermute | solution.py:385
  20.1 9.2 %copy-start.5 = (bf16[16,32,128]{2,1,0:T(8,128)(2,1)S(1)}, bf16[16,32,128]{2,1,0:T(8,128)(2,1)}, u32[]{:S(2)}) copy-start(bf16[16,32,128]{2,1,0:T(8,128)(2,1)} %get-tuple-element.44.refs_0_) | copy-start | bytes 393220
  20.1 8.7 %collective-permute-start.6 = (bf16[16,32,128]{2,1,0:T(8,128)(2,1)}, bf16[16,32,128]{2,1,0:T(8,128)(2,1)S(1)}, u32[]{:S(2)}, u32[]{:S(2)}) collective-permute-start(bf16[16,32,128]{2,1,0:T(8,128)(2,1)} %get-tuple-element.45), channel_id=1, source_target_pairs={{0,2},{1,3},{2,0},{3,1},{4,6},{5,7},{6,4},{7,5},{8,10},{9,11},{10,... | collective-permute-start | bytes 393224 | tf_op jit(solution)/shard_map/ppermute | solution.py:385
  21.7 7.6 %collective-permute-start.7 = (bf16[16,32,128]{2,1,0:T(8,128)(2,1)}, bf16[16,32,128]{2,1,0:T(8,128)(2,1)S(1)}, u32[]{:S(2)}, u32[]{:S(2)}) collective-permute-start(bf16[16,32,128]{2,1,0:T(8,128)(2,1)} %get-tuple-element.46), channel_id=1, source_target_pairs={{0,4},{1,5},{2,6},{3,7},{4,0},{5,1},{6,2},{7,3},{8,12},{9,13},{10,... | collective-permute-start | bytes 393224 | tf_op jit(solution)/shard_map/ppermute | solution.py:385
  22.2 7.1 %collective-permute-start.8 = (bf16[16,32,128]{2,1,0:T(8,128)(2,1)}, bf16[16,32,128]{2,1,0:T(8,128)(2,1)S(1)}, u32[]{:S(2)}, u32[]{:S(2)}) collective-permute-start(bf16[16,32,128]{2,1,0:T(8,128)(2,1)} %get-tuple-element.47), channel_id=1, source_target_pairs={{0,6},{1,7},{2,4},{3,5},{4,2},{5,3},{6,0},{7,1},{8,14},{9,15},{10,... | collective-permute-start | bytes 393224 | tf_op jit(solution)/shard_map/ppermute | solution.py:385
  25.2 9.8 %collective-permute-start.3 = (bf16[64,16,128]{2,1,0:T(8,128)(2,1)S(1)}, bf16[64,16,128]{2,1,0:T(8,128)(2,1)S(1)}, u32[]{:S(2)}, u32[]{:S(2)}) collective-permute-start(bf16[64,16,128]{2,1,0:T(8,128)(2,1)S(1)} %get-tuple-element.41.refs_0_), channel_id=1, source_target_pairs={{0,8},{4,12},{8,0},{12,4},{16,24},{20,28},{24,16},{28,20},{1,9},{5... | collective-permute-start | bytes 786440 | tf_op jit(solution)/shard_map/ppermute | solution.py:425
  26.9 10.4 %collective-permute-start.4 = (bf16[64,16,128]{2,1,0:T(8,128)(2,1)S(1)}, bf16[64,16,128]{2,1,0:T(8,128)(2,1)S(1)}, u32[]{:S(2)}, u32[]{:S(2)}) collective-permute-start(bf16[64,16,128]{2,1,0:T(8,128)(2,1)S(1)} %get-tuple-element.42.refs_1_), channel_id=1, source_target_pairs={{8,16},{12,20},{16,8},{20,12},{9,17},{13,21},{17,9},{21,13},{10,18... | collective-permute-start | bytes 786440 | tf_op jit(solution)/shard_map/ppermute | solution.py:425
  29.3 28.8 %copy-start = (f32[64,1024]{1,0:T(8,128)S(1)}, f32[64,1024]{1,0:T(8,128)}, u32[]{:S(2)}) copy-start(f32[64,1024]{1,0:T(8,128)} %constant.119.clone.cos_ref) | copy-start | bytes 786436
  29.3 28.8 %copy-start.2 = (f32[8,1024]{1,0:T(8,128)S(1)}, f32[8,1024]{1,0:T(8,128)}, u32[]{:S(2)}) copy-start(f32[8,1024]{1,0:T(8,128)} %constant.121.clone.cos0_ref) | copy-start | bytes 98308
  29.3 28.7 %copy-start.3 = (f32[8,1024]{1,0:T(8,128)S(1)}, f32[8,1024]{1,0:T(8,128)}, u32[]{:S(2)}) copy-start(f32[8,1024]{1,0:T(8,128)} %constant.122.clone.msin0_ref) | copy-start | bytes 98308
  30.8 10.0 %collective-permute-start.10 = (bf16[64,16,128]{2,1,0:T(8,128)(2,1)S(1)}, bf16[64,16,128]{2,1,0:T(8,128)(2,1)S(1)}, u32[]{:S(2)}, u32[]{:S(2)}) collective-permute-start(bf16[64,16,128]{2,1,0:T(8,128)(2,1)S(1)} %get-tuple-element.49.refs_6_), channel_id=1, source_target_pairs={{8,16},{12,20},{16,8},{20,12},{9,17},{13,21},{17,9},{21,13},{10,18... | collective-permute-start | bytes 786440 | tf_op jit(solution)/shard_map/ppermute | solution.py:425
  34.5 6.4 %collective-permute-start.9 = (bf16[64,16,128]{2,1,0:T(8,128)(2,1)S(1)}, bf16[64,16,128]{2,1,0:T(8,128)(2,1)S(1)}, u32[]{:S(2)}, u32[]{:S(2)}) collective-permute-start(bf16[64,16,128]{2,1,0:T(8,128)(2,1)S(1)} %get-tuple-element.48.refs_5_), channel_id=1, source_target_pairs={{0,8},{4,12},{8,0},{12,4},{16,24},{20,28},{24,16},{28,20},{1,9},{5... | collective-permute-start | bytes 786440 | tf_op jit(solution)/shard_map/ppermute | solution.py:425
  34.7 23.4 %copy-start.1 = (f32[64,1024]{1,0:T(8,128)S(1)}, f32[64,1024]{1,0:T(8,128)}, u32[]{:S(2)}) copy-start(f32[64,1024]{1,0:T(8,128)} %constant.120.clone.msin_ref) | copy-start | bytes 786436
  44.5 9.0 %collective-permute-start.17 = (f32[2,16,16,128]{3,2,1,0:T(8,128)S(1)}, f32[2,16,16,128]{3,2,1,0:T(8,128)S(1)}, u32[]{:S(2)}, u32[]{:S(2)}) collective-permute-start(f32[2,16,16,128]{3,2,1,0:T(8,128)S(1)} %get-tuple-element.56), channel_id=1, source_target_pairs={{0,2},{1,3},{2,0},{3,1},{4,6},{5,7},{6,4},{7,5},{8,10},{9,11},{10,... | collective-permute-start | bytes 786440 | tf_op jit(solution)/shard_map/ppermute | solution.py:385
  46.0 11.5 %collective-permute-start.12 = (f32[2,16,16,128]{3,2,1,0:T(8,128)S(1)}, f32[2,16,16,128]{3,2,1,0:T(8,128)S(1)}, u32[]{:S(2)}, u32[]{:S(2)}) collective-permute-start(f32[2,16,16,128]{3,2,1,0:T(8,128)S(1)} %get-tuple-element.53), channel_id=1, source_target_pairs={{0,4},{1,5},{2,6},{3,7},{4,0},{5,1},{6,2},{7,3},{8,12},{9,13},{10,... | collective-permute-start | bytes 786440 | tf_op jit(solution)/shard_map/ppermute | solution.py:385
  46.5 11.0 %collective-permute-start.14 = (f32[2,16,16,128]{3,2,1,0:T(8,128)S(1)}, f32[2,16,16,128]{3,2,1,0:T(8,128)S(1)}, u32[]{:S(2)}, u32[]{:S(2)}) collective-permute-start(f32[2,16,16,128]{3,2,1,0:T(8,128)S(1)} %get-tuple-element.54), channel_id=1, source_target_pairs={{0,6},{1,7},{2,4},{3,5},{4,2},{5,3},{6,0},{7,1},{8,14},{9,15},{10,... | collective-permute-start | bytes 786440 | tf_op jit(solution)/shard_map/ppermute | solution.py:385
  48.0 11.1 %collective-permute-start.16 = (f32[2,16,16,128]{3,2,1,0:T(8,128)S(1)}, f32[2,16,16,128]{3,2,1,0:T(8,128)S(1)}, u32[]{:S(2)}, u32[]{:S(2)}) collective-permute-start(f32[2,16,16,128]{3,2,1,0:T(8,128)S(1)} %get-tuple-element.55.refs_0_), channel_id=1, source_target_pairs={{0,1},{1,0},{2,3},{3,2},{4,5},{5,4},{6,7},{7,6},{8,9},{9,8},{10,11... | collective-permute-start | bytes 786440 | tf_op jit(solution)/shard_map/ppermute | solution.py:385
  53.5 5.7 %collective-permute-start.18 = (f32[2,16,16,128]{3,2,1,0:T(8,128)S(1)}, f32[2,16,16,128]{3,2,1,0:T(8,128)S(1)}, u32[]{:S(2)}, u32[]{:S(2)}) collective-permute-start(f32[2,16,16,128]{3,2,1,0:T(8,128)S(1)} %collective-permute-done.17.refs_2_), channel_id=1, source_target_pairs={{0,1},{1,0},{2,3},{3,2},{4,5},{5,4},{6,7},{7,6},{8,9},{9,8},{10,11... | collective-permute-start | bytes 786440 | tf_op jit(solution)/shard_map/ppermute | solution.py:385
  57.5 4.0 %collective-permute-start.13 = (f32[2,16,16,128]{3,2,1,0:T(8,128)S(1)}, f32[2,16,16,128]{3,2,1,0:T(8,128)S(1)}, u32[]{:S(2)}, u32[]{:S(2)}) collective-permute-start(f32[2,16,16,128]{3,2,1,0:T(8,128)S(1)} %collective-permute-done.12.refs_0_), channel_id=1, source_target_pairs={{0,1},{1,0},{2,3},{3,2},{4,5},{5,4},{6,7},{7,6},{8,9},{9,8},{10,11... | collective-permute-start | bytes 786440 | tf_op jit(solution)/shard_map/ppermute | solution.py:385
  57.5 4.0 %collective-permute-start.15 = (f32[2,16,16,128]{3,2,1,0:T(8,128)S(1)}, f32[2,16,16,128]{3,2,1,0:T(8,128)S(1)}, u32[]{:S(2)}, u32[]{:S(2)}) collective-permute-start(f32[2,16,16,128]{3,2,1,0:T(8,128)S(1)} %collective-permute-done.14.refs_2_), channel_id=1, source_target_pairs={{0,1},{1,0},{2,3},{3,2},{4,5},{5,4},{6,7},{7,6},{8,9},{9,8},{10,11... | collective-permute-start | bytes 786440 | tf_op jit(solution)/shard_map/ppermute | solution.py:385

commit v8 on v7

--- a/solution.py
+++ b/solution.py
@@ -424,9 +424,11 @@
         a, b, turned = by_bin(blocks)
         halves.append((a, b, turned, lax.ppermute(a, "pairs", swap_a), lax.ppermute(b, "pairs", swap_b)))
     stack = cross_products(halves, select, wins)
-    blocks = within_chip(between_chips(stack))
-    total = inverse(blocks[:wins], high, low, 0, [])
-    return inverse(blocks[wins:], high, low, 1, [total])
+    moved = between_chips(stack)
+    near, far = moved[: wins // 2], moved[wins // 2 :]
+    near, high, low = lax.optimization_barrier((near, high, low))
+    total = inverse(within_chip(near), high, low, 0, [])
+    return inverse(within_chip(far), high, low, 1, [total])
 
 
 def solution(mesh):

time: 65.1 us -> 64 us (0.983)
  waiting for transfers between devices: 15.9 us -> 14.3 us
    ppermute x14, waiting for transfers between devices: 9.97 us -> 8.35 us  [hop(): return lax.ppermute(array, ('pairs', 'win'), pairing)]
where the time goes in v8:
time: 64 us; the launch traced here: 63.6 us
  Pallas kernels  27.9 us (44%)
  starting transfers between devices  20.5 us (32%)
  waiting for transfers between devices  14.3 us (22%)
    pallas_call x2, Pallas kernels, own_spectra(): pl.pallas_call(functools.partial(spectra_kernel, steps=steps, wins=len(st...  14.6 us
    ppermute x14, starting transfers between devices, hop(): return lax.ppermute(array, ('pairs', 'win'), pairing)  11.6 us
    ppermute x14, waiting for transfers between devices, hop(): return lax.ppermute(array, ('pairs', 'win'), pairing)  8.35 us
    ppermute x2, waiting for transfers between devices, per_device(): lax.ppermute(b, 'pairs', swap_b)  5.79 us
    ppermute x2, starting transfers between devices, per_device(): lax.ppermute(b, 'pairs', swap_b)  5.57 us
    pallas_call x2, Pallas kernels, inverse(): pl.pallas_call(functools.partial(inverse_kernel, far=far, wins=wins), gri...  5.56 us
    pallas_call x1, Pallas kernels, cross_products(): pl.pallas_call(cross_kernel, out_shape=[block] * wins, in_specs=[vmem] *...  3.53 us
    pallas_call x2, Pallas kernels, by_bin(): pl.pallas_call(functools.partial(by_bin_kernel, steps=steps), out_shape=[...  3.08 us
  transfers between devices with their start and end apart: 19, of which 6 were waited for; matrix products, arithmetic and copies ran while one was open for 1% of the time, Pallas kernels for 33%

profile of v8, /device:TPU:16, one launch (start us, length us, event | category | flops | bytes accessed | tf_op | source)
XLA Modules:
  0.0 63.6 jit_solution(10581445832165945564)
XLA Ops:
  0.0 0.0 collective-permute-start.5
  0.1 7.3 %own_spectra.2 = (bf16[16,32,128]{2,1,0:T(8,128)(2,1)}, bf16[16,32,128]{2,1,0:T(8,128)(2,1)}, bf16[16,32,128]{2,1,0:T(8,128)(2,1)}, bf16[16,32,128]{2,1,0:T(8,128)(2,1)}) custom-call(bf16[512,4096]{1,0:T(8,128)(2,1)} %bitcast.17, f32[1,129]{1,0:T(1,128)} %bitcast.18, f32[129,1024]{1,0:T(8,128)} %constant.116.clone.fine_hbm, ...), custom_call_target="tpu_custom_call" | custom-call | flops 2147483648 | bytes 4194304 | tf_op jit(solution)/shard_map/own_spectra/pallas_call | solution.py:167
  7.4 1.6 %collective-permute-start.11 = (s32[16,64]{1,0:T(8,128)S(1)}, s32[16,64]{1,0:T(8,128)S(1)}, u32[]{:S(2)}, u32[]{:S(2)}) collective-permute-start(s32[16,64]{1,0:T(8,128)S(1)} %fusion.3), channel_id=1, source_target_pairs={{0,4},{4,0},{8,12},{12,8},{16,20},{20,16},{24,28},{28,24},{1,5},{5... | collective-permute-start | bytes 12296 | tf_op jit(solution)/shard_map/ppermute | solution.py:405
  9.0 1.5 %collective-permute-start = (bf16[16,32,128]{2,1,0:T(8,128)(2,1)}, bf16[16,32,128]{2,1,0:T(8,128)(2,1)S(1)}, u32[]{:S(2)}, u32[]{:S(2)}) collective-permute-start(bf16[16,32,128]{2,1,0:T(8,128)(2,1)} %get-tuple-element.40), channel_id=1, source_target_pairs={{0,2},{1,3},{2,0},{3,1},{4,6},{5,7},{6,4},{7,5},{8,10},{9,11},{10,... | collective-permute-start | bytes 393224 | tf_op jit(solution)/shard_map/ppermute | solution.py:385
  10.5 0.5 collective-permute-start.1
  11.0 1.5 %collective-permute-start.2 = (bf16[16,32,128]{2,1,0:T(8,128)(2,1)}, bf16[16,32,128]{2,1,0:T(8,128)(2,1)S(1)}, u32[]{:S(2)}, u32[]{:S(2)}) collective-permute-start(bf16[16,32,128]{2,1,0:T(8,128)(2,1)} %get-tuple-element.42), channel_id=1, source_target_pairs={{0,6},{1,7},{2,4},{3,5},{4,2},{5,3},{6,0},{7,1},{8,14},{9,15},{10,... | collective-permute-start | bytes 393224 | tf_op jit(solution)/shard_map/ppermute | solution.py:385
  12.5 0.1 copy.15
  12.6 0.0 collective-permute-done.11
  12.6 0.1 copy.16
  12.7 0.1 add_select_fusion
  12.8 0.0 collective-permute-done.5.x_hbm
  12.8 7.3 %own_spectra.3 = (bf16[16,32,128]{2,1,0:T(8,128)(2,1)}, bf16[16,32,128]{2,1,0:T(8,128)(2,1)}, bf16[16,32,128]{2,1,0:T(8,128)(2,1)}, bf16[16,32,128]{2,1,0:T(8,128)(2,1)}) custom-call(bf16[512,4096]{1,0:T(8,128)(2,1)} %collective-permute-done.5.x_hbm, f32[1,129]{1,0:T(1,128)} %bitcast.19, f32[129,1024]{1,0:T(8,128)} %constant.116.clone.fine_hbm, ...), custom_call_target="tpu_custom_call" | custom-call | flops 2147483648 | bytes 4194304 | tf_op jit(solution)/shard_map/own_spectra/pallas_call | solution.py:167
  20.1 1.5 %collective-permute-start.6 = (bf16[16,32,128]{2,1,0:T(8,128)(2,1)}, bf16[16,32,128]{2,1,0:T(8,128)(2,1)S(1)}, u32[]{:S(2)}, u32[]{:S(2)}) collective-permute-start(bf16[16,32,128]{2,1,0:T(8,128)(2,1)} %get-tuple-element.47), channel_id=1, source_target_pairs={{0,2},{1,3},{2,0},{3,1},{4,6},{5,7},{6,4},{7,5},{8,10},{9,11},{10,... | collective-permute-start | bytes 393224 | tf_op jit(solution)/shard_map/ppermute | solution.py:385
  21.7 0.5 collective-permute-start.7
  22.2 0.0 collective-permute-done.refs_1_
  22.2 1.5 %collective-permute-start.8 = (bf16[16,32,128]{2,1,0:T(8,128)(2,1)}, bf16[16,32,128]{2,1,0:T(8,128)(2,1)S(1)}, u32[]{:S(2)}, u32[]{:S(2)}) collective-permute-start(bf16[16,32,128]{2,1,0:T(8,128)(2,1)} %get-tuple-element.49), channel_id=1, source_target_pairs={{0,6},{1,7},{2,4},{3,5},{4,2},{5,3},{6,0},{7,1},{8,14},{9,15},{10,... | collective-permute-start | bytes 393224 | tf_op jit(solution)/shard_map/ppermute | solution.py:385
  23.7 0.0 collective-permute-done.1.refs_2_
  23.7 0.0 collective-permute-done.2.refs_3_
  23.7 1.5 %by_bin.2 = (bf16[64,16,128]{2,1,0:T(8,128)(2,1)S(1)}, bf16[64,16,128]{2,1,0:T(8,128)(2,1)S(1)}, bf16[64,32,128]{2,1,0:T(8,128)(2,1)S(1)}) custom-call(bf16[16,32,128]{2,1,0:T(8,128)(2,1)S(1)} %copy-done.4, bf16[16,32,128]{2,1,0:T(8,128)(2,1)S(1)} %collective-permute-done.refs_1_, bf16[16,32,128]{2,1,0:T(8,128)(2,1)S(1)} %collective-permute-done.1.refs_2_, ...), custom_call_target="tpu_custom_call" | custom-call | flops 2147483648 | bytes 4194304 | tf_op jit(solution)/shard_map/by_bin/pallas_call | solution.py:256
  25.2 1.6 %collective-permute-start.3 = (bf16[64,16,128]{2,1,0:T(8,128)(2,1)S(1)}, bf16[64,16,128]{2,1,0:T(8,128)(2,1)S(1)}, u32[]{:S(2)}, u32[]{:S(2)}) collective-permute-start(bf16[64,16,128]{2,1,0:T(8,128)(2,1)S(1)} %get-tuple-element.43.refs_0_), channel_id=1, source_target_pairs={{0,8},{4,12},{8,0},{12,4},{16,24},{20,28},{24,16},{28,20},{1,9},{5... | collective-permute-start | bytes 786440 | tf_op jit(solution)/shard_map/ppermute | solution.py:425
  26.9 1.9 %collective-permute-start.4 = (bf16[64,16,128]{2,1,0:T(8,128)(2,1)S(1)}, bf16[64,16,128]{2,1,0:T(8,128)(2,1)S(1)}, u32[]{:S(2)}, u32[]{:S(2)}) collective-permute-start(bf16[64,16,128]{2,1,0:T(8,128)(2,1)S(1)} %get-tuple-element.44.refs_1_), channel_id=1, source_target_pairs={{8,16},{12,20},{16,8},{20,12},{9,17},{13,21},{17,9},{21,13},{10,18... | collective-permute-start | bytes 786440 | tf_op jit(solution)/shard_map/ppermute | solution.py:425
  28.8 0.0 collective-permute-done.6.refs_1_
  28.8 0.5 collective-permute-done.7.refs_2_
  29.3 0.0 collective-permute-done.8.refs_3_
  29.3 0.0 copy-start.2
  29.3 0.0 copy-start.3
  29.3 1.5 %by_bin.3 = (bf16[64,16,128]{2,1,0:T(8,128)(2,1)S(1)}, bf16[64,16,128]{2,1,0:T(8,128)(2,1)S(1)}, bf16[64,32,128]{2,1,0:T(8,128)(2,1)S(1)}) custom-call(bf16[16,32,128]{2,1,0:T(8,128)(2,1)S(1)} %copy-done.5, bf16[16,32,128]{2,1,0:T(8,128)(2,1)S(1)} %collective-permute-done.6.refs_1_, bf16[16,32,128]{2,1,0:T(8,128)(2,1)S(1)} %collective-permute-done.7.refs_2_, ...), custom_call_target="tpu_custom_call" | custom-call | flops 2147483648 | bytes 4194304 | tf_op jit(solution)/shard_map/by_bin/pallas_call | solution.py:256
  30.8 3.7 %collective-permute-start.10 = (bf16[64,16,128]{2,1,0:T(8,128)(2,1)S(1)}, bf16[64,16,128]{2,1,0:T(8,128)(2,1)S(1)}, u32[]{:S(2)}, u32[]{:S(2)}) collective-permute-start(bf16[64,16,128]{2,1,0:T(8,128)(2,1)S(1)} %get-tuple-element.51.refs_6_), channel_id=1, source_target_pairs={{8,16},{12,20},{16,8},{20,12},{9,17},{13,21},{17,9},{21,13},{10,18... | collective-permute-start | bytes 786440 | tf_op jit(solution)/shard_map/ppermute | solution.py:425
  34.5 0.1 collective-permute-start.9
  34.6 0.1 copy.17
  34.7 0.3 compare_convert_fusion.refs_10_
  35.0 0.0 collective-permute-done.3.refs_3_
  35.0 2.3 %collective-permute-done.4.refs_4_ = bf16[64,16,128]{2,1,0:T(8,128)(2,1)S(1)} collective-permute-done((bf16[64,16,128]{2,1,0:T(8,128)(2,1)S(1)}, bf16[64,16,128]{2,1,0:T(8,128)(2,1)S(1)}, u32[]{:S(2)}, u32[]{:S(2)}) %collective-permute-start.4) | collective-permute-done | bytes 262176 | tf_op jit(solution)/shard_map/ppermute | solution.py:425
  37.3 3.5 %collective-permute-done.10.refs_9_ = bf16[64,16,128]{2,1,0:T(8,128)(2,1)S(1)} collective-permute-done((bf16[64,16,128]{2,1,0:T(8,128)(2,1)S(1)}, bf16[64,16,128]{2,1,0:T(8,128)(2,1)S(1)}, u32[]{:S(2)}, u32[]{:S(2)}) %collective-permute-start.10) | collective-permute-done | bytes 262176 | tf_op jit(solution)/shard_map/ppermute | solution.py:425
  40.8 0.1 collective-permute-done.9.refs_8_
  41.0 3.5 %cross_products.1 = (f32[2,16,16,128]{3,2,1,0:T(8,128)S(1)}, f32[2,16,16,128]{3,2,1,0:T(8,128)S(1)}, f32[2,16,16,128]{3,2,1,0:T(8,128)S(1)}, f32[2,16,16,128]{3,2,1,0:T(8,128)S(1)}) custom-call(bf16[64,16,128]{2,1,0:T(8,128)(2,1)S(1)} %get-tuple-element.43.refs_0_, bf16[64,16,128]{2,1,0:T(8,128)(2,1)S(1)} %get-tuple-element.44.refs_1_, ...), custom_call_target="tpu_custom_call" | custom-call | tf_op jit(solution)/shard_map/cross_products/pallas_call | solution.py:317
  44.5 1.5 %collective-permute-start.12 = (f32[2,16,16,128]{3,2,1,0:T(8,128)S(1)}, f32[2,16,16,128]{3,2,1,0:T(8,128)S(1)}, u32[]{:S(2)}, u32[]{:S(2)}) collective-permute-start(f32[2,16,16,128]{3,2,1,0:T(8,128)S(1)} %get-tuple-element.56), channel_id=1, source_target_pairs={{0,2},{1,3},{2,0},{3,1},{4,6},{5,7},{6,4},{7,5},{8,10},{9,11},{10,... | collective-permute-start | bytes 786440 | tf_op jit(solution)/shard_map/ppermute | solution.py:385
  46.0 0.5 collective-permute-start.13
  46.5 1.5 %collective-permute-start.15 = (f32[2,16,16,128]{3,2,1,0:T(8,128)S(1)}, f32[2,16,16,128]{3,2,1,0:T(8,128)S(1)}, u32[]{:S(2)}, u32[]{:S(2)}) collective-permute-start(f32[2,16,16,128]{3,2,1,0:T(8,128)S(1)} %get-tuple-element.62), channel_id=1, source_target_pairs={{0,6},{1,7},{2,4},{3,5},{4,2},{5,3},{6,0},{7,1},{8,14},{9,15},{10,... | collective-permute-start | bytes 786440 | tf_op jit(solution)/shard_map/ppermute | solution.py:385
  48.0 1.1 %lag_tables.1 = (bf16[8,128,1024]{2,1,0:T(8,128)(2,1)S(1)}, bf16[8,128,1024]{2,1,0:T(8,128)(2,1)S(1)}) custom-call(f32[64,1024]{1,0:T(8,128)S(1)} %copy-done, f32[64,1024]{1,0:T(8,128)S(1)} %copy-done.1, f32[8,1024]{1,0:T(8,128)S(1)} %copy-done.2, f32[8,1024]{1,0:T(8,128)S(1)} %copy-done.3), custom_call_target="tpu_custom_call" | custom-call | tf_op jit(solution)/shard_map/lag_tables/pallas_call | solution.py:204
  49.1 4.3 %collective-permute-done.12.refs_2_ = f32[2,16,16,128]{3,2,1,0:T(8,128)S(1)} collective-permute-done((f32[2,16,16,128]{3,2,1,0:T(8,128)S(1)}, f32[2,16,16,128]{3,2,1,0:T(8,128)S(1)}, u32[]{:S(2)}, u32[]{:S(2)}) %collective-permute-start.12) | collective-permute-done | bytes 262176 | tf_op jit(solution)/shard_map/ppermute | solution.py:385
  53.5 0.0 collective-permute-start.17
  53.5 0.5 collective-permute-start.18
  54.0 3.5 %collective-permute-done.13.refs_0_ = f32[2,16,16,128]{3,2,1,0:T(8,128)S(1)} collective-permute-done((f32[2,16,16,128]{3,2,1,0:T(8,128)S(1)}, f32[2,16,16,128]{3,2,1,0:T(8,128)S(1)}, u32[]{:S(2)}, u32[]{:S(2)}) %collective-permute-start.13) | collective-permute-done | bytes 262176 | tf_op jit(solution)/shard_map/ppermute | solution.py:385
  57.5 0.5 collective-permute-start.16
  58.0 2.3 %inverse.2.refs_4_ = f32[16,16,1024]{2,1,0:T(8,128)S(1)} custom-call(bf16[1024,1024]{1,0:T(8,128)(2,1)S(1)} %bitcast.8, bf16[1024,1024]{1,0:T(8,128)(2,1)S(1)} %bitcast.10, f32[2,16,16,128]{3,2,1,0:T(8,128)S(1)} %get-tuple-element.63.refs_0_, f32[2,16,16,128]{3,2,1,0:T(8,128)S(1)} %collective-permute-done.17.refs_1_, ...), custom_call_target="tpu_custom_call" | custom-call | flops 2147483648 | bytes 4194304 | tf_op jit(solution)/shard_map/inverse/pallas_call | solution.py:360
  60.4 0.0 collective-permute-done.14.refs_1_
  60.4 3.2 %inverse.3 = f32[16,16,1024]{2,1,0:T(8,128)} custom-call(bf16[1024,1024]{1,0:T(8,128)(2,1)S(1)} %bitcast.9, bf16[1024,1024]{1,0:T(8,128)(2,1)S(1)} %bitcast.11, f32[2,16,16,128]{3,2,1,0:T(8,128)S(1)} %collective-permute-done.13.refs_0_, f32[2,16,16,128]{3,2,1,0:T(8,128)S(1)} %collective-permute-done.14.refs_1_, ...), custom_call_target="tpu_custom_call" | custom-call | flops 2147483648 | bytes 4194304 | tf_op jit(solution)/shard_map/inverse/pallas_call | solution.py:360
  (23 shorter events, 0.1 us)
Async XLA Ops:
  0.0 7.4 %copy-start.6 = (s32[16,64]{1,0:T(8,128)S(1)}, s32[16,64]{1,0:T(8,128)}, u32[]{:S(2)}) copy-start(s32[16,64]{1,0:T(8,128)} %param.16) | copy-start | bytes 12292
  0.0 7.4 %copy-start.7 = (s32[16,64]{1,0:T(8,128)S(1)}, s32[16,64]{1,0:T(8,128)}, u32[]{:S(2)}) copy-start(s32[16,64]{1,0:T(8,128)} %param.17) | copy-start | bytes 12292
  0.0 12.8 %collective-permute-start.5 = (bf16[512,4096]{1,0:T(8,128)(2,1)}, bf16[512,4096]{1,0:T(8,128)(2,1)}, u32[]{:S(2)}, u32[]{:S(2)}) collective-permute-start(bf16[512,4096]{1,0:T(8,128)(2,1)} %bitcast.16), channel_id=1, source_target_pairs={{0,1},{1,0},{2,3},{3,2},{4,5},{5,4},{6,7},{7,6},{8,9},{9,8},{10,11... | collective-permute-start | bytes 12582920 | tf_op jit(solution)/shard_map/ppermute | solution.py:385
  7.3 16.3 %copy-start.4 = (bf16[16,32,128]{2,1,0:T(8,128)(2,1)S(1)}, bf16[16,32,128]{2,1,0:T(8,128)(2,1)}, u32[]{:S(2)}) copy-start(bf16[16,32,128]{2,1,0:T(8,128)(2,1)} %get-tuple-element.39.refs_0_) | copy-start | bytes 393220
  7.4 5.2 %collective-permute-start.11 = (s32[16,64]{1,0:T(8,128)S(1)}, s32[16,64]{1,0:T(8,128)S(1)}, u32[]{:S(2)}, u32[]{:S(2)}) collective-permute-start(s32[16,64]{1,0:T(8,128)S(1)} %fusion.3), channel_id=1, source_target_pairs={{0,4},{4,0},{8,12},{12,8},{16,20},{20,16},{24,28},{28,24},{1,5},{5... | collective-permute-start | bytes 12296 | tf_op jit(solution)/shard_map/ppermute | solution.py:405
  9.0 13.2 %collective-permute-start = (bf16[16,32,128]{2,1,0:T(8,128)(2,1)}, bf16[16,32,128]{2,1,0:T(8,128)(2,1)S(1)}, u32[]{:S(2)}, u32[]{:S(2)}) collective-permute-start(bf16[16,32,128]{2,1,0:T(8,128)(2,1)} %get-tuple-element.40), channel_id=1, source_target_pairs={{0,2},{1,3},{2,0},{3,1},{4,6},{5,7},{6,4},{7,5},{8,10},{9,11},{10,... | collective-permute-start | bytes 393224 | tf_op jit(solution)/shard_map/ppermute | solution.py:385
  10.5 13.2 %collective-permute-start.1 = (bf16[16,32,128]{2,1,0:T(8,128)(2,1)}, bf16[16,32,128]{2,1,0:T(8,128)(2,1)S(1)}, u32[]{:S(2)}, u32[]{:S(2)}) collective-permute-start(bf16[16,32,128]{2,1,0:T(8,128)(2,1)} %get-tuple-element.41), channel_id=1, source_target_pairs={{0,4},{1,5},{2,6},{3,7},{4,0},{5,1},{6,2},{7,3},{8,12},{9,13},{10,... | collective-permute-start | bytes 393224 | tf_op jit(solution)/shard_map/ppermute | solution.py:385
  11.0 12.7 %collective-permute-start.2 = (bf16[16,32,128]{2,1,0:T(8,128)(2,1)}, bf16[16,32,128]{2,1,0:T(8,128)(2,1)S(1)}, u32[]{:S(2)}, u32[]{:S(2)}) collective-permute-start(bf16[16,32,128]{2,1,0:T(8,128)(2,1)} %get-tuple-element.42), channel_id=1, source_target_pairs={{0,6},{1,7},{2,4},{3,5},{4,2},{5,3},{6,0},{7,1},{8,14},{9,15},{10,... | collective-permute-start | bytes 393224 | tf_op jit(solution)/shard_map/ppermute | solution.py:385
  20.1 9.2 %copy-start.5 = (bf16[16,32,128]{2,1,0:T(8,128)(2,1)S(1)}, bf16[16,32,128]{2,1,0:T(8,128)(2,1)}, u32[]{:S(2)}) copy-start(bf16[16,32,128]{2,1,0:T(8,128)(2,1)} %get-tuple-element.46.refs_0_) | copy-start | bytes 393220
  20.1 8.7 %collective-permute-start.6 = (bf16[16,32,128]{2,1,0:T(8,128)(2,1)}, bf16[16,32,128]{2,1,0:T(8,128)(2,1)S(1)}, u32[]{:S(2)}, u32[]{:S(2)}) collective-permute-start(bf16[16,32,128]{2,1,0:T(8,128)(2,1)} %get-tuple-element.47), channel_id=1, source_target_pairs={{0,2},{1,3},{2,0},{3,1},{4,6},{5,7},{6,4},{7,5},{8,10},{9,11},{10,... | collective-permute-start | bytes 393224 | tf_op jit(solution)/shard_map/ppermute | solution.py:385
  21.7 7.6 %collective-permute-start.7 = (bf16[16,32,128]{2,1,0:T(8,128)(2,1)}, bf16[16,32,128]{2,1,0:T(8,128)(2,1)S(1)}, u32[]{:S(2)}, u32[]{:S(2)}) collective-permute-start(bf16[16,32,128]{2,1,0:T(8,128)(2,1)} %get-tuple-element.48), channel_id=1, source_target_pairs={{0,4},{1,5},{2,6},{3,7},{4,0},{5,1},{6,2},{7,3},{8,12},{9,13},{10,... | collective-permute-start | bytes 393224 | tf_op jit(solution)/shard_map/ppermute | solution.py:385
  22.2 7.1 %collective-permute-start.8 = (bf16[16,32,128]{2,1,0:T(8,128)(2,1)}, bf16[16,32,128]{2,1,0:T(8,128)(2,1)S(1)}, u32[]{:S(2)}, u32[]{:S(2)}) collective-permute-start(bf16[16,32,128]{2,1,0:T(8,128)(2,1)} %get-tuple-element.49), channel_id=1, source_target_pairs={{0,6},{1,7},{2,4},{3,5},{4,2},{5,3},{6,0},{7,1},{8,14},{9,15},{10,... | collective-permute-start | bytes 393224 | tf_op jit(solution)/shard_map/ppermute | solution.py:385
  25.2 9.8 %collective-permute-start.3 = (bf16[64,16,128]{2,1,0:T(8,128)(2,1)S(1)}, bf16[64,16,128]{2,1,0:T(8,128)(2,1)S(1)}, u32[]{:S(2)}, u32[]{:S(2)}) collective-permute-start(bf16[64,16,128]{2,1,0:T(8,128)(2,1)S(1)} %get-tuple-element.43.refs_0_), channel_id=1, source_target_pairs={{0,8},{4,12},{8,0},{12,4},{16,24},{20,28},{24,16},{28,20},{1,9},{5... | collective-permute-start | bytes 786440 | tf_op jit(solution)/shard_map/ppermute | solution.py:425
  26.9 10.4 %collective-permute-start.4 = (bf16[64,16,128]{2,1,0:T(8,128)(2,1)S(1)}, bf16[64,16,128]{2,1,0:T(8,128)(2,1)S(1)}, u32[]{:S(2)}, u32[]{:S(2)}) collective-permute-start(bf16[64,16,128]{2,1,0:T(8,128)(2,1)S(1)} %get-tuple-element.44.refs_1_), channel_id=1, source_target_pairs={{8,16},{12,20},{16,8},{20,12},{9,17},{13,21},{17,9},{21,13},{10,18... | collective-permute-start | bytes 786440 | tf_op jit(solution)/shard_map/ppermute | solution.py:425
  29.3 18.8 %copy-start = (f32[64,1024]{1,0:T(8,128)S(1)}, f32[64,1024]{1,0:T(8,128)}, u32[]{:S(2)}) copy-start(f32[64,1024]{1,0:T(8,128)} %constant.119.clone.cos_ref) | copy-start | bytes 786436
  29.3 18.8 %copy-start.2 = (f32[8,1024]{1,0:T(8,128)S(1)}, f32[8,1024]{1,0:T(8,128)}, u32[]{:S(2)}) copy-start(f32[8,1024]{1,0:T(8,128)} %constant.121.clone.cos0_ref) | copy-start | bytes 98308
  29.3 18.7 %copy-start.3 = (f32[8,1024]{1,0:T(8,128)S(1)}, f32[8,1024]{1,0:T(8,128)}, u32[]{:S(2)}) copy-start(f32[8,1024]{1,0:T(8,128)} %constant.122.clone.msin0_ref) | copy-start | bytes 98308
  30.8 10.0 %collective-permute-start.10 = (bf16[64,16,128]{2,1,0:T(8,128)(2,1)S(1)}, bf16[64,16,128]{2,1,0:T(8,128)(2,1)S(1)}, u32[]{:S(2)}, u32[]{:S(2)}) collective-permute-start(bf16[64,16,128]{2,1,0:T(8,128)(2,1)S(1)} %get-tuple-element.51.refs_6_), channel_id=1, source_target_pairs={{8,16},{12,20},{16,8},{20,12},{9,17},{13,21},{17,9},{21,13},{10,18... | collective-permute-start | bytes 786440 | tf_op jit(solution)/shard_map/ppermute | solution.py:425
  34.5 6.4 %collective-permute-start.9 = (bf16[64,16,128]{2,1,0:T(8,128)(2,1)S(1)}, bf16[64,16,128]{2,1,0:T(8,128)(2,1)S(1)}, u32[]{:S(2)}, u32[]{:S(2)}) collective-permute-start(bf16[64,16,128]{2,1,0:T(8,128)(2,1)S(1)} %get-tuple-element.50.refs_5_), channel_id=1, source_target_pairs={{0,8},{4,12},{8,0},{12,4},{16,24},{20,28},{24,16},{28,20},{1,9},{5... | collective-permute-start | bytes 786440 | tf_op jit(solution)/shard_map/ppermute | solution.py:425
  34.7 13.4 %copy-start.1 = (f32[64,1024]{1,0:T(8,128)S(1)}, f32[64,1024]{1,0:T(8,128)}, u32[]{:S(2)}) copy-start(f32[64,1024]{1,0:T(8,128)} %constant.120.clone.msin_ref) | copy-start | bytes 786436
  44.5 9.0 %collective-permute-start.12 = (f32[2,16,16,128]{3,2,1,0:T(8,128)S(1)}, f32[2,16,16,128]{3,2,1,0:T(8,128)S(1)}, u32[]{:S(2)}, u32[]{:S(2)}) collective-permute-start(f32[2,16,16,128]{3,2,1,0:T(8,128)S(1)} %get-tuple-element.56), channel_id=1, source_target_pairs={{0,2},{1,3},{2,0},{3,1},{4,6},{5,7},{6,4},{7,5},{8,10},{9,11},{10,... | collective-permute-start | bytes 786440 | tf_op jit(solution)/shard_map/ppermute | solution.py:385
  46.0 11.5 %collective-permute-start.13 = (f32[2,16,16,128]{3,2,1,0:T(8,128)S(1)}, f32[2,16,16,128]{3,2,1,0:T(8,128)S(1)}, u32[]{:S(2)}, u32[]{:S(2)}) collective-permute-start(f32[2,16,16,128]{3,2,1,0:T(8,128)S(1)} %get-tuple-element.61), channel_id=1, source_target_pairs={{0,4},{1,5},{2,6},{3,7},{4,0},{5,1},{6,2},{7,3},{8,12},{9,13},{10,... | collective-permute-start | bytes 786440 | tf_op jit(solution)/shard_map/ppermute | solution.py:385
  46.5 11.0 %collective-permute-start.15 = (f32[2,16,16,128]{3,2,1,0:T(8,128)S(1)}, f32[2,16,16,128]{3,2,1,0:T(8,128)S(1)}, u32[]{:S(2)}, u32[]{:S(2)}) collective-permute-start(f32[2,16,16,128]{3,2,1,0:T(8,128)S(1)} %get-tuple-element.62), channel_id=1, source_target_pairs={{0,6},{1,7},{2,4},{3,5},{4,2},{5,3},{6,0},{7,1},{8,14},{9,15},{10,... | collective-permute-start | bytes 786440 | tf_op jit(solution)/shard_map/ppermute | solution.py:385
  53.5 4.6 %collective-permute-start.17 = (f32[2,16,16,128]{3,2,1,0:T(8,128)S(1)}, f32[2,16,16,128]{3,2,1,0:T(8,128)S(1)}, u32[]{:S(2)}, u32[]{:S(2)}) collective-permute-start(f32[2,16,16,128]{3,2,1,0:T(8,128)S(1)} %get-tuple-element.63.refs_0_), channel_id=1, source_target_pairs={{0,1},{1,0},{2,3},{3,2},{4,5},{5,4},{6,7},{7,6},{8,9},{9,8},{10,11... | collective-permute-start | bytes 786440 | tf_op jit(solution)/shard_map/ppermute | solution.py:385
  53.5 4.6 %collective-permute-start.18 = (f32[2,16,16,128]{3,2,1,0:T(8,128)S(1)}, f32[2,16,16,128]{3,2,1,0:T(8,128)S(1)}, u32[]{:S(2)}, u32[]{:S(2)}) collective-permute-start(f32[2,16,16,128]{3,2,1,0:T(8,128)S(1)} %collective-permute-done.12.refs_2_), channel_id=1, source_target_pairs={{0,1},{1,0},{2,3},{3,2},{4,5},{5,4},{6,7},{7,6},{8,9},{9,8},{10,11... | collective-permute-start | bytes 786440 | tf_op jit(solution)/shard_map/ppermute | solution.py:385
  57.5 2.9 %collective-permute-start.14 = (f32[2,16,16,128]{3,2,1,0:T(8,128)S(1)}, f32[2,16,16,128]{3,2,1,0:T(8,128)S(1)}, u32[]{:S(2)}, u32[]{:S(2)}) collective-permute-start(f32[2,16,16,128]{3,2,1,0:T(8,128)S(1)} %collective-permute-done.13.refs_0_), channel_id=1, source_target_pairs={{0,1},{1,0},{2,3},{3,2},{4,5},{5,4},{6,7},{7,6},{8,9},{9,8},{10,11... | collective-permute-start | bytes 786440 | tf_op jit(solution)/shard_map/ppermute | solution.py:385
  57.5 2.9 %collective-permute-start.16 = (f32[2,16,16,128]{3,2,1,0:T(8,128)S(1)}, f32[2,16,16,128]{3,2,1,0:T(8,128)S(1)}, u32[]{:S(2)}, u32[]{:S(2)}) collective-permute-start(f32[2,16,16,128]{3,2,1,0:T(8,128)S(1)} %collective-permute-done.15.refs_2_), channel_id=1, source_target_pairs={{0,1},{1,0},{2,3},{3,2},{4,5},{5,4},{6,7},{7,6},{8,9},{9,8},{10,11... | collective-permute-start | bytes 786440 | tf_op jit(solution)/shard_map/ppermute | solution.py:385

commit v9 on v8

--- a/solution.py
+++ b/solution.py
@@ -325,51 +325,50 @@
     )(*operands, select)
 
 
-def inverse_kernel(high_ref, low_ref, *refs, far, wins):
-    *refs, out_ref, both = refs
-    blocks, before = refs[:wins], refs[wins:]
+def inverse_kernel(high_ref, low_ref, *refs):
+    *blocks, out_hbm, both, out_ref, sems = refs
     _, nodes, slots, _ = blocks[0].shape
-    rows, depth = nodes * slots, both.shape[1]
-    me, _ = position(wins)
-
-    @pl.when(pl.program_id(0) == 0)
-    def _():
-        for d, block in enumerate(blocks):
-            columns = pl.ds(pl.multiple_of(((me ^ d) % wins) * LANES, LANES), LANES)
-            values = block[0].reshape(rows, LANES)
-            high = values.astype(jnp.bfloat16)
-            both[0:rows, columns] = high
-            both[rows : 2 * rows, columns] = (values - high.astype(jnp.float32)).astype(jnp.bfloat16)
-
-    here = pl.ds(pl.multiple_of(((me // wins) ^ far) * depth, depth), depth)
-    first = jnp.dot(both[...], high_ref[here, :], preferred_element_type=jnp.float32)
-    second = jnp.dot(both[0:rows, :], low_ref[here, :], preferred_element_type=jnp.float32)
-    total = (first[0:rows, :] + (first[rows : 2 * rows, :] + second)).reshape(out_ref.shape)
-    for ref in before:
-        total = total + ref[...]
-    out_ref[...] = total
-
-
-def inverse(blocks, high, low, far, before):
+    rows = nodes * slots
+    me, _ = position(len(blocks) // 2)
+    for d, block in enumerate(blocks):
+        columns = pl.ds(pl.multiple_of((me ^ d) * LANES, LANES), LANES)
+        values = block[d % 2].reshape(rows, LANES)
+        high = values.astype(jnp.bfloat16)
+        both[0:rows, columns] = high
+        both[rows : 2 * rows, columns] = (values - high.astype(jnp.float32)).astype(jnp.bfloat16)
+    width = out_ref.shape[3]
+    copies = []
+    for i in range(LAGS // width):
+        here = slice(i * width, (i + 1) * width)
+        first = jnp.dot(both[...], high_ref[:, here], preferred_element_type=jnp.float32)
+        second = jnp.dot(both[0:rows, :], low_ref[:, here], preferred_element_type=jnp.float32)
+        total = first[0:rows, :] + (first[rows : 2 * rows, :] + second)
+        out_ref[i] = total.reshape(nodes, slots, width)
+        copy = pltpu.make_async_copy(out_ref.at[i], out_hbm.at[:, :, pl.ds(i * width, width)], sems.at[i])
+        copy.start()
+        copies.append(copy)
+    for copy in copies:
+        copy.wait()
+
+
+def inverse(blocks, high, low):
     _, nodes, slots, _ = blocks[0].shape
-    wins = len(blocks)
     depth = high.shape[0] * LANES
     width = 256
-    table = pl.BlockSpec((depth, width), lambda i: (0, i))
-    lags = pl.BlockSpec((nodes, slots, width), lambda i: (0, 0, i))
+    vmem = pl.BlockSpec(memory_space=pltpu.VMEM)
     return pl.pallas_call(
-        functools.partial(inverse_kernel, far=far, wins=wins),
-        grid=(LAGS // width,),
-        in_specs=[table, table]
-        + [pl.BlockSpec((1, nodes, slots, LANES), lambda i, j=d % 2: (j, 0, 0, 0)) for d in range(wins)]
-        + [lags] * len(before),
-        out_specs=lags,
+        inverse_kernel,
+        in_specs=[vmem] * (2 + len(blocks)),
+        out_specs=pl.BlockSpec(memory_space=pl.ANY),
         out_shape=jax.ShapeDtypeStruct((nodes, slots, LAGS), jnp.float32),
-        scratch_shapes=[pltpu.VMEM((2 * nodes * slots, wins * LANES), jnp.bfloat16)],
+        scratch_shapes=[
+            pltpu.VMEM((2 * nodes * slots, depth), jnp.bfloat16),
+            pltpu.VMEM((LAGS // width, nodes, slots, width), jnp.float32),
+            pltpu.SemaphoreType.DMA((LAGS // width,)),
+        ],
         compiler_params=pltpu.CompilerParams(vmem_limit_bytes=12 * MIB),
-        cost_estimate=pl.CostEstimate(flops=1 << 31, bytes_accessed=1 << 22, transcendentals=0),
         name="inverse",
-    )(high.reshape(depth, LAGS), low.reshape(depth, LAGS), *blocks, *before)
+    )(high.reshape(depth, LAGS), low.reshape(depth, LAGS), *blocks)
 
 
 def per_device(traces, taps, neighbours, valid, *, pairs, wins):
@@ -425,10 +424,8 @@
         halves.append((a, b, turned, lax.ppermute(a, "pairs", swap_a), lax.ppermute(b, "pairs", swap_b)))
     stack = cross_products(halves, select, wins)
     moved = between_chips(stack)
-    near, far = moved[: wins // 2], moved[wins // 2 :]
-    near, high, low = lax.optimization_barrier((near, high, low))
-    total = inverse(within_chip(near), high, low, 0, [])
-    return inverse(within_chip(far), high, low, 1, [total])
+    moved[1], high, low = lax.optimization_barrier((moved[1], high, low))
+    return inverse(within_chip(moved), high, low)
 
 
 def solution(mesh):

time: 64 us -> 63 us (0.984)
  Pallas kernels: 27.9 us -> 25.2 us
  waiting for transfers between devices: 14.3 us -> 16.1 us
    pallas_call x2 -> x1, Pallas kernels: 5.56 us -> 2.91 us  [inverse(): pl.pallas_call(inverse_kernel, in_specs=[vmem] * (2 + len(blocks)), out_s...]
    ppermute x14, waiting for transfers between devices: 8.35 us -> 10.2 us  [hop(): return lax.ppermute(array, ('pairs', 'win'), pairing)]
  transfers between devices with their start and end apart: 19 -> 19, of which waited for: 6 -> 8; matrix products, arithmetic and copies ran while one was open for 1% -> 1% of each run, Pallas kernels for 33% -> 30%
where the time goes in v9:
time: 63 us; the launch traced here: 62.5 us
  Pallas kernels  25.2 us (40%)
  starting transfers between devices  20 us (32%)
  waiting for transfers between devices  16.1 us (26%)
    pallas_call x2, Pallas kernels, own_spectra(): pl.pallas_call(functools.partial(spectra_kernel, steps=steps, wins=len(st...  14.6 us
    ppermute x14, starting transfers between devices, hop(): return lax.ppermute(array, ('pairs', 'win'), pairing)  11.2 us
    ppermute x14, waiting for transfers between devices, hop(): return lax.ppermute(array, ('pairs', 'win'), pairing)  10.2 us
    ppermute x2, waiting for transfers between devices, per_device(): lax.ppermute(b, 'pairs', swap_b)  5.79 us
    ppermute x2, starting transfers between devices, per_device(): lax.ppermute(b, 'pairs', swap_b)  5.57 us
    pallas_call x1, Pallas kernels, cross_products(): pl.pallas_call(cross_kernel, out_shape=[block] * wins, in_specs=[vmem] *...  3.53 us
    pallas_call x2, Pallas kernels, by_bin(): pl.pallas_call(functools.partial(by_bin_kernel, steps=steps), out_shape=[...  3.08 us
    pallas_call x1, Pallas kernels, inverse(): pl.pallas_call(inverse_kernel, in_specs=[vmem] * (2 + len(blocks)), out_s...  2.91 us
  transfers between devices with their start and end apart: 19, of which 8 were waited for; matrix products, arithmetic and copies ran while one was open for 1% of the time, Pallas kernels for 30%

profile of v9, /device:TPU:16, one launch (start us, length us, event | category | flops | bytes accessed | tf_op | source)
XLA Modules:
  0.0 62.5 jit_solution(15969450275117131226)
XLA Ops:
  0.1 7.3 %own_spectra.2 = (bf16[16,32,128]{2,1,0:T(8,128)(2,1)}, bf16[16,32,128]{2,1,0:T(8,128)(2,1)}, bf16[16,32,128]{2,1,0:T(8,128)(2,1)}, bf16[16,32,128]{2,1,0:T(8,128)(2,1)}) custom-call(bf16[512,4096]{1,0:T(8,128)(2,1)} %bitcast.15, f32[1,129]{1,0:T(1,128)} %bitcast.16, f32[129,1024]{1,0:T(8,128)} %constant.116.clone.fine_hbm, ...), custom_call_target="tpu_custom_call" | custom-call | flops 2147483648 | bytes 4194304 | tf_op jit(solution)/shard_map/own_spectra/pallas_call | solution.py:167
  7.4 1.6 %collective-permute-start.11 = (s32[16,64]{1,0:T(8,128)S(1)}, s32[16,64]{1,0:T(8,128)S(1)}, u32[]{:S(2)}, u32[]{:S(2)}) collective-permute-start(s32[16,64]{1,0:T(8,128)S(1)} %fusion.3), channel_id=1, source_target_pairs={{0,4},{4,0},{8,12},{12,8},{16,20},{20,16},{24,28},{28,24},{1,5},{5... | collective-permute-start | bytes 12296 | tf_op jit(solution)/shard_map/ppermute | solution.py:404
  9.0 1.5 %collective-permute-start = (bf16[16,32,128]{2,1,0:T(8,128)(2,1)}, bf16[16,32,128]{2,1,0:T(8,128)(2,1)S(1)}, u32[]{:S(2)}, u32[]{:S(2)}) collective-permute-start(bf16[16,32,128]{2,1,0:T(8,128)(2,1)} %get-tuple-element.39), channel_id=1, source_target_pairs={{0,2},{1,3},{2,0},{3,1},{4,6},{5,7},{6,4},{7,5},{8,10},{9,11},{10,... | collective-permute-start | bytes 393224 | tf_op jit(solution)/shard_map/ppermute | solution.py:384
  10.5 0.5 collective-permute-start.1
  11.0 1.5 %collective-permute-start.2 = (bf16[16,32,128]{2,1,0:T(8,128)(2,1)}, bf16[16,32,128]{2,1,0:T(8,128)(2,1)S(1)}, u32[]{:S(2)}, u32[]{:S(2)}) collective-permute-start(bf16[16,32,128]{2,1,0:T(8,128)(2,1)} %get-tuple-element.41), channel_id=1, source_target_pairs={{0,6},{1,7},{2,4},{3,5},{4,2},{5,3},{6,0},{7,1},{8,14},{9,15},{10,... | collective-permute-start | bytes 393224 | tf_op jit(solution)/shard_map/ppermute | solution.py:384
  12.5 0.1 copy.15
  12.6 0.0 collective-permute-done.11
  12.6 0.1 copy.16
  12.7 0.1 add_select_fusion
  12.8 7.3 %own_spectra.3 = (bf16[16,32,128]{2,1,0:T(8,128)(2,1)}, bf16[16,32,128]{2,1,0:T(8,128)(2,1)}, bf16[16,32,128]{2,1,0:T(8,128)(2,1)}, bf16[16,32,128]{2,1,0:T(8,128)(2,1)}) custom-call(bf16[512,4096]{1,0:T(8,128)(2,1)} %collective-permute-done.5.x_hbm, f32[1,129]{1,0:T(1,128)} %bitcast.17, f32[129,1024]{1,0:T(8,128)} %constant.116.clone.fine_hbm, ...), custom_call_target="tpu_custom_call" | custom-call | flops 2147483648 | bytes 4194304 | tf_op jit(solution)/shard_map/own_spectra/pallas_call | solution.py:167
  20.1 1.5 %collective-permute-start.6 = (bf16[16,32,128]{2,1,0:T(8,128)(2,1)}, bf16[16,32,128]{2,1,0:T(8,128)(2,1)S(1)}, u32[]{:S(2)}, u32[]{:S(2)}) collective-permute-start(bf16[16,32,128]{2,1,0:T(8,128)(2,1)} %get-tuple-element.46), channel_id=1, source_target_pairs={{0,2},{1,3},{2,0},{3,1},{4,6},{5,7},{6,4},{7,5},{8,10},{9,11},{10,... | collective-permute-start | bytes 393224 | tf_op jit(solution)/shard_map/ppermute | solution.py:384
  21.7 0.5 collective-permute-start.7
  22.2 0.0 collective-permute-done.refs_1_
  22.2 1.5 %collective-permute-start.8 = (bf16[16,32,128]{2,1,0:T(8,128)(2,1)}, bf16[16,32,128]{2,1,0:T(8,128)(2,1)S(1)}, u32[]{:S(2)}, u32[]{:S(2)}) collective-permute-start(bf16[16,32,128]{2,1,0:T(8,128)(2,1)} %get-tuple-element.48), channel_id=1, source_target_pairs={{0,6},{1,7},{2,4},{3,5},{4,2},{5,3},{6,0},{7,1},{8,14},{9,15},{10,... | collective-permute-start | bytes 393224 | tf_op jit(solution)/shard_map/ppermute | solution.py:384
  23.7 0.0 collective-permute-done.1.refs_2_
  23.7 0.0 collective-permute-done.2.refs_3_
  23.7 1.5 %by_bin.2 = (bf16[64,16,128]{2,1,0:T(8,128)(2,1)S(1)}, bf16[64,16,128]{2,1,0:T(8,128)(2,1)S(1)}, bf16[64,32,128]{2,1,0:T(8,128)(2,1)S(1)}) custom-call(bf16[16,32,128]{2,1,0:T(8,128)(2,1)S(1)} %copy-done.4, bf16[16,32,128]{2,1,0:T(8,128)(2,1)S(1)} %collective-permute-done.refs_1_, bf16[16,32,128]{2,1,0:T(8,128)(2,1)S(1)} %collective-permute-done.1.refs_2_, ...), custom_call_target="tpu_custom_call" | custom-call | flops 2147483648 | bytes 4194304 | tf_op jit(solution)/shard_map/by_bin/pallas_call | solution.py:256
  25.2 1.6 %collective-permute-start.3 = (bf16[64,16,128]{2,1,0:T(8,128)(2,1)S(1)}, bf16[64,16,128]{2,1,0:T(8,128)(2,1)S(1)}, u32[]{:S(2)}, u32[]{:S(2)}) collective-permute-start(bf16[64,16,128]{2,1,0:T(8,128)(2,1)S(1)} %get-tuple-element.42.refs_0_), channel_id=1, source_target_pairs={{0,8},{4,12},{8,0},{12,4},{16,24},{20,28},{24,16},{28,20},{1,9},{5... | collective-permute-start | bytes 786440 | tf_op jit(solution)/shard_map/ppermute | solution.py:424
  26.9 1.9 %collective-permute-start.4 = (bf16[64,16,128]{2,1,0:T(8,128)(2,1)S(1)}, bf16[64,16,128]{2,1,0:T(8,128)(2,1)S(1)}, u32[]{:S(2)}, u32[]{:S(2)}) collective-permute-start(bf16[64,16,128]{2,1,0:T(8,128)(2,1)S(1)} %get-tuple-element.43.refs_1_), channel_id=1, source_target_pairs={{8,16},{12,20},{16,8},{20,12},{9,17},{13,21},{17,9},{21,13},{10,18... | collective-permute-start | bytes 786440 | tf_op jit(solution)/shard_map/ppermute | solution.py:424
  28.8 0.5 collective-permute-done.7.refs_2_
  29.3 0.0 copy-start.2
  29.3 0.0 copy-start.3
  29.3 1.5 %by_bin.3 = (bf16[64,16,128]{2,1,0:T(8,128)(2,1)S(1)}, bf16[64,16,128]{2,1,0:T(8,128)(2,1)S(1)}, bf16[64,32,128]{2,1,0:T(8,128)(2,1)S(1)}) custom-call(bf16[16,32,128]{2,1,0:T(8,128)(2,1)S(1)} %copy-done.5, bf16[16,32,128]{2,1,0:T(8,128)(2,1)S(1)} %collective-permute-done.6.refs_1_, bf16[16,32,128]{2,1,0:T(8,128)(2,1)S(1)} %collective-permute-done.7.refs_2_, ...), custom_call_target="tpu_custom_call" | custom-call | flops 2147483648 | bytes 4194304 | tf_op jit(solution)/shard_map/by_bin/pallas_call | solution.py:256
  30.8 3.7 %collective-permute-start.10 = (bf16[64,16,128]{2,1,0:T(8,128)(2,1)S(1)}, bf16[64,16,128]{2,1,0:T(8,128)(2,1)S(1)}, u32[]{:S(2)}, u32[]{:S(2)}) collective-permute-start(bf16[64,16,128]{2,1,0:T(8,128)(2,1)S(1)} %get-tuple-element.50.refs_6_), channel_id=1, source_target_pairs={{8,16},{12,20},{16,8},{20,12},{9,17},{13,21},{17,9},{21,13},{10,18... | collective-permute-start | bytes 786440 | tf_op jit(solution)/shard_map/ppermute | solution.py:424
  34.5 0.1 collective-permute-start.9
  34.6 0.1 copy.17
  34.7 0.3 compare_convert_fusion.refs_10_
  35.0 0.0 collective-permute-done.3.refs_3_
  35.0 2.3 %collective-permute-done.4.refs_4_ = bf16[64,16,128]{2,1,0:T(8,128)(2,1)S(1)} collective-permute-done((bf16[64,16,128]{2,1,0:T(8,128)(2,1)S(1)}, bf16[64,16,128]{2,1,0:T(8,128)(2,1)S(1)}, u32[]{:S(2)}, u32[]{:S(2)}) %collective-permute-start.4) | collective-permute-done | bytes 262176 | tf_op jit(solution)/shard_map/ppermute | solution.py:424
  37.3 3.5 %collective-permute-done.10.refs_9_ = bf16[64,16,128]{2,1,0:T(8,128)(2,1)S(1)} collective-permute-done((bf16[64,16,128]{2,1,0:T(8,128)(2,1)S(1)}, bf16[64,16,128]{2,1,0:T(8,128)(2,1)S(1)}, u32[]{:S(2)}, u32[]{:S(2)}) %collective-permute-start.10) | collective-permute-done | bytes 262176 | tf_op jit(solution)/shard_map/ppermute | solution.py:424
  40.8 0.1 collective-permute-done.9.refs_8_
  41.0 3.5 %cross_products.1 = (f32[2,16,16,128]{3,2,1,0:T(8,128)S(1)}, f32[2,16,16,128]{3,2,1,0:T(8,128)S(1)}, f32[2,16,16,128]{3,2,1,0:T(8,128)S(1)}, f32[2,16,16,128]{3,2,1,0:T(8,128)S(1)}) custom-call(bf16[64,16,128]{2,1,0:T(8,128)(2,1)S(1)} %get-tuple-element.42.refs_0_, bf16[64,16,128]{2,1,0:T(8,128)(2,1)S(1)} %get-tuple-element.43.refs_1_, ...), custom_call_target="tpu_custom_call" | custom-call | tf_op jit(solution)/shard_map/cross_products/pallas_call | solution.py:317
  44.5 1.5 %collective-permute-start.12 = (f32[2,16,16,128]{3,2,1,0:T(8,128)S(1)}, f32[2,16,16,128]{3,2,1,0:T(8,128)S(1)}, u32[]{:S(2)}, u32[]{:S(2)}) collective-permute-start(f32[2,16,16,128]{3,2,1,0:T(8,128)S(1)} %get-tuple-element.54), channel_id=1, source_target_pairs={{0,2},{1,3},{2,0},{3,1},{4,6},{5,7},{6,4},{7,5},{8,10},{9,11},{10,... | collective-permute-start | bytes 786440 | tf_op jit(solution)/shard_map/ppermute | solution.py:384
  46.0 0.5 collective-permute-start.15
  46.5 1.5 %collective-permute-start.17 = (f32[2,16,16,128]{3,2,1,0:T(8,128)S(1)}, f32[2,16,16,128]{3,2,1,0:T(8,128)S(1)}, u32[]{:S(2)}, u32[]{:S(2)}) collective-permute-start(f32[2,16,16,128]{3,2,1,0:T(8,128)S(1)} %get-tuple-element.62), channel_id=1, source_target_pairs={{0,6},{1,7},{2,4},{3,5},{4,2},{5,3},{6,0},{7,1},{8,14},{9,15},{10,... | collective-permute-start | bytes 786440 | tf_op jit(solution)/shard_map/ppermute | solution.py:384
  48.0 1.1 %lag_tables.1 = (bf16[8,128,1024]{2,1,0:T(8,128)(2,1)S(1)}, bf16[8,128,1024]{2,1,0:T(8,128)(2,1)S(1)}) custom-call(f32[64,1024]{1,0:T(8,128)S(1)} %copy-done, f32[64,1024]{1,0:T(8,128)S(1)} %copy-done.1, f32[8,1024]{1,0:T(8,128)S(1)} %copy-done.2, f32[8,1024]{1,0:T(8,128)S(1)} %copy-done.3), custom_call_target="tpu_custom_call" | custom-call | tf_op jit(solution)/shard_map/lag_tables/pallas_call | solution.py:204
  49.1 0.1 collective-permute-start.13
  49.2 4.2 %collective-permute-done.12.refs_2_ = f32[2,16,16,128]{3,2,1,0:T(8,128)S(1)} collective-permute-done((f32[2,16,16,128]{3,2,1,0:T(8,128)S(1)}, f32[2,16,16,128]{3,2,1,0:T(8,128)S(1)}, u32[]{:S(2)}, u32[]{:S(2)}) %collective-permute-start.12) | collective-permute-done | bytes 262176 | tf_op jit(solution)/shard_map/ppermute | solution.py:384
  53.5 0.0 collective-permute-start.14
  53.5 4.1 %collective-permute-done.15.refs_4_ = f32[2,16,16,128]{3,2,1,0:T(8,128)S(1)} collective-permute-done((f32[2,16,16,128]{3,2,1,0:T(8,128)S(1)}, f32[2,16,16,128]{3,2,1,0:T(8,128)S(1)}, u32[]{:S(2)}, u32[]{:S(2)}) %collective-permute-start.15) | collective-permute-done | bytes 262176 | tf_op jit(solution)/shard_map/ppermute | solution.py:384
  57.5 0.0 collective-permute-start.16
  57.5 0.0 collective-permute-done.17.refs_6_
  57.5 0.5 collective-permute-start.18
  58.0 0.0 collective-permute-done.13.refs_1_
  58.0 0.0 collective-permute-done.14.refs_3_
  58.0 1.0 %collective-permute-done.16.refs_5_ = f32[2,16,16,128]{3,2,1,0:T(8,128)S(1)} collective-permute-done((f32[2,16,16,128]{3,2,1,0:T(8,128)S(1)}, f32[2,16,16,128]{3,2,1,0:T(8,128)S(1)}, u32[]{:S(2)}, u32[]{:S(2)}) %collective-permute-start.16) | collective-permute-done | bytes 262176 | tf_op jit(solution)/shard_map/ppermute | solution.py:384
  59.0 0.4 collective-permute-done.18.refs_7_
  59.4 2.9 %inverse.1 = f32[16,16,1024]{2,1,0:T(8,128)} custom-call(bf16[1024,1024]{1,0:T(8,128)(2,1)S(1)} %bitcast.8, bf16[1024,1024]{1,0:T(8,128)(2,1)S(1)} %bitcast.9, f32[2,16,16,128]{3,2,1,0:T(8,128)S(1)} %get-tuple-element.59.refs_0_, f32[2,16,16,128]{3,2,1,0:T(8,128)S(1)} %collective-permute-done.13.refs_1_, ...), custom_call_target="tpu_custom_call" | custom-call | tf_op jit(solution)/shard_map/inverse/pallas_call | solution.py:359
  (22 shorter events, 0.1 us)
Async XLA Ops:
  0.0 7.4 %copy-start.6 = (s32[16,64]{1,0:T(8,128)S(1)}, s32[16,64]{1,0:T(8,128)}, u32[]{:S(2)}) copy-start(s32[16,64]{1,0:T(8,128)} %param.16) | copy-start | bytes 12292
  0.0 7.4 %copy-start.7 = (s32[16,64]{1,0:T(8,128)S(1)}, s32[16,64]{1,0:T(8,128)}, u32[]{:S(2)}) copy-start(s32[16,64]{1,0:T(8,128)} %param.17) | copy-start | bytes 12292
  0.0 12.8 %collective-permute-start.5 = (bf16[512,4096]{1,0:T(8,128)(2,1)}, bf16[512,4096]{1,0:T(8,128)(2,1)}, u32[]{:S(2)}, u32[]{:S(2)}) collective-permute-start(bf16[512,4096]{1,0:T(8,128)(2,1)} %bitcast.14), channel_id=1, source_target_pairs={{0,1},{1,0},{2,3},{3,2},{4,5},{5,4},{6,7},{7,6},{8,9},{9,8},{10,11... | collective-permute-start | bytes 12582920 | tf_op jit(solution)/shard_map/ppermute | solution.py:384
  7.3 16.3 %copy-start.4 = (bf16[16,32,128]{2,1,0:T(8,128)(2,1)S(1)}, bf16[16,32,128]{2,1,0:T(8,128)(2,1)}, u32[]{:S(2)}) copy-start(bf16[16,32,128]{2,1,0:T(8,128)(2,1)} %get-tuple-element.38.refs_0_) | copy-start | bytes 393220
  7.4 5.2 %collective-permute-start.11 = (s32[16,64]{1,0:T(8,128)S(1)}, s32[16,64]{1,0:T(8,128)S(1)}, u32[]{:S(2)}, u32[]{:S(2)}) collective-permute-start(s32[16,64]{1,0:T(8,128)S(1)} %fusion.3), channel_id=1, source_target_pairs={{0,4},{4,0},{8,12},{12,8},{16,20},{20,16},{24,28},{28,24},{1,5},{5... | collective-permute-start | bytes 12296 | tf_op jit(solution)/shard_map/ppermute | solution.py:404
  9.0 13.2 %collective-permute-start = (bf16[16,32,128]{2,1,0:T(8,128)(2,1)}, bf16[16,32,128]{2,1,0:T(8,128)(2,1)S(1)}, u32[]{:S(2)}, u32[]{:S(2)}) collective-permute-start(bf16[16,32,128]{2,1,0:T(8,128)(2,1)} %get-tuple-element.39), channel_id=1, source_target_pairs={{0,2},{1,3},{2,0},{3,1},{4,6},{5,7},{6,4},{7,5},{8,10},{9,11},{10,... | collective-permute-start | bytes 393224 | tf_op jit(solution)/shard_map/ppermute | solution.py:384
  10.5 13.2 %collective-permute-start.1 = (bf16[16,32,128]{2,1,0:T(8,128)(2,1)}, bf16[16,32,128]{2,1,0:T(8,128)(2,1)S(1)}, u32[]{:S(2)}, u32[]{:S(2)}) collective-permute-start(bf16[16,32,128]{2,1,0:T(8,128)(2,1)} %get-tuple-element.40), channel_id=1, source_target_pairs={{0,4},{1,5},{2,6},{3,7},{4,0},{5,1},{6,2},{7,3},{8,12},{9,13},{10,... | collective-permute-start | bytes 393224 | tf_op jit(solution)/shard_map/ppermute | solution.py:384
  11.0 12.7 %collective-permute-start.2 = (bf16[16,32,128]{2,1,0:T(8,128)(2,1)}, bf16[16,32,128]{2,1,0:T(8,128)(2,1)S(1)}, u32[]{:S(2)}, u32[]{:S(2)}) collective-permute-start(bf16[16,32,128]{2,1,0:T(8,128)(2,1)} %get-tuple-element.41), channel_id=1, source_target_pairs={{0,6},{1,7},{2,4},{3,5},{4,2},{5,3},{6,0},{7,1},{8,14},{9,15},{10,... | collective-permute-start | bytes 393224 | tf_op jit(solution)/shard_map/ppermute | solution.py:384
  20.1 9.2 %copy-start.5 = (bf16[16,32,128]{2,1,0:T(8,128)(2,1)S(1)}, bf16[16,32,128]{2,1,0:T(8,128)(2,1)}, u32[]{:S(2)}) copy-start(bf16[16,32,128]{2,1,0:T(8,128)(2,1)} %get-tuple-element.45.refs_0_) | copy-start | bytes 393220
  20.1 8.7 %collective-permute-start.6 = (bf16[16,32,128]{2,1,0:T(8,128)(2,1)}, bf16[16,32,128]{2,1,0:T(8,128)(2,1)S(1)}, u32[]{:S(2)}, u32[]{:S(2)}) collective-permute-start(bf16[16,32,128]{2,1,0:T(8,128)(2,1)} %get-tuple-element.46), channel_id=1, source_target_pairs={{0,2},{1,3},{2,0},{3,1},{4,6},{5,7},{6,4},{7,5},{8,10},{9,11},{10,... | collective-permute-start | bytes 393224 | tf_op jit(solution)/shard_map/ppermute | solution.py:384
  21.7 7.6 %collective-permute-start.7 = (bf16[16,32,128]{2,1,0:T(8,128)(2,1)}, bf16[16,32,128]{2,1,0:T(8,128)(2,1)S(1)}, u32[]{:S(2)}, u32[]{:S(2)}) collective-permute-start(bf16[16,32,128]{2,1,0:T(8,128)(2,1)} %get-tuple-element.47), channel_id=1, source_target_pairs={{0,4},{1,5},{2,6},{3,7},{4,0},{5,1},{6,2},{7,3},{8,12},{9,13},{10,... | collective-permute-start | bytes 393224 | tf_op jit(solution)/shard_map/ppermute | solution.py:384
  22.2 7.1 %collective-permute-start.8 = (bf16[16,32,128]{2,1,0:T(8,128)(2,1)}, bf16[16,32,128]{2,1,0:T(8,128)(2,1)S(1)}, u32[]{:S(2)}, u32[]{:S(2)}) collective-permute-start(bf16[16,32,128]{2,1,0:T(8,128)(2,1)} %get-tuple-element.48), channel_id=1, source_target_pairs={{0,6},{1,7},{2,4},{3,5},{4,2},{5,3},{6,0},{7,1},{8,14},{9,15},{10,... | collective-permute-start | bytes 393224 | tf_op jit(solution)/shard_map/ppermute | solution.py:384
  25.2 9.8 %collective-permute-start.3 = (bf16[64,16,128]{2,1,0:T(8,128)(2,1)S(1)}, bf16[64,16,128]{2,1,0:T(8,128)(2,1)S(1)}, u32[]{:S(2)}, u32[]{:S(2)}) collective-permute-start(bf16[64,16,128]{2,1,0:T(8,128)(2,1)S(1)} %get-tuple-element.42.refs_0_), channel_id=1, source_target_pairs={{0,8},{4,12},{8,0},{12,4},{16,24},{20,28},{24,16},{28,20},{1,9},{5... | collective-permute-start | bytes 786440 | tf_op jit(solution)/shard_map/ppermute | solution.py:424
  26.9 10.4 %collective-permute-start.4 = (bf16[64,16,128]{2,1,0:T(8,128)(2,1)S(1)}, bf16[64,16,128]{2,1,0:T(8,128)(2,1)S(1)}, u32[]{:S(2)}, u32[]{:S(2)}) collective-permute-start(bf16[64,16,128]{2,1,0:T(8,128)(2,1)S(1)} %get-tuple-element.43.refs_1_), channel_id=1, source_target_pairs={{8,16},{12,20},{16,8},{20,12},{9,17},{13,21},{17,9},{21,13},{10,18... | collective-permute-start | bytes 786440 | tf_op jit(solution)/shard_map/ppermute | solution.py:424
  29.3 18.8 %copy-start = (f32[64,1024]{1,0:T(8,128)S(1)}, f32[64,1024]{1,0:T(8,128)}, u32[]{:S(2)}) copy-start(f32[64,1024]{1,0:T(8,128)} %constant.119.clone.cos_ref) | copy-start | bytes 786436
  29.3 18.8 %copy-start.2 = (f32[8,1024]{1,0:T(8,128)S(1)}, f32[8,1024]{1,0:T(8,128)}, u32[]{:S(2)}) copy-start(f32[8,1024]{1,0:T(8,128)} %constant.121.clone.cos0_ref) | copy-start | bytes 98308
  29.3 18.7 %copy-start.3 = (f32[8,1024]{1,0:T(8,128)S(1)}, f32[8,1024]{1,0:T(8,128)}, u32[]{:S(2)}) copy-start(f32[8,1024]{1,0:T(8,128)} %constant.122.clone.msin0_ref) | copy-start | bytes 98308
  30.8 10.0 %collective-permute-start.10 = (bf16[64,16,128]{2,1,0:T(8,128)(2,1)S(1)}, bf16[64,16,128]{2,1,0:T(8,128)(2,1)S(1)}, u32[]{:S(2)}, u32[]{:S(2)}) collective-permute-start(bf16[64,16,128]{2,1,0:T(8,128)(2,1)S(1)} %get-tuple-element.50.refs_6_), channel_id=1, source_target_pairs={{8,16},{12,20},{16,8},{20,12},{9,17},{13,21},{17,9},{21,13},{10,18... | collective-permute-start | bytes 786440 | tf_op jit(solution)/shard_map/ppermute | solution.py:424
  34.5 6.4 %collective-permute-start.9 = (bf16[64,16,128]{2,1,0:T(8,128)(2,1)S(1)}, bf16[64,16,128]{2,1,0:T(8,128)(2,1)S(1)}, u32[]{:S(2)}, u32[]{:S(2)}) collective-permute-start(bf16[64,16,128]{2,1,0:T(8,128)(2,1)S(1)} %get-tuple-element.49.refs_5_), channel_id=1, source_target_pairs={{0,8},{4,12},{8,0},{12,4},{16,24},{20,28},{24,16},{28,20},{1,9},{5... | collective-permute-start | bytes 786440 | tf_op jit(solution)/shard_map/ppermute | solution.py:424
  34.7 13.4 %copy-start.1 = (f32[64,1024]{1,0:T(8,128)S(1)}, f32[64,1024]{1,0:T(8,128)}, u32[]{:S(2)}) copy-start(f32[64,1024]{1,0:T(8,128)} %constant.120.clone.msin_ref) | copy-start | bytes 786436
  44.5 9.0 %collective-permute-start.12 = (f32[2,16,16,128]{3,2,1,0:T(8,128)S(1)}, f32[2,16,16,128]{3,2,1,0:T(8,128)S(1)}, u32[]{:S(2)}, u32[]{:S(2)}) collective-permute-start(f32[2,16,16,128]{3,2,1,0:T(8,128)S(1)} %get-tuple-element.54), channel_id=1, source_target_pairs={{0,2},{1,3},{2,0},{3,1},{4,6},{5,7},{6,4},{7,5},{8,10},{9,11},{10,... | collective-permute-start | bytes 786440 | tf_op jit(solution)/shard_map/ppermute | solution.py:384
  46.0 11.5 %collective-permute-start.15 = (f32[2,16,16,128]{3,2,1,0:T(8,128)S(1)}, f32[2,16,16,128]{3,2,1,0:T(8,128)S(1)}, u32[]{:S(2)}, u32[]{:S(2)}) collective-permute-start(f32[2,16,16,128]{3,2,1,0:T(8,128)S(1)} %get-tuple-element.61), channel_id=1, source_target_pairs={{0,4},{1,5},{2,6},{3,7},{4,0},{5,1},{6,2},{7,3},{8,12},{9,13},{10,... | collective-permute-start | bytes 786440 | tf_op jit(solution)/shard_map/ppermute | solution.py:384
  46.5 11.0 %collective-permute-start.17 = (f32[2,16,16,128]{3,2,1,0:T(8,128)S(1)}, f32[2,16,16,128]{3,2,1,0:T(8,128)S(1)}, u32[]{:S(2)}, u32[]{:S(2)}) collective-permute-start(f32[2,16,16,128]{3,2,1,0:T(8,128)S(1)} %get-tuple-element.62), channel_id=1, source_target_pairs={{0,6},{1,7},{2,4},{3,5},{4,2},{5,3},{6,0},{7,1},{8,14},{9,15},{10,... | collective-permute-start | bytes 786440 | tf_op jit(solution)/shard_map/ppermute | solution.py:384
  49.1 8.9 %collective-permute-start.13 = (f32[2,16,16,128]{3,2,1,0:T(8,128)S(1)}, f32[2,16,16,128]{3,2,1,0:T(8,128)S(1)}, u32[]{:S(2)}, u32[]{:S(2)}) collective-permute-start(f32[2,16,16,128]{3,2,1,0:T(8,128)S(1)} %get-tuple-element.59.refs_0_), channel_id=1, source_target_pairs={{0,1},{1,0},{2,3},{3,2},{4,5},{5,4},{6,7},{7,6},{8,9},{9,8},{10,11... | collective-permute-start | bytes 786440 | tf_op jit(solution)/shard_map/ppermute | solution.py:384
  53.5 4.6 %collective-permute-start.14 = (f32[2,16,16,128]{3,2,1,0:T(8,128)S(1)}, f32[2,16,16,128]{3,2,1,0:T(8,128)S(1)}, u32[]{:S(2)}, u32[]{:S(2)}) collective-permute-start(f32[2,16,16,128]{3,2,1,0:T(8,128)S(1)} %collective-permute-done.12.refs_2_), channel_id=1, source_target_pairs={{0,1},{1,0},{2,3},{3,2},{4,5},{5,4},{6,7},{7,6},{8,9},{9,8},{10,11... | collective-permute-start | bytes 786440 | tf_op jit(solution)/shard_map/ppermute | solution.py:384
  57.5 1.5 %collective-permute-start.16 = (f32[2,16,16,128]{3,2,1,0:T(8,128)S(1)}, f32[2,16,16,128]{3,2,1,0:T(8,128)S(1)}, u32[]{:S(2)}, u32[]{:S(2)}) collective-permute-start(f32[2,16,16,128]{3,2,1,0:T(8,128)S(1)} %collective-permute-done.15.refs_4_), channel_id=1, source_target_pairs={{0,1},{1,0},{2,3},{3,2},{4,5},{5,4},{6,7},{7,6},{8,9},{9,8},{10,11... | collective-permute-start | bytes 786440 | tf_op jit(solution)/shard_map/ppermute | solution.py:384
  57.5 1.9 %collective-permute-start.18 = (f32[2,16,16,128]{3,2,1,0:T(8,128)S(1)}, f32[2,16,16,128]{3,2,1,0:T(8,128)S(1)}, u32[]{:S(2)}, u32[]{:S(2)}) collective-permute-start(f32[2,16,16,128]{3,2,1,0:T(8,128)S(1)} %collective-permute-done.17.refs_6_), channel_id=1, source_target_pairs={{0,1},{1,0},{2,3},{3,2},{4,5},{5,4},{6,7},{7,6},{8,9},{9,8},{10,11... | collective-permute-start | bytes 786440 | tf_op jit(solution)/shard_map/ppermute | solution.py:384

commit v10 on v9

--- a/solution.py
+++ b/solution.py
@@ -245,7 +245,7 @@
             turned_ref[f, which * nodes : (which + 1) * nodes, :] = jnp.where(left, imag, -real).astype(jnp.bfloat16)
             return 0
 
-        lax.fori_loop(0, BAND, one, 0, unroll=16)
+        lax.fori_loop(0, BAND, one, 0, unroll=32)
 
 
 def by_bin(blocks):
@@ -287,7 +287,7 @@
         )
         return 0
 
-    lax.fori_loop(0, BAND, one_bin, 0, unroll=8)
+    lax.fori_loop(0, BAND, one_bin, 0, unroll=32)
     _, is_first = position(len(outs))
     own_at = jnp.where(is_first, 0, 1)
     left = lax.broadcasted_iota(jnp.int32, (2 * BAND, 2 * count), 1) < count
@@ -306,7 +306,7 @@
                 shares[d // 2][d % 2, node] = picked[d * slots : (d + 1) * slots, :]
             return 0
 
-        lax.fori_loop(0, nodes, one_node, 0, unroll=8)
+        lax.fori_loop(0, nodes, one_node, 0, unroll=16)
 
 
 def cross_products(halves, select, wins):

time: 63 us -> 61.9 us (0.983)
  Pallas kernels: 25.2 us -> 24.1 us
    pallas_call x1, Pallas kernels: 3.53 us -> 2.48 us  [cross_products(): pl.pallas_call(cross_kernel, out_shape=[block] * wins, in_specs=[vmem] *...]
where the time goes in v10:
time: 61.9 us; the launch traced here: 61.4 us
  Pallas kernels  24.1 us (39%)
  starting transfers between devices  20 us (32%)
  waiting for transfers between devices  16.1 us (26%)
    pallas_call x2, Pallas kernels, own_spectra(): pl.pallas_call(functools.partial(spectra_kernel, steps=steps, wins=len(st...  14.6 us
    ppermute x14, starting transfers between devices, hop(): return lax.ppermute(array, ('pairs', 'win'), pairing)  11.2 us
    ppermute x14, waiting for transfers between devices, hop(): return lax.ppermute(array, ('pairs', 'win'), pairing)  10.2 us
    ppermute x2, waiting for transfers between devices, per_device(): lax.ppermute(b, 'pairs', swap_b)  5.81 us
    ppermute x2, starting transfers between devices, per_device(): lax.ppermute(b, 'pairs', swap_b)  5.55 us
    pallas_call x2, Pallas kernels, by_bin(): pl.pallas_call(functools.partial(by_bin_kernel, steps=steps), out_shape=[...  3.03 us
    pallas_call x1, Pallas kernels, inverse(): pl.pallas_call(inverse_kernel, in_specs=[vmem] * (2 + len(blocks)), out_s...  2.91 us
    pallas_call x1, Pallas kernels, cross_products(): pl.pallas_call(cross_kernel, out_shape=[block] * wins, in_specs=[vmem] *...  2.48 us
  transfers between devices with their start and end apart: 19, of which 8 were waited for; matrix products, arithmetic and copies ran while one was open for 1% of the time, Pallas kernels for 30%

profile of v10, /device:TPU:16, one launch (start us, length us, event | category | flops | bytes accessed | tf_op | source)
XLA Modules:
  0.0 61.4 jit_solution(1289221767549602101)
XLA Ops:
  0.0 0.0 collective-permute-start.5
  0.1 7.3 %own_spectra.2 = (bf16[16,32,128]{2,1,0:T(8,128)(2,1)}, bf16[16,32,128]{2,1,0:T(8,128)(2,1)}, bf16[16,32,128]{2,1,0:T(8,128)(2,1)}, bf16[16,32,128]{2,1,0:T(8,128)(2,1)}) custom-call(bf16[512,4096]{1,0:T(8,128)(2,1)} %bitcast.15, f32[1,129]{1,0:T(1,128)} %bitcast.16, f32[129,1024]{1,0:T(8,128)} %constant.116.clone.fine_hbm, ...), custom_call_target="tpu_custom_call" | custom-call | flops 2147483648 | bytes 4194304 | tf_op jit(solution)/shard_map/own_spectra/pallas_call | solution.py:167
  7.4 1.6 %collective-permute-start.11 = (s32[16,64]{1,0:T(8,128)S(1)}, s32[16,64]{1,0:T(8,128)S(1)}, u32[]{:S(2)}, u32[]{:S(2)}) collective-permute-start(s32[16,64]{1,0:T(8,128)S(1)} %fusion.3), channel_id=1, source_target_pairs={{0,4},{4,0},{8,12},{12,8},{16,20},{20,16},{24,28},{28,24},{1,5},{5... | collective-permute-start | bytes 12296 | tf_op jit(solution)/shard_map/ppermute | solution.py:404
  9.0 1.5 %collective-permute-start = (bf16[16,32,128]{2,1,0:T(8,128)(2,1)}, bf16[16,32,128]{2,1,0:T(8,128)(2,1)S(1)}, u32[]{:S(2)}, u32[]{:S(2)}) collective-permute-start(bf16[16,32,128]{2,1,0:T(8,128)(2,1)} %get-tuple-element.39), channel_id=1, source_target_pairs={{0,2},{1,3},{2,0},{3,1},{4,6},{5,7},{6,4},{7,5},{8,10},{9,11},{10,... | collective-permute-start | bytes 393224 | tf_op jit(solution)/shard_map/ppermute | solution.py:384
  10.5 0.5 collective-permute-start.1
  11.0 1.5 %collective-permute-start.2 = (bf16[16,32,128]{2,1,0:T(8,128)(2,1)}, bf16[16,32,128]{2,1,0:T(8,128)(2,1)S(1)}, u32[]{:S(2)}, u32[]{:S(2)}) collective-permute-start(bf16[16,32,128]{2,1,0:T(8,128)(2,1)} %get-tuple-element.41), channel_id=1, source_target_pairs={{0,6},{1,7},{2,4},{3,5},{4,2},{5,3},{6,0},{7,1},{8,14},{9,15},{10,... | collective-permute-start | bytes 393224 | tf_op jit(solution)/shard_map/ppermute | solution.py:384
  12.5 0.1 copy.15
  12.6 0.0 collective-permute-done.11
  12.6 0.1 copy.16
  12.7 0.1 add_select_fusion
  12.8 0.0 collective-permute-done.5.x_hbm
  12.8 7.3 %own_spectra.3 = (bf16[16,32,128]{2,1,0:T(8,128)(2,1)}, bf16[16,32,128]{2,1,0:T(8,128)(2,1)}, bf16[16,32,128]{2,1,0:T(8,128)(2,1)}, bf16[16,32,128]{2,1,0:T(8,128)(2,1)}) custom-call(bf16[512,4096]{1,0:T(8,128)(2,1)} %collective-permute-done.5.x_hbm, f32[1,129]{1,0:T(1,128)} %bitcast.17, f32[129,1024]{1,0:T(8,128)} %constant.116.clone.fine_hbm, ...), custom_call_target="tpu_custom_call" | custom-call | flops 2147483648 | bytes 4194304 | tf_op jit(solution)/shard_map/own_spectra/pallas_call | solution.py:167
  20.1 1.5 %collective-permute-start.6 = (bf16[16,32,128]{2,1,0:T(8,128)(2,1)}, bf16[16,32,128]{2,1,0:T(8,128)(2,1)S(1)}, u32[]{:S(2)}, u32[]{:S(2)}) collective-permute-start(bf16[16,32,128]{2,1,0:T(8,128)(2,1)} %get-tuple-element.46), channel_id=1, source_target_pairs={{0,2},{1,3},{2,0},{3,1},{4,6},{5,7},{6,4},{7,5},{8,10},{9,11},{10,... | collective-permute-start | bytes 393224 | tf_op jit(solution)/shard_map/ppermute | solution.py:384
  21.7 0.5 collective-permute-start.7
  22.2 0.0 collective-permute-done.refs_1_
  22.2 1.5 %collective-permute-start.8 = (bf16[16,32,128]{2,1,0:T(8,128)(2,1)}, bf16[16,32,128]{2,1,0:T(8,128)(2,1)S(1)}, u32[]{:S(2)}, u32[]{:S(2)}) collective-permute-start(bf16[16,32,128]{2,1,0:T(8,128)(2,1)} %get-tuple-element.48), channel_id=1, source_target_pairs={{0,6},{1,7},{2,4},{3,5},{4,2},{5,3},{6,0},{7,1},{8,14},{9,15},{10,... | collective-permute-start | bytes 393224 | tf_op jit(solution)/shard_map/ppermute | solution.py:384
  23.7 0.0 collective-permute-done.1.refs_2_
  23.7 0.0 collective-permute-done.2.refs_3_
  23.7 1.5 %by_bin.2 = (bf16[64,16,128]{2,1,0:T(8,128)(2,1)S(1)}, bf16[64,16,128]{2,1,0:T(8,128)(2,1)S(1)}, bf16[64,32,128]{2,1,0:T(8,128)(2,1)S(1)}) custom-call(bf16[16,32,128]{2,1,0:T(8,128)(2,1)S(1)} %copy-done.4, bf16[16,32,128]{2,1,0:T(8,128)(2,1)S(1)} %collective-permute-done.refs_1_, bf16[16,32,128]{2,1,0:T(8,128)(2,1)S(1)} %collective-permute-done.1.refs_2_, ...), custom_call_target="tpu_custom_call" | custom-call | flops 2147483648 | bytes 4194304 | tf_op jit(solution)/shard_map/by_bin/pallas_call | solution.py:256
  25.2 1.6 %collective-permute-start.3 = (bf16[64,16,128]{2,1,0:T(8,128)(2,1)S(1)}, bf16[64,16,128]{2,1,0:T(8,128)(2,1)S(1)}, u32[]{:S(2)}, u32[]{:S(2)}) collective-permute-start(bf16[64,16,128]{2,1,0:T(8,128)(2,1)S(1)} %get-tuple-element.42.refs_0_), channel_id=1, source_target_pairs={{0,8},{4,12},{8,0},{12,4},{16,24},{20,28},{24,16},{28,20},{1,9},{5... | collective-permute-start | bytes 786440 | tf_op jit(solution)/shard_map/ppermute | solution.py:424
  26.8 1.9 %collective-permute-start.4 = (bf16[64,16,128]{2,1,0:T(8,128)(2,1)S(1)}, bf16[64,16,128]{2,1,0:T(8,128)(2,1)S(1)}, u32[]{:S(2)}, u32[]{:S(2)}) collective-permute-start(bf16[64,16,128]{2,1,0:T(8,128)(2,1)S(1)} %get-tuple-element.43.refs_1_), channel_id=1, source_target_pairs={{8,16},{12,20},{16,8},{20,12},{9,17},{13,21},{17,9},{21,13},{10,18... | collective-permute-start | bytes 786440 | tf_op jit(solution)/shard_map/ppermute | solution.py:424
  28.8 0.0 collective-permute-done.6.refs_1_
  28.8 0.5 collective-permute-done.7.refs_2_
  29.3 0.0 collective-permute-done.8.refs_3_
  29.3 0.0 copy-start.2
  29.3 0.0 copy-start.3
  29.3 1.5 %by_bin.3 = (bf16[64,16,128]{2,1,0:T(8,128)(2,1)S(1)}, bf16[64,16,128]{2,1,0:T(8,128)(2,1)S(1)}, bf16[64,32,128]{2,1,0:T(8,128)(2,1)S(1)}) custom-call(bf16[16,32,128]{2,1,0:T(8,128)(2,1)S(1)} %copy-done.5, bf16[16,32,128]{2,1,0:T(8,128)(2,1)S(1)} %collective-permute-done.6.refs_1_, bf16[16,32,128]{2,1,0:T(8,128)(2,1)S(1)} %collective-permute-done.7.refs_2_, ...), custom_call_target="tpu_custom_call" | custom-call | flops 2147483648 | bytes 4194304 | tf_op jit(solution)/shard_map/by_bin/pallas_call | solution.py:256
  30.8 3.6 %collective-permute-start.10 = (bf16[64,16,128]{2,1,0:T(8,128)(2,1)S(1)}, bf16[64,16,128]{2,1,0:T(8,128)(2,1)S(1)}, u32[]{:S(2)}, u32[]{:S(2)}) collective-permute-start(bf16[64,16,128]{2,1,0:T(8,128)(2,1)S(1)} %get-tuple-element.50.refs_6_), channel_id=1, source_target_pairs={{8,16},{12,20},{16,8},{20,12},{9,17},{13,21},{17,9},{21,13},{10,18... | collective-permute-start | bytes 786440 | tf_op jit(solution)/shard_map/ppermute | solution.py:424
  34.5 0.1 collective-permute-start.9
  34.6 0.1 copy.17
  34.6 0.3 compare_convert_fusion.refs_10_
  35.0 0.0 collective-permute-done.3.refs_3_
  35.0 2.3 %collective-permute-done.4.refs_4_ = bf16[64,16,128]{2,1,0:T(8,128)(2,1)S(1)} collective-permute-done((bf16[64,16,128]{2,1,0:T(8,128)(2,1)S(1)}, bf16[64,16,128]{2,1,0:T(8,128)(2,1)S(1)}, u32[]{:S(2)}, u32[]{:S(2)}) %collective-permute-start.4) | collective-permute-done | bytes 262176 | tf_op jit(solution)/shard_map/ppermute | solution.py:424
  37.3 3.5 %collective-permute-done.10.refs_9_ = bf16[64,16,128]{2,1,0:T(8,128)(2,1)S(1)} collective-permute-done((bf16[64,16,128]{2,1,0:T(8,128)(2,1)S(1)}, bf16[64,16,128]{2,1,0:T(8,128)(2,1)S(1)}, u32[]{:S(2)}, u32[]{:S(2)}) %collective-permute-start.10) | collective-permute-done | bytes 262176 | tf_op jit(solution)/shard_map/ppermute | solution.py:424
  40.8 0.1 collective-permute-done.9.refs_8_
  40.9 2.5 %cross_products.1 = (f32[2,16,16,128]{3,2,1,0:T(8,128)S(1)}, f32[2,16,16,128]{3,2,1,0:T(8,128)S(1)}, f32[2,16,16,128]{3,2,1,0:T(8,128)S(1)}, f32[2,16,16,128]{3,2,1,0:T(8,128)S(1)}) custom-call(bf16[64,16,128]{2,1,0:T(8,128)(2,1)S(1)} %get-tuple-element.42.refs_0_, bf16[64,16,128]{2,1,0:T(8,128)(2,1)S(1)} %get-tuple-element.43.refs_1_, ...), custom_call_target="tpu_custom_call" | custom-call | tf_op jit(solution)/shard_map/cross_products/pallas_call | solution.py:317
  43.4 1.5 %collective-permute-start.12 = (f32[2,16,16,128]{3,2,1,0:T(8,128)S(1)}, f32[2,16,16,128]{3,2,1,0:T(8,128)S(1)}, u32[]{:S(2)}, u32[]{:S(2)}) collective-permute-start(f32[2,16,16,128]{3,2,1,0:T(8,128)S(1)} %get-tuple-element.54), channel_id=1, source_target_pairs={{0,2},{1,3},{2,0},{3,1},{4,6},{5,7},{6,4},{7,5},{8,10},{9,11},{10,... | collective-permute-start | bytes 786440 | tf_op jit(solution)/shard_map/ppermute | solution.py:384
  44.9 0.5 collective-permute-start.15
  45.4 1.5 %collective-permute-start.17 = (f32[2,16,16,128]{3,2,1,0:T(8,128)S(1)}, f32[2,16,16,128]{3,2,1,0:T(8,128)S(1)}, u32[]{:S(2)}, u32[]{:S(2)}) collective-permute-start(f32[2,16,16,128]{3,2,1,0:T(8,128)S(1)} %get-tuple-element.62), channel_id=1, source_target_pairs={{0,6},{1,7},{2,4},{3,5},{4,2},{5,3},{6,0},{7,1},{8,14},{9,15},{10,... | collective-permute-start | bytes 786440 | tf_op jit(solution)/shard_map/ppermute | solution.py:384
  46.9 1.1 %lag_tables.1 = (bf16[8,128,1024]{2,1,0:T(8,128)(2,1)S(1)}, bf16[8,128,1024]{2,1,0:T(8,128)(2,1)S(1)}) custom-call(f32[64,1024]{1,0:T(8,128)S(1)} %copy-done, f32[64,1024]{1,0:T(8,128)S(1)} %copy-done.1, f32[8,1024]{1,0:T(8,128)S(1)} %copy-done.2, f32[8,1024]{1,0:T(8,128)S(1)} %copy-done.3), custom_call_target="tpu_custom_call" | custom-call | tf_op jit(solution)/shard_map/lag_tables/pallas_call | solution.py:204
  48.0 0.1 collective-permute-start.13
  48.1 4.2 %collective-permute-done.12.refs_2_ = f32[2,16,16,128]{3,2,1,0:T(8,128)S(1)} collective-permute-done((f32[2,16,16,128]{3,2,1,0:T(8,128)S(1)}, f32[2,16,16,128]{3,2,1,0:T(8,128)S(1)}, u32[]{:S(2)}, u32[]{:S(2)}) %collective-permute-start.12) | collective-permute-done | bytes 262176 | tf_op jit(solution)/shard_map/ppermute | solution.py:384
  52.4 4.1 %collective-permute-done.15.refs_4_ = f32[2,16,16,128]{3,2,1,0:T(8,128)S(1)} collective-permute-done((f32[2,16,16,128]{3,2,1,0:T(8,128)S(1)}, f32[2,16,16,128]{3,2,1,0:T(8,128)S(1)}, u32[]{:S(2)}, u32[]{:S(2)}) %collective-permute-start.15) | collective-permute-done | bytes 262176 | tf_op jit(solution)/shard_map/ppermute | solution.py:384
  56.4 0.0 collective-permute-start.16
  56.4 0.5 collective-permute-start.18
  56.9 1.0 %collective-permute-done.16.refs_5_ = f32[2,16,16,128]{3,2,1,0:T(8,128)S(1)} collective-permute-done((f32[2,16,16,128]{3,2,1,0:T(8,128)S(1)}, f32[2,16,16,128]{3,2,1,0:T(8,128)S(1)}, u32[]{:S(2)}, u32[]{:S(2)}) %collective-permute-start.16) | collective-permute-done | bytes 262176 | tf_op jit(solution)/shard_map/ppermute | solution.py:384
  58.0 0.4 collective-permute-done.18.refs_7_
  58.3 2.9 %inverse.1 = f32[16,16,1024]{2,1,0:T(8,128)} custom-call(bf16[1024,1024]{1,0:T(8,128)(2,1)S(1)} %bitcast.8, bf16[1024,1024]{1,0:T(8,128)(2,1)S(1)} %bitcast.9, f32[2,16,16,128]{3,2,1,0:T(8,128)S(1)} %get-tuple-element.59.refs_0_, f32[2,16,16,128]{3,2,1,0:T(8,128)S(1)} %collective-permute-done.13.refs_1_, ...), custom_call_target="tpu_custom_call" | custom-call | tf_op jit(solution)/shard_map/inverse/pallas_call | solution.py:359
  (22 shorter events, 0.1 us)
Async XLA Ops:
  0.0 7.4 %copy-start.6 = (s32[16,64]{1,0:T(8,128)S(1)}, s32[16,64]{1,0:T(8,128)}, u32[]{:S(2)}) copy-start(s32[16,64]{1,0:T(8,128)} %param.16) | copy-start | bytes 12292
  0.0 7.4 %copy-start.7 = (s32[16,64]{1,0:T(8,128)S(1)}, s32[16,64]{1,0:T(8,128)}, u32[]{:S(2)}) copy-start(s32[16,64]{1,0:T(8,128)} %param.17) | copy-start | bytes 12292
  0.0 12.8 %collective-permute-start.5 = (bf16[512,4096]{1,0:T(8,128)(2,1)}, bf16[512,4096]{1,0:T(8,128)(2,1)}, u32[]{:S(2)}, u32[]{:S(2)}) collective-permute-start(bf16[512,4096]{1,0:T(8,128)(2,1)} %bitcast.14), channel_id=1, source_target_pairs={{0,1},{1,0},{2,3},{3,2},{4,5},{5,4},{6,7},{7,6},{8,9},{9,8},{10,11... | collective-permute-start | bytes 12582920 | tf_op jit(solution)/shard_map/ppermute | solution.py:384
  7.3 16.3 %copy-start.4 = (bf16[16,32,128]{2,1,0:T(8,128)(2,1)S(1)}, bf16[16,32,128]{2,1,0:T(8,128)(2,1)}, u32[]{:S(2)}) copy-start(bf16[16,32,128]{2,1,0:T(8,128)(2,1)} %get-tuple-element.38.refs_0_) | copy-start | bytes 393220
  7.4 5.2 %collective-permute-start.11 = (s32[16,64]{1,0:T(8,128)S(1)}, s32[16,64]{1,0:T(8,128)S(1)}, u32[]{:S(2)}, u32[]{:S(2)}) collective-permute-start(s32[16,64]{1,0:T(8,128)S(1)} %fusion.3), channel_id=1, source_target_pairs={{0,4},{4,0},{8,12},{12,8},{16,20},{20,16},{24,28},{28,24},{1,5},{5... | collective-permute-start | bytes 12296 | tf_op jit(solution)/shard_map/ppermute | solution.py:404
  9.0 13.2 %collective-permute-start = (bf16[16,32,128]{2,1,0:T(8,128)(2,1)}, bf16[16,32,128]{2,1,0:T(8,128)(2,1)S(1)}, u32[]{:S(2)}, u32[]{:S(2)}) collective-permute-start(bf16[16,32,128]{2,1,0:T(8,128)(2,1)} %get-tuple-element.39), channel_id=1, source_target_pairs={{0,2},{1,3},{2,0},{3,1},{4,6},{5,7},{6,4},{7,5},{8,10},{9,11},{10,... | collective-permute-start | bytes 393224 | tf_op jit(solution)/shard_map/ppermute | solution.py:384
  10.5 13.2 %collective-permute-start.1 = (bf16[16,32,128]{2,1,0:T(8,128)(2,1)}, bf16[16,32,128]{2,1,0:T(8,128)(2,1)S(1)}, u32[]{:S(2)}, u32[]{:S(2)}) collective-permute-start(bf16[16,32,128]{2,1,0:T(8,128)(2,1)} %get-tuple-element.40), channel_id=1, source_target_pairs={{0,4},{1,5},{2,6},{3,7},{4,0},{5,1},{6,2},{7,3},{8,12},{9,13},{10,... | collective-permute-start | bytes 393224 | tf_op jit(solution)/shard_map/ppermute | solution.py:384
  11.0 12.7 %collective-permute-start.2 = (bf16[16,32,128]{2,1,0:T(8,128)(2,1)}, bf16[16,32,128]{2,1,0:T(8,128)(2,1)S(1)}, u32[]{:S(2)}, u32[]{:S(2)}) collective-permute-start(bf16[16,32,128]{2,1,0:T(8,128)(2,1)} %get-tuple-element.41), channel_id=1, source_target_pairs={{0,6},{1,7},{2,4},{3,5},{4,2},{5,3},{6,0},{7,1},{8,14},{9,15},{10,... | collective-permute-start | bytes 393224 | tf_op jit(solution)/shard_map/ppermute | solution.py:384
  20.1 9.2 %copy-start.5 = (bf16[16,32,128]{2,1,0:T(8,128)(2,1)S(1)}, bf16[16,32,128]{2,1,0:T(8,128)(2,1)}, u32[]{:S(2)}) copy-start(bf16[16,32,128]{2,1,0:T(8,128)(2,1)} %get-tuple-element.45.refs_0_) | copy-start | bytes 393220
  20.1 8.6 %collective-permute-start.6 = (bf16[16,32,128]{2,1,0:T(8,128)(2,1)}, bf16[16,32,128]{2,1,0:T(8,128)(2,1)S(1)}, u32[]{:S(2)}, u32[]{:S(2)}) collective-permute-start(bf16[16,32,128]{2,1,0:T(8,128)(2,1)} %get-tuple-element.46), channel_id=1, source_target_pairs={{0,2},{1,3},{2,0},{3,1},{4,6},{5,7},{6,4},{7,5},{8,10},{9,11},{10,... | collective-permute-start | bytes 393224 | tf_op jit(solution)/shard_map/ppermute | solution.py:384
  21.7 7.6 %collective-permute-start.7 = (bf16[16,32,128]{2,1,0:T(8,128)(2,1)}, bf16[16,32,128]{2,1,0:T(8,128)(2,1)S(1)}, u32[]{:S(2)}, u32[]{:S(2)}) collective-permute-start(bf16[16,32,128]{2,1,0:T(8,128)(2,1)} %get-tuple-element.47), channel_id=1, source_target_pairs={{0,4},{1,5},{2,6},{3,7},{4,0},{5,1},{6,2},{7,3},{8,12},{9,13},{10,... | collective-permute-start | bytes 393224 | tf_op jit(solution)/shard_map/ppermute | solution.py:384
  22.2 7.1 %collective-permute-start.8 = (bf16[16,32,128]{2,1,0:T(8,128)(2,1)}, bf16[16,32,128]{2,1,0:T(8,128)(2,1)S(1)}, u32[]{:S(2)}, u32[]{:S(2)}) collective-permute-start(bf16[16,32,128]{2,1,0:T(8,128)(2,1)} %get-tuple-element.48), channel_id=1, source_target_pairs={{0,6},{1,7},{2,4},{3,5},{4,2},{5,3},{6,0},{7,1},{8,14},{9,15},{10,... | collective-permute-start | bytes 393224 | tf_op jit(solution)/shard_map/ppermute | solution.py:384
  25.2 9.8 %collective-permute-start.3 = (bf16[64,16,128]{2,1,0:T(8,128)(2,1)S(1)}, bf16[64,16,128]{2,1,0:T(8,128)(2,1)S(1)}, u32[]{:S(2)}, u32[]{:S(2)}) collective-permute-start(bf16[64,16,128]{2,1,0:T(8,128)(2,1)S(1)} %get-tuple-element.42.refs_0_), channel_id=1, source_target_pairs={{0,8},{4,12},{8,0},{12,4},{16,24},{20,28},{24,16},{28,20},{1,9},{5... | collective-permute-start | bytes 786440 | tf_op jit(solution)/shard_map/ppermute | solution.py:424
  26.8 10.5 %collective-permute-start.4 = (bf16[64,16,128]{2,1,0:T(8,128)(2,1)S(1)}, bf16[64,16,128]{2,1,0:T(8,128)(2,1)S(1)}, u32[]{:S(2)}, u32[]{:S(2)}) collective-permute-start(bf16[64,16,128]{2,1,0:T(8,128)(2,1)S(1)} %get-tuple-element.43.refs_1_), channel_id=1, source_target_pairs={{8,16},{12,20},{16,8},{20,12},{9,17},{13,21},{17,9},{21,13},{10,18... | collective-permute-start | bytes 786440 | tf_op jit(solution)/shard_map/ppermute | solution.py:424
  29.3 17.7 %copy-start = (f32[64,1024]{1,0:T(8,128)S(1)}, f32[64,1024]{1,0:T(8,128)}, u32[]{:S(2)}) copy-start(f32[64,1024]{1,0:T(8,128)} %constant.119.clone.cos_ref) | copy-start | bytes 786436
  29.3 17.6 %copy-start.2 = (f32[8,1024]{1,0:T(8,128)S(1)}, f32[8,1024]{1,0:T(8,128)}, u32[]{:S(2)}) copy-start(f32[8,1024]{1,0:T(8,128)} %constant.121.clone.cos0_ref) | copy-start | bytes 98308
  29.3 17.6 %copy-start.3 = (f32[8,1024]{1,0:T(8,128)S(1)}, f32[8,1024]{1,0:T(8,128)}, u32[]{:S(2)}) copy-start(f32[8,1024]{1,0:T(8,128)} %constant.122.clone.msin0_ref) | copy-start | bytes 98308
  30.8 10.0 %collective-permute-start.10 = (bf16[64,16,128]{2,1,0:T(8,128)(2,1)S(1)}, bf16[64,16,128]{2,1,0:T(8,128)(2,1)S(1)}, u32[]{:S(2)}, u32[]{:S(2)}) collective-permute-start(bf16[64,16,128]{2,1,0:T(8,128)(2,1)S(1)} %get-tuple-element.50.refs_6_), channel_id=1, source_target_pairs={{8,16},{12,20},{16,8},{20,12},{9,17},{13,21},{17,9},{21,13},{10,18... | collective-permute-start | bytes 786440 | tf_op jit(solution)/shard_map/ppermute | solution.py:424
  34.5 6.4 %collective-permute-start.9 = (bf16[64,16,128]{2,1,0:T(8,128)(2,1)S(1)}, bf16[64,16,128]{2,1,0:T(8,128)(2,1)S(1)}, u32[]{:S(2)}, u32[]{:S(2)}) collective-permute-start(bf16[64,16,128]{2,1,0:T(8,128)(2,1)S(1)} %get-tuple-element.49.refs_5_), channel_id=1, source_target_pairs={{0,8},{4,12},{8,0},{12,4},{16,24},{20,28},{24,16},{28,20},{1,9},{5... | collective-permute-start | bytes 786440 | tf_op jit(solution)/shard_map/ppermute | solution.py:424
  34.6 12.3 %copy-start.1 = (f32[64,1024]{1,0:T(8,128)S(1)}, f32[64,1024]{1,0:T(8,128)}, u32[]{:S(2)}) copy-start(f32[64,1024]{1,0:T(8,128)} %constant.120.clone.msin_ref) | copy-start | bytes 786436
  43.4 9.0 %collective-permute-start.12 = (f32[2,16,16,128]{3,2,1,0:T(8,128)S(1)}, f32[2,16,16,128]{3,2,1,0:T(8,128)S(1)}, u32[]{:S(2)}, u32[]{:S(2)}) collective-permute-start(f32[2,16,16,128]{3,2,1,0:T(8,128)S(1)} %get-tuple-element.54), channel_id=1, source_target_pairs={{0,2},{1,3},{2,0},{3,1},{4,6},{5,7},{6,4},{7,5},{8,10},{9,11},{10,... | collective-permute-start | bytes 786440 | tf_op jit(solution)/shard_map/ppermute | solution.py:384
  44.9 11.5 %collective-permute-start.15 = (f32[2,16,16,128]{3,2,1,0:T(8,128)S(1)}, f32[2,16,16,128]{3,2,1,0:T(8,128)S(1)}, u32[]{:S(2)}, u32[]{:S(2)}) collective-permute-start(f32[2,16,16,128]{3,2,1,0:T(8,128)S(1)} %get-tuple-element.61), channel_id=1, source_target_pairs={{0,4},{1,5},{2,6},{3,7},{4,0},{5,1},{6,2},{7,3},{8,12},{9,13},{10,... | collective-permute-start | bytes 786440 | tf_op jit(solution)/shard_map/ppermute | solution.py:384
  45.4 11.0 %collective-permute-start.17 = (f32[2,16,16,128]{3,2,1,0:T(8,128)S(1)}, f32[2,16,16,128]{3,2,1,0:T(8,128)S(1)}, u32[]{:S(2)}, u32[]{:S(2)}) collective-permute-start(f32[2,16,16,128]{3,2,1,0:T(8,128)S(1)} %get-tuple-element.62), channel_id=1, source_target_pairs={{0,6},{1,7},{2,4},{3,5},{4,2},{5,3},{6,0},{7,1},{8,14},{9,15},{10,... | collective-permute-start | bytes 786440 | tf_op jit(solution)/shard_map/ppermute | solution.py:384
  48.0 8.9 %collective-permute-start.13 = (f32[2,16,16,128]{3,2,1,0:T(8,128)S(1)}, f32[2,16,16,128]{3,2,1,0:T(8,128)S(1)}, u32[]{:S(2)}, u32[]{:S(2)}) collective-permute-start(f32[2,16,16,128]{3,2,1,0:T(8,128)S(1)} %get-tuple-element.59.refs_0_), channel_id=1, source_target_pairs={{0,1},{1,0},{2,3},{3,2},{4,5},{5,4},{6,7},{7,6},{8,9},{9,8},{10,11... | collective-permute-start | bytes 786440 | tf_op jit(solution)/shard_map/ppermute | solution.py:384
  52.4 4.6 %collective-permute-start.14 = (f32[2,16,16,128]{3,2,1,0:T(8,128)S(1)}, f32[2,16,16,128]{3,2,1,0:T(8,128)S(1)}, u32[]{:S(2)}, u32[]{:S(2)}) collective-permute-start(f32[2,16,16,128]{3,2,1,0:T(8,128)S(1)} %collective-permute-done.12.refs_2_), channel_id=1, source_target_pairs={{0,1},{1,0},{2,3},{3,2},{4,5},{5,4},{6,7},{7,6},{8,9},{9,8},{10,11... | collective-permute-start | bytes 786440 | tf_op jit(solution)/shard_map/ppermute | solution.py:384
  56.4 1.5 %collective-permute-start.16 = (f32[2,16,16,128]{3,2,1,0:T(8,128)S(1)}, f32[2,16,16,128]{3,2,1,0:T(8,128)S(1)}, u32[]{:S(2)}, u32[]{:S(2)}) collective-permute-start(f32[2,16,16,128]{3,2,1,0:T(8,128)S(1)} %collective-permute-done.15.refs_4_), channel_id=1, source_target_pairs={{0,1},{1,0},{2,3},{3,2},{4,5},{5,4},{6,7},{7,6},{8,9},{9,8},{10,11... | collective-permute-start | bytes 786440 | tf_op jit(solution)/shard_map/ppermute | solution.py:384
  56.4 1.9 %collective-permute-start.18 = (f32[2,16,16,128]{3,2,1,0:T(8,128)S(1)}, f32[2,16,16,128]{3,2,1,0:T(8,128)S(1)}, u32[]{:S(2)}, u32[]{:S(2)}) collective-permute-start(f32[2,16,16,128]{3,2,1,0:T(8,128)S(1)} %collective-permute-done.17.refs_6_), channel_id=1, source_target_pairs={{0,1},{1,0},{2,3},{3,2},{4,5},{5,4},{6,7},{7,6},{8,9},{9,8},{10,11... | collective-permute-start | bytes 786440 | tf_op jit(solution)/shard_map/ppermute | solution.py:384

commit v11 on v10

--- a/solution.py
+++ b/solution.py
@@ -245,7 +245,7 @@
             turned_ref[f, which * nodes : (which + 1) * nodes, :] = jnp.where(left, imag, -real).astype(jnp.bfloat16)
             return 0
 
-        lax.fori_loop(0, BAND, one, 0, unroll=32)
+        lax.fori_loop(0, BAND, one, 0, unroll=64)
 
 
 def by_bin(blocks):
@@ -271,6 +271,7 @@
 
 def cross_kernel(*refs):
     halves = [refs[5 * h : 5 * h + 5] for h in range(HALVES)]
+    halves[-1] = (*halves[-1][0:3], halves[-1][4], halves[-1][3])
     select_ref, *outs, cross = refs[5 * HALVES :]
     nodes = halves[0][0].shape[1]
     slots = outs[0].shape[2]
@@ -287,7 +288,7 @@
         )
         return 0
 
-    lax.fori_loop(0, BAND, one_bin, 0, unroll=32)
+    lax.fori_loop(0, BAND, one_bin, 0, unroll=64)
     _, is_first = position(len(outs))
     own_at = jnp.where(is_first, 0, 1)
     left = lax.broadcasted_iota(jnp.int32, (2 * BAND, 2 * count), 1) < count
@@ -313,6 +314,7 @@
     nodes = halves[0][0].shape[1]
     block = jax.ShapeDtypeStruct((2, nodes, select.shape[1] // wins, LANES), jnp.float32)
     vmem = pl.BlockSpec(memory_space=pltpu.VMEM)
+    halves = [*halves[:-1], (*halves[-1][0:3], halves[-1][4], halves[-1][3])]
     operands = [x for half in halves for x in half]
     return pl.pallas_call(
         cross_kernel,

time: 61.9 us -> 62.1 us (level)
    ppermute x2, starting transfers between devices: 1.7 us -> 3.26 us  [per_device(): lax.ppermute(a, 'pairs', swap_a)]
    ppermute x2, starting transfers between devices: 5.55 us -> 4.06 us  [per_device(): lax.ppermute(b, 'pairs', swap_b)]
    ppermute x2, waiting for transfers between devices: 5.81 us -> 4.49 us  [per_device(): lax.ppermute(b, 'pairs', swap_b)]
    ppermute x2, waiting for transfers between devices: 0.1 us -> 1.27 us  [per_device(): lax.ppermute(a, 'pairs', swap_a)]
  transfers between devices with their start and end apart: 19 -> 19, of which waited for: 8 -> 8; matrix products, arithmetic and copies ran while one was open for 1% -> 1% of each run, Pallas kernels for 30% -> 31%
where the time goes in v11:
time: 62.1 us; the launch traced here: 61.6 us
  Pallas kernels  24.1 us (39%)
  starting transfers between devices  20.1 us (32%)
  waiting for transfers between devices  16.3 us (26%)
    pallas_call x2, Pallas kernels, own_spectra(): pl.pallas_call(functools.partial(spectra_kernel, steps=steps, wins=len(st...  14.6 us
    ppermute x14, starting transfers between devices, hop(): return lax.ppermute(array, ('pairs', 'win'), pairing)  11.2 us
    ppermute x14, waiting for transfers between devices, hop(): return lax.ppermute(array, ('pairs', 'win'), pairing)  10.5 us
    ppermute x2, waiting for transfers between devices, per_device(): lax.ppermute(b, 'pairs', swap_b)  4.49 us
    ppermute x2, starting transfers between devices, per_device(): lax.ppermute(b, 'pairs', swap_b)  4.06 us
    ppermute x2, starting transfers between devices, per_device(): lax.ppermute(a, 'pairs', swap_a)  3.26 us
    pallas_call x2, Pallas kernels, by_bin(): pl.pallas_call(functools.partial(by_bin_kernel, steps=steps), out_shape=[...  3.15 us
    pallas_call x1, Pallas kernels, inverse(): pl.pallas_call(inverse_kernel, in_specs=[vmem] * (2 + len(blocks)), out_s...  2.91 us
  transfers between devices with their start and end apart: 19, of which 8 were waited for; matrix products, arithmetic and copies ran while one was open for 1% of the time, Pallas kernels for 31%

profile of v11, /device:TPU:16, one launch (start us, length us, event | category | flops | bytes accessed | tf_op | source)
XLA Modules:
  0.0 61.6 jit_solution(14486053676057500756)
XLA Ops:
  0.0 0.0 collective-permute-start.5
  0.1 7.3 %own_spectra.2 = (bf16[16,32,128]{2,1,0:T(8,128)(2,1)}, bf16[16,32,128]{2,1,0:T(8,128)(2,1)}, bf16[16,32,128]{2,1,0:T(8,128)(2,1)}, bf16[16,32,128]{2,1,0:T(8,128)(2,1)}) custom-call(bf16[512,4096]{1,0:T(8,128)(2,1)} %bitcast.15, f32[1,129]{1,0:T(1,128)} %bitcast.16, f32[129,1024]{1,0:T(8,128)} %constant.116.clone.fine_hbm, ...), custom_call_target="tpu_custom_call" | custom-call | flops 2147483648 | bytes 4194304 | tf_op jit(solution)/shard_map/own_spectra/pallas_call | solution.py:167
  7.4 1.6 %collective-permute-start.11 = (s32[16,64]{1,0:T(8,128)S(1)}, s32[16,64]{1,0:T(8,128)S(1)}, u32[]{:S(2)}, u32[]{:S(2)}) collective-permute-start(s32[16,64]{1,0:T(8,128)S(1)} %fusion.3), channel_id=1, source_target_pairs={{0,4},{4,0},{8,12},{12,8},{16,20},{20,16},{24,28},{28,24},{1,5},{5... | collective-permute-start | bytes 12296 | tf_op jit(solution)/shard_map/ppermute | solution.py:406
  9.0 1.5 %collective-permute-start = (bf16[16,32,128]{2,1,0:T(8,128)(2,1)}, bf16[16,32,128]{2,1,0:T(8,128)(2,1)S(1)}, u32[]{:S(2)}, u32[]{:S(2)}) collective-permute-start(bf16[16,32,128]{2,1,0:T(8,128)(2,1)} %get-tuple-element.39), channel_id=1, source_target_pairs={{0,2},{1,3},{2,0},{3,1},{4,6},{5,7},{6,4},{7,5},{8,10},{9,11},{10,... | collective-permute-start | bytes 393224 | tf_op jit(solution)/shard_map/ppermute | solution.py:386
  10.5 0.5 collective-permute-start.1
  11.0 1.5 %collective-permute-start.2 = (bf16[16,32,128]{2,1,0:T(8,128)(2,1)}, bf16[16,32,128]{2,1,0:T(8,128)(2,1)S(1)}, u32[]{:S(2)}, u32[]{:S(2)}) collective-permute-start(bf16[16,32,128]{2,1,0:T(8,128)(2,1)} %get-tuple-element.41), channel_id=1, source_target_pairs={{0,6},{1,7},{2,4},{3,5},{4,2},{5,3},{6,0},{7,1},{8,14},{9,15},{10,... | collective-permute-start | bytes 393224 | tf_op jit(solution)/shard_map/ppermute | solution.py:386
  12.5 0.1 copy.15
  12.6 0.0 collective-permute-done.11
  12.6 0.1 copy.16
  12.7 0.1 add_select_fusion
  12.8 0.0 collective-permute-done.5.x_hbm
  12.8 7.3 %own_spectra.3 = (bf16[16,32,128]{2,1,0:T(8,128)(2,1)}, bf16[16,32,128]{2,1,0:T(8,128)(2,1)}, bf16[16,32,128]{2,1,0:T(8,128)(2,1)}, bf16[16,32,128]{2,1,0:T(8,128)(2,1)}) custom-call(bf16[512,4096]{1,0:T(8,128)(2,1)} %collective-permute-done.5.x_hbm, f32[1,129]{1,0:T(1,128)} %bitcast.17, f32[129,1024]{1,0:T(8,128)} %constant.116.clone.fine_hbm, ...), custom_call_target="tpu_custom_call" | custom-call | flops 2147483648 | bytes 4194304 | tf_op jit(solution)/shard_map/own_spectra/pallas_call | solution.py:167
  20.1 1.5 %collective-permute-start.6 = (bf16[16,32,128]{2,1,0:T(8,128)(2,1)}, bf16[16,32,128]{2,1,0:T(8,128)(2,1)S(1)}, u32[]{:S(2)}, u32[]{:S(2)}) collective-permute-start(bf16[16,32,128]{2,1,0:T(8,128)(2,1)} %get-tuple-element.46), channel_id=1, source_target_pairs={{0,2},{1,3},{2,0},{3,1},{4,6},{5,7},{6,4},{7,5},{8,10},{9,11},{10,... | collective-permute-start | bytes 393224 | tf_op jit(solution)/shard_map/ppermute | solution.py:386
  21.7 0.5 collective-permute-start.7
  22.2 0.0 collective-permute-done.refs_1_
  22.2 1.5 %collective-permute-start.8 = (bf16[16,32,128]{2,1,0:T(8,128)(2,1)}, bf16[16,32,128]{2,1,0:T(8,128)(2,1)S(1)}, u32[]{:S(2)}, u32[]{:S(2)}) collective-permute-start(bf16[16,32,128]{2,1,0:T(8,128)(2,1)} %get-tuple-element.48), channel_id=1, source_target_pairs={{0,6},{1,7},{2,4},{3,5},{4,2},{5,3},{6,0},{7,1},{8,14},{9,15},{10,... | collective-permute-start | bytes 393224 | tf_op jit(solution)/shard_map/ppermute | solution.py:386
  23.7 0.0 collective-permute-done.1.refs_2_
  23.7 0.0 collective-permute-done.2.refs_3_
  23.7 1.6 %by_bin.2 = (bf16[64,16,128]{2,1,0:T(8,128)(2,1)S(1)}, bf16[64,16,128]{2,1,0:T(8,128)(2,1)S(1)}, bf16[64,32,128]{2,1,0:T(8,128)(2,1)S(1)}) custom-call(bf16[16,32,128]{2,1,0:T(8,128)(2,1)S(1)} %copy-done.4, bf16[16,32,128]{2,1,0:T(8,128)(2,1)S(1)} %collective-permute-done.refs_1_, bf16[16,32,128]{2,1,0:T(8,128)(2,1)S(1)} %collective-permute-done.1.refs_2_, ...), custom_call_target="tpu_custom_call" | custom-call | flops 2147483648 | bytes 4194304 | tf_op jit(solution)/shard_map/by_bin/pallas_call | solution.py:256
  25.3 1.6 %collective-permute-start.3 = (bf16[64,16,128]{2,1,0:T(8,128)(2,1)S(1)}, bf16[64,16,128]{2,1,0:T(8,128)(2,1)S(1)}, u32[]{:S(2)}, u32[]{:S(2)}) collective-permute-start(bf16[64,16,128]{2,1,0:T(8,128)(2,1)S(1)} %get-tuple-element.42.refs_0_), channel_id=1, source_target_pairs={{0,8},{4,12},{8,0},{12,4},{16,24},{20,28},{24,16},{28,20},{1,9},{5... | collective-permute-start | bytes 786440 | tf_op jit(solution)/shard_map/ppermute | solution.py:426
  26.9 1.9 %collective-permute-start.4 = (bf16[64,16,128]{2,1,0:T(8,128)(2,1)S(1)}, bf16[64,16,128]{2,1,0:T(8,128)(2,1)S(1)}, u32[]{:S(2)}, u32[]{:S(2)}) collective-permute-start(bf16[64,16,128]{2,1,0:T(8,128)(2,1)S(1)} %get-tuple-element.43.refs_1_), channel_id=1, source_target_pairs={{8,16},{12,20},{16,8},{20,12},{9,17},{13,21},{17,9},{21,13},{10,18... | collective-permute-start | bytes 786440 | tf_op jit(solution)/shard_map/ppermute | solution.py:426
  28.8 0.0 collective-permute-done.6.refs_1_
  28.8 0.4 collective-permute-done.7.refs_2_
  29.3 0.0 collective-permute-done.8.refs_3_
  29.3 0.0 copy-start.2
  29.3 0.0 copy-start.3
  29.3 1.6 %by_bin.3 = (bf16[64,16,128]{2,1,0:T(8,128)(2,1)S(1)}, bf16[64,16,128]{2,1,0:T(8,128)(2,1)S(1)}, bf16[64,32,128]{2,1,0:T(8,128)(2,1)S(1)}) custom-call(bf16[16,32,128]{2,1,0:T(8,128)(2,1)S(1)} %copy-done.5, bf16[16,32,128]{2,1,0:T(8,128)(2,1)S(1)} %collective-permute-done.6.refs_1_, bf16[16,32,128]{2,1,0:T(8,128)(2,1)S(1)} %collective-permute-done.7.refs_2_, ...), custom_call_target="tpu_custom_call" | custom-call | flops 2147483648 | bytes 4194304 | tf_op jit(solution)/shard_map/by_bin/pallas_call | solution.py:256
  30.9 1.6 %collective-permute-start.10 = (bf16[64,16,128]{2,1,0:T(8,128)(2,1)S(1)}, bf16[64,16,128]{2,1,0:T(8,128)(2,1)S(1)}, u32[]{:S(2)}, u32[]{:S(2)}) collective-permute-start(bf16[64,16,128]{2,1,0:T(8,128)(2,1)S(1)} %get-tuple-element.49.refs_5_), channel_id=1, source_target_pairs={{0,8},{4,12},{8,0},{12,4},{16,24},{20,28},{24,16},{28,20},{1,9},{5... | collective-permute-start | bytes 786440 | tf_op jit(solution)/shard_map/ppermute | solution.py:426
  32.5 2.1 %collective-permute-start.9 = (bf16[64,16,128]{2,1,0:T(8,128)(2,1)S(1)}, bf16[64,16,128]{2,1,0:T(8,128)(2,1)S(1)}, u32[]{:S(2)}, u32[]{:S(2)}) collective-permute-start(bf16[64,16,128]{2,1,0:T(8,128)(2,1)S(1)} %get-tuple-element.50.refs_6_), channel_id=1, source_target_pairs={{8,16},{12,20},{16,8},{20,12},{9,17},{13,21},{17,9},{21,13},{10,18... | collective-permute-start | bytes 786440 | tf_op jit(solution)/shard_map/ppermute | solution.py:426
  34.7 0.1 copy.17
  34.8 0.3 compare_convert_fusion.refs_10_
  35.1 0.0 collective-permute-done.3.refs_3_
  35.1 1.3 %collective-permute-done.4.refs_4_ = bf16[64,16,128]{2,1,0:T(8,128)(2,1)S(1)} collective-permute-done((bf16[64,16,128]{2,1,0:T(8,128)(2,1)S(1)}, bf16[64,16,128]{2,1,0:T(8,128)(2,1)S(1)}, u32[]{:S(2)}, u32[]{:S(2)}) %collective-permute-start.4) | collective-permute-done | bytes 262176 | tf_op jit(solution)/shard_map/ppermute | solution.py:426
  36.4 1.3 %collective-permute-done.10.refs_9_ = bf16[64,16,128]{2,1,0:T(8,128)(2,1)S(1)} collective-permute-done((bf16[64,16,128]{2,1,0:T(8,128)(2,1)S(1)}, bf16[64,16,128]{2,1,0:T(8,128)(2,1)S(1)}, u32[]{:S(2)}, u32[]{:S(2)}) %collective-permute-start.10) | collective-permute-done | bytes 262176 | tf_op jit(solution)/shard_map/ppermute | solution.py:426
  37.7 3.2 %collective-permute-done.9.refs_8_ = bf16[64,16,128]{2,1,0:T(8,128)(2,1)S(1)} collective-permute-done((bf16[64,16,128]{2,1,0:T(8,128)(2,1)S(1)}, bf16[64,16,128]{2,1,0:T(8,128)(2,1)S(1)}, u32[]{:S(2)}, u32[]{:S(2)}) %collective-permute-start.9) | collective-permute-done | bytes 262176 | tf_op jit(solution)/shard_map/ppermute | solution.py:426
  40.9 2.4 %cross_products.1 = (f32[2,16,16,128]{3,2,1,0:T(8,128)S(1)}, f32[2,16,16,128]{3,2,1,0:T(8,128)S(1)}, f32[2,16,16,128]{3,2,1,0:T(8,128)S(1)}, f32[2,16,16,128]{3,2,1,0:T(8,128)S(1)}) custom-call(bf16[64,16,128]{2,1,0:T(8,128)(2,1)S(1)} %get-tuple-element.42.refs_0_, bf16[64,16,128]{2,1,0:T(8,128)(2,1)S(1)} %get-tuple-element.43.refs_1_, ...), custom_call_target="tpu_custom_call" | custom-call | tf_op jit(solution)/shard_map/cross_products/pallas_call | solution.py:319
  43.3 1.5 %collective-permute-start.12 = (f32[2,16,16,128]{3,2,1,0:T(8,128)S(1)}, f32[2,16,16,128]{3,2,1,0:T(8,128)S(1)}, u32[]{:S(2)}, u32[]{:S(2)}) collective-permute-start(f32[2,16,16,128]{3,2,1,0:T(8,128)S(1)} %get-tuple-element.54), channel_id=1, source_target_pairs={{0,2},{1,3},{2,0},{3,1},{4,6},{5,7},{6,4},{7,5},{8,10},{9,11},{10,... | collective-permute-start | bytes 786440 | tf_op jit(solution)/shard_map/ppermute | solution.py:386
  44.8 0.5 collective-permute-start.15
  45.3 1.5 %collective-permute-start.17 = (f32[2,16,16,128]{3,2,1,0:T(8,128)S(1)}, f32[2,16,16,128]{3,2,1,0:T(8,128)S(1)}, u32[]{:S(2)}, u32[]{:S(2)}) collective-permute-start(f32[2,16,16,128]{3,2,1,0:T(8,128)S(1)} %get-tuple-element.62), channel_id=1, source_target_pairs={{0,6},{1,7},{2,4},{3,5},{4,2},{5,3},{6,0},{7,1},{8,14},{9,15},{10,... | collective-permute-start | bytes 786440 | tf_op jit(solution)/shard_map/ppermute | solution.py:386
  46.8 1.1 %lag_tables.1 = (bf16[8,128,1024]{2,1,0:T(8,128)(2,1)S(1)}, bf16[8,128,1024]{2,1,0:T(8,128)(2,1)S(1)}) custom-call(f32[64,1024]{1,0:T(8,128)S(1)} %copy-done, f32[64,1024]{1,0:T(8,128)S(1)} %copy-done.1, f32[8,1024]{1,0:T(8,128)S(1)} %copy-done.2, f32[8,1024]{1,0:T(8,128)S(1)} %copy-done.3), custom_call_target="tpu_custom_call" | custom-call | tf_op jit(solution)/shard_map/lag_tables/pallas_call | solution.py:204
  47.9 0.1 collective-permute-start.13
  48.0 4.4 %collective-permute-done.12.refs_2_ = f32[2,16,16,128]{3,2,1,0:T(8,128)S(1)} collective-permute-done((f32[2,16,16,128]{3,2,1,0:T(8,128)S(1)}, f32[2,16,16,128]{3,2,1,0:T(8,128)S(1)}, u32[]{:S(2)}, u32[]{:S(2)}) %collective-permute-start.12) | collective-permute-done | bytes 262176 | tf_op jit(solution)/shard_map/ppermute | solution.py:386
  52.4 0.0 collective-permute-start.14
  52.4 4.3 %collective-permute-done.15.refs_4_ = f32[2,16,16,128]{3,2,1,0:T(8,128)S(1)} collective-permute-done((f32[2,16,16,128]{3,2,1,0:T(8,128)S(1)}, f32[2,16,16,128]{3,2,1,0:T(8,128)S(1)}, u32[]{:S(2)}, u32[]{:S(2)}) %collective-permute-start.15) | collective-permute-done | bytes 262176 | tf_op jit(solution)/shard_map/ppermute | solution.py:386
  56.7 0.5 collective-permute-start.18
  57.2 1.0 %collective-permute-done.16.refs_5_ = f32[2,16,16,128]{3,2,1,0:T(8,128)S(1)} collective-permute-done((f32[2,16,16,128]{3,2,1,0:T(8,128)S(1)}, f32[2,16,16,128]{3,2,1,0:T(8,128)S(1)}, u32[]{:S(2)}, u32[]{:S(2)}) %collective-permute-start.16) | collective-permute-done | bytes 262176 | tf_op jit(solution)/shard_map/ppermute | solution.py:386
  58.2 0.4 collective-permute-done.18.refs_7_
  58.6 2.9 %inverse.1 = f32[16,16,1024]{2,1,0:T(8,128)} custom-call(bf16[1024,1024]{1,0:T(8,128)(2,1)S(1)} %bitcast.8, bf16[1024,1024]{1,0:T(8,128)(2,1)S(1)} %bitcast.9, f32[2,16,16,128]{3,2,1,0:T(8,128)S(1)} %get-tuple-element.59.refs_0_, f32[2,16,16,128]{3,2,1,0:T(8,128)S(1)} %collective-permute-done.13.refs_1_, ...), custom_call_target="tpu_custom_call" | custom-call | tf_op jit(solution)/shard_map/inverse/pallas_call | solution.py:361
  (22 shorter events, 0.1 us)
Async XLA Ops:
  0.0 7.4 %copy-start.6 = (s32[16,64]{1,0:T(8,128)S(1)}, s32[16,64]{1,0:T(8,128)}, u32[]{:S(2)}) copy-start(s32[16,64]{1,0:T(8,128)} %param.16) | copy-start | bytes 12292
  0.0 7.4 %copy-start.7 = (s32[16,64]{1,0:T(8,128)S(1)}, s32[16,64]{1,0:T(8,128)}, u32[]{:S(2)}) copy-start(s32[16,64]{1,0:T(8,128)} %param.17) | copy-start | bytes 12292
  0.0 12.8 %collective-permute-start.5 = (bf16[512,4096]{1,0:T(8,128)(2,1)}, bf16[512,4096]{1,0:T(8,128)(2,1)}, u32[]{:S(2)}, u32[]{:S(2)}) collective-permute-start(bf16[512,4096]{1,0:T(8,128)(2,1)} %bitcast.14), channel_id=1, source_target_pairs={{0,1},{1,0},{2,3},{3,2},{4,5},{5,4},{6,7},{7,6},{8,9},{9,8},{10,11... | collective-permute-start | bytes 12582920 | tf_op jit(solution)/shard_map/ppermute | solution.py:386
  7.3 16.3 %copy-start.4 = (bf16[16,32,128]{2,1,0:T(8,128)(2,1)S(1)}, bf16[16,32,128]{2,1,0:T(8,128)(2,1)}, u32[]{:S(2)}) copy-start(bf16[16,32,128]{2,1,0:T(8,128)(2,1)} %get-tuple-element.38.refs_0_) | copy-start | bytes 393220
  7.4 5.2 %collective-permute-start.11 = (s32[16,64]{1,0:T(8,128)S(1)}, s32[16,64]{1,0:T(8,128)S(1)}, u32[]{:S(2)}, u32[]{:S(2)}) collective-permute-start(s32[16,64]{1,0:T(8,128)S(1)} %fusion.3), channel_id=1, source_target_pairs={{0,4},{4,0},{8,12},{12,8},{16,20},{20,16},{24,28},{28,24},{1,5},{5... | collective-permute-start | bytes 12296 | tf_op jit(solution)/shard_map/ppermute | solution.py:406
  9.0 13.2 %collective-permute-start = (bf16[16,32,128]{2,1,0:T(8,128)(2,1)}, bf16[16,32,128]{2,1,0:T(8,128)(2,1)S(1)}, u32[]{:S(2)}, u32[]{:S(2)}) collective-permute-start(bf16[16,32,128]{2,1,0:T(8,128)(2,1)} %get-tuple-element.39), channel_id=1, source_target_pairs={{0,2},{1,3},{2,0},{3,1},{4,6},{5,7},{6,4},{7,5},{8,10},{9,11},{10,... | collective-permute-start | bytes 393224 | tf_op jit(solution)/shard_map/ppermute | solution.py:386
  10.5 13.2 %collective-permute-start.1 = (bf16[16,32,128]{2,1,0:T(8,128)(2,1)}, bf16[16,32,128]{2,1,0:T(8,128)(2,1)S(1)}, u32[]{:S(2)}, u32[]{:S(2)}) collective-permute-start(bf16[16,32,128]{2,1,0:T(8,128)(2,1)} %get-tuple-element.40), channel_id=1, source_target_pairs={{0,4},{1,5},{2,6},{3,7},{4,0},{5,1},{6,2},{7,3},{8,12},{9,13},{10,... | collective-permute-start | bytes 393224 | tf_op jit(solution)/shard_map/ppermute | solution.py:386
  11.0 12.7 %collective-permute-start.2 = (bf16[16,32,128]{2,1,0:T(8,128)(2,1)}, bf16[16,32,128]{2,1,0:T(8,128)(2,1)S(1)}, u32[]{:S(2)}, u32[]{:S(2)}) collective-permute-start(bf16[16,32,128]{2,1,0:T(8,128)(2,1)} %get-tuple-element.41), channel_id=1, source_target_pairs={{0,6},{1,7},{2,4},{3,5},{4,2},{5,3},{6,0},{7,1},{8,14},{9,15},{10,... | collective-permute-start | bytes 393224 | tf_op jit(solution)/shard_map/ppermute | solution.py:386
  20.1 9.2 %copy-start.5 = (bf16[16,32,128]{2,1,0:T(8,128)(2,1)S(1)}, bf16[16,32,128]{2,1,0:T(8,128)(2,1)}, u32[]{:S(2)}) copy-start(bf16[16,32,128]{2,1,0:T(8,128)(2,1)} %get-tuple-element.45.refs_0_) | copy-start | bytes 393220
  20.1 8.7 %collective-permute-start.6 = (bf16[16,32,128]{2,1,0:T(8,128)(2,1)}, bf16[16,32,128]{2,1,0:T(8,128)(2,1)S(1)}, u32[]{:S(2)}, u32[]{:S(2)}) collective-permute-start(bf16[16,32,128]{2,1,0:T(8,128)(2,1)} %get-tuple-element.46), channel_id=1, source_target_pairs={{0,2},{1,3},{2,0},{3,1},{4,6},{5,7},{6,4},{7,5},{8,10},{9,11},{10,... | collective-permute-start | bytes 393224 | tf_op jit(solution)/shard_map/ppermute | solution.py:386
  21.7 7.6 %collective-permute-start.7 = (bf16[16,32,128]{2,1,0:T(8,128)(2,1)}, bf16[16,32,128]{2,1,0:T(8,128)(2,1)S(1)}, u32[]{:S(2)}, u32[]{:S(2)}) collective-permute-start(bf16[16,32,128]{2,1,0:T(8,128)(2,1)} %get-tuple-element.47), channel_id=1, source_target_pairs={{0,4},{1,5},{2,6},{3,7},{4,0},{5,1},{6,2},{7,3},{8,12},{9,13},{10,... | collective-permute-start | bytes 393224 | tf_op jit(solution)/shard_map/ppermute | solution.py:386
  22.2 7.1 %collective-permute-start.8 = (bf16[16,32,128]{2,1,0:T(8,128)(2,1)}, bf16[16,32,128]{2,1,0:T(8,128)(2,1)S(1)}, u32[]{:S(2)}, u32[]{:S(2)}) collective-permute-start(bf16[16,32,128]{2,1,0:T(8,128)(2,1)} %get-tuple-element.48), channel_id=1, source_target_pairs={{0,6},{1,7},{2,4},{3,5},{4,2},{5,3},{6,0},{7,1},{8,14},{9,15},{10,... | collective-permute-start | bytes 393224 | tf_op jit(solution)/shard_map/ppermute | solution.py:386
  25.3 9.8 %collective-permute-start.3 = (bf16[64,16,128]{2,1,0:T(8,128)(2,1)S(1)}, bf16[64,16,128]{2,1,0:T(8,128)(2,1)S(1)}, u32[]{:S(2)}, u32[]{:S(2)}) collective-permute-start(bf16[64,16,128]{2,1,0:T(8,128)(2,1)S(1)} %get-tuple-element.42.refs_0_), channel_id=1, source_target_pairs={{0,8},{4,12},{8,0},{12,4},{16,24},{20,28},{24,16},{28,20},{1,9},{5... | collective-permute-start | bytes 786440 | tf_op jit(solution)/shard_map/ppermute | solution.py:426
  26.9 9.5 %collective-permute-start.4 = (bf16[64,16,128]{2,1,0:T(8,128)(2,1)S(1)}, bf16[64,16,128]{2,1,0:T(8,128)(2,1)S(1)}, u32[]{:S(2)}, u32[]{:S(2)}) collective-permute-start(bf16[64,16,128]{2,1,0:T(8,128)(2,1)S(1)} %get-tuple-element.43.refs_1_), channel_id=1, source_target_pairs={{8,16},{12,20},{16,8},{20,12},{9,17},{13,21},{17,9},{21,13},{10,18... | collective-permute-start | bytes 786440 | tf_op jit(solution)/shard_map/ppermute | solution.py:426
  29.3 17.5 %copy-start = (f32[64,1024]{1,0:T(8,128)S(1)}, f32[64,1024]{1,0:T(8,128)}, u32[]{:S(2)}) copy-start(f32[64,1024]{1,0:T(8,128)} %constant.119.clone.cos_ref) | copy-start | bytes 786436
  29.3 17.5 %copy-start.2 = (f32[8,1024]{1,0:T(8,128)S(1)}, f32[8,1024]{1,0:T(8,128)}, u32[]{:S(2)}) copy-start(f32[8,1024]{1,0:T(8,128)} %constant.121.clone.cos0_ref) | copy-start | bytes 98308
  29.3 17.5 %copy-start.3 = (f32[8,1024]{1,0:T(8,128)S(1)}, f32[8,1024]{1,0:T(8,128)}, u32[]{:S(2)}) copy-start(f32[8,1024]{1,0:T(8,128)} %constant.122.clone.msin0_ref) | copy-start | bytes 98308
  30.9 6.8 %collective-permute-start.10 = (bf16[64,16,128]{2,1,0:T(8,128)(2,1)S(1)}, bf16[64,16,128]{2,1,0:T(8,128)(2,1)S(1)}, u32[]{:S(2)}, u32[]{:S(2)}) collective-permute-start(bf16[64,16,128]{2,1,0:T(8,128)(2,1)S(1)} %get-tuple-element.49.refs_5_), channel_id=1, source_target_pairs={{0,8},{4,12},{8,0},{12,4},{16,24},{20,28},{24,16},{28,20},{1,9},{5... | collective-permute-start | bytes 786440 | tf_op jit(solution)/shard_map/ppermute | solution.py:426
  32.5 8.4 %collective-permute-start.9 = (bf16[64,16,128]{2,1,0:T(8,128)(2,1)S(1)}, bf16[64,16,128]{2,1,0:T(8,128)(2,1)S(1)}, u32[]{:S(2)}, u32[]{:S(2)}) collective-permute-start(bf16[64,16,128]{2,1,0:T(8,128)(2,1)S(1)} %get-tuple-element.50.refs_6_), channel_id=1, source_target_pairs={{8,16},{12,20},{16,8},{20,12},{9,17},{13,21},{17,9},{21,13},{10,18... | collective-permute-start | bytes 786440 | tf_op jit(solution)/shard_map/ppermute | solution.py:426
  34.7 12.0 %copy-start.1 = (f32[64,1024]{1,0:T(8,128)S(1)}, f32[64,1024]{1,0:T(8,128)}, u32[]{:S(2)}) copy-start(f32[64,1024]{1,0:T(8,128)} %constant.120.clone.msin_ref) | copy-start | bytes 786436
  43.3 9.1 %collective-permute-start.12 = (f32[2,16,16,128]{3,2,1,0:T(8,128)S(1)}, f32[2,16,16,128]{3,2,1,0:T(8,128)S(1)}, u32[]{:S(2)}, u32[]{:S(2)}) collective-permute-start(f32[2,16,16,128]{3,2,1,0:T(8,128)S(1)} %get-tuple-element.54), channel_id=1, source_target_pairs={{0,2},{1,3},{2,0},{3,1},{4,6},{5,7},{6,4},{7,5},{8,10},{9,11},{10,... | collective-permute-start | bytes 786440 | tf_op jit(solution)/shard_map/ppermute | solution.py:386
  44.8 11.9 %collective-permute-start.15 = (f32[2,16,16,128]{3,2,1,0:T(8,128)S(1)}, f32[2,16,16,128]{3,2,1,0:T(8,128)S(1)}, u32[]{:S(2)}, u32[]{:S(2)}) collective-permute-start(f32[2,16,16,128]{3,2,1,0:T(8,128)S(1)} %get-tuple-element.61), channel_id=1, source_target_pairs={{0,4},{1,5},{2,6},{3,7},{4,0},{5,1},{6,2},{7,3},{8,12},{9,13},{10,... | collective-permute-start | bytes 786440 | tf_op jit(solution)/shard_map/ppermute | solution.py:386
  45.3 11.4 %collective-permute-start.17 = (f32[2,16,16,128]{3,2,1,0:T(8,128)S(1)}, f32[2,16,16,128]{3,2,1,0:T(8,128)S(1)}, u32[]{:S(2)}, u32[]{:S(2)}) collective-permute-start(f32[2,16,16,128]{3,2,1,0:T(8,128)S(1)} %get-tuple-element.62), channel_id=1, source_target_pairs={{0,6},{1,7},{2,4},{3,5},{4,2},{5,3},{6,0},{7,1},{8,14},{9,15},{10,... | collective-permute-start | bytes 786440 | tf_op jit(solution)/shard_map/ppermute | solution.py:386
  47.9 9.3 %collective-permute-start.13 = (f32[2,16,16,128]{3,2,1,0:T(8,128)S(1)}, f32[2,16,16,128]{3,2,1,0:T(8,128)S(1)}, u32[]{:S(2)}, u32[]{:S(2)}) collective-permute-start(f32[2,16,16,128]{3,2,1,0:T(8,128)S(1)} %get-tuple-element.59.refs_0_), channel_id=1, source_target_pairs={{0,1},{1,0},{2,3},{3,2},{4,5},{5,4},{6,7},{7,6},{8,9},{9,8},{10,11... | collective-permute-start | bytes 786440 | tf_op jit(solution)/shard_map/ppermute | solution.py:386
  52.4 4.8 %collective-permute-start.14 = (f32[2,16,16,128]{3,2,1,0:T(8,128)S(1)}, f32[2,16,16,128]{3,2,1,0:T(8,128)S(1)}, u32[]{:S(2)}, u32[]{:S(2)}) collective-permute-start(f32[2,16,16,128]{3,2,1,0:T(8,128)S(1)} %collective-permute-done.12.refs_2_), channel_id=1, source_target_pairs={{0,1},{1,0},{2,3},{3,2},{4,5},{5,4},{6,7},{7,6},{8,9},{9,8},{10,11... | collective-permute-start | bytes 786440 | tf_op jit(solution)/shard_map/ppermute | solution.py:386
  56.7 1.5 %collective-permute-start.16 = (f32[2,16,16,128]{3,2,1,0:T(8,128)S(1)}, f32[2,16,16,128]{3,2,1,0:T(8,128)S(1)}, u32[]{:S(2)}, u32[]{:S(2)}) collective-permute-start(f32[2,16,16,128]{3,2,1,0:T(8,128)S(1)} %collective-permute-done.15.refs_4_), channel_id=1, source_target_pairs={{0,1},{1,0},{2,3},{3,2},{4,5},{5,4},{6,7},{7,6},{8,9},{9,8},{10,11... | collective-permute-start | bytes 786440 | tf_op jit(solution)/shard_map/ppermute | solution.py:386
  56.7 1.9 %collective-permute-start.18 = (f32[2,16,16,128]{3,2,1,0:T(8,128)S(1)}, f32[2,16,16,128]{3,2,1,0:T(8,128)S(1)}, u32[]{:S(2)}, u32[]{:S(2)}) collective-permute-start(f32[2,16,16,128]{3,2,1,0:T(8,128)S(1)} %collective-permute-done.17.refs_6_), channel_id=1, source_target_pairs={{0,1},{1,0},{2,3},{3,2},{4,5},{5,4},{6,7},{7,6},{8,9},{9,8},{10,11... | collective-permute-start | bytes 786440 | tf_op jit(solution)/shard_map/ppermute | solution.py:386

commit v12 on v11

--- a/solution.py
+++ b/solution.py
@@ -68,6 +68,7 @@
     width = 2 * LANES
     pitch = stages[0].shape[1] // windows
     pieces = SAMPLES // CHUNK
+    share = count // pieces
     me, _ = position(wins)
     copies = [
         pltpu.make_async_copy(source, target, sems.at[pieces + i])
@@ -77,7 +78,7 @@
     ]
     chunks = [
         pltpu.make_async_copy(
-            x_hbm.at[:, pl.ds(i * CHUNK, CHUNK)], x_ref.at[:, pl.ds(i * CHUNK, CHUNK)], sems.at[i]
+            x_hbm.at[pl.ds(i * share, share), :], x_ref.at[pl.ds(i * share, share), :], sems.at[i]
         )
         for i in range(pieces)
     ]
@@ -271,7 +272,6 @@
 
 def cross_kernel(*refs):
     halves = [refs[5 * h : 5 * h + 5] for h in range(HALVES)]
-    halves[-1] = (*halves[-1][0:3], halves[-1][4], halves[-1][3])
     select_ref, *outs, cross = refs[5 * HALVES :]
     nodes = halves[0][0].shape[1]
     slots = outs[0].shape[2]
@@ -314,7 +314,6 @@
     nodes = halves[0][0].shape[1]
     block = jax.ShapeDtypeStruct((2, nodes, select.shape[1] // wins, LANES), jnp.float32)
     vmem = pl.BlockSpec(memory_space=pltpu.VMEM)
-    halves = [*halves[:-1], (*halves[-1][0:3], halves[-1][4], halves[-1][3])]
     operands = [x for half in halves for x in half]
     return pl.pallas_call(
         cross_kernel,

time: 62.1 us -> 61.8 us (level)
    ppermute x2, starting transfers between devices: 4.06 us -> 5.62 us  [per_device(): lax.ppermute(b, 'pairs', swap_b)]
    ppermute x2, starting transfers between devices: 3.26 us -> 1.72 us  [per_device(): lax.ppermute(a, 'pairs', swap_a)]
    ppermute x2, waiting for transfers between devices: 4.49 us -> 5.75 us  [per_device(): lax.ppermute(b, 'pairs', swap_b)]
    ppermute x2, waiting for transfers between devices: 1.27 us -> 0.16 us  [per_device(): lax.ppermute(a, 'pairs', swap_a)]
where the time goes in v12:
time: 61.8 us; the launch traced here: 61.3 us
  Pallas kernels  24.1 us (39%)
  starting transfers between devices  20.1 us (33%)
  waiting for transfers between devices  16 us (26%)
    pallas_call x2, Pallas kernels, own_spectra(): pl.pallas_call(functools.partial(spectra_kernel, steps=steps, wins=len(st...  14.5 us
    ppermute x14, starting transfers between devices, hop(): return lax.ppermute(array, ('pairs', 'win'), pairing)  11.2 us
    ppermute x14, waiting for transfers between devices, hop(): return lax.ppermute(array, ('pairs', 'win'), pairing)  10.1 us
    ppermute x2, waiting for transfers between devices, per_device(): lax.ppermute(b, 'pairs', swap_b)  5.75 us
    ppermute x2, starting transfers between devices, per_device(): lax.ppermute(b, 'pairs', swap_b)  5.62 us
    pallas_call x2, Pallas kernels, by_bin(): pl.pallas_call(functools.partial(by_bin_kernel, steps=steps), out_shape=[...  3.12 us
    pallas_call x1, Pallas kernels, inverse(): pl.pallas_call(inverse_kernel, in_specs=[vmem] * (2 + len(blocks)), out_s...  2.91 us
    pallas_call x1, Pallas kernels, cross_products(): pl.pallas_call(cross_kernel, out_shape=[block] * wins, in_specs=[vmem] *...  2.38 us
  transfers between devices with their start and end apart: 19, of which 8 were waited for; matrix products, arithmetic and copies ran while one was open for 1% of the time, Pallas kernels for 31%

profile of v12, /device:TPU:16, one launch (start us, length us, event | category | flops | bytes accessed | tf_op | source)
XLA Modules:
  0.0 61.3 jit_solution(6000905677609512423)
XLA Ops:
  0.0 0.0 collective-permute-start.5
  0.1 7.3 %own_spectra.2 = (bf16[16,32,128]{2,1,0:T(8,128)(2,1)}, bf16[16,32,128]{2,1,0:T(8,128)(2,1)}, bf16[16,32,128]{2,1,0:T(8,128)(2,1)}, bf16[16,32,128]{2,1,0:T(8,128)(2,1)}) custom-call(bf16[512,4096]{1,0:T(8,128)(2,1)} %bitcast.15, f32[1,129]{1,0:T(1,128)} %bitcast.16, f32[129,1024]{1,0:T(8,128)} %constant.116.clone.fine_hbm, ...), custom_call_target="tpu_custom_call" | custom-call | flops 2147483648 | bytes 4194304 | tf_op jit(solution)/shard_map/own_spectra/pallas_call | solution.py:168
  7.4 1.6 %collective-permute-start.11 = (s32[16,64]{1,0:T(8,128)S(1)}, s32[16,64]{1,0:T(8,128)S(1)}, u32[]{:S(2)}, u32[]{:S(2)}) collective-permute-start(s32[16,64]{1,0:T(8,128)S(1)} %fusion.3), channel_id=1, source_target_pairs={{0,4},{4,0},{8,12},{12,8},{16,20},{20,16},{24,28},{28,24},{1,5},{5... | collective-permute-start | bytes 12296 | tf_op jit(solution)/shard_map/ppermute | solution.py:405
  9.0 1.5 %collective-permute-start = (bf16[16,32,128]{2,1,0:T(8,128)(2,1)}, bf16[16,32,128]{2,1,0:T(8,128)(2,1)S(1)}, u32[]{:S(2)}, u32[]{:S(2)}) collective-permute-start(bf16[16,32,128]{2,1,0:T(8,128)(2,1)} %get-tuple-element.39), channel_id=1, source_target_pairs={{0,2},{1,3},{2,0},{3,1},{4,6},{5,7},{6,4},{7,5},{8,10},{9,11},{10,... | collective-permute-start | bytes 393224 | tf_op jit(solution)/shard_map/ppermute | solution.py:385
  10.5 0.5 collective-permute-start.1
  11.0 1.5 %collective-permute-start.2 = (bf16[16,32,128]{2,1,0:T(8,128)(2,1)}, bf16[16,32,128]{2,1,0:T(8,128)(2,1)S(1)}, u32[]{:S(2)}, u32[]{:S(2)}) collective-permute-start(bf16[16,32,128]{2,1,0:T(8,128)(2,1)} %get-tuple-element.41), channel_id=1, source_target_pairs={{0,6},{1,7},{2,4},{3,5},{4,2},{5,3},{6,0},{7,1},{8,14},{9,15},{10,... | collective-permute-start | bytes 393224 | tf_op jit(solution)/shard_map/ppermute | solution.py:385
  12.5 0.1 copy.15
  12.5 0.0 collective-permute-done.11
  12.6 0.1 copy.16
  12.6 0.1 add_select_fusion
  12.7 0.0 collective-permute-done.5.x_hbm
  12.8 7.3 %own_spectra.3 = (bf16[16,32,128]{2,1,0:T(8,128)(2,1)}, bf16[16,32,128]{2,1,0:T(8,128)(2,1)}, bf16[16,32,128]{2,1,0:T(8,128)(2,1)}, bf16[16,32,128]{2,1,0:T(8,128)(2,1)}) custom-call(bf16[512,4096]{1,0:T(8,128)(2,1)} %collective-permute-done.5.x_hbm, f32[1,129]{1,0:T(1,128)} %bitcast.17, f32[129,1024]{1,0:T(8,128)} %constant.116.clone.fine_hbm, ...), custom_call_target="tpu_custom_call" | custom-call | flops 2147483648 | bytes 4194304 | tf_op jit(solution)/shard_map/own_spectra/pallas_call | solution.py:168
  20.1 1.5 %collective-permute-start.6 = (bf16[16,32,128]{2,1,0:T(8,128)(2,1)}, bf16[16,32,128]{2,1,0:T(8,128)(2,1)S(1)}, u32[]{:S(2)}, u32[]{:S(2)}) collective-permute-start(bf16[16,32,128]{2,1,0:T(8,128)(2,1)} %get-tuple-element.46), channel_id=1, source_target_pairs={{0,2},{1,3},{2,0},{3,1},{4,6},{5,7},{6,4},{7,5},{8,10},{9,11},{10,... | collective-permute-start | bytes 393224 | tf_op jit(solution)/shard_map/ppermute | solution.py:385
  21.6 0.5 collective-permute-start.7
  22.1 0.0 collective-permute-done.refs_1_
  22.1 1.5 %collective-permute-start.8 = (bf16[16,32,128]{2,1,0:T(8,128)(2,1)}, bf16[16,32,128]{2,1,0:T(8,128)(2,1)S(1)}, u32[]{:S(2)}, u32[]{:S(2)}) collective-permute-start(bf16[16,32,128]{2,1,0:T(8,128)(2,1)} %get-tuple-element.48), channel_id=1, source_target_pairs={{0,6},{1,7},{2,4},{3,5},{4,2},{5,3},{6,0},{7,1},{8,14},{9,15},{10,... | collective-permute-start | bytes 393224 | tf_op jit(solution)/shard_map/ppermute | solution.py:385
  23.6 1.6 %by_bin.2 = (bf16[64,16,128]{2,1,0:T(8,128)(2,1)S(1)}, bf16[64,16,128]{2,1,0:T(8,128)(2,1)S(1)}, bf16[64,32,128]{2,1,0:T(8,128)(2,1)S(1)}) custom-call(bf16[16,32,128]{2,1,0:T(8,128)(2,1)S(1)} %copy-done.4, bf16[16,32,128]{2,1,0:T(8,128)(2,1)S(1)} %collective-permute-done.refs_1_, bf16[16,32,128]{2,1,0:T(8,128)(2,1)S(1)} %collective-permute-done.1.refs_2_, ...), custom_call_target="tpu_custom_call" | custom-call | flops 2147483648 | bytes 4194304 | tf_op jit(solution)/shard_map/by_bin/pallas_call | solution.py:257
  25.2 1.6 %collective-permute-start.3 = (bf16[64,16,128]{2,1,0:T(8,128)(2,1)S(1)}, bf16[64,16,128]{2,1,0:T(8,128)(2,1)S(1)}, u32[]{:S(2)}, u32[]{:S(2)}) collective-permute-start(bf16[64,16,128]{2,1,0:T(8,128)(2,1)S(1)} %get-tuple-element.42.refs_0_), channel_id=1, source_target_pairs={{0,8},{4,12},{8,0},{12,4},{16,24},{20,28},{24,16},{28,20},{1,9},{5... | collective-permute-start | bytes 786440 | tf_op jit(solution)/shard_map/ppermute | solution.py:425
  26.8 1.9 %collective-permute-start.4 = (bf16[64,16,128]{2,1,0:T(8,128)(2,1)S(1)}, bf16[64,16,128]{2,1,0:T(8,128)(2,1)S(1)}, u32[]{:S(2)}, u32[]{:S(2)}) collective-permute-start(bf16[64,16,128]{2,1,0:T(8,128)(2,1)S(1)} %get-tuple-element.43.refs_1_), channel_id=1, source_target_pairs={{8,16},{12,20},{16,8},{20,12},{9,17},{13,21},{17,9},{21,13},{10,18... | collective-permute-start | bytes 786440 | tf_op jit(solution)/shard_map/ppermute | solution.py:425
  28.8 0.0 collective-permute-done.6.refs_1_
  28.8 0.4 collective-permute-done.7.refs_2_
  29.2 0.0 collective-permute-done.8.refs_3_
  29.2 0.0 copy-start.2
  29.2 0.0 copy-start.3
  29.2 1.6 %by_bin.3 = (bf16[64,16,128]{2,1,0:T(8,128)(2,1)S(1)}, bf16[64,16,128]{2,1,0:T(8,128)(2,1)S(1)}, bf16[64,32,128]{2,1,0:T(8,128)(2,1)S(1)}) custom-call(bf16[16,32,128]{2,1,0:T(8,128)(2,1)S(1)} %copy-done.5, bf16[16,32,128]{2,1,0:T(8,128)(2,1)S(1)} %collective-permute-done.6.refs_1_, bf16[16,32,128]{2,1,0:T(8,128)(2,1)S(1)} %collective-permute-done.7.refs_2_, ...), custom_call_target="tpu_custom_call" | custom-call | flops 2147483648 | bytes 4194304 | tf_op jit(solution)/shard_map/by_bin/pallas_call | solution.py:257
  30.8 3.7 %collective-permute-start.10 = (bf16[64,16,128]{2,1,0:T(8,128)(2,1)S(1)}, bf16[64,16,128]{2,1,0:T(8,128)(2,1)S(1)}, u32[]{:S(2)}, u32[]{:S(2)}) collective-permute-start(bf16[64,16,128]{2,1,0:T(8,128)(2,1)S(1)} %get-tuple-element.50.refs_6_), channel_id=1, source_target_pairs={{8,16},{12,20},{16,8},{20,12},{9,17},{13,21},{17,9},{21,13},{10,18... | collective-permute-start | bytes 786440 | tf_op jit(solution)/shard_map/ppermute | solution.py:425
  34.5 0.1 collective-permute-start.9
  34.6 0.1 copy.17
  34.7 0.3 compare_convert_fusion.refs_10_
  35.0 0.0 collective-permute-done.3.refs_3_
  35.1 2.2 %collective-permute-done.4.refs_4_ = bf16[64,16,128]{2,1,0:T(8,128)(2,1)S(1)} collective-permute-done((bf16[64,16,128]{2,1,0:T(8,128)(2,1)S(1)}, bf16[64,16,128]{2,1,0:T(8,128)(2,1)S(1)}, u32[]{:S(2)}, u32[]{:S(2)}) %collective-permute-start.4) | collective-permute-done | bytes 262176 | tf_op jit(solution)/shard_map/ppermute | solution.py:425
  37.2 3.6 %collective-permute-done.10.refs_9_ = bf16[64,16,128]{2,1,0:T(8,128)(2,1)S(1)} collective-permute-done((bf16[64,16,128]{2,1,0:T(8,128)(2,1)S(1)}, bf16[64,16,128]{2,1,0:T(8,128)(2,1)S(1)}, u32[]{:S(2)}, u32[]{:S(2)}) %collective-permute-start.10) | collective-permute-done | bytes 262176 | tf_op jit(solution)/shard_map/ppermute | solution.py:425
  40.8 0.2 collective-permute-done.9.refs_8_
  41.0 2.4 %cross_products.1 = (f32[2,16,16,128]{3,2,1,0:T(8,128)S(1)}, f32[2,16,16,128]{3,2,1,0:T(8,128)S(1)}, f32[2,16,16,128]{3,2,1,0:T(8,128)S(1)}, f32[2,16,16,128]{3,2,1,0:T(8,128)S(1)}) custom-call(bf16[64,16,128]{2,1,0:T(8,128)(2,1)S(1)} %get-tuple-element.42.refs_0_, bf16[64,16,128]{2,1,0:T(8,128)(2,1)S(1)} %get-tuple-element.43.refs_1_, ...), custom_call_target="tpu_custom_call" | custom-call | tf_op jit(solution)/shard_map/cross_products/pallas_call | solution.py:318
  43.4 1.5 %collective-permute-start.12 = (f32[2,16,16,128]{3,2,1,0:T(8,128)S(1)}, f32[2,16,16,128]{3,2,1,0:T(8,128)S(1)}, u32[]{:S(2)}, u32[]{:S(2)}) collective-permute-start(f32[2,16,16,128]{3,2,1,0:T(8,128)S(1)} %get-tuple-element.54), channel_id=1, source_target_pairs={{0,2},{1,3},{2,0},{3,1},{4,6},{5,7},{6,4},{7,5},{8,10},{9,11},{10,... | collective-permute-start | bytes 786440 | tf_op jit(solution)/shard_map/ppermute | solution.py:385
  44.9 0.5 collective-permute-start.15
  45.4 1.5 %collective-permute-start.17 = (f32[2,16,16,128]{3,2,1,0:T(8,128)S(1)}, f32[2,16,16,128]{3,2,1,0:T(8,128)S(1)}, u32[]{:S(2)}, u32[]{:S(2)}) collective-permute-start(f32[2,16,16,128]{3,2,1,0:T(8,128)S(1)} %get-tuple-element.62), channel_id=1, source_target_pairs={{0,6},{1,7},{2,4},{3,5},{4,2},{5,3},{6,0},{7,1},{8,14},{9,15},{10,... | collective-permute-start | bytes 786440 | tf_op jit(solution)/shard_map/ppermute | solution.py:385
  46.9 1.1 %lag_tables.1 = (bf16[8,128,1024]{2,1,0:T(8,128)(2,1)S(1)}, bf16[8,128,1024]{2,1,0:T(8,128)(2,1)S(1)}) custom-call(f32[64,1024]{1,0:T(8,128)S(1)} %copy-done, f32[64,1024]{1,0:T(8,128)S(1)} %copy-done.1, f32[8,1024]{1,0:T(8,128)S(1)} %copy-done.2, f32[8,1024]{1,0:T(8,128)S(1)} %copy-done.3), custom_call_target="tpu_custom_call" | custom-call | tf_op jit(solution)/shard_map/lag_tables/pallas_call | solution.py:205
  48.0 0.1 collective-permute-start.13
  48.1 4.2 %collective-permute-done.12.refs_2_ = f32[2,16,16,128]{3,2,1,0:T(8,128)S(1)} collective-permute-done((f32[2,16,16,128]{3,2,1,0:T(8,128)S(1)}, f32[2,16,16,128]{3,2,1,0:T(8,128)S(1)}, u32[]{:S(2)}, u32[]{:S(2)}) %collective-permute-start.12) | collective-permute-done | bytes 262176 | tf_op jit(solution)/shard_map/ppermute | solution.py:385
  52.3 4.0 %collective-permute-done.15.refs_4_ = f32[2,16,16,128]{3,2,1,0:T(8,128)S(1)} collective-permute-done((f32[2,16,16,128]{3,2,1,0:T(8,128)S(1)}, f32[2,16,16,128]{3,2,1,0:T(8,128)S(1)}, u32[]{:S(2)}, u32[]{:S(2)}) %collective-permute-start.15) | collective-permute-done | bytes 262176 | tf_op jit(solution)/shard_map/ppermute | solution.py:385
  56.3 0.0 collective-permute-done.17.refs_6_
  56.3 0.5 collective-permute-start.18
  56.8 0.0 collective-permute-done.13.refs_1_
  56.9 0.0 collective-permute-done.14.refs_3_
  56.9 1.0 %collective-permute-done.16.refs_5_ = f32[2,16,16,128]{3,2,1,0:T(8,128)S(1)} collective-permute-done((f32[2,16,16,128]{3,2,1,0:T(8,128)S(1)}, f32[2,16,16,128]{3,2,1,0:T(8,128)S(1)}, u32[]{:S(2)}, u32[]{:S(2)}) %collective-permute-start.16) | collective-permute-done | bytes 262176 | tf_op jit(solution)/shard_map/ppermute | solution.py:385
  57.9 0.4 collective-permute-done.18.refs_7_
  58.2 2.9 %inverse.1 = f32[16,16,1024]{2,1,0:T(8,128)} custom-call(bf16[1024,1024]{1,0:T(8,128)(2,1)S(1)} %bitcast.8, bf16[1024,1024]{1,0:T(8,128)(2,1)S(1)} %bitcast.9, f32[2,16,16,128]{3,2,1,0:T(8,128)S(1)} %get-tuple-element.59.refs_0_, f32[2,16,16,128]{3,2,1,0:T(8,128)S(1)} %collective-permute-done.13.refs_1_, ...), custom_call_target="tpu_custom_call" | custom-call | tf_op jit(solution)/shard_map/inverse/pallas_call | solution.py:360
  (22 shorter events, 0.1 us)
Async XLA Ops:
  0.0 7.3 %copy-start.6 = (s32[16,64]{1,0:T(8,128)S(1)}, s32[16,64]{1,0:T(8,128)}, u32[]{:S(2)}) copy-start(s32[16,64]{1,0:T(8,128)} %param.16) | copy-start | bytes 12292
  0.0 7.3 %copy-start.7 = (s32[16,64]{1,0:T(8,128)S(1)}, s32[16,64]{1,0:T(8,128)}, u32[]{:S(2)}) copy-start(s32[16,64]{1,0:T(8,128)} %param.17) | copy-start | bytes 12292
  0.0 12.7 %collective-permute-start.5 = (bf16[512,4096]{1,0:T(8,128)(2,1)}, bf16[512,4096]{1,0:T(8,128)(2,1)}, u32[]{:S(2)}, u32[]{:S(2)}) collective-permute-start(bf16[512,4096]{1,0:T(8,128)(2,1)} %bitcast.14), channel_id=1, source_target_pairs={{0,1},{1,0},{2,3},{3,2},{4,5},{5,4},{6,7},{7,6},{8,9},{9,8},{10,11... | collective-permute-start | bytes 12582920 | tf_op jit(solution)/shard_map/ppermute | solution.py:385
  7.3 16.3 %copy-start.4 = (bf16[16,32,128]{2,1,0:T(8,128)(2,1)S(1)}, bf16[16,32,128]{2,1,0:T(8,128)(2,1)}, u32[]{:S(2)}) copy-start(bf16[16,32,128]{2,1,0:T(8,128)(2,1)} %get-tuple-element.38.refs_0_) | copy-start | bytes 393220
  7.4 5.2 %collective-permute-start.11 = (s32[16,64]{1,0:T(8,128)S(1)}, s32[16,64]{1,0:T(8,128)S(1)}, u32[]{:S(2)}, u32[]{:S(2)}) collective-permute-start(s32[16,64]{1,0:T(8,128)S(1)} %fusion.3), channel_id=1, source_target_pairs={{0,4},{4,0},{8,12},{12,8},{16,20},{20,16},{24,28},{28,24},{1,5},{5... | collective-permute-start | bytes 12296 | tf_op jit(solution)/shard_map/ppermute | solution.py:405
  9.0 13.1 %collective-permute-start = (bf16[16,32,128]{2,1,0:T(8,128)(2,1)}, bf16[16,32,128]{2,1,0:T(8,128)(2,1)S(1)}, u32[]{:S(2)}, u32[]{:S(2)}) collective-permute-start(bf16[16,32,128]{2,1,0:T(8,128)(2,1)} %get-tuple-element.39), channel_id=1, source_target_pairs={{0,2},{1,3},{2,0},{3,1},{4,6},{5,7},{6,4},{7,5},{8,10},{9,11},{10,... | collective-permute-start | bytes 393224 | tf_op jit(solution)/shard_map/ppermute | solution.py:385
  10.5 13.2 %collective-permute-start.1 = (bf16[16,32,128]{2,1,0:T(8,128)(2,1)}, bf16[16,32,128]{2,1,0:T(8,128)(2,1)S(1)}, u32[]{:S(2)}, u32[]{:S(2)}) collective-permute-start(bf16[16,32,128]{2,1,0:T(8,128)(2,1)} %get-tuple-element.40), channel_id=1, source_target_pairs={{0,4},{1,5},{2,6},{3,7},{4,0},{5,1},{6,2},{7,3},{8,12},{9,13},{10,... | collective-permute-start | bytes 393224 | tf_op jit(solution)/shard_map/ppermute | solution.py:385
  11.0 12.7 %collective-permute-start.2 = (bf16[16,32,128]{2,1,0:T(8,128)(2,1)}, bf16[16,32,128]{2,1,0:T(8,128)(2,1)S(1)}, u32[]{:S(2)}, u32[]{:S(2)}) collective-permute-start(bf16[16,32,128]{2,1,0:T(8,128)(2,1)} %get-tuple-element.41), channel_id=1, source_target_pairs={{0,6},{1,7},{2,4},{3,5},{4,2},{5,3},{6,0},{7,1},{8,14},{9,15},{10,... | collective-permute-start | bytes 393224 | tf_op jit(solution)/shard_map/ppermute | solution.py:385
  20.1 9.2 %copy-start.5 = (bf16[16,32,128]{2,1,0:T(8,128)(2,1)S(1)}, bf16[16,32,128]{2,1,0:T(8,128)(2,1)}, u32[]{:S(2)}) copy-start(bf16[16,32,128]{2,1,0:T(8,128)(2,1)} %get-tuple-element.45.refs_0_) | copy-start | bytes 393220
  20.1 8.7 %collective-permute-start.6 = (bf16[16,32,128]{2,1,0:T(8,128)(2,1)}, bf16[16,32,128]{2,1,0:T(8,128)(2,1)S(1)}, u32[]{:S(2)}, u32[]{:S(2)}) collective-permute-start(bf16[16,32,128]{2,1,0:T(8,128)(2,1)} %get-tuple-element.46), channel_id=1, source_target_pairs={{0,2},{1,3},{2,0},{3,1},{4,6},{5,7},{6,4},{7,5},{8,10},{9,11},{10,... | collective-permute-start | bytes 393224 | tf_op jit(solution)/shard_map/ppermute | solution.py:385
  21.6 7.6 %collective-permute-start.7 = (bf16[16,32,128]{2,1,0:T(8,128)(2,1)}, bf16[16,32,128]{2,1,0:T(8,128)(2,1)S(1)}, u32[]{:S(2)}, u32[]{:S(2)}) collective-permute-start(bf16[16,32,128]{2,1,0:T(8,128)(2,1)} %get-tuple-element.47), channel_id=1, source_target_pairs={{0,4},{1,5},{2,6},{3,7},{4,0},{5,1},{6,2},{7,3},{8,12},{9,13},{10,... | collective-permute-start | bytes 393224 | tf_op jit(solution)/shard_map/ppermute | solution.py:385
  22.1 7.1 %collective-permute-start.8 = (bf16[16,32,128]{2,1,0:T(8,128)(2,1)}, bf16[16,32,128]{2,1,0:T(8,128)(2,1)S(1)}, u32[]{:S(2)}, u32[]{:S(2)}) collective-permute-start(bf16[16,32,128]{2,1,0:T(8,128)(2,1)} %get-tuple-element.48), channel_id=1, source_target_pairs={{0,6},{1,7},{2,4},{3,5},{4,2},{5,3},{6,0},{7,1},{8,14},{9,15},{10,... | collective-permute-start | bytes 393224 | tf_op jit(solution)/shard_map/ppermute | solution.py:385
  25.2 9.8 %collective-permute-start.3 = (bf16[64,16,128]{2,1,0:T(8,128)(2,1)S(1)}, bf16[64,16,128]{2,1,0:T(8,128)(2,1)S(1)}, u32[]{:S(2)}, u32[]{:S(2)}) collective-permute-start(bf16[64,16,128]{2,1,0:T(8,128)(2,1)S(1)} %get-tuple-element.42.refs_0_), channel_id=1, source_target_pairs={{0,8},{4,12},{8,0},{12,4},{16,24},{20,28},{24,16},{28,20},{1,9},{5... | collective-permute-start | bytes 786440 | tf_op jit(solution)/shard_map/ppermute | solution.py:425
  26.8 10.4 %collective-permute-start.4 = (bf16[64,16,128]{2,1,0:T(8,128)(2,1)S(1)}, bf16[64,16,128]{2,1,0:T(8,128)(2,1)S(1)}, u32[]{:S(2)}, u32[]{:S(2)}) collective-permute-start(bf16[64,16,128]{2,1,0:T(8,128)(2,1)S(1)} %get-tuple-element.43.refs_1_), channel_id=1, source_target_pairs={{8,16},{12,20},{16,8},{20,12},{9,17},{13,21},{17,9},{21,13},{10,18... | collective-permute-start | bytes 786440 | tf_op jit(solution)/shard_map/ppermute | solution.py:425
  29.2 17.7 %copy-start = (f32[64,1024]{1,0:T(8,128)S(1)}, f32[64,1024]{1,0:T(8,128)}, u32[]{:S(2)}) copy-start(f32[64,1024]{1,0:T(8,128)} %constant.119.clone.cos_ref) | copy-start | bytes 786436
  29.2 17.7 %copy-start.2 = (f32[8,1024]{1,0:T(8,128)S(1)}, f32[8,1024]{1,0:T(8,128)}, u32[]{:S(2)}) copy-start(f32[8,1024]{1,0:T(8,128)} %constant.121.clone.cos0_ref) | copy-start | bytes 98308
  29.2 17.7 %copy-start.3 = (f32[8,1024]{1,0:T(8,128)S(1)}, f32[8,1024]{1,0:T(8,128)}, u32[]{:S(2)}) copy-start(f32[8,1024]{1,0:T(8,128)} %constant.122.clone.msin0_ref) | copy-start | bytes 98308
  30.8 10.0 %collective-permute-start.10 = (bf16[64,16,128]{2,1,0:T(8,128)(2,1)S(1)}, bf16[64,16,128]{2,1,0:T(8,128)(2,1)S(1)}, u32[]{:S(2)}, u32[]{:S(2)}) collective-permute-start(bf16[64,16,128]{2,1,0:T(8,128)(2,1)S(1)} %get-tuple-element.50.refs_6_), channel_id=1, source_target_pairs={{8,16},{12,20},{16,8},{20,12},{9,17},{13,21},{17,9},{21,13},{10,18... | collective-permute-start | bytes 786440 | tf_op jit(solution)/shard_map/ppermute | solution.py:425
  34.5 6.4 %collective-permute-start.9 = (bf16[64,16,128]{2,1,0:T(8,128)(2,1)S(1)}, bf16[64,16,128]{2,1,0:T(8,128)(2,1)S(1)}, u32[]{:S(2)}, u32[]{:S(2)}) collective-permute-start(bf16[64,16,128]{2,1,0:T(8,128)(2,1)S(1)} %get-tuple-element.49.refs_5_), channel_id=1, source_target_pairs={{0,8},{4,12},{8,0},{12,4},{16,24},{20,28},{24,16},{28,20},{1,9},{5... | collective-permute-start | bytes 786440 | tf_op jit(solution)/shard_map/ppermute | solution.py:425
  34.7 12.2 %copy-start.1 = (f32[64,1024]{1,0:T(8,128)S(1)}, f32[64,1024]{1,0:T(8,128)}, u32[]{:S(2)}) copy-start(f32[64,1024]{1,0:T(8,128)} %constant.120.clone.msin_ref) | copy-start | bytes 786436
  43.4 9.0 %collective-permute-start.12 = (f32[2,16,16,128]{3,2,1,0:T(8,128)S(1)}, f32[2,16,16,128]{3,2,1,0:T(8,128)S(1)}, u32[]{:S(2)}, u32[]{:S(2)}) collective-permute-start(f32[2,16,16,128]{3,2,1,0:T(8,128)S(1)} %get-tuple-element.54), channel_id=1, source_target_pairs={{0,2},{1,3},{2,0},{3,1},{4,6},{5,7},{6,4},{7,5},{8,10},{9,11},{10,... | collective-permute-start | bytes 786440 | tf_op jit(solution)/shard_map/ppermute | solution.py:385
  44.9 11.4 %collective-permute-start.15 = (f32[2,16,16,128]{3,2,1,0:T(8,128)S(1)}, f32[2,16,16,128]{3,2,1,0:T(8,128)S(1)}, u32[]{:S(2)}, u32[]{:S(2)}) collective-permute-start(f32[2,16,16,128]{3,2,1,0:T(8,128)S(1)} %get-tuple-element.61), channel_id=1, source_target_pairs={{0,4},{1,5},{2,6},{3,7},{4,0},{5,1},{6,2},{7,3},{8,12},{9,13},{10,... | collective-permute-start | bytes 786440 | tf_op jit(solution)/shard_map/ppermute | solution.py:385
  45.4 11.0 %collective-permute-start.17 = (f32[2,16,16,128]{3,2,1,0:T(8,128)S(1)}, f32[2,16,16,128]{3,2,1,0:T(8,128)S(1)}, u32[]{:S(2)}, u32[]{:S(2)}) collective-permute-start(f32[2,16,16,128]{3,2,1,0:T(8,128)S(1)} %get-tuple-element.62), channel_id=1, source_target_pairs={{0,6},{1,7},{2,4},{3,5},{4,2},{5,3},{6,0},{7,1},{8,14},{9,15},{10,... | collective-permute-start | bytes 786440 | tf_op jit(solution)/shard_map/ppermute | solution.py:385
  48.0 8.9 %collective-permute-start.13 = (f32[2,16,16,128]{3,2,1,0:T(8,128)S(1)}, f32[2,16,16,128]{3,2,1,0:T(8,128)S(1)}, u32[]{:S(2)}, u32[]{:S(2)}) collective-permute-start(f32[2,16,16,128]{3,2,1,0:T(8,128)S(1)} %get-tuple-element.59.refs_0_), channel_id=1, source_target_pairs={{0,1},{1,0},{2,3},{3,2},{4,5},{5,4},{6,7},{7,6},{8,9},{9,8},{10,11... | collective-permute-start | bytes 786440 | tf_op jit(solution)/shard_map/ppermute | solution.py:385
  52.3 4.5 %collective-permute-start.14 = (f32[2,16,16,128]{3,2,1,0:T(8,128)S(1)}, f32[2,16,16,128]{3,2,1,0:T(8,128)S(1)}, u32[]{:S(2)}, u32[]{:S(2)}) collective-permute-start(f32[2,16,16,128]{3,2,1,0:T(8,128)S(1)} %collective-permute-done.12.refs_2_), channel_id=1, source_target_pairs={{0,1},{1,0},{2,3},{3,2},{4,5},{5,4},{6,7},{7,6},{8,9},{9,8},{10,11... | collective-permute-start | bytes 786440 | tf_op jit(solution)/shard_map/ppermute | solution.py:385
  56.3 1.5 %collective-permute-start.16 = (f32[2,16,16,128]{3,2,1,0:T(8,128)S(1)}, f32[2,16,16,128]{3,2,1,0:T(8,128)S(1)}, u32[]{:S(2)}, u32[]{:S(2)}) collective-permute-start(f32[2,16,16,128]{3,2,1,0:T(8,128)S(1)} %collective-permute-done.15.refs_4_), channel_id=1, source_target_pairs={{0,1},{1,0},{2,3},{3,2},{4,5},{5,4},{6,7},{7,6},{8,9},{9,8},{10,11... | collective-permute-start | bytes 786440 | tf_op jit(solution)/shard_map/ppermute | solution.py:385
  56.3 1.9 %collective-permute-start.18 = (f32[2,16,16,128]{3,2,1,0:T(8,128)S(1)}, f32[2,16,16,128]{3,2,1,0:T(8,128)S(1)}, u32[]{:S(2)}, u32[]{:S(2)}) collective-permute-start(f32[2,16,16,128]{3,2,1,0:T(8,128)S(1)} %collective-permute-done.17.refs_6_), channel_id=1, source_target_pairs={{0,1},{1,0},{2,3},{3,2},{4,5},{5,4},{6,7},{7,6},{8,9},{9,8},{10,11... | collective-permute-start | bytes 786440 | tf_op jit(solution)/shard_map/ppermute | solution.py:385

commit v13 on v12

--- a/solution.py
+++ b/solution.py
@@ -328,6 +328,7 @@
 
 def inverse_kernel(high_ref, low_ref, *refs):
     *blocks, out_hbm, both, out_ref, sems = refs
+    blocks = blocks[::-1]
     _, nodes, slots, _ = blocks[0].shape
     rows = nodes * slots
     me, _ = position(len(blocks) // 2)
@@ -425,8 +426,8 @@
         halves.append((a, b, turned, lax.ppermute(a, "pairs", swap_a), lax.ppermute(b, "pairs", swap_b)))
     stack = cross_products(halves, select, wins)
     moved = between_chips(stack)
-    moved[1], high, low = lax.optimization_barrier((moved[1], high, low))
-    return inverse(within_chip(moved), high, low)
+    moved[-1], high, low = lax.optimization_barrier((moved[-1], high, low))
+    return inverse(within_chip(moved)[::-1], high, low)
 
 
 def solution(mesh):

time: 61.8 us -> 61.5 us (level)
  no operation moved by 1% of the time
where the time goes in v13:
time: 61.5 us; the launch traced here: 61 us
  Pallas kernels  24.1 us (39%)
  starting transfers between devices  20.1 us (33%)
  waiting for transfers between devices  15.7 us (26%)
    pallas_call x2, Pallas kernels, own_spectra(): pl.pallas_call(functools.partial(spectra_kernel, steps=steps, wins=len(st...  14.5 us
    ppermute x14, starting transfers between devices, hop(): return lax.ppermute(array, ('pairs', 'win'), pairing)  11.2 us
    ppermute x14, waiting for transfers between devices, hop(): return lax.ppermute(array, ('pairs', 'win'), pairing)  9.79 us
    ppermute x2, waiting for transfers between devices, per_device(): lax.ppermute(b, 'pairs', swap_b)  5.75 us
    ppermute x2, starting transfers between devices, per_device(): lax.ppermute(b, 'pairs', swap_b)  5.62 us
    pallas_call x2, Pallas kernels, by_bin(): pl.pallas_call(functools.partial(by_bin_kernel, steps=steps), out_shape=[...  3.12 us
    pallas_call x1, Pallas kernels, inverse(): pl.pallas_call(inverse_kernel, in_specs=[vmem] * (2 + len(blocks)), out_s...  2.91 us
    pallas_call x1, Pallas kernels, cross_products(): pl.pallas_call(cross_kernel, out_shape=[block] * wins, in_specs=[vmem] *...  2.38 us
  transfers between devices with their start and end apart: 19, of which 8 were waited for; matrix products, arithmetic and copies ran while one was open for 1% of the time, Pallas kernels for 31%

profile of v13, /device:TPU:16, one launch (start us, length us, event | category | flops | bytes accessed | tf_op | source)
XLA Modules:
  0.0 61.0 jit_solution(12601087332859860488)
XLA Ops:
  0.0 0.0 collective-permute-start.5
  0.1 7.3 %own_spectra.2 = (bf16[16,32,128]{2,1,0:T(8,128)(2,1)}, bf16[16,32,128]{2,1,0:T(8,128)(2,1)}, bf16[16,32,128]{2,1,0:T(8,128)(2,1)}, bf16[16,32,128]{2,1,0:T(8,128)(2,1)}) custom-call(bf16[512,4096]{1,0:T(8,128)(2,1)} %bitcast.15, f32[1,129]{1,0:T(1,128)} %bitcast.16, f32[129,1024]{1,0:T(8,128)} %constant.116.clone.fine_hbm, ...), custom_call_target="tpu_custom_call" | custom-call | flops 2147483648 | bytes 4194304 | tf_op jit(solution)/shard_map/own_spectra/pallas_call | solution.py:168
  7.4 1.6 %collective-permute-start.11 = (s32[16,64]{1,0:T(8,128)S(1)}, s32[16,64]{1,0:T(8,128)S(1)}, u32[]{:S(2)}, u32[]{:S(2)}) collective-permute-start(s32[16,64]{1,0:T(8,128)S(1)} %fusion.3), channel_id=1, source_target_pairs={{0,4},{4,0},{8,12},{12,8},{16,20},{20,16},{24,28},{28,24},{1,5},{5... | collective-permute-start | bytes 12296 | tf_op jit(solution)/shard_map/ppermute | solution.py:406
  9.0 1.5 %collective-permute-start = (bf16[16,32,128]{2,1,0:T(8,128)(2,1)}, bf16[16,32,128]{2,1,0:T(8,128)(2,1)S(1)}, u32[]{:S(2)}, u32[]{:S(2)}) collective-permute-start(bf16[16,32,128]{2,1,0:T(8,128)(2,1)} %get-tuple-element.39), channel_id=1, source_target_pairs={{0,2},{1,3},{2,0},{3,1},{4,6},{5,7},{6,4},{7,5},{8,10},{9,11},{10,... | collective-permute-start | bytes 393224 | tf_op jit(solution)/shard_map/ppermute | solution.py:386
  10.5 0.5 collective-permute-start.1
  11.0 1.5 %collective-permute-start.2 = (bf16[16,32,128]{2,1,0:T(8,128)(2,1)}, bf16[16,32,128]{2,1,0:T(8,128)(2,1)S(1)}, u32[]{:S(2)}, u32[]{:S(2)}) collective-permute-start(bf16[16,32,128]{2,1,0:T(8,128)(2,1)} %get-tuple-element.41), channel_id=1, source_target_pairs={{0,6},{1,7},{2,4},{3,5},{4,2},{5,3},{6,0},{7,1},{8,14},{9,15},{10,... | collective-permute-start | bytes 393224 | tf_op jit(solution)/shard_map/ppermute | solution.py:386
  12.5 0.1 copy.15
  12.5 0.0 collective-permute-done.11
  12.6 0.1 copy.16
  12.6 0.1 add_select_fusion
  12.7 0.0 collective-permute-done.5.x_hbm
  12.8 7.3 %own_spectra.3 = (bf16[16,32,128]{2,1,0:T(8,128)(2,1)}, bf16[16,32,128]{2,1,0:T(8,128)(2,1)}, bf16[16,32,128]{2,1,0:T(8,128)(2,1)}, bf16[16,32,128]{2,1,0:T(8,128)(2,1)}) custom-call(bf16[512,4096]{1,0:T(8,128)(2,1)} %collective-permute-done.5.x_hbm, f32[1,129]{1,0:T(1,128)} %bitcast.17, f32[129,1024]{1,0:T(8,128)} %constant.116.clone.fine_hbm, ...), custom_call_target="tpu_custom_call" | custom-call | flops 2147483648 | bytes 4194304 | tf_op jit(solution)/shard_map/own_spectra/pallas_call | solution.py:168
  20.1 1.5 %collective-permute-start.6 = (bf16[16,32,128]{2,1,0:T(8,128)(2,1)}, bf16[16,32,128]{2,1,0:T(8,128)(2,1)S(1)}, u32[]{:S(2)}, u32[]{:S(2)}) collective-permute-start(bf16[16,32,128]{2,1,0:T(8,128)(2,1)} %get-tuple-element.46), channel_id=1, source_target_pairs={{0,2},{1,3},{2,0},{3,1},{4,6},{5,7},{6,4},{7,5},{8,10},{9,11},{10,... | collective-permute-start | bytes 393224 | tf_op jit(solution)/shard_map/ppermute | solution.py:386
  21.6 0.5 collective-permute-start.7
  22.1 0.0 collective-permute-done.refs_1_
  22.1 1.5 %collective-permute-start.8 = (bf16[16,32,128]{2,1,0:T(8,128)(2,1)}, bf16[16,32,128]{2,1,0:T(8,128)(2,1)S(1)}, u32[]{:S(2)}, u32[]{:S(2)}) collective-permute-start(bf16[16,32,128]{2,1,0:T(8,128)(2,1)} %get-tuple-element.48), channel_id=1, source_target_pairs={{0,6},{1,7},{2,4},{3,5},{4,2},{5,3},{6,0},{7,1},{8,14},{9,15},{10,... | collective-permute-start | bytes 393224 | tf_op jit(solution)/shard_map/ppermute | solution.py:386
  23.6 0.0 collective-permute-done.1.refs_2_
  23.6 0.0 collective-permute-done.2.refs_3_
  23.6 1.6 %by_bin.2 = (bf16[64,16,128]{2,1,0:T(8,128)(2,1)S(1)}, bf16[64,16,128]{2,1,0:T(8,128)(2,1)S(1)}, bf16[64,32,128]{2,1,0:T(8,128)(2,1)S(1)}) custom-call(bf16[16,32,128]{2,1,0:T(8,128)(2,1)S(1)} %copy-done.4, bf16[16,32,128]{2,1,0:T(8,128)(2,1)S(1)} %collective-permute-done.refs_1_, bf16[16,32,128]{2,1,0:T(8,128)(2,1)S(1)} %collective-permute-done.1.refs_2_, ...), custom_call_target="tpu_custom_call" | custom-call | flops 2147483648 | bytes 4194304 | tf_op jit(solution)/shard_map/by_bin/pallas_call | solution.py:257
  25.2 1.6 %collective-permute-start.3 = (bf16[64,16,128]{2,1,0:T(8,128)(2,1)S(1)}, bf16[64,16,128]{2,1,0:T(8,128)(2,1)S(1)}, u32[]{:S(2)}, u32[]{:S(2)}) collective-permute-start(bf16[64,16,128]{2,1,0:T(8,128)(2,1)S(1)} %get-tuple-element.42.refs_0_), channel_id=1, source_target_pairs={{0,8},{4,12},{8,0},{12,4},{16,24},{20,28},{24,16},{28,20},{1,9},{5... | collective-permute-start | bytes 786440 | tf_op jit(solution)/shard_map/ppermute | solution.py:426
  26.8 1.9 %collective-permute-start.4 = (bf16[64,16,128]{2,1,0:T(8,128)(2,1)S(1)}, bf16[64,16,128]{2,1,0:T(8,128)(2,1)S(1)}, u32[]{:S(2)}, u32[]{:S(2)}) collective-permute-start(bf16[64,16,128]{2,1,0:T(8,128)(2,1)S(1)} %get-tuple-element.43.refs_1_), channel_id=1, source_target_pairs={{8,16},{12,20},{16,8},{20,12},{9,17},{13,21},{17,9},{21,13},{10,18... | collective-permute-start | bytes 786440 | tf_op jit(solution)/shard_map/ppermute | solution.py:426
  28.8 0.4 collective-permute-done.7.refs_2_
  29.2 0.0 collective-permute-done.8.refs_3_
  29.2 0.0 copy-start.2
  29.2 0.0 copy-start.3
  29.2 1.6 %by_bin.3 = (bf16[64,16,128]{2,1,0:T(8,128)(2,1)S(1)}, bf16[64,16,128]{2,1,0:T(8,128)(2,1)S(1)}, bf16[64,32,128]{2,1,0:T(8,128)(2,1)S(1)}) custom-call(bf16[16,32,128]{2,1,0:T(8,128)(2,1)S(1)} %copy-done.5, bf16[16,32,128]{2,1,0:T(8,128)(2,1)S(1)} %collective-permute-done.6.refs_1_, bf16[16,32,128]{2,1,0:T(8,128)(2,1)S(1)} %collective-permute-done.7.refs_2_, ...), custom_call_target="tpu_custom_call" | custom-call | flops 2147483648 | bytes 4194304 | tf_op jit(solution)/shard_map/by_bin/pallas_call | solution.py:257
  30.8 3.7 %collective-permute-start.10 = (bf16[64,16,128]{2,1,0:T(8,128)(2,1)S(1)}, bf16[64,16,128]{2,1,0:T(8,128)(2,1)S(1)}, u32[]{:S(2)}, u32[]{:S(2)}) collective-permute-start(bf16[64,16,128]{2,1,0:T(8,128)(2,1)S(1)} %get-tuple-element.50.refs_6_), channel_id=1, source_target_pairs={{8,16},{12,20},{16,8},{20,12},{9,17},{13,21},{17,9},{21,13},{10,18... | collective-permute-start | bytes 786440 | tf_op jit(solution)/shard_map/ppermute | solution.py:426
  34.5 0.1 collective-permute-start.9
  34.6 0.1 copy.17
  34.7 0.3 compare_convert_fusion.refs_10_
  35.0 0.0 collective-permute-done.3.refs_3_
  35.1 2.2 %collective-permute-done.4.refs_4_ = bf16[64,16,128]{2,1,0:T(8,128)(2,1)S(1)} collective-permute-done((bf16[64,16,128]{2,1,0:T(8,128)(2,1)S(1)}, bf16[64,16,128]{2,1,0:T(8,128)(2,1)S(1)}, u32[]{:S(2)}, u32[]{:S(2)}) %collective-permute-start.4) | collective-permute-done | bytes 262176 | tf_op jit(solution)/shard_map/ppermute | solution.py:426
  37.2 3.6 %collective-permute-done.10.refs_9_ = bf16[64,16,128]{2,1,0:T(8,128)(2,1)S(1)} collective-permute-done((bf16[64,16,128]{2,1,0:T(8,128)(2,1)S(1)}, bf16[64,16,128]{2,1,0:T(8,128)(2,1)S(1)}, u32[]{:S(2)}, u32[]{:S(2)}) %collective-permute-start.10) | collective-permute-done | bytes 262176 | tf_op jit(solution)/shard_map/ppermute | solution.py:426
  40.8 0.2 collective-permute-done.9.refs_8_
  41.0 2.4 %cross_products.1 = (f32[2,16,16,128]{3,2,1,0:T(8,128)S(1)}, f32[2,16,16,128]{3,2,1,0:T(8,128)S(1)}, f32[2,16,16,128]{3,2,1,0:T(8,128)S(1)}, f32[2,16,16,128]{3,2,1,0:T(8,128)S(1)}) custom-call(bf16[64,16,128]{2,1,0:T(8,128)(2,1)S(1)} %get-tuple-element.42.refs_0_, bf16[64,16,128]{2,1,0:T(8,128)(2,1)S(1)} %get-tuple-element.43.refs_1_, ...), custom_call_target="tpu_custom_call" | custom-call | tf_op jit(solution)/shard_map/cross_products/pallas_call | solution.py:318
  43.4 1.5 %collective-permute-start.12 = (f32[2,16,16,128]{3,2,1,0:T(8,128)S(1)}, f32[2,16,16,128]{3,2,1,0:T(8,128)S(1)}, u32[]{:S(2)}, u32[]{:S(2)}) collective-permute-start(f32[2,16,16,128]{3,2,1,0:T(8,128)S(1)} %get-tuple-element.54), channel_id=1, source_target_pairs={{0,6},{1,7},{2,4},{3,5},{4,2},{5,3},{6,0},{7,1},{8,14},{9,15},{10,... | collective-permute-start | bytes 786440 | tf_op jit(solution)/shard_map/ppermute | solution.py:386
  44.8 1.5 %collective-permute-start.14 = (f32[2,16,16,128]{3,2,1,0:T(8,128)S(1)}, f32[2,16,16,128]{3,2,1,0:T(8,128)S(1)}, u32[]{:S(2)}, u32[]{:S(2)}) collective-permute-start(f32[2,16,16,128]{3,2,1,0:T(8,128)S(1)} %get-tuple-element.60), channel_id=1, source_target_pairs={{0,4},{1,5},{2,6},{3,7},{4,0},{5,1},{6,2},{7,3},{8,12},{9,13},{10,... | collective-permute-start | bytes 786440 | tf_op jit(solution)/shard_map/ppermute | solution.py:386
  46.3 0.5 collective-permute-start.16
  46.9 1.1 %lag_tables.1 = (bf16[8,128,1024]{2,1,0:T(8,128)(2,1)S(1)}, bf16[8,128,1024]{2,1,0:T(8,128)(2,1)S(1)}) custom-call(f32[64,1024]{1,0:T(8,128)S(1)} %copy-done, f32[64,1024]{1,0:T(8,128)S(1)} %copy-done.1, f32[8,1024]{1,0:T(8,128)S(1)} %copy-done.2, f32[8,1024]{1,0:T(8,128)S(1)} %copy-done.3), custom_call_target="tpu_custom_call" | custom-call | tf_op jit(solution)/shard_map/lag_tables/pallas_call | solution.py:205
  48.0 0.1 collective-permute-start.18
  48.1 5.2 %collective-permute-done.12.refs_1_ = f32[2,16,16,128]{3,2,1,0:T(8,128)S(1)} collective-permute-done((f32[2,16,16,128]{3,2,1,0:T(8,128)S(1)}, f32[2,16,16,128]{3,2,1,0:T(8,128)S(1)}, u32[]{:S(2)}, u32[]{:S(2)}) %collective-permute-start.12) | collective-permute-done | bytes 262176 | tf_op jit(solution)/shard_map/ppermute | solution.py:386
  53.3 0.0 collective-permute-start.13
  53.3 2.7 %collective-permute-done.14.refs_3_ = f32[2,16,16,128]{3,2,1,0:T(8,128)S(1)} collective-permute-done((f32[2,16,16,128]{3,2,1,0:T(8,128)S(1)}, f32[2,16,16,128]{3,2,1,0:T(8,128)S(1)}, u32[]{:S(2)}, u32[]{:S(2)}) %collective-permute-start.14) | collective-permute-done | bytes 262176 | tf_op jit(solution)/shard_map/ppermute | solution.py:386
  56.0 0.5 collective-permute-start.17
  56.5 0.0 collective-permute-done.13.refs_0_
  56.6 1.0 %collective-permute-done.15.refs_2_ = f32[2,16,16,128]{3,2,1,0:T(8,128)S(1)} collective-permute-done((f32[2,16,16,128]{3,2,1,0:T(8,128)S(1)}, f32[2,16,16,128]{3,2,1,0:T(8,128)S(1)}, u32[]{:S(2)}, u32[]{:S(2)}) %collective-permute-start.15) | collective-permute-done | bytes 262176 | tf_op jit(solution)/shard_map/ppermute | solution.py:386
  57.6 0.4 collective-permute-done.17.refs_4_
  57.9 2.9 %inverse.1 = f32[16,16,1024]{2,1,0:T(8,128)} custom-call(bf16[1024,1024]{1,0:T(8,128)(2,1)S(1)} %bitcast.8, bf16[1024,1024]{1,0:T(8,128)(2,1)S(1)} %bitcast.9, f32[2,16,16,128]{3,2,1,0:T(8,128)S(1)} %collective-permute-done.13.refs_0_, f32[2,16,16,128]{3,2,1,0:T(8,128)S(1)} %collective-permute-done.12.refs_1_, ...), custom_call_target="tpu_custom_call" | custom-call | tf_op jit(solution)/shard_map/inverse/pallas_call | solution.py:361
  (22 shorter events, 0.1 us)
Async XLA Ops:
  0.0 7.3 %copy-start.6 = (s32[16,64]{1,0:T(8,128)S(1)}, s32[16,64]{1,0:T(8,128)}, u32[]{:S(2)}) copy-start(s32[16,64]{1,0:T(8,128)} %param.16) | copy-start | bytes 12292
  0.0 7.3 %copy-start.7 = (s32[16,64]{1,0:T(8,128)S(1)}, s32[16,64]{1,0:T(8,128)}, u32[]{:S(2)}) copy-start(s32[16,64]{1,0:T(8,128)} %param.17) | copy-start | bytes 12292
  0.0 12.7 %collective-permute-start.5 = (bf16[512,4096]{1,0:T(8,128)(2,1)}, bf16[512,4096]{1,0:T(8,128)(2,1)}, u32[]{:S(2)}, u32[]{:S(2)}) collective-permute-start(bf16[512,4096]{1,0:T(8,128)(2,1)} %bitcast.14), channel_id=1, source_target_pairs={{0,1},{1,0},{2,3},{3,2},{4,5},{5,4},{6,7},{7,6},{8,9},{9,8},{10,11... | collective-permute-start | bytes 12582920 | tf_op jit(solution)/shard_map/ppermute | solution.py:386
  7.3 16.3 %copy-start.4 = (bf16[16,32,128]{2,1,0:T(8,128)(2,1)S(1)}, bf16[16,32,128]{2,1,0:T(8,128)(2,1)}, u32[]{:S(2)}) copy-start(bf16[16,32,128]{2,1,0:T(8,128)(2,1)} %get-tuple-element.38.refs_0_) | copy-start | bytes 393220
  7.4 5.2 %collective-permute-start.11 = (s32[16,64]{1,0:T(8,128)S(1)}, s32[16,64]{1,0:T(8,128)S(1)}, u32[]{:S(2)}, u32[]{:S(2)}) collective-permute-start(s32[16,64]{1,0:T(8,128)S(1)} %fusion.3), channel_id=1, source_target_pairs={{0,4},{4,0},{8,12},{12,8},{16,20},{20,16},{24,28},{28,24},{1,5},{5... | collective-permute-start | bytes 12296 | tf_op jit(solution)/shard_map/ppermute | solution.py:406
  9.0 13.1 %collective-permute-start = (bf16[16,32,128]{2,1,0:T(8,128)(2,1)}, bf16[16,32,128]{2,1,0:T(8,128)(2,1)S(1)}, u32[]{:S(2)}, u32[]{:S(2)}) collective-permute-start(bf16[16,32,128]{2,1,0:T(8,128)(2,1)} %get-tuple-element.39), channel_id=1, source_target_pairs={{0,2},{1,3},{2,0},{3,1},{4,6},{5,7},{6,4},{7,5},{8,10},{9,11},{10,... | collective-permute-start | bytes 393224 | tf_op jit(solution)/shard_map/ppermute | solution.py:386
  10.5 13.2 %collective-permute-start.1 = (bf16[16,32,128]{2,1,0:T(8,128)(2,1)}, bf16[16,32,128]{2,1,0:T(8,128)(2,1)S(1)}, u32[]{:S(2)}, u32[]{:S(2)}) collective-permute-start(bf16[16,32,128]{2,1,0:T(8,128)(2,1)} %get-tuple-element.40), channel_id=1, source_target_pairs={{0,4},{1,5},{2,6},{3,7},{4,0},{5,1},{6,2},{7,3},{8,12},{9,13},{10,... | collective-permute-start | bytes 393224 | tf_op jit(solution)/shard_map/ppermute | solution.py:386
  11.0 12.7 %collective-permute-start.2 = (bf16[16,32,128]{2,1,0:T(8,128)(2,1)}, bf16[16,32,128]{2,1,0:T(8,128)(2,1)S(1)}, u32[]{:S(2)}, u32[]{:S(2)}) collective-permute-start(bf16[16,32,128]{2,1,0:T(8,128)(2,1)} %get-tuple-element.41), channel_id=1, source_target_pairs={{0,6},{1,7},{2,4},{3,5},{4,2},{5,3},{6,0},{7,1},{8,14},{9,15},{10,... | collective-permute-start | bytes 393224 | tf_op jit(solution)/shard_map/ppermute | solution.py:386
  20.1 9.2 %copy-start.5 = (bf16[16,32,128]{2,1,0:T(8,128)(2,1)S(1)}, bf16[16,32,128]{2,1,0:T(8,128)(2,1)}, u32[]{:S(2)}) copy-start(bf16[16,32,128]{2,1,0:T(8,128)(2,1)} %get-tuple-element.45.refs_0_) | copy-start | bytes 393220
  20.1 8.7 %collective-permute-start.6 = (bf16[16,32,128]{2,1,0:T(8,128)(2,1)}, bf16[16,32,128]{2,1,0:T(8,128)(2,1)S(1)}, u32[]{:S(2)}, u32[]{:S(2)}) collective-permute-start(bf16[16,32,128]{2,1,0:T(8,128)(2,1)} %get-tuple-element.46), channel_id=1, source_target_pairs={{0,2},{1,3},{2,0},{3,1},{4,6},{5,7},{6,4},{7,5},{8,10},{9,11},{10,... | collective-permute-start | bytes 393224 | tf_op jit(solution)/shard_map/ppermute | solution.py:386
  21.6 7.6 %collective-permute-start.7 = (bf16[16,32,128]{2,1,0:T(8,128)(2,1)}, bf16[16,32,128]{2,1,0:T(8,128)(2,1)S(1)}, u32[]{:S(2)}, u32[]{:S(2)}) collective-permute-start(bf16[16,32,128]{2,1,0:T(8,128)(2,1)} %get-tuple-element.47), channel_id=1, source_target_pairs={{0,4},{1,5},{2,6},{3,7},{4,0},{5,1},{6,2},{7,3},{8,12},{9,13},{10,... | collective-permute-start | bytes 393224 | tf_op jit(solution)/shard_map/ppermute | solution.py:386
  22.1 7.1 %collective-permute-start.8 = (bf16[16,32,128]{2,1,0:T(8,128)(2,1)}, bf16[16,32,128]{2,1,0:T(8,128)(2,1)S(1)}, u32[]{:S(2)}, u32[]{:S(2)}) collective-permute-start(bf16[16,32,128]{2,1,0:T(8,128)(2,1)} %get-tuple-element.48), channel_id=1, source_target_pairs={{0,6},{1,7},{2,4},{3,5},{4,2},{5,3},{6,0},{7,1},{8,14},{9,15},{10,... | collective-permute-start | bytes 393224 | tf_op jit(solution)/shard_map/ppermute | solution.py:386
  25.2 9.8 %collective-permute-start.3 = (bf16[64,16,128]{2,1,0:T(8,128)(2,1)S(1)}, bf16[64,16,128]{2,1,0:T(8,128)(2,1)S(1)}, u32[]{:S(2)}, u32[]{:S(2)}) collective-permute-start(bf16[64,16,128]{2,1,0:T(8,128)(2,1)S(1)} %get-tuple-element.42.refs_0_), channel_id=1, source_target_pairs={{0,8},{4,12},{8,0},{12,4},{16,24},{20,28},{24,16},{28,20},{1,9},{5... | collective-permute-start | bytes 786440 | tf_op jit(solution)/shard_map/ppermute | solution.py:426
  26.8 10.4 %collective-permute-start.4 = (bf16[64,16,128]{2,1,0:T(8,128)(2,1)S(1)}, bf16[64,16,128]{2,1,0:T(8,128)(2,1)S(1)}, u32[]{:S(2)}, u32[]{:S(2)}) collective-permute-start(bf16[64,16,128]{2,1,0:T(8,128)(2,1)S(1)} %get-tuple-element.43.refs_1_), channel_id=1, source_target_pairs={{8,16},{12,20},{16,8},{20,12},{9,17},{13,21},{17,9},{21,13},{10,18... | collective-permute-start | bytes 786440 | tf_op jit(solution)/shard_map/ppermute | solution.py:426
  29.2 17.7 %copy-start = (f32[64,1024]{1,0:T(8,128)S(1)}, f32[64,1024]{1,0:T(8,128)}, u32[]{:S(2)}) copy-start(f32[64,1024]{1,0:T(8,128)} %constant.119.clone.cos_ref) | copy-start | bytes 786436
  29.2 17.7 %copy-start.2 = (f32[8,1024]{1,0:T(8,128)S(1)}, f32[8,1024]{1,0:T(8,128)}, u32[]{:S(2)}) copy-start(f32[8,1024]{1,0:T(8,128)} %constant.121.clone.cos0_ref) | copy-start | bytes 98308
  29.2 17.7 %copy-start.3 = (f32[8,1024]{1,0:T(8,128)S(1)}, f32[8,1024]{1,0:T(8,128)}, u32[]{:S(2)}) copy-start(f32[8,1024]{1,0:T(8,128)} %constant.122.clone.msin0_ref) | copy-start | bytes 98308
  30.8 10.0 %collective-permute-start.10 = (bf16[64,16,128]{2,1,0:T(8,128)(2,1)S(1)}, bf16[64,16,128]{2,1,0:T(8,128)(2,1)S(1)}, u32[]{:S(2)}, u32[]{:S(2)}) collective-permute-start(bf16[64,16,128]{2,1,0:T(8,128)(2,1)S(1)} %get-tuple-element.50.refs_6_), channel_id=1, source_target_pairs={{8,16},{12,20},{16,8},{20,12},{9,17},{13,21},{17,9},{21,13},{10,18... | collective-permute-start | bytes 786440 | tf_op jit(solution)/shard_map/ppermute | solution.py:426
  34.5 6.4 %collective-permute-start.9 = (bf16[64,16,128]{2,1,0:T(8,128)(2,1)S(1)}, bf16[64,16,128]{2,1,0:T(8,128)(2,1)S(1)}, u32[]{:S(2)}, u32[]{:S(2)}) collective-permute-start(bf16[64,16,128]{2,1,0:T(8,128)(2,1)S(1)} %get-tuple-element.49.refs_5_), channel_id=1, source_target_pairs={{0,8},{4,12},{8,0},{12,4},{16,24},{20,28},{24,16},{28,20},{1,9},{5... | collective-permute-start | bytes 786440 | tf_op jit(solution)/shard_map/ppermute | solution.py:426
  34.7 12.2 %copy-start.1 = (f32[64,1024]{1,0:T(8,128)S(1)}, f32[64,1024]{1,0:T(8,128)}, u32[]{:S(2)}) copy-start(f32[64,1024]{1,0:T(8,128)} %constant.120.clone.msin_ref) | copy-start | bytes 786436
  43.4 9.9 %collective-permute-start.12 = (f32[2,16,16,128]{3,2,1,0:T(8,128)S(1)}, f32[2,16,16,128]{3,2,1,0:T(8,128)S(1)}, u32[]{:S(2)}, u32[]{:S(2)}) collective-permute-start(f32[2,16,16,128]{3,2,1,0:T(8,128)S(1)} %get-tuple-element.54), channel_id=1, source_target_pairs={{0,6},{1,7},{2,4},{3,5},{4,2},{5,3},{6,0},{7,1},{8,14},{9,15},{10,... | collective-permute-start | bytes 786440 | tf_op jit(solution)/shard_map/ppermute | solution.py:386
  44.8 11.2 %collective-permute-start.14 = (f32[2,16,16,128]{3,2,1,0:T(8,128)S(1)}, f32[2,16,16,128]{3,2,1,0:T(8,128)S(1)}, u32[]{:S(2)}, u32[]{:S(2)}) collective-permute-start(f32[2,16,16,128]{3,2,1,0:T(8,128)S(1)} %get-tuple-element.60), channel_id=1, source_target_pairs={{0,4},{1,5},{2,6},{3,7},{4,0},{5,1},{6,2},{7,3},{8,12},{9,13},{10,... | collective-permute-start | bytes 786440 | tf_op jit(solution)/shard_map/ppermute | solution.py:386
  46.3 9.7 %collective-permute-start.16 = (f32[2,16,16,128]{3,2,1,0:T(8,128)S(1)}, f32[2,16,16,128]{3,2,1,0:T(8,128)S(1)}, u32[]{:S(2)}, u32[]{:S(2)}) collective-permute-start(f32[2,16,16,128]{3,2,1,0:T(8,128)S(1)} %get-tuple-element.61), channel_id=1, source_target_pairs={{0,2},{1,3},{2,0},{3,1},{4,6},{5,7},{6,4},{7,5},{8,10},{9,11},{10,... | collective-permute-start | bytes 786440 | tf_op jit(solution)/shard_map/ppermute | solution.py:386
  48.0 8.6 %collective-permute-start.18 = (f32[2,16,16,128]{3,2,1,0:T(8,128)S(1)}, f32[2,16,16,128]{3,2,1,0:T(8,128)S(1)}, u32[]{:S(2)}, u32[]{:S(2)}) collective-permute-start(f32[2,16,16,128]{3,2,1,0:T(8,128)S(1)} %get-tuple-element.62.refs_7_), channel_id=1, source_target_pairs={{0,1},{1,0},{2,3},{3,2},{4,5},{5,4},{6,7},{7,6},{8,9},{9,8},{10,11... | collective-permute-start | bytes 786440 | tf_op jit(solution)/shard_map/ppermute | solution.py:386
  53.3 3.3 %collective-permute-start.13 = (f32[2,16,16,128]{3,2,1,0:T(8,128)S(1)}, f32[2,16,16,128]{3,2,1,0:T(8,128)S(1)}, u32[]{:S(2)}, u32[]{:S(2)}) collective-permute-start(f32[2,16,16,128]{3,2,1,0:T(8,128)S(1)} %collective-permute-done.12.refs_1_), channel_id=1, source_target_pairs={{0,1},{1,0},{2,3},{3,2},{4,5},{5,4},{6,7},{7,6},{8,9},{9,8},{10,11... | collective-permute-start | bytes 786440 | tf_op jit(solution)/shard_map/ppermute | solution.py:386
  56.0 1.5 %collective-permute-start.15 = (f32[2,16,16,128]{3,2,1,0:T(8,128)S(1)}, f32[2,16,16,128]{3,2,1,0:T(8,128)S(1)}, u32[]{:S(2)}, u32[]{:S(2)}) collective-permute-start(f32[2,16,16,128]{3,2,1,0:T(8,128)S(1)} %collective-permute-done.14.refs_3_), channel_id=1, source_target_pairs={{0,1},{1,0},{2,3},{3,2},{4,5},{5,4},{6,7},{7,6},{8,9},{9,8},{10,11... | collective-permute-start | bytes 786440 | tf_op jit(solution)/shard_map/ppermute | solution.py:386
  56.0 1.9 %collective-permute-start.17 = (f32[2,16,16,128]{3,2,1,0:T(8,128)S(1)}, f32[2,16,16,128]{3,2,1,0:T(8,128)S(1)}, u32[]{:S(2)}, u32[]{:S(2)}) collective-permute-start(f32[2,16,16,128]{3,2,1,0:T(8,128)S(1)} %collective-permute-done.16.refs_5_), channel_id=1, source_target_pairs={{0,1},{1,0},{2,3},{3,2},{4,5},{5,4},{6,7},{7,6},{8,9},{9,8},{10,11... | collective-permute-start | bytes 786440 | tf_op jit(solution)/shard_map/ppermute | solution.py:386
